TPU v7x, 32 devices: a whole 2x2x4 slice. The times are simulated.
32 devices in a mesh: groups: 2 (over y), row: 8 (over z, x), col: 2 (over core).
Axes of the slice: x: 2, y: 2, z: 4, core: 2. Of those that a mesh axis runs over, the one named last changes fastest.
Arguments:
- teacher: bfloat16 [16384, 4096], P(('groups', 'row'), 'col'), parts along dimension 0, may hold values from -6 to 6
- proj_weight: bfloat16 [4096, 512], P('col'), may hold values from -0.09375 to 0.09375
- student: bfloat16 [512, 32, 512], P(('groups', 'col'), 'row'), parts along dimension 0, may hold values from -6 to 6
- dw_kernel: float32 [7, 7, 512], replicated, may hold values from -2 to 2
- dw_bias: float32 [512], replicated, may hold values from -4 to 4
- norm_gain: float32 [512], replicated, may hold values from 0.1 to 1.9
- norm_bias: float32 [512], replicated, may hold values from -4 to 4
- w_in: bfloat16 [512, 2048], replicated, may hold values from -0.25 to 0.25
- b_in: float32 [2048], replicated, may hold values from -4 to 4
- w_out: bfloat16 [2048, 512], replicated, may hold values from -0.125 to 0.125
- b_out: float32 [512], replicated, may hold values from -4 to 4
- layer_scale: float32 [512], replicated, may hold values from 0.25 to 1
Outputs:
- student_grad: float32 [512, 32, 512], P(('groups', 'col'), 'row'), parts along dimension 0
There are 2 independent parts, one for each index of `groups`. A program takes and returns all parts, laid end to end along the dimension named above; an argument that names none is the same for every part. Nothing has to cross between parts.
All inputs are finite; a program needn't handle non-finite values.
Results may differ from a plain program's by a relative error of at most 0.0044.
Values may be sent and summed in bfloat16 or wider, within the bound.
No kernel may reach another device: no remote copies, remote signals or barrier semaphores. Data moves between devices by JAX's collectives and lax.ppermute only.
A program may use at most 64 MiB of HBM per device.

v0:
```python
import jax
import jax.numpy as jnp
from jax import lax
from jax.sharding import PartitionSpec as P

NORM_EPSILON = 1e-06


def with_halo(block, sides, width):
    for axis, dim in sides:
        count = lax.axis_size(axis)
        forward = [(i, i + 1) for i in range(count - 1)]
        backward = [(target, source) for source, target in forward]
        low = lax.ppermute(
            lax.slice_in_dim(block, block.shape[dim] - width, None, axis=dim), axis, forward
        )
        high = lax.ppermute(lax.slice_in_dim(block, 0, width, axis=dim), axis, backward)
        block = jnp.concatenate([low, block, high], axis=dim)
    return block


def depthwise(padded, kernel, out_rows, out_cols):
    summed = jnp.zeros((out_rows, out_cols, padded.shape[2]), jnp.float32)
    for row_tap in range(7):
        for col_tap in range(7):
            window = padded[row_tap : row_tap + out_rows, col_tap : col_tap + out_cols].astype(
                jnp.float32
            )
            summed = summed + kernel[row_tap, col_tap] * window
    return summed


def gelu_slope(values):
    return (
        0.5 * (1.0 + lax.erf(values * 0.7071067811865476))
        + values * jnp.exp(-0.5 * values * values) * 0.3989422804014327
    )


def on_device(
    teacher,
    proj_weight,
    student,
    dw_kernel,
    dw_bias,
    norm_gain,
    norm_bias,
    w_in,
    b_in,
    w_out,
    b_out,
    layer_scale,
):
    row_count = lax.axis_size("row")
    tile_v, tile_u, channels = student.shape
    grid_u = tile_u * row_count
    local_lines = teacher.shape[0] // grid_u
    raw_tokens = teacher.reshape(local_lines, grid_u, teacher.shape[1])
    arrived = lax.all_to_all(raw_tokens, "row", split_axis=1, concat_axis=0, tiled=True)
    partial_value = jnp.dot(
        arrived.reshape(-1, arrived.shape[2]), proj_weight, preferred_element_type=jnp.float32
    )
    partial_value = partial_value.reshape(arrived.shape[0], tile_u, channels)
    target = lax.psum_scatter(partial_value, "col", scatter_dimension=0, tiled=True).astype(
        jnp.bfloat16
    )
    padded = with_halo(student, (("row", 1), ("col", 0)), 3)
    conv_out = depthwise(padded, dw_kernel, tile_v, tile_u) + dw_bias
    mean_val = jnp.mean(conv_out, axis=-1, keepdims=True)
    centred = conv_out - mean_val
    variance = jnp.mean(centred * centred, axis=-1, keepdims=True)
    inv_scale = lax.rsqrt(variance + NORM_EPSILON)
    normal_form = centred * inv_scale
    normed = (normal_form * norm_gain + norm_bias).astype(jnp.bfloat16).reshape(-1, channels)
    hidden_pre = jnp.dot(normed, w_in, preferred_element_type=jnp.float32) + b_in
    activated = jax.nn.gelu(hidden_pre, approximate=False).astype(jnp.bfloat16)
    branch = jnp.dot(activated, w_out, preferred_element_type=jnp.float32) + b_out
    branch = branch.reshape(tile_v, tile_u, channels)
    mismatch = student.astype(jnp.float32) + layer_scale * branch - target.astype(jnp.float32)
    d_branch = (layer_scale * mismatch).astype(jnp.bfloat16).reshape(-1, channels)
    d_activated = jnp.dot(d_branch, w_out.T, preferred_element_type=jnp.float32)
    d_hidden = (d_activated * gelu_slope(hidden_pre)).astype(jnp.bfloat16)
    d_normed = jnp.dot(d_hidden, w_in.T, preferred_element_type=jnp.float32).reshape(
        tile_v, tile_u, channels
    )
    scaled = d_normed * norm_gain
    d_conv_out = inv_scale * (
        scaled
        - jnp.mean(scaled, axis=-1, keepdims=True)
        - normal_form * jnp.mean(scaled * normal_form, axis=-1, keepdims=True)
    )
    d_padded = with_halo(d_conv_out, (("row", 1), ("col", 0)), 3)
    return mismatch + depthwise(d_padded, dw_kernel[::-1, ::-1], tile_v, tile_u)


def solution(mesh):
    placed = (
        P(("groups", "row"), "col"),
        P("col", None),
        P(("groups", "col"), "row", None),
        P(),
        P(),
        P(),
        P(),
        P(),
        P(),
        P(),
        P(),
        P(),
    )
    return jax.shard_map(
        on_device,
        mesh=mesh,
        in_specs=placed,
        out_specs=P(("groups", "col"), "row", None),
        check_vma=False,
    )
```

profile of v0, /device:TPU:13, one launch (start us, length us, event | category | flops | bytes accessed | tf_op | source)
XLA Modules:
  0.0 257.3 jit_solution(15804994926780199484)
XLA Ops:
  6.5 6.7 %copy.56 = bf16[32,32,2048]{2,0,1:T(8,128)(2,1)} copy(bf16[32,32,2048]{2,1,0:T(8,128)(2,1)} %bitcast.64) | data formatting | bytes 8388608 | tf_op jit(solution)/shard_map/reshape | solution.py:58
  13.2 5.8 %all-to-all-start = ((bf16[32,32,2048]{2,0,1:T(8,128)(2,1)}), bf16[32,32,2048]{2,0,1:T(8,128)(2,1)}, u32[]{:S(2)}, u32[]{:S(2)}) async-start(bf16[32,32,2048]{2,0,1:T(8,128)(2,1)} %copy.56), calls=%async_computation | async-start | bytes 8388608 | tf_op jit(solution)/shard_map/all_to_all | solution.py:59
  19.5 3.1 %collective-permute-start = (bf16[128,3,512]{2,0,1:T(8,128)(2,1)S(1)}, bf16[128,3,512]{2,0,1:T(8,128)(2,1)S(1)}, u32[]{:S(2)}, u32[]{:S(2)}) collective-permute-start(bf16[128,3,512]{2,0,1:T(8,128)(2,1)S(1)} %copy.80), channel_id=1, source_target_pairs={{0,2},{2,4},{4,6},{6,8},{8,10},{10,12},{12,14},{1,3},{3,5},{5,7},{... | collective-permute-start | bytes 1179656 | tf_op jit(solution)/shard_map/ppermute | solution.py:14
  22.7 3.1 %collective-permute-start.1 = (bf16[128,3,512]{2,0,1:T(8,128)(2,1)S(1)}, bf16[128,3,512]{2,0,1:T(8,128)(2,1)S(1)}, u32[]{:S(2)}, u32[]{:S(2)}) collective-permute-start(bf16[128,3,512]{2,0,1:T(8,128)(2,1)S(1)} %copy.81), channel_id=1, source_target_pairs={{2,0},{4,2},{6,4},{8,6},{10,8},{12,10},{14,12},{3,1},{5,3},{7,5},{... | collective-permute-start | bytes 1179656 | tf_op jit(solution)/shard_map/ppermute | solution.py:17
  25.9 75.9 %collective-permute-done = bf16[128,3,512]{2,0,1:T(8,128)(2,1)S(1)} collective-permute-done((bf16[128,3,512]{2,0,1:T(8,128)(2,1)S(1)}, bf16[128,3,512]{2,0,1:T(8,128)(2,1)S(1)}, u32[]{:S(2)}, u32[]{:S(2)}) %collective-permute-start) | collective-permute-done | bytes 393248 | tf_op jit(solution)/shard_map/ppermute | solution.py:14
  104.7 1.1 copy-done.7
  105.8 5.5 %collective-permute-start.3 = (bf16[3,10,512]{2,0,1:T(4,128)(2,1)S(1)}, bf16[3,10,512]{2,0,1:T(4,128)(2,1)S(1)}, u32[]{:S(2)}, u32[]{:S(2)}) collective-permute-start(bf16[3,10,512]{2,0,1:T(4,128)(2,1)S(1)} %get-tuple-element.12), channel_id=1, source_target_pairs={{1,0},{3,2},{5,4},{7,6},{9,8},{11,10},{13,12},{15,14},{17,16},{19,... | collective-permute-start | bytes 92168 | tf_op jit(solution)/shard_map/ppermute | solution.py:17
  111.3 1.3 collective-permute-start.2
  112.7 2.6 %copy.57 = bf16[8,32,4,2048]{3,1,0,2:T(8,128)(2,1)S(1)} copy(bf16[8,32,4,2048]{3,1,2,0:T(8,128)(2,1)} %bitcast.51) | data formatting | bytes 8388608 | tf_op jit(solution)/shard_map/all_to_all | solution.py:59
  115.5 3.7 %fusion.16 = f32[256,4,512]{2,0,1:T(8,128)} fusion(bf16[256,4,2048]{2,0,1:T(8,128)(2,1)S(1)} %bitcast.65, bf16[2048,512]{1,0:T(8,128)(2,1)S(1)} %copy-done.13), kind=kOutput, calls=%fused_computation.76 | convolution fusion | flops 2147483648 | bytes 8388608 | tf_op jit(solution)/shard_map/dot_general | solution.py:60
  119.3 21.4 %fusion.185 = (f32[128,4]{0,1:T(4,128)S(1)}, f32[128,4,512]{2,0,1:T(8,128)S(1)}) fusion(f32[512]{0:T(512)S(1)} %copy-done.11, bf16[3,10,512]{2,0,1:T(4,128)(2,1)S(1)} %collective-permute-done.3, bf16[128,10,512]{2,0,1:T(8,128)(2,1)} %copy-done.7, f32[512]{0:T(512)S(1)} %bitcast.122, f32[512]{0:T(512)S(1)} %bitcast.124, f32[512]{0:T(512)S(1)} %bitcast.68, ...), kind=kLoop, calls=%fused_computation.343 | loop fusion | flops 71826944 | bytes 6195200 | tf_op jit(solution)/shard_map/reduce_sum | solution.py:69
  141.2 1.2 copy.54
  142.4 2.0 reshape.52
  144.5 2.4 fusion.193
  146.9 1.9 copy-done.6
  148.9 10.1 %fusion.20 = f32[512,512]{1,0:T(8,128)} fusion(bf16[2048,512]{1,0:T(8,128)(2,1)S(1)} %copy-done.14, f32[512,2048]{1,0:T(8,128)S(1)} %fusion.193, f32[2048]{0:T(1024)S(1)} %copy-done.15, f32[512]{0:T(512)S(1)} %copy-done.16), kind=kOutput, calls=%fused_computation.79 | convolution fusion | flops 1143209984 | bytes 7350272 | tf_op jit(solution)/shard_map/dot_general | solution.py:77
  159.0 2.6 %reshape.53 = f32[128,4,512]{2,1,0:T(4,128)} reshape(f32[512,512]{1,0:T(8,128)} %fusion.20) | data formatting | bytes 2097152 | tf_op jit(solution)/shard_map/reshape | solution.py:78
  161.6 2.1 multiply_convert_fusion
  163.7 1.2 copy.58
  164.9 2.0 reshape.55
  166.9 7.0 %multiply_reduce_fusion.1 = (f32[512]{0:T(512)S(1)}, f32[512,512]{1,0:T(8,128)}) fusion(f32[512]{0:T(512)S(1)} %copy-done.9, bf16[512,2048]{1,0:T(8,128)(2,1)S(1)} %copy-done, f32[512,2048]{1,0:T(8,128)} %copy-done.6, bf16[512,512]{1,0:T(8,128)(2,1)} %reshape.55, bf16[2048,512]{1,0:T(8,128)(2,1)} %param.21, f32[2048]{0:T(1024)S(1)} %copy-done.15), kind=kOutput, calls=%fused_computation.216 | convolution fusion | flops 2159541760 | bytes 9973760 | tf_op jit(solution)/shard_map/dot_general | solution.py:83
  173.9 2.5 reshape.56
  176.5 1.7 multiply_reduce_fusion
  178.3 1.7 subtract_multiply_fusion
  180.2 8.9 %collective-permute-start.5 = (f32[128,3,512]{2,0,1:T(8,128)S(1)}, f32[128,3,512]{2,0,1:T(8,128)S(1)}, u32[]{:S(2)}, u32[]{:S(2)}) collective-permute-start(f32[128,3,512]{2,0,1:T(8,128)S(1)} %get-tuple-element.14), channel_id=1, source_target_pairs={{2,0},{4,2},{6,4},{8,6},{10,8},{12,10},{14,12},{3,1},{5,3},{7,5},{... | collective-permute-start | bytes 2359304 | tf_op jit(solution)/shard_map/ppermute | solution.py:17
  189.1 9.1 %collective-permute-start.4 = (f32[128,3,512]{2,0,1:T(8,128)S(1)}, f32[128,3,512]{2,0,1:T(8,128)S(1)}, u32[]{:S(2)}, u32[]{:S(2)}) collective-permute-start(f32[128,3,512]{2,0,1:T(8,128)S(1)} %get-tuple-element.13), channel_id=1, source_target_pairs={{0,2},{2,4},{4,6},{6,8},{8,10},{10,12},{12,14},{1,3},{3,5},{5,7},{... | collective-permute-start | bytes 2359304 | tf_op jit(solution)/shard_map/ppermute | solution.py:14
  198.2 30.0 %collective-permute-done.5 = f32[128,3,512]{2,0,1:T(8,128)S(1)} collective-permute-done((f32[128,3,512]{2,0,1:T(8,128)S(1)}, f32[128,3,512]{2,0,1:T(8,128)S(1)}, u32[]{:S(2)}, u32[]{:S(2)}) %collective-permute-start.5) | collective-permute-done | bytes 786464 | tf_op jit(solution)/shard_map/ppermute | solution.py:17
  228.2 3.8 %collective-permute-done.4 = f32[128,3,512]{2,0,1:T(8,128)S(1)} collective-permute-done((f32[128,3,512]{2,0,1:T(8,128)S(1)}, f32[128,3,512]{2,0,1:T(8,128)S(1)}, u32[]{:S(2)}, u32[]{:S(2)}) %collective-permute-start.4) | collective-permute-done | bytes 786464 | tf_op jit(solution)/shard_map/ppermute | solution.py:14
  232.1 1.4 collective-permute-start.6
  233.5 3.0 %collective-permute-start.7 = (f32[3,10,512]{2,0,1:T(4,128)S(1)}, f32[3,10,512]{2,0,1:T(4,128)S(1)}, u32[]{:S(2)}, u32[]{:S(2)}) collective-permute-start(f32[3,10,512]{2,0,1:T(4,128)S(1)} %get-tuple-element.10), channel_id=1, source_target_pairs={{1,0},{3,2},{5,4},{7,6},{9,8},{11,10},{13,12},{15,14},{17,16},{19,... | collective-permute-start | bytes 184328 | tf_op jit(solution)/shard_map/ppermute | solution.py:17
  238.6 10.3 %fusion.85 = f32[128,4,512]{2,0,1:T(8,128)S(1)} fusion(f32[131,10,512]{2,0,1:T(8,128)S(1)} %get-tuple-element.8, f32[128,3,512]{2,0,1:T(8,128)S(1)} %collective-permute-done.5, f32[128,4,512]{2,0,1:T(8,128)S(1)} %subtract_multiply_fusion, f32[128,3,512]{2,0,1:T(8,128)S(1)} %collective-permute-done.4, f32[131,10,512]{2,0,1:T(8,128)S(1)} %get-tuple-element.7, ...), kind=kLoop, calls=%fused_computation.145 | loop fusion | flops 28835840 | bytes 50434048 | tf_op jit(solution)/shard_map/add | solution.py:93
  248.9 1.6 copy.61
  (62 shorter events, 6.6 us)
Async XLA Ops:
  6.5 137.9 %copy-start = (bf16[512,2048]{1,0:T(8,128)(2,1)S(1)}, bf16[512,2048]{1,0:T(8,128)(2,1)}, u32[]{:S(2)}) copy-start(bf16[512,2048]{1,0:T(8,128)(2,1)} %param.19) | copy-start | bytes 6291460
  13.2 5.8 %copy-start.1 = (bf16[128,4,512]{2,1,0:T(4,128)(2,1)S(1)}, bf16[128,4,512]{2,1,0:T(4,128)(2,1)}, u32[]{:S(2)}) copy-start(bf16[128,4,512]{2,1,0:T(4,128)(2,1)} %param.14) | copy-start | bytes 1572868
  13.2 12.6 %copy-start.8 = (f32[7,7,512]{2,1,0:T(8,128)S(1)}, f32[7,7,512]{2,1,0:T(8,128)}, u32[]{:S(2)}) copy-start(f32[7,7,512]{2,1,0:T(8,128)} %param.15) | copy-start | bytes 301060
  13.2 99.4 %all-to-all-start = ((bf16[32,32,2048]{2,0,1:T(8,128)(2,1)}), bf16[32,32,2048]{2,0,1:T(8,128)(2,1)}, u32[]{:S(2)}, u32[]{:S(2)}) async-start(bf16[32,32,2048]{2,0,1:T(8,128)(2,1)} %copy.56), calls=%async_computation | async-start | bytes 8388608 | tf_op jit(solution)/shard_map/all_to_all | solution.py:59
  19.0 142.6 %reduce-scatter.2.cloned.1.call-start = ((), (), s32[]{:S(2)}) async-start(), calls=%async_computation.2 | async-start | bytes 3145728 | tf_op jit(solution)/shard_map/reduce_scatter | solution.py:64
  19.5 82.4 %collective-permute-start = (bf16[128,3,512]{2,0,1:T(8,128)(2,1)S(1)}, bf16[128,3,512]{2,0,1:T(8,128)(2,1)S(1)}, u32[]{:S(2)}, u32[]{:S(2)}) collective-permute-start(bf16[128,3,512]{2,0,1:T(8,128)(2,1)S(1)} %copy.80), channel_id=1, source_target_pairs={{0,2},{2,4},{4,6},{6,8},{8,10},{10,12},{12,14},{1,3},{3,5},{5,7},{... | collective-permute-start | bytes 1179656 | tf_op jit(solution)/shard_map/ppermute | solution.py:14
  22.7 81.1 %collective-permute-start.1 = (bf16[128,3,512]{2,0,1:T(8,128)(2,1)S(1)}, bf16[128,3,512]{2,0,1:T(8,128)(2,1)S(1)}, u32[]{:S(2)}, u32[]{:S(2)}) collective-permute-start(bf16[128,3,512]{2,0,1:T(8,128)(2,1)S(1)} %copy.81), channel_id=1, source_target_pairs={{2,0},{4,2},{6,4},{8,6},{10,8},{12,10},{14,12},{3,1},{5,3},{7,5},{... | collective-permute-start | bytes 1179656 | tf_op jit(solution)/shard_map/ppermute | solution.py:17
  102.9 0.9 copy-start.4
  104.7 1.1 copy-start.7
  105.8 13.4 %collective-permute-start.3 = (bf16[3,10,512]{2,0,1:T(4,128)(2,1)S(1)}, bf16[3,10,512]{2,0,1:T(4,128)(2,1)S(1)}, u32[]{:S(2)}, u32[]{:S(2)}) collective-permute-start(bf16[3,10,512]{2,0,1:T(4,128)(2,1)S(1)} %get-tuple-element.12), channel_id=1, source_target_pairs={{1,0},{3,2},{5,4},{7,6},{9,8},{11,10},{13,12},{15,14},{17,16},{19,... | collective-permute-start | bytes 92168 | tf_op jit(solution)/shard_map/ppermute | solution.py:17
  111.3 7.9 %collective-permute-start.2 = (bf16[3,10,512]{2,0,1:T(4,128)(2,1)S(1)}, bf16[3,10,512]{2,0,1:T(4,128)(2,1)S(1)}, u32[]{:S(2)}, u32[]{:S(2)}) collective-permute-start(bf16[3,10,512]{2,0,1:T(4,128)(2,1)S(1)} %get-tuple-element.11), channel_id=1, source_target_pairs={{0,1},{2,3},{4,5},{6,7},{8,9},{10,11},{12,13},{14,15},{16,17},{18,... | collective-permute-start | bytes 92168 | tf_op jit(solution)/shard_map/ppermute | solution.py:14
  112.7 2.9 %copy-start.13 = (bf16[2048,512]{1,0:T(8,128)(2,1)S(1)}, bf16[2048,512]{1,0:T(8,128)(2,1)}, u32[]{:S(2)}) copy-start(bf16[2048,512]{1,0:T(8,128)(2,1)} %param.13) | copy-start | bytes 6291460
  115.5 3.8 %copy-start.11 = (f32[512]{0:T(512)S(1)}, f32[512]{0:T(512)}, u32[]{:S(2)}) copy-start(f32[512]{0:T(512)} %param.16) | copy-start | bytes 6148
  119.2 21.7 %copy-start.9 = (f32[512]{0:T(512)S(1)}, f32[512]{0:T(512)}, u32[]{:S(2)}) copy-start(f32[512]{0:T(512)} %param.17) | copy-start | bytes 6148
  119.2 21.7 %copy-start.12 = (f32[512]{0:T(512)S(1)}, f32[512]{0:T(512)}, u32[]{:S(2)}) copy-start(f32[512]{0:T(512)} %param.18) | copy-start | bytes 6148
  142.4 6.4 %copy-start.15 = (f32[2048]{0:T(1024)S(1)}, f32[2048]{0:T(1024)}, u32[]{:S(2)}) copy-start(f32[2048]{0:T(1024)} %param.20) | copy-start | bytes 24580
  142.4 6.4 %copy-start.16 = (f32[512]{0:T(512)S(1)}, f32[512]{0:T(512)}, u32[]{:S(2)}) copy-start(f32[512]{0:T(512)} %param.22) | copy-start | bytes 6148
  144.5 4.4 %copy-start.14 = (bf16[2048,512]{1,0:T(8,128)(2,1)S(1)}, bf16[2048,512]{1,0:T(8,128)(2,1)}, u32[]{:S(2)}) copy-start(bf16[2048,512]{1,0:T(8,128)(2,1)} %param.21) | copy-start | bytes 6291460
  146.9 1.9 copy-start.6
  148.9 12.7 %copy-start.10 = (f32[512]{0:T(512)S(1)}, f32[512]{0:T(512)}, u32[]{:S(2)}) copy-start(f32[512]{0:T(512)} %param.23) | copy-start | bytes 6148
  180.2 48.0 %collective-permute-start.5 = (f32[128,3,512]{2,0,1:T(8,128)S(1)}, f32[128,3,512]{2,0,1:T(8,128)S(1)}, u32[]{:S(2)}, u32[]{:S(2)}) collective-permute-start(f32[128,3,512]{2,0,1:T(8,128)S(1)} %get-tuple-element.14), channel_id=1, source_target_pairs={{2,0},{4,2},{6,4},{8,6},{10,8},{12,10},{14,12},{3,1},{5,3},{7,5},{... | collective-permute-start | bytes 2359304 | tf_op jit(solution)/shard_map/ppermute | solution.py:17
  189.1 42.9 %collective-permute-start.4 = (f32[128,3,512]{2,0,1:T(8,128)S(1)}, f32[128,3,512]{2,0,1:T(8,128)S(1)}, u32[]{:S(2)}, u32[]{:S(2)}) collective-permute-start(f32[128,3,512]{2,0,1:T(8,128)S(1)} %get-tuple-element.13), channel_id=1, source_target_pairs={{0,2},{2,4},{4,6},{6,8},{8,10},{10,12},{12,14},{1,3},{3,5},{5,7},{... | collective-permute-start | bytes 2359304 | tf_op jit(solution)/shard_map/ppermute | solution.py:14
  232.1 6.5 %copy-start.2 = (bf16[128,4,512]{2,1,0:T(4,128)(2,1)S(1)}, bf16[128,4,512]{2,1,0:T(4,128)(2,1)}, u32[]{:S(2)}) copy-start(bf16[128,4,512]{2,1,0:T(4,128)(2,1)} %param.14) | copy-start | bytes 1572868
  232.1 6.5 %copy-start.3 = (f32[128,4,512]{2,1,0:T(4,128)S(1)}, f32[128,4,512]{2,1,0:T(4,128)}, u32[]{:S(2)}) copy-start(f32[128,4,512]{2,1,0:T(4,128)} %reshape.53) | copy-start | bytes 3145732
  232.1 6.5 %copy-start.5 = (f32[128,4,512]{2,0,1:T(8,128)S(1)}, f32[128,4,512]{2,0,1:T(8,128)}, u32[]{:S(2)}) copy-start(f32[128,4,512]{2,0,1:T(8,128)} %reduce-scatter.2.cloned.1.call-done) | copy-start | bytes 3145732
  232.1 4.5 %collective-permute-start.6 = (f32[3,10,512]{2,0,1:T(4,128)S(1)}, f32[3,10,512]{2,0,1:T(4,128)S(1)}, u32[]{:S(2)}, u32[]{:S(2)}) collective-permute-start(f32[3,10,512]{2,0,1:T(4,128)S(1)} %get-tuple-element.9), channel_id=1, source_target_pairs={{0,1},{2,3},{4,5},{6,7},{8,9},{10,11},{12,13},{14,15},{16,17},{18,... | collective-permute-start | bytes 184328 | tf_op jit(solution)/shard_map/ppermute | solution.py:14
  233.5 3.9 %collective-permute-start.7 = (f32[3,10,512]{2,0,1:T(4,128)S(1)}, f32[3,10,512]{2,0,1:T(4,128)S(1)}, u32[]{:S(2)}, u32[]{:S(2)}) collective-permute-start(f32[3,10,512]{2,0,1:T(4,128)S(1)} %get-tuple-element.10), channel_id=1, source_target_pairs={{1,0},{3,2},{5,4},{7,6},{9,8},{11,10},{13,12},{15,14},{17,16},{19,... | collective-permute-start | bytes 184328 | tf_op jit(solution)/shard_map/ppermute | solution.py:17
Sparse Core Ops, SparseCore 0:
  119.3 24.7 reduce-scatter.1
where the time goes:
time: 259 us; the launch traced here: 257 us
  waiting for transfers between devices  111 us (43%)
  starting transfers between devices  41.3 us (16%)
  other arithmetic  38.8 us (15%)
  local copies, waits for them, and re-layouts  29.6 us (11%)
  matrix products  23.3 us (9%)
  between operations  13.8 us (5%)
    ppermute x4, waiting for transfers between devices, with_halo(): lax.ppermute(lax.slice_in_dim(block, block.shape[dim] - width, None, axis...  79.8 us
    ppermute x4, waiting for transfers between devices, with_halo(): lax.ppermute(lax.slice_in_dim(block, 0, width, axis=dim), axis, backward)  30.9 us
    reduce_sum x1, other arithmetic, on_device(): mean_val = jnp.mean(conv_out, axis=-1, keepdims=True)  21.4 us
    ppermute x4, starting transfers between devices, with_halo(): lax.ppermute(lax.slice_in_dim(block, 0, width, axis=dim), axis, backward)  20.5 us
    ppermute x4, starting transfers between devices, with_halo(): lax.ppermute(lax.slice_in_dim(block, block.shape[dim] - width, None, axis...  14.9 us
    add x1, other arithmetic, on_device(): return mismatch + depthwise(d_padded, dw_kernel[::-1, ::-1], tile_v, tile_u)  10.3 us
    dot_general x1, matrix products, on_device(): jnp.dot(activated, w_out, preferred_element_type=jnp.float32) + b_out  10.1 us
    dot_general x1, matrix products, on_device(): jnp.dot(d_hidden, w_in.T, preferred_element_type=jnp.float32)  7.03 us
  transfers between devices with their start and end apart: 10, of which 4 were waited for; matrix products, arithmetic and copies ran while one was open for 19% of the time, Pallas kernels for 0%

commit v1 on v0

v1 whole, which is shorter than its diff:
```python
import functools

import jax
import jax.numpy as jnp
from jax import lax
from jax.experimental import pallas as pl
from jax.experimental.pallas import tpu as pltpu
from jax.sharding import PartitionSpec as P

NORM_EPSILON = 1e-06
REACH = 3
TAPS = 2 * REACH + 1
LANES = 128
SUBLANES = 8
MLP_TILE = 256


def fill_padded(padded, parts):
    place = 0
    for part in parts:
        for u in range(part.shape[0]):
            for tile in range(padded.shape[0]):
                padded[tile, place] = part[u, :, tile * LANES : (tile + 1) * LANES].astype(
                    jnp.float32
                )
            place += 1


def depthwise(padded, taps, store, tile_u, tile_v, flip):
    tiles = padded.shape[0]
    blocks = tile_v // (2 * SUBLANES)

    def step(index, carry):
        tile = index // blocks
        base = (index % blocks) * (2 * SUBLANES)
        sums = [[None] * tile_u for _ in range(2)]
        for row_tap in range(TAPS):
            weights = []
            for col_tap in range(TAPS):
                tap = row_tap * TAPS + col_tap
                weights.append(taps[TAPS * TAPS - 1 - tap if flip else tap, tile])
            for source in range(tile_u + TAPS - 1):
                for half in range(2):
                    values = padded[
                        tile, source, pl.ds(base + half * SUBLANES + row_tap, SUBLANES), :
                    ]
                    for u in range(max(0, source - TAPS + 1), min(tile_u, source + 1)):
                        term = weights[source - u] * values
                        sums[half][u] = term if sums[half][u] is None else sums[half][u] + term
        for half in range(2):
            for u in range(tile_u):
                store(tile, u, base + half * SUBLANES, sums[half][u])
        return carry

    lax.fori_loop(0, tiles * blocks, step, 0)


def block_kernel(
    left,
    middle,
    right,
    taps,
    dw_bias,
    norm_gain,
    norm_bias,
    w_in,
    b_in,
    w_out,
    b_out,
    layer_scale,
    target,
    mismatch_out,
    d_conv_out,
    padded,
    normal_form,
    inv_scale,
    normed,
    activated,
    slope,
    d_branch,
    d_hidden,
    d_normed,
):
    tile_u, tile_v, channels = target.shape
    rows = tile_u * tile_v
    hidden = w_in.shape[1]
    fill_padded(padded, (left, middle, right))

    def store_conv(tile, u, base, value):
        row = pl.multiple_of(u * tile_v + base, SUBLANES)
        lane = pl.multiple_of(tile * LANES, LANES)
        normal_form[pl.ds(row, SUBLANES), pl.ds(lane, LANES)] = value

    depthwise(padded, taps, store_conv, tile_u, tile_v, False)

    chunk = 32

    def norm_step(index, carry):
        here = pl.ds(pl.multiple_of(index * chunk, chunk), chunk)
        conv = normal_form[here, :] + dw_bias[...]
        centred = conv - jnp.mean(conv, axis=-1, keepdims=True)
        variance = jnp.mean(centred * centred, axis=-1, keepdims=True)
        inverse = lax.rsqrt(variance + NORM_EPSILON)
        form = centred * inverse
        normal_form[here, :] = form
        inv_scale[here, :] = jnp.broadcast_to(inverse, (chunk, LANES))
        normed[here, :] = (form * norm_gain[...] + norm_bias[...]).astype(jnp.bfloat16)
        return carry

    lax.fori_loop(0, rows // chunk, norm_step, 0)

    half_rows = rows // 2

    def up_step(index, carry):
        here = pl.ds(pl.multiple_of((index % 2) * half_rows, half_rows), half_rows)
        tile = pl.ds(pl.multiple_of((index // 2) * MLP_TILE, MLP_TILE), MLP_TILE)
        pre = (
            jnp.dot(normed[here, :], w_in[:, tile], preferred_element_type=jnp.float32)
            + b_in[:, tile]
        )
        phi = 0.5 * (1.0 + lax.erf(pre * 0.7071067811865476))
        activated[here, tile] = (pre * phi).astype(jnp.bfloat16)
        slope[here, tile] = phi + pre * jnp.exp(-0.5 * pre * pre) * 0.3989422804014327
        return carry

    lax.fori_loop(0, 2 * (hidden // MLP_TILE), up_step, 0)

    def down_step(u, carry):
        here = pl.ds(pl.multiple_of(u * tile_v, tile_v), tile_v)
        branch = (
            jnp.dot(activated[here, :], w_out[...], preferred_element_type=jnp.float32)
            + b_out[...]
        )
        mismatch = (
            middle[u, REACH : REACH + tile_v, :].astype(jnp.float32)
            + layer_scale[...] * branch
            - target[u].astype(jnp.float32)
        )
        mismatch_out[u] = mismatch
        d_branch[here, :] = (layer_scale[...] * mismatch).astype(jnp.bfloat16)
        return carry

    lax.fori_loop(0, tile_u, down_step, 0)

    contract_last = (((1,), (1,)), ((), ()))

    def back_step(index, carry):
        here = pl.ds(pl.multiple_of((index % 2) * half_rows, half_rows), half_rows)
        tile = pl.ds(pl.multiple_of((index // 2) * MLP_TILE, MLP_TILE), MLP_TILE)
        d_activated = lax.dot_general(
            d_branch[here, :], w_out[tile, :], contract_last, preferred_element_type=jnp.float32
        )
        d_hidden[here, tile] = (d_activated * slope[here, tile]).astype(jnp.bfloat16)
        return carry

    lax.fori_loop(0, 2 * (hidden // MLP_TILE), back_step, 0)

    def in_step(u, carry):
        here = pl.ds(pl.multiple_of(u * tile_v, tile_v), tile_v)
        d_normed[here, :] = lax.dot_general(
            d_hidden[here, :], w_in[...], contract_last, preferred_element_type=jnp.float32
        )
        return carry

    lax.fori_loop(0, tile_u, in_step, 0)

    def d_norm_step(index, carry):
        here = pl.ds(pl.multiple_of(index * chunk, chunk), chunk)
        scaled = d_normed[here, :] * norm_gain[...]
        form = normal_form[here, :]
        d_conv = inv_scale[here, :1] * (
            scaled
            - jnp.mean(scaled, axis=-1, keepdims=True)
            - form * jnp.mean(scaled * form, axis=-1, keepdims=True)
        )
        d_conv_out[index // (tile_v // chunk), pl.ds(pl.multiple_of(
            (index % (tile_v // chunk)) * chunk, chunk), chunk), :] = d_conv.astype(jnp.bfloat16)
        return carry

    lax.fori_loop(0, rows // chunk, d_norm_step, 0)


def final_kernel(left, middle, right, taps, mismatch, out, padded):
    tile_u, tile_v, channels = mismatch.shape
    fill_padded(padded, (left, middle, right))

    def store_out(tile, u, base, value):
        here = pl.ds(pl.multiple_of(base, SUBLANES), SUBLANES)
        lanes = pl.ds(pl.multiple_of(tile * LANES, LANES), LANES)
        out[u, here, lanes] = mismatch[u, here, lanes] + value

    depthwise(padded, taps, store_out, tile_u, tile_v, True)


def in_vmem(count):
    return [pl.BlockSpec(memory_space=pltpu.VMEM)] * count


def with_halo(tile, core):
    row_count = lax.axis_size("row")
    tile_u, tile_v, channels = tile.shape
    own_edge = jnp.where(core == 0, tile[:, tile_v - REACH :], tile[:, :REACH])
    other_edge = lax.ppermute(own_edge, "col", [(0, 1), (1, 0)])
    nothing = jnp.zeros_like(other_edge)
    fill = -(tile_v + 2 * REACH) % SUBLANES
    extended = jnp.concatenate(
        [
            jnp.where(core == 1, other_edge, nothing),
            tile,
            jnp.where(core == 0, other_edge, nothing),
            jnp.zeros((tile_u, fill, channels), tile.dtype),
        ],
        axis=1,
    )
    forward = [(i, i + 1) for i in range(row_count - 1)]
    backward = [(b, a) for a, b in forward]
    left = lax.ppermute(extended[tile_u - REACH :], "row", forward)
    right = lax.ppermute(extended[:REACH], "row", backward)
    return left, extended, right


def find_target(teacher, proj_weight, core, tile_u):
    row_count = lax.axis_size("row")
    channels = proj_weight.shape[1]
    grid_u = tile_u * row_count
    lines = teacher.shape[0] // (2 * grid_u)
    tokens = lines * grid_u
    away = lax.dynamic_slice_in_dim(teacher, (1 - core) * tokens, tokens)
    sent = jnp.dot(away, proj_weight, preferred_element_type=jnp.float32)
    received = lax.ppermute(sent, "col", [(0, 1), (1, 0)])
    home = lax.dynamic_slice_in_dim(teacher, core * tokens, tokens)
    kept = jnp.dot(home, proj_weight, preferred_element_type=jnp.float32)
    summed = (kept + received).astype(jnp.bfloat16)
    by_u = summed.reshape(lines, row_count, tile_u, channels).transpose(1, 2, 0, 3)
    arrived = lax.all_to_all(by_u, "row", split_axis=0, concat_axis=0, tiled=True)
    halves = row_count // 2
    for_other = lax.dynamic_slice_in_dim(arrived, (1 - core) * halves, halves)
    mine = lax.dynamic_slice_in_dim(arrived, core * halves, halves)
    from_other = lax.ppermute(for_other, "col", [(0, 1), (1, 0)])
    first = jnp.where(core == 0, mine, from_other)
    second = jnp.where(core == 0, from_other, mine)
    both = jnp.stack([first, second], axis=1)
    return both.transpose(2, 0, 1, 3, 4).reshape(tile_u, halves * 2 * lines, channels)


def on_device(
    teacher,
    proj_weight,
    student,
    dw_kernel,
    dw_bias,
    norm_gain,
    norm_bias,
    w_in,
    b_in,
    w_out,
    b_out,
    layer_scale,
):
    core = lax.axis_index("col")
    tile_v, tile_u, channels = student.shape
    hidden = w_in.shape[1]
    rows = tile_u * tile_v
    tiles = channels // LANES
    halo = with_halo(student.transpose(1, 0, 2), core)
    target = find_target(teacher, proj_weight, core, tile_u)
    taps = jnp.broadcast_to(
        dw_kernel.reshape(TAPS * TAPS, tiles, 1, LANES), (TAPS * TAPS, tiles, SUBLANES, LANES)
    )
    padded = pltpu.VMEM((tiles, tile_u + 2 * REACH, halo[1].shape[1], LANES), jnp.float32)
    tile_shape = (tile_u, tile_v, channels)
    mismatch, d_conv = pl.pallas_call(
        block_kernel,
        out_shape=(
            jax.ShapeDtypeStruct(tile_shape, jnp.float32),
            jax.ShapeDtypeStruct(tile_shape, jnp.bfloat16),
        ),
        in_specs=in_vmem(13),
        out_specs=tuple(in_vmem(2)),
        scratch_shapes=[
            padded,
            pltpu.VMEM((rows, channels), jnp.float32),
            pltpu.VMEM((rows, LANES), jnp.float32),
            pltpu.VMEM((rows, channels), jnp.bfloat16),
            pltpu.VMEM((rows, hidden), jnp.bfloat16),
            pltpu.VMEM((rows, hidden), jnp.float32),
            pltpu.VMEM((rows, channels), jnp.bfloat16),
            pltpu.VMEM((rows, hidden), jnp.bfloat16),
            pltpu.VMEM((rows, channels), jnp.float32),
        ],
        compiler_params=pltpu.CompilerParams(vmem_limit_bytes=40 << 20),
        name="block",
    )(
        *halo,
        taps,
        dw_bias[None],
        norm_gain[None],
        norm_bias[None],
        w_in,
        b_in[None],
        w_out,
        b_out[None],
        layer_scale[None],
        target,
    )
    d_halo = with_halo(d_conv, core)
    grad = pl.pallas_call(
        final_kernel,
        out_shape=jax.ShapeDtypeStruct(tile_shape, jnp.float32),
        in_specs=in_vmem(5),
        out_specs=in_vmem(1)[0],
        scratch_shapes=[padded],
        compiler_params=pltpu.CompilerParams(vmem_limit_bytes=24 << 20),
        name="final",
    )(*d_halo, taps, mismatch)
    return grad.transpose(1, 0, 2)


def solution(mesh):
    placed = (
        P(("groups", "row"), "col"),
        P("col", None),
        P(("groups", "col"), "row", None),
        P(),
        P(),
        P(),
        P(),
        P(),
        P(),
        P(),
        P(),
        P(),
    )
    return jax.shard_map(
        on_device,
        mesh=mesh,
        in_specs=placed,
        out_specs=P(("groups", "col"), "row", None),
        check_vma=False,
    )
```

time: 259 us -> 116 us (0.45)
  waiting for transfers between devices: 111 us -> 43.6 us
  other arithmetic: 38.8 us -> 1.85 us
  Pallas kernels: 0 us -> 28.8 us
  local copies, waits for them, and re-layouts: 29.6 us -> 11.7 us
  starting transfers between devices: 41.3 us -> 23.5 us
  matrix products: 23.3 us -> 5.93 us
  between operations: 13.8 us -> 0.24 us
    ppermute x8, waiting for transfers between devices: 111 us -> 35.5 us  [the longest x2 24.9 us: with_halo(): left = lax.ppermute(extended[tile_u - REACH:], 'row', forward)]
    pallas_call x0 -> x2, Pallas kernels: none -> 28.8 us  [the longest x1 23.9 us: on_device(): pl.pallas_call(block_kernel, out_shape=(jax.ShapeDtypeStruct(tile_shape,...]
    reduce_sum x3 -> x0, other arithmetic: 23.3 us -> none  [the longest x1 21.4 us: on_device(): mean_val = jnp.mean(conv_out, axis=-1, keepdims=True)]
    ppermute x8, starting transfers between devices: 35.4 us -> 17.8 us  [the longest x2 8.52 us: with_halo(): right = lax.ppermute(extended[:REACH], 'row', backward)]
    dot_general x4 -> x2, matrix products: 23.3 us -> 5.93 us  [the longest x1 3.1 us: find_target(): kept = jnp.dot(home, proj_weight, preferred_element_type=jnp.float32)]
    reshape x5 -> x2, local copies, waits for them, and re-layouts: 15.8 us -> 1.21 us  [find_target(): summed.reshape(lines, row_count, tile_u, channels).transpose(1, 2, 0, 3)]
    add x1 -> x0, other arithmetic: 10.3 us -> none  [on_device(): return mismatch + depthwise(d_padded, dw_kernel[::-1, ::-1], tile_v, tile_u)]
    all_to_all x1, waiting for transfers between devices: 0.01 us -> 8.07 us  [find_target(): lax.all_to_all(by_u, 'row', split_axis=0, concat_axis=0, tiled=True)]
  transfers between devices with their start and end apart: 10 -> 9, of which waited for: 4 -> 8; matrix products, arithmetic and copies ran while one was open for 19% -> 5% of each run, Pallas kernels for 0% -> 0%
where the time goes in v1:
time: 116 us
  waiting for transfers between devices  43.6 us (38%)
  Pallas kernels  28.8 us (25%)
  starting transfers between devices  23.5 us (20%)
  local copies, waits for them, and re-layouts  11.7 us (10%)
  matrix products  5.93 us (5%)
  other arithmetic  1.85 us (2%)
    ppermute x2, waiting for transfers between devices, with_halo(): left = lax.ppermute(extended[tile_u - REACH:], 'row', forward)  24.9 us
    pallas_call x1, Pallas kernels, on_device(): pl.pallas_call(block_kernel, out_shape=(jax.ShapeDtypeStruct(tile_shape,...  23.9 us
    ppermute x2, starting transfers between devices, with_halo(): right = lax.ppermute(extended[:REACH], 'row', backward)  8.52 us
    all_to_all x1, waiting for transfers between devices, find_target(): lax.all_to_all(by_u, 'row', split_axis=0, concat_axis=0, tiled=True)  8.07 us
    ppermute x2, waiting for transfers between devices, with_halo(): right = lax.ppermute(extended[:REACH], 'row', backward)  6.59 us
    all_to_all x1, starting transfers between devices, find_target(): lax.all_to_all(by_u, 'row', split_axis=0, concat_axis=0, tiled=True)  5.69 us
    pallas_call x1, Pallas kernels, on_device(): pl.pallas_call(final_kernel, out_shape=jax.ShapeDtypeStruct(tile_shape, j...  4.95 us
    unnamed x21, local copies, waits for them, and re-layouts  4.35 us
  transfers between devices with their start and end apart: 9, of which 8 were waited for; matrix products, arithmetic and copies ran while one was open for 5% of the time, Pallas kernels for 0%

profile of v1, /device:TPU:13, one launch (start us, length us, event | category | flops | bytes accessed | tf_op | source)
XLA Modules:
  0.0 115.7 jit_solution(17100950693857673345)
XLA Ops:
  0.0 1.6 %copy-done = bf16[2048,512]{1,0:T(8,128)(2,1)S(1)} copy-done((bf16[2048,512]{1,0:T(8,128)(2,1)S(1)}, bf16[2048,512]{1,0:T(8,128)(2,1)}, u32[]{:S(2)}) %copy-start) | copy-done | bytes 2097176
  1.6 2.8 %fusion = f32[512,512]{1,0:T(8,128)S(1)} fusion(bf16[2048,512]{1,0:T(8,128)(2,1)S(1)} %copy-done, bf16[1024,2048]{1,0:T(8,128)(2,1)} %param.12, s32[]{:T(128)S(6)} %select_n.61), kind=kOutput, calls=%fused_computation | convolution fusion | flops 1073741824 | bytes 5242884 | tf_op jit(solution)/shard_map/dot_general | solution.py:229
  4.4 0.7 collective-permute-start.3
  5.2 2.4 %collective-permute-done.3 = f32[512,512]{1,0:T(8,128)} collective-permute-done((f32[512,512]{1,0:T(8,128)S(1)}, f32[512,512]{1,0:T(8,128)}, u32[]{:S(2)}, u32[]{:S(2)}) %collective-permute-start.3) | collective-permute-done | bytes 1048608 | tf_op jit(solution)/shard_map/ppermute | solution.py:230
  7.6 3.1 %fusion.7 = bf16[512,512]{1,0:T(8,128)(2,1)S(1)} fusion(f32[512,512]{1,0:T(8,128)} %collective-permute-done.3, bf16[2048,512]{1,0:T(8,128)(2,1)S(1)} %copy-done, bf16[1024,2048]{1,0:T(8,128)(2,1)} %param.12, s32[]{:T(128)S(6)} %select_n.60), kind=kOutput, calls=%fused_computation.5 | convolution fusion | flops 1074266112 | bytes 5767172 | tf_op jit(solution)/shard_map/dot_general | solution.py:232
  10.8 1.1 copy.23
  11.9 5.7 %all-to-all-start = ((bf16[8,4,16,512]{3,2,1,0:T(8,128)(2,1)}), bf16[8,4,16,512]{3,2,1,0:T(8,128)(2,1)}, u32[]{:S(2)}, u32[]{:S(2)}) async-start(bf16[8,4,16,512]{3,2,1,0:T(8,128)(2,1)} %bitcast.20), calls=%async_computation | async-start | bytes 1048576 | tf_op jit(solution)/shard_map/all_to_all | solution.py:235
  17.6 1.1 copy.24
  18.8 1.0 collective-permute-start
  19.9 0.8 collective-permute-done
  20.6 0.3 maximum_maximum_fusion.middle
  20.9 8.1 %all-to-all-done = bf16[8,4,16,512]{3,2,1,0:T(8,128)(2,1)} async-done(((bf16[8,4,16,512]{3,2,1,0:T(8,128)(2,1)}), bf16[8,4,16,512]{3,2,1,0:T(8,128)(2,1)}, u32[]{:S(2)}, u32[]{:S(2)}) %all-to-all-start) | async-done | bytes 524320 | tf_op jit(solution)/shard_map/all_to_all | solution.py:235
  29.0 1.7 %constant_dynamic-slice_fusion = bf16[4,4,16,512]{3,2,1,0:T(8,128)(2,1)} fusion(bf16[8,4,16,512]{3,2,1,0:T(8,128)(2,1)} %all-to-all-done, s32[]{:T(128)S(6)} %select_n.63), kind=kLoop, calls=%fused_computation.19 | loop fusion | bytes 524292 | tf_op jit(solution)/shard_map/dynamic_slice | solution.py:237
  30.6 3.2 %collective-permute-start.4 = (bf16[4,4,16,512]{3,2,1,0:T(8,128)(2,1)}, bf16[4,4,16,512]{3,2,1,0:T(8,128)(2,1)}, u32[]{:S(2)}, u32[]{:S(2)}) collective-permute-start(bf16[4,4,16,512]{3,2,1,0:T(8,128)(2,1)} %constant_dynamic-slice_fusion), channel_id=1, source_target_pairs={{0,1},{1,0},{2,3},{3,2},{4,5},{5,4},{6,7},{7,6},{8,9},{9,8},{10,11... | collective-permute-start | bytes 786440 | tf_op jit(solution)/shard_map/ppermute | solution.py:239
  33.8 1.0 fusion.13
  34.8 1.9 %collective-permute-start.1 = (bf16[3,136,512]{2,1,0:T(8,128)(2,1)}, bf16[3,136,512]{2,1,0:T(8,128)(2,1)S(1)}, u32[]{:S(2)}, u32[]{:S(2)}) collective-permute-start(bf16[3,136,512]{2,1,0:T(8,128)(2,1)} %get-tuple-element.14), channel_id=1, source_target_pairs={{0,2},{2,4},{4,6},{6,8},{8,10},{10,12},{12,14},{1,3},{3,5},{5,7},{... | collective-permute-start | bytes 1253384 | tf_op jit(solution)/shard_map/ppermute | solution.py:217
  36.7 4.3 %collective-permute-start.2 = (bf16[3,136,512]{2,1,0:T(8,128)(2,1)}, bf16[3,136,512]{2,1,0:T(8,128)(2,1)S(1)}, u32[]{:S(2)}, u32[]{:S(2)}) collective-permute-start(bf16[3,136,512]{2,1,0:T(8,128)(2,1)} %get-tuple-element.13), channel_id=1, source_target_pairs={{2,0},{4,2},{6,4},{8,6},{10,8},{12,10},{14,12},{3,1},{5,3},{7,5},{... | collective-permute-start | bytes 1253384 | tf_op jit(solution)/shard_map/ppermute | solution.py:218
  41.1 1.6 %broadcast_in_dim.25 = f32[49,4,128]{2,1,0:T(4,128)} reshape(f32[7,7,512]{2,1,0:T(8,128)} %param.15) | data formatting | bytes 200704 | tf_op jit(solution)/shard_map/broadcast_in_dim | solution.py:267
  42.7 1.2 %select_bitcast_fusion.1 = (bf16[4,1,4,16,512]{4,3,2,0,1:T(8,128)(2,1)S(1)}, bf16[4,1,4,16,512]{4,3,2,0,1:T(8,128)(2,1)S(1)}) fusion(bf16[4,4,16,512]{3,2,1,0:T(8,128)(2,1)} %collective-permute-done.4, pred[]{:T(512)S(6)} %eq.5, bf16[8,4,16,512]{3,2,1,0:T(8,128)(2,1)} %all-to-all-done, s32[]{:T(128)S(6)} %select_n.62), kind=kLoop, calls=%fused_computation.12 | loop fusion | flops 262144 | bytes 1048581 | tf_op jit(solution)/shard_map/stack | solution.py:242
  44.0 11.3 %collective-permute-done.1.left = bf16[3,136,512]{2,1,0:T(8,128)(2,1)S(1)} collective-permute-done((bf16[3,136,512]{2,1,0:T(8,128)(2,1)}, bf16[3,136,512]{2,1,0:T(8,128)(2,1)S(1)}, u32[]{:S(2)}, u32[]{:S(2)}) %collective-permute-start.1) | collective-permute-done | bytes 417824 | tf_op jit(solution)/shard_map/ppermute | solution.py:217
  55.2 3.1 %collective-permute-done.2.right = bf16[3,136,512]{2,1,0:T(8,128)(2,1)S(1)} collective-permute-done((bf16[3,136,512]{2,1,0:T(8,128)(2,1)}, bf16[3,136,512]{2,1,0:T(8,128)(2,1)S(1)}, u32[]{:S(2)}, u32[]{:S(2)}) %collective-permute-start.2) | collective-permute-done | bytes 417824 | tf_op jit(solution)/shard_map/ppermute | solution.py:218
  58.5 1.6 %copy-done.2 = bf16[2048,512]{1,0:T(8,128)(2,1)S(1)} copy-done((bf16[2048,512]{1,0:T(8,128)(2,1)S(1)}, bf16[2048,512]{1,0:T(8,128)(2,1)}, u32[]{:S(2)}) %copy-start.2) | copy-done | bytes 2097176
  60.1 23.9 %block.1 = (f32[4,128,512]{2,1,0:T(8,128)S(1)}, bf16[4,128,512]{2,1,0:T(8,128)(2,1)S(1)}) custom-call(bf16[3,136,512]{2,1,0:T(8,128)(2,1)S(1)} %collective-permute-done.1.left, bf16[4,136,512]{2,1,0:T(8,128)(2,1)S(1)} %maximum_maximum_fusion.middle, bf16[3,136,512]{2,1,0:T(8,128)(2,1)S(1)} %collective-permute-done.2.right, ...), custom_call_target="tpu_custom_call" | custom-call | tf_op jit(solution)/shard_map/block/pallas_call | solution.py:272
  84.1 0.5 collective-permute-start.5
  84.6 0.8 collective-permute-done.5
  85.4 0.3 maximum_maximum_fusion.1.middle
  85.8 1.9 %collective-permute-start.6 = (bf16[3,136,512]{2,1,0:T(8,128)(2,1)S(1)}, bf16[3,136,512]{2,1,0:T(8,128)(2,1)S(1)}, u32[]{:S(2)}, u32[]{:S(2)}) collective-permute-start(bf16[3,136,512]{2,1,0:T(8,128)(2,1)S(1)} %get-tuple-element.12), channel_id=1, source_target_pairs={{0,2},{2,4},{4,6},{6,8},{8,10},{10,12},{12,14},{1,3},{3,5},{5,7},{... | collective-permute-start | bytes 1253384 | tf_op jit(solution)/shard_map/ppermute | solution.py:217
  87.7 4.3 %collective-permute-start.7 = (bf16[3,136,512]{2,1,0:T(8,128)(2,1)S(1)}, bf16[3,136,512]{2,1,0:T(8,128)(2,1)S(1)}, u32[]{:S(2)}, u32[]{:S(2)}) collective-permute-start(bf16[3,136,512]{2,1,0:T(8,128)(2,1)S(1)} %get-tuple-element.11), channel_id=1, source_target_pairs={{2,0},{4,2},{6,4},{8,6},{10,8},{12,10},{14,12},{3,1},{5,3},{7,5},{... | collective-permute-start | bytes 1253384 | tf_op jit(solution)/shard_map/ppermute | solution.py:218
  92.0 13.7 %collective-permute-done.6.left = bf16[3,136,512]{2,1,0:T(8,128)(2,1)S(1)} collective-permute-done((bf16[3,136,512]{2,1,0:T(8,128)(2,1)S(1)}, bf16[3,136,512]{2,1,0:T(8,128)(2,1)S(1)}, u32[]{:S(2)}, u32[]{:S(2)}) %collective-permute-start.6) | collective-permute-done | bytes 417824 | tf_op jit(solution)/shard_map/ppermute | solution.py:217
  105.6 3.5 %collective-permute-done.7.right = bf16[3,136,512]{2,1,0:T(8,128)(2,1)S(1)} collective-permute-done((bf16[3,136,512]{2,1,0:T(8,128)(2,1)S(1)}, bf16[3,136,512]{2,1,0:T(8,128)(2,1)S(1)}, u32[]{:S(2)}, u32[]{:S(2)}) %collective-permute-start.7) | collective-permute-done | bytes 417824 | tf_op jit(solution)/shard_map/ppermute | solution.py:218
  109.1 4.9 %final.1 = f32[4,128,512]{2,1,0:T(8,128)S(1)} custom-call(bf16[3,136,512]{2,1,0:T(8,128)(2,1)S(1)} %collective-permute-done.6.left, bf16[4,136,512]{2,1,0:T(8,128)(2,1)S(1)} %maximum_maximum_fusion.1.middle, bf16[3,136,512]{2,1,0:T(8,128)(2,1)S(1)} %collective-permute-done.7.right, f32[49,4,8,128]{3,2,1,0:T(8,128)S(1)} %broadcast_in_dim.26.taps, ...), custom_call_target="tpu_custom_call" | custom-call | tf_op jit(solution)/shard_map/final/pallas_call | solution.py:307
  114.0 1.6 %copy.20 = f32[128,4,512]{2,1,0:T(4,128)} copy(f32[128,4,512]{2,0,1:T(8,128)S(1)} %bitcast.22) | data formatting | bytes 2097152 | tf_op jit(solution)/shard_map/transpose | solution.py:316
  (30 shorter events, 0.6 us)
Async XLA Ops:
  0.0 1.6 %copy-start = (bf16[2048,512]{1,0:T(8,128)(2,1)S(1)}, bf16[2048,512]{1,0:T(8,128)(2,1)}, u32[]{:S(2)}) copy-start(bf16[2048,512]{1,0:T(8,128)(2,1)} %param.13) | copy-start | bytes 6291460
  4.4 3.2 %collective-permute-start.3 = (f32[512,512]{1,0:T(8,128)S(1)}, f32[512,512]{1,0:T(8,128)}, u32[]{:S(2)}, u32[]{:S(2)}) collective-permute-start(f32[512,512]{1,0:T(8,128)S(1)} %fusion), channel_id=1, source_target_pairs={{0,1},{1,0},{2,3},{3,2},{4,5},{5,4},{6,7},{7,6},{8,9},{9,8},{10,11... | collective-permute-start | bytes 3145736 | tf_op jit(solution)/shard_map/ppermute | solution.py:230
  11.9 17.0 %all-to-all-start = ((bf16[8,4,16,512]{3,2,1,0:T(8,128)(2,1)}), bf16[8,4,16,512]{3,2,1,0:T(8,128)(2,1)}, u32[]{:S(2)}, u32[]{:S(2)}) async-start(bf16[8,4,16,512]{3,2,1,0:T(8,128)(2,1)} %bitcast.20), calls=%async_computation | async-start | bytes 1048576 | tf_op jit(solution)/shard_map/all_to_all | solution.py:235
  18.8 1.8 %collective-permute-start = (bf16[4,3,512]{2,1,0:T(4,128)(2,1)S(1)}, bf16[4,3,512]{2,1,0:T(4,128)(2,1)S(1)}, u32[]{:S(2)}, u32[]{:S(2)}) collective-permute-start(bf16[4,3,512]{2,1,0:T(4,128)(2,1)S(1)} %slice_select_fusion), channel_id=1, source_target_pairs={{0,1},{1,0},{2,3},{3,2},{4,5},{5,4},{6,7},{7,6},{8,9},{9,8},{10,11... | collective-permute-start | bytes 36872 | tf_op jit(solution)/shard_map/ppermute | solution.py:203
  30.6 12.0 %collective-permute-start.4 = (bf16[4,4,16,512]{3,2,1,0:T(8,128)(2,1)}, bf16[4,4,16,512]{3,2,1,0:T(8,128)(2,1)}, u32[]{:S(2)}, u32[]{:S(2)}) collective-permute-start(bf16[4,4,16,512]{3,2,1,0:T(8,128)(2,1)} %constant_dynamic-slice_fusion), channel_id=1, source_target_pairs={{0,1},{1,0},{2,3},{3,2},{4,5},{5,4},{6,7},{7,6},{8,9},{9,8},{10,11... | collective-permute-start | bytes 786440 | tf_op jit(solution)/shard_map/ppermute | solution.py:239
  34.8 20.4 %collective-permute-start.1 = (bf16[3,136,512]{2,1,0:T(8,128)(2,1)}, bf16[3,136,512]{2,1,0:T(8,128)(2,1)S(1)}, u32[]{:S(2)}, u32[]{:S(2)}) collective-permute-start(bf16[3,136,512]{2,1,0:T(8,128)(2,1)} %get-tuple-element.14), channel_id=1, source_target_pairs={{0,2},{2,4},{4,6},{6,8},{8,10},{10,12},{12,14},{1,3},{3,5},{5,7},{... | collective-permute-start | bytes 1253384 | tf_op jit(solution)/shard_map/ppermute | solution.py:217
  36.7 21.6 %collective-permute-start.2 = (bf16[3,136,512]{2,1,0:T(8,128)(2,1)}, bf16[3,136,512]{2,1,0:T(8,128)(2,1)S(1)}, u32[]{:S(2)}, u32[]{:S(2)}) collective-permute-start(bf16[3,136,512]{2,1,0:T(8,128)(2,1)} %get-tuple-element.13), channel_id=1, source_target_pairs={{2,0},{4,2},{6,4},{8,6},{10,8},{12,10},{14,12},{3,1},{5,3},{7,5},{... | collective-permute-start | bytes 1253384 | tf_op jit(solution)/shard_map/ppermute | solution.py:218
  41.0 17.5 %copy-start.3 = (f32[2048]{0:T(1024)S(1)}, f32[2048]{0:T(1024)}, u32[]{:S(2)}) copy-start(f32[2048]{0:T(1024)} %param.20) | copy-start | bytes 24580
  41.0 17.5 %copy-start.4 = (f32[512]{0:T(512)S(1)}, f32[512]{0:T(512)}, u32[]{:S(2)}) copy-start(f32[512]{0:T(512)} %param.16) | copy-start | bytes 6148
  41.0 17.5 %copy-start.5 = (f32[512]{0:T(512)S(1)}, f32[512]{0:T(512)}, u32[]{:S(2)}) copy-start(f32[512]{0:T(512)} %param.17) | copy-start | bytes 6148
  41.0 17.5 %copy-start.6 = (f32[512]{0:T(512)S(1)}, f32[512]{0:T(512)}, u32[]{:S(2)}) copy-start(f32[512]{0:T(512)} %param.18) | copy-start | bytes 6148
  41.0 17.5 %copy-start.7 = (f32[512]{0:T(512)S(1)}, f32[512]{0:T(512)}, u32[]{:S(2)}) copy-start(f32[512]{0:T(512)} %param.22) | copy-start | bytes 6148
  41.0 17.5 %copy-start.8 = (f32[512]{0:T(512)S(1)}, f32[512]{0:T(512)}, u32[]{:S(2)}) copy-start(f32[512]{0:T(512)} %param.23) | copy-start | bytes 6148
  42.7 15.7 %copy-start.9 = (f32[49,4,128]{2,1,0:T(4,128)S(1)}, f32[49,4,128]{2,1,0:T(4,128)}, u32[]{:S(2)}) copy-start(f32[49,4,128]{2,1,0:T(4,128)} %broadcast_in_dim.25) | copy-start | bytes 301060
  42.7 15.9 %copy-start.1 = (bf16[512,2048]{1,0:T(8,128)(2,1)S(1)}, bf16[512,2048]{1,0:T(8,128)(2,1)}, u32[]{:S(2)}) copy-start(bf16[512,2048]{1,0:T(8,128)(2,1)} %w_in.1) | copy-start | bytes 6291460
  58.5 1.6 %copy-start.2 = (bf16[2048,512]{1,0:T(8,128)(2,1)S(1)}, bf16[2048,512]{1,0:T(8,128)(2,1)}, u32[]{:S(2)}) copy-start(bf16[2048,512]{1,0:T(8,128)(2,1)} %w_out.1) | copy-start | bytes 6291460
  84.1 1.4 %collective-permute-start.5 = (bf16[4,3,512]{2,1,0:T(4,128)(2,1)S(1)}, bf16[4,3,512]{2,1,0:T(4,128)(2,1)S(1)}, u32[]{:S(2)}, u32[]{:S(2)}) collective-permute-start(bf16[4,3,512]{2,1,0:T(4,128)(2,1)S(1)} %slice_select_fusion.1), channel_id=1, source_target_pairs={{0,1},{1,0},{2,3},{3,2},{4,5},{5,4},{6,7},{7,6},{8,9},{9,8},{10,11... | collective-permute-start | bytes 36872 | tf_op jit(solution)/shard_map/ppermute | solution.py:203
  85.8 19.9 %collective-permute-start.6 = (bf16[3,136,512]{2,1,0:T(8,128)(2,1)S(1)}, bf16[3,136,512]{2,1,0:T(8,128)(2,1)S(1)}, u32[]{:S(2)}, u32[]{:S(2)}) collective-permute-start(bf16[3,136,512]{2,1,0:T(8,128)(2,1)S(1)} %get-tuple-element.12), channel_id=1, source_target_pairs={{0,2},{2,4},{4,6},{6,8},{8,10},{10,12},{12,14},{1,3},{3,5},{5,7},{... | collective-permute-start | bytes 1253384 | tf_op jit(solution)/shard_map/ppermute | solution.py:217
  87.7 21.4 %collective-permute-start.7 = (bf16[3,136,512]{2,1,0:T(8,128)(2,1)S(1)}, bf16[3,136,512]{2,1,0:T(8,128)(2,1)S(1)}, u32[]{:S(2)}, u32[]{:S(2)}) collective-permute-start(bf16[3,136,512]{2,1,0:T(8,128)(2,1)S(1)} %get-tuple-element.11), channel_id=1, source_target_pairs={{2,0},{4,2},{6,4},{8,6},{10,8},{12,10},{14,12},{3,1},{5,3},{7,5},{... | collective-permute-start | bytes 1253384 | tf_op jit(solution)/shard_map/ppermute | solution.py:218

commit v2 on v0

v2 whole, which is shorter than its diff:
```python
import functools

import jax
import jax.numpy as jnp
from jax import lax
from jax.experimental import pallas as pl
from jax.experimental.pallas import tpu as pltpu
from jax.sharding import PartitionSpec as P

NORM_EPSILON = 1e-06
REACH = 3
TAPS = 2 * REACH + 1
LANES = 128
SUBLANES = 8
EDGE = 8
CHUNK = 32
MLP_TILE = 512
CONTRACT_LAST = (((1,), (1,)), ((), ()))
SWAP = [(0, 1), (1, 0)]


def aligned(start, size):
    return pl.ds(pl.multiple_of(start, size), size)


def spread(padded, place, part, source, row, count):
    for tile in range(padded.shape[0]):
        padded[tile, place, pl.ds(row, count), :] = part[
            source, :count, tile * LANES : (tile + 1) * LANES
        ].astype(jnp.float32)


def spread_edge(padded, place, part, source, start, core, tile_v):
    for tile in range(padded.shape[0]):
        lanes = slice(tile * LANES, (tile + 1) * LANES)
        edge = part[source, start : start + EDGE, lanes].astype(jnp.float32)
        nothing = jnp.zeros_like(edge)
        padded[tile, place, 0:EDGE, :] = jnp.where(core == 1, edge, nothing)
        padded[tile, place, EDGE + tile_v : 2 * EDGE + tile_v, :] = jnp.where(
            core == 0, edge, nothing
        )


def depthwise(padded, taps, begin, store, tile_u, tile_v, sources, flip):
    tiles = padded.shape[0]
    blocks = tile_v // (2 * SUBLANES)

    def step(index, carry):
        tile = index // blocks
        base = pl.multiple_of((index % blocks) * (2 * SUBLANES), 2 * SUBLANES)
        sums = [
            [begin(tile, u, base + half * SUBLANES) for u in range(tile_u)] for half in range(2)
        ]
        for row_tap in range(TAPS):
            weights = []
            for col_tap in range(TAPS):
                tap = row_tap * TAPS + col_tap
                weights.append(taps[TAPS * TAPS - 1 - tap if flip else tap, tile])
            for place, source in enumerate(sources):
                for half in range(2):
                    row = base + (half * SUBLANES + EDGE - REACH + row_tap)
                    values = padded[tile, place, pl.ds(row, SUBLANES), :]
                    for u in range(max(0, source - TAPS + 1), min(tile_u, source + 1)):
                        term = weights[source - u] * values
                        sums[half][u] = term if sums[half][u] is None else sums[half][u] + term
        for half in range(2):
            for u in range(tile_u):
                if sums[half][u] is not None:
                    store(tile, u, base + half * SUBLANES, sums[half][u])
        return carry

    lax.fori_loop(0, tiles * blocks, step, 0)


def project_kernel(core_ref, teacher, weight, upper, lower, home):
    core = core_ref[0]
    lines, _, wide, depth = teacher.shape
    for half, outs in ((1 - core, (upper, lower)), (core, (home,))):
        rows = teacher[:, half].reshape(lines * wide, depth)
        size = lines * wide // len(outs)
        for index, out in enumerate(outs):
            here = rows[index * size : (index + 1) * size]
            product = jnp.dot(here, weight[...], preferred_element_type=jnp.float32)
            out[...] = product.astype(out.dtype)


def combine_kernel(wide, turns_ref, home, upper, lower, *rest):
    *blocks, summed = rest
    for tile in range(summed.shape[0]):
        lanes = slice(tile * LANES, (tile + 1) * LANES)
        half = upper.shape[0]
        for start, received in ((0, upper), (half, lower)):
            here = slice(start, start + half)
            summed[tile, here] = home[here, lanes] + received[:, lanes].astype(jnp.float32)
    for index, block in enumerate(blocks):
        tile_u, lines, _ = block.shape
        for u in range(tile_u):
            rows = pl.ds(turns_ref[index] + u, lines, stride=wide)
            for tile in range(summed.shape[0]):
                lanes = slice(tile * LANES, (tile + 1) * LANES)
                block[u, :, lanes] = summed[tile, rows, :].astype(jnp.bfloat16)


def fill(padded, parts, edges, core, tile_v):
    place = 0
    for part, (edge, start) in zip(parts, edges):
        for u in range(part.shape[0]):
            spread(padded, place, part, u, EDGE, tile_v)
            spread_edge(padded, place, edge, u, start, core, tile_v)
            place += 1


def up_kernel(
    core_ref,
    left,
    middle,
    right,
    edge,
    taps,
    dw_bias,
    norm_gain,
    norm_bias,
    w_in,
    b_in,
    normal_form,
    inv_scale,
    activated,
    slope,
    padded,
    normed,
):
    tile_u, tile_v, channels = middle.shape
    rows = tile_u * tile_v
    hidden = w_in.shape[1]
    sides = [(left, tile_v), (edge, 0), (right, tile_v)]
    fill(padded, (left, middle, right), sides, core_ref[0], tile_v)

    def begin(tile, u, base):
        return None

    def store(tile, u, base, value):
        row = aligned(u * tile_v + base, SUBLANES)
        normal_form[row, aligned(tile * LANES, LANES)] = value

    depthwise(padded, taps, begin, store, tile_u, tile_v, range(tile_u + 2 * REACH), False)

    def norm_step(index, carry):
        here = aligned(index * CHUNK, CHUNK)
        conv = normal_form[here, :] + dw_bias[...]
        centred = conv - jnp.mean(conv, axis=-1, keepdims=True)
        variance = jnp.mean(centred * centred, axis=-1, keepdims=True)
        inverse = lax.rsqrt(variance + NORM_EPSILON)
        form = centred * inverse
        normal_form[here, :] = form
        inv_scale[here, :] = jnp.broadcast_to(inverse, (CHUNK, LANES))
        normed[here, :] = (form * norm_gain[...] + norm_bias[...]).astype(jnp.bfloat16)
        return carry

    lax.fori_loop(0, rows // CHUNK, norm_step, 0)

    for start in range(0, hidden, MLP_TILE):
        tile = slice(start, start + MLP_TILE)
        for here in row_halves(rows):
            pre = (
                jnp.dot(normed[here, :], w_in[:, tile], preferred_element_type=jnp.float32)
                + b_in[:, tile]
            )
            phi = 0.5 * (1.0 + lax.erf(pre * 0.7071067811865476))
            activated[here, tile] = (pre * phi).astype(jnp.bfloat16)
            slope[here, tile] = phi + pre * jnp.exp(-0.5 * pre * pre) * 0.3989422804014327


def row_halves(rows):
    return slice(0, rows // 2), slice(rows // 2, rows)


def back_kernel(
    pieces,
    places_ref,
    middle,
    normal_form,
    inv_scale,
    activated,
    slope,
    norm_gain,
    w_in,
    w_out,
    b_out,
    layer_scale,
    *rest,
):
    targets = rest[:pieces]
    mismatch_out, d_out, target, d_branch, d_hidden, d_normed = rest[pieces:]
    tile_u, tile_v, channels = middle.shape
    rows = tile_u * tile_v
    hidden = w_in.shape[1]
    chunks = tile_v // CHUNK
    for index, piece in enumerate(targets):
        target[:, aligned(places_ref[index], piece.shape[1]), :] = piece[...]

    for here in row_halves(rows):
        d_normed[here, :] = jnp.dot(
            activated[here, :], w_out[...], preferred_element_type=jnp.float32
        )

    def mismatch_step(index, carry):
        u = index // chunks
        inside = aligned((index % chunks) * CHUNK, CHUNK)
        here = aligned(index * CHUNK, CHUNK)
        mismatch = (
            middle[u, inside, :].astype(jnp.float32)
            + layer_scale[...] * (d_normed[here, :] + b_out[...])
            - target[u, inside, :].astype(jnp.float32)
        )
        mismatch_out[u, inside, :] = mismatch
        d_branch[here, :] = (layer_scale[...] * mismatch).astype(jnp.bfloat16)
        return carry

    lax.fori_loop(0, tile_u * chunks, mismatch_step, 0)

    for start in range(0, hidden, MLP_TILE):
        tile = slice(start, start + MLP_TILE)
        for here in row_halves(rows):
            d_activated = lax.dot_general(
                d_branch[here, :], w_out[tile, :], CONTRACT_LAST, preferred_element_type=jnp.float32
            )
            d_hidden[here, tile] = (d_activated * slope[here, tile]).astype(jnp.bfloat16)
    for here in row_halves(rows):
        d_normed[here, :] = lax.dot_general(
            d_hidden[here, :], w_in[...], CONTRACT_LAST, preferred_element_type=jnp.float32
        )

    def d_norm_step(index, carry):
        u = index // chunks
        inside = aligned((index % chunks) * CHUNK, CHUNK)
        here = aligned(index * CHUNK, CHUNK)
        scaled = d_normed[here, :] * norm_gain[...]
        form = normal_form[here, :]
        d_conv = inv_scale[here, :1] * (
            scaled
            - jnp.mean(scaled, axis=-1, keepdims=True)
            - form * jnp.mean(scaled * form, axis=-1, keepdims=True)
        )
        d_out[u, inside, :] = d_conv.astype(jnp.bfloat16)
        return carry

    lax.fori_loop(0, tile_u * chunks, d_norm_step, 0)


def inner_kernel(core_ref, middle, edge, taps, mismatch, out, padded):
    tile_u, tile_v, channels = mismatch.shape
    fill(padded, (middle,), [(edge, 0)], core_ref[0], tile_v)

    def place(tile, u, base):
        return u, aligned(base, SUBLANES), aligned(tile * LANES, LANES)

    def begin(tile, u, base):
        return mismatch[place(tile, u, base)]

    def store(tile, u, base, value):
        out[place(tile, u, base)] = value

    own = range(REACH, REACH + tile_u)
    depthwise(padded, taps, begin, store, tile_u, tile_v, own, True)


def rim_kernel(core_ref, left, right, left_edge, right_edge, taps, inner, out, padded):
    tile_u, tile_v, channels = inner.shape
    fill(padded, (left, right), [(left_edge, 0), (right_edge, 0)], core_ref[0], tile_v)

    def place(tile, u, base):
        return u, aligned(base, SUBLANES), aligned(tile * LANES, LANES)

    def begin(tile, u, base):
        return inner[place(tile, u, base)]

    def store(tile, u, base, value):
        out[place(tile, u, base)] = value

    sides = [*range(REACH), *range(REACH + tile_u, 2 * REACH + tile_u)]
    depthwise(padded, taps, begin, store, tile_u, tile_v, sides, True)


def call(kernel, name, outs, scratch, scalars, arrays, flops, limit):
    vmem = pl.BlockSpec(memory_space=pltpu.VMEM)
    smem = pl.BlockSpec(memory_space=pltpu.SMEM)
    moved = 1 if flops == 1 else sum(a.size * a.dtype.itemsize for a in arrays) + sum(
        o.size * o.dtype.itemsize for o in outs
    )
    return pl.pallas_call(
        kernel,
        out_shape=tuple(outs),
        in_specs=[smem] * len(scalars) + [vmem] * len(arrays),
        out_specs=(vmem,) * len(outs),
        scratch_shapes=scratch,
        compiler_params=pltpu.CompilerParams(vmem_limit_bytes=limit << 20),
        cost_estimate=pl.CostEstimate(flops=flops, bytes_accessed=moved, transcendentals=0),
        name=name,
    )(*scalars, *arrays)


def edge_lines(tile, core):
    return jnp.where(core == 0, tile[:, -EDGE:], tile[:, :EDGE])


def to_sides_with_edge(tile, core):
    row_count = lax.axis_size("row")
    forward = [(i, i + 1) for i in range(row_count - 1)]
    backward = [(b, a) for a, b in forward]
    edge = lax.ppermute(edge_lines(tile, core), "col", SWAP)
    last = jnp.concatenate([tile[-REACH:], edge[-REACH:]], axis=1)
    first = jnp.concatenate([tile[:REACH], edge[:REACH]], axis=1)
    left = lax.ppermute(last, "row", forward)
    right = lax.ppermute(first, "row", backward)
    return left, right, edge, last, first


def to_sides(tile, core):
    row_count = lax.axis_size("row")
    forward = [(i, i + 1) for i in range(row_count - 1)]
    backward = [(b, a) for a, b in forward]
    left = lax.ppermute(tile[-REACH:], "row", forward)
    right = lax.ppermute(tile[:REACH], "row", backward)
    own = edge_lines(tile, core)
    edge = lax.ppermute(own, "col", SWAP)

    def across(pairs):
        return [(a * 2 + c, b * 2 + 1 - c) for a, b in pairs for c in range(2)]

    left_edge = lax.ppermute(own[-REACH:], ("row", "col"), across(forward))
    right_edge = lax.ppermute(own[:REACH], ("row", "col"), across(backward))
    return left, right, left_edge, edge, right_edge


def find_target(teacher, proj_weight, core, row, tile_u, tile_v):
    row_count = lax.axis_size("row")
    halves = row_count // 2
    channels = proj_weight.shape[1]
    grid_u = tile_u * row_count
    lines = teacher.shape[0] // grid_u
    scalar = core.astype(jnp.int32)[None]
    half_line = grid_u // 2
    by_half = teacher.reshape(lines, 2, half_line, teacher.shape[1])
    size = (lines * half_line, channels)
    fourth = jax.ShapeDtypeStruct((size[0] // 2, channels), jnp.bfloat16)
    outs = [fourth, fourth, jax.ShapeDtypeStruct(size, jnp.float32)]
    upper, lower, home = call(project_kernel, "project", outs, [], [scalar], [by_half, proj_weight], 1, 12)
    received = [lax.ppermute(away, "col", SWAP) for away in (upper, lower)]
    turns = [lax.rem(turn + row, halves) * tile_u for turn in range(halves)]
    if lines % 16:
        received = jnp.concatenate(received).astype(jnp.float32)
        summed = (home + received).astype(jnp.bfloat16)
        by_u = summed.reshape(lines, half_line, channels).transpose(1, 0, 2)
        blocks = [lax.dynamic_slice_in_dim(by_u, turn, tile_u) for turn in turns]
    else:
        blocks = call(
            functools.partial(combine_kernel, half_line),
            "combine",
            [jax.ShapeDtypeStruct((tile_u, lines, channels), jnp.bfloat16)] * halves,
            [pltpu.VMEM((channels // LANES, *size[:1], LANES), jnp.float32)],
            [jnp.stack(turns).astype(jnp.int32)],
            [home, *received],
            1,
            8,
        )
    pieces, places = [], []
    for turn in range(halves):
        pairs = []
        for r in range(row_count):
            for c in range(2):
                goal = (halves * c + (turn + r) % halves) * 2 + r // halves
                pairs.append((r * 2 + c, goal))
        pieces.append(lax.ppermute(blocks[turn], ("row", "col"), pairs))
        places.append(lax.rem(row + (halves - turn), halves) * lines)
    places = jnp.stack(places).astype(jnp.int32)
    if lines % 16:
        whole = jnp.zeros((tile_u, tile_v, channels), jnp.bfloat16)
        for index, piece in enumerate(pieces):
            whole = lax.dynamic_update_slice_in_dim(whole, piece, places[index], axis=1)
        return [whole], jnp.zeros((1,), jnp.int32)
    return pieces, places


def on_device(
    teacher,
    proj_weight,
    student,
    dw_kernel,
    dw_bias,
    norm_gain,
    norm_bias,
    w_in,
    b_in,
    w_out,
    b_out,
    layer_scale,
):
    core = lax.axis_index("col")
    row = lax.axis_index("row")
    tile_v, tile_u, channels = student.shape
    hidden = w_in.shape[1]
    tiles = channels // LANES
    wide = tile_v + 2 * EDGE
    scalar = core.astype(jnp.int32)[None]
    f32, bf16 = jnp.float32, jnp.bfloat16

    middle = student.transpose(1, 0, 2)
    left, right, edge, last, first = to_sides_with_edge(middle, core)
    held, _, _ = lax.optimization_barrier((proj_weight, last, first))
    targets, places = find_target(teacher, held, core, row, tile_u, tile_v)
    taps = jnp.broadcast_to(
        dw_kernel.reshape(TAPS * TAPS, tiles, 1, LANES), (TAPS * TAPS, tiles, SUBLANES, LANES)
    )
    matmul = 2 * tile_u * tile_v * channels * hidden
    rows = tile_u * tile_v
    whole_tile = (tile_u, tile_v, channels)
    normal_form, inv_scale, activated, slope = call(
        up_kernel,
        "up",
        [
            jax.ShapeDtypeStruct((rows, channels), f32),
            jax.ShapeDtypeStruct((rows, LANES), f32),
            jax.ShapeDtypeStruct((rows, hidden), bf16),
            jax.ShapeDtypeStruct((rows, hidden), f32),
        ],
        [
            pltpu.VMEM((tiles, tile_u + 2 * REACH, wide, LANES), f32),
            pltpu.VMEM((rows, channels), bf16),
        ],
        [scalar],
        [left, middle, right, edge, taps, dw_bias[None]]
        + [norm_gain[None], norm_bias[None], w_in, b_in[None]],
        4 * matmul,
        16,
    )
    mismatch, d_conv = call(
        functools.partial(back_kernel, len(targets)),
        "back",
        [jax.ShapeDtypeStruct(whole_tile, f32), jax.ShapeDtypeStruct(whole_tile, bf16)],
        [
            pltpu.VMEM(whole_tile, bf16),
            pltpu.VMEM((rows, channels), bf16),
            pltpu.VMEM((rows, hidden), bf16),
            pltpu.VMEM((rows, channels), f32),
        ],
        [places],
        [middle, normal_form, inv_scale, activated, slope, norm_gain[None], w_in, w_out]
        + [b_out[None], layer_scale[None]]
        + targets,
        4 * matmul,
        16,
    )
    left, right, left_edge, edge, right_edge = to_sides(d_conv, core)
    (inner,) = call(
        inner_kernel,
        "inner",
        [jax.ShapeDtypeStruct(whole_tile, f32)],
        [pltpu.VMEM((tiles, tile_u, wide, LANES), f32)],
        [scalar],
        [d_conv, edge, taps, mismatch],
        matmul,
        8,
    )
    (grad,) = call(
        rim_kernel,
        "rim",
        [jax.ShapeDtypeStruct(whole_tile, f32)],
        [pltpu.VMEM((tiles, 2 * REACH, wide, LANES), f32)],
        [scalar],
        [left, right, left_edge, right_edge, taps, inner],
        matmul,
        8,
    )
    return grad.transpose(1, 0, 2)


def solution(mesh):
    placed = (
        P(("groups", "row"), "col"),
        P("col", None),
        P(("groups", "col"), "row", None),
        P(),
        P(),
        P(),
        P(),
        P(),
        P(),
        P(),
        P(),
        P(),
    )
    return jax.shard_map(
        on_device,
        mesh=mesh,
        in_specs=placed,
        out_specs=P(("groups", "col"), "row", None),
        check_vma=False,
    )
```

time: 259 us -> 74.4 us (0.29)
  waiting for transfers between devices: 111 us -> 8.85 us
  other arithmetic: 38.8 us -> 1.75 us
  Pallas kernels: 0 us -> 25 us
  matrix products: 23.3 us -> 0 us
  local copies, waits for them, and re-layouts: 29.6 us -> 10.1 us
  starting transfers between devices: 41.3 us -> 27.5 us
  between operations: 13.8 us -> 0.3 us
    ppermute x8 -> x14, waiting for transfers between devices: 111 us -> 8.85 us  [the longest x1 7.44 us: to_sides(): right_edge = lax.ppermute(own[:REACH], ('row', 'col'), across(backward))]
    pallas_call x0 -> x6, Pallas kernels: none -> 25 us  [call(): pl.pallas_call(kernel, out_shape=tuple(outs), in_specs=[smem] * len(scala...]
    reduce_sum x3 -> x0, other arithmetic: 23.3 us -> none  [the longest x1 21.4 us: on_device(): mean_val = jnp.mean(conv_out, axis=-1, keepdims=True)]
    dot_general x4 -> x0, matrix products: 23.3 us -> none  [the longest x1 10.1 us: on_device(): jnp.dot(activated, w_out, preferred_element_type=jnp.float32) + b_out]
    reshape x5 -> x0, local copies, waits for them, and re-layouts: 15.8 us -> none  [the longest x1 6.67 us: on_device(): raw_tokens = teacher.reshape(local_lines, grid_u, teacher.shape[1])]
    add x1 -> x0, other arithmetic: 10.3 us -> none  [on_device(): return mismatch + depthwise(d_padded, dw_kernel[::-1, ::-1], tile_v, tile_u)]
    ppermute x8 -> x14, starting transfers between devices: 35.4 us -> 27.5 us  [the longest x4 8.12 us: find_target(): pieces.append(lax.ppermute(blocks[turn], ('row', 'col'), pairs))]
    all_to_all x1 -> x0, starting transfers between devices: 5.82 us -> none  [on_device(): lax.all_to_all(raw_tokens, 'row', split_axis=1, concat_axis=0, tiled=True)]
  transfers between devices with their start and end apart: 10 -> 14, of which waited for: 4 -> 4; matrix products, arithmetic and copies ran while one was open for 19% -> 3% of each run, Pallas kernels for 0% -> 22%
where the time goes in v2:
time: 74.4 us; the launch traced here: 73.5 us
  starting transfers between devices  27.5 us (37%)
  Pallas kernels  25 us (34%)
  local copies, waits for them, and re-layouts  10.1 us (14%)
  waiting for transfers between devices  8.85 us (12%)
  other arithmetic  1.75 us (2%)
    pallas_call x6, Pallas kernels, call(): pl.pallas_call(kernel, out_shape=tuple(outs), in_specs=[smem] * len(scala...  25 us
    ppermute x4, starting transfers between devices, find_target(): pieces.append(lax.ppermute(blocks[turn], ('row', 'col'), pairs))  8.12 us
    ppermute x1, waiting for transfers between devices, to_sides(): right_edge = lax.ppermute(own[:REACH], ('row', 'col'), across(backward))  7.44 us
    unnamed x27, local copies, waits for them, and re-layouts  7.28 us
    ppermute x1, starting transfers between devices, to_sides(): right_edge = lax.ppermute(own[:REACH], ('row', 'col'), across(backward))  4.2 us
    ppermute x1, starting transfers between devices, to_sides_with_edge(): left = lax.ppermute(last, 'row', forward)  3.11 us
    ppermute x1, starting transfers between devices, to_sides_with_edge(): right = lax.ppermute(first, 'row', backward)  3.05 us
    ppermute x1, starting transfers between devices, to_sides(): right = lax.ppermute(tile[:REACH], 'row', backward)  2.94 us
  transfers between devices with their start and end apart: 14, of which 4 were waited for; matrix products, arithmetic and copies ran while one was open for 3% of the time, Pallas kernels for 22%

profile of v2, /device:TPU:13, one launch (start us, length us, event | category | flops | bytes accessed | tf_op | source)
XLA Modules:
  0.0 73.5 jit_solution(4799156795912383432)
XLA Ops:
  0.0 1.3 %copy.16 = bf16[128,4,512]{2,0,1:T(8,128)(2,1)S(1)} copy(bf16[128,4,512]{2,1,0:T(4,128)(2,1)} %param.14) | data formatting | bytes 1048576 | tf_op args[2]
  1.3 0.7 %collective-permute-start = (bf16[4,8,512]{2,1,0:T(8,128)(2,1)S(1)}, bf16[4,8,512]{2,1,0:T(8,128)(2,1)S(1)}, u32[]{:S(2)}, u32[]{:S(2)}) collective-permute-start(bf16[4,8,512]{2,1,0:T(8,128)(2,1)S(1)} %slice_select_fusion), channel_id=1, source_target_pairs={{0,1},{1,0},{2,3},{3,2},{4,5},{5,4},{6,7},{7,6},{8,9},{9,8},{10,11... | collective-permute-start | bytes 98312 | tf_op jit(solution)/shard_map/ppermute | solution.py:310
  2.1 0.8 %collective-permute-done.edge = bf16[4,8,512]{2,1,0:T(8,128)(2,1)S(1)} collective-permute-done((bf16[4,8,512]{2,1,0:T(8,128)(2,1)S(1)}, bf16[4,8,512]{2,1,0:T(8,128)(2,1)S(1)}, u32[]{:S(2)}, u32[]{:S(2)}) %collective-permute-start) | collective-permute-done | bytes 32800 | tf_op jit(solution)/shard_map/ppermute | solution.py:310
  2.9 0.8 %pad_maximum_fusion = bf16[3,136,512]{2,1,0:T(8,128)(2,1)} fusion(bf16[3,8,512]{2,1,0:T(8,128)(2,1)S(1)} %get-tuple-element.40, bf16[3,128,512]{2,1,0:T(8,128)(2,1)S(1)} %get-tuple-element.36), kind=kLoop, calls=%fused_computation.1 | loop fusion | flops 835584 | bytes 835584 | tf_op jit(solution)/shard_map/concatenate | solution.py:311
  3.7 3.1 %collective-permute-start.1 = (bf16[3,136,512]{2,1,0:T(8,128)(2,1)}, bf16[3,136,512]{2,1,0:T(8,128)(2,1)S(1)}, u32[]{:S(2)}, u32[]{:S(2)}) collective-permute-start(bf16[3,136,512]{2,1,0:T(8,128)(2,1)} %pad_maximum_fusion), channel_id=1, source_target_pairs={{0,2},{2,4},{4,6},{6,8},{8,10},{10,12},{12,14},{1,3},{3,5},{5,7},{... | collective-permute-start | bytes 1253384 | tf_op jit(solution)/shard_map/ppermute | solution.py:313
  6.8 0.8 %pad_maximum_fusion.1 = bf16[3,136,512]{2,1,0:T(8,128)(2,1)} fusion(bf16[3,8,512]{2,1,0:T(8,128)(2,1)S(1)} %get-tuple-element.39, bf16[3,128,512]{2,1,0:T(8,128)(2,1)S(1)} %get-tuple-element.35), kind=kLoop, calls=%fused_computation.2 | loop fusion | flops 835584 | bytes 835584 | tf_op jit(solution)/shard_map/concatenate | solution.py:312
  7.6 3.0 %collective-permute-start.2 = (bf16[3,136,512]{2,1,0:T(8,128)(2,1)}, bf16[3,136,512]{2,1,0:T(8,128)(2,1)S(1)}, u32[]{:S(2)}, u32[]{:S(2)}) collective-permute-start(bf16[3,136,512]{2,1,0:T(8,128)(2,1)} %pad_maximum_fusion.1), channel_id=1, source_target_pairs={{2,0},{4,2},{6,4},{8,6},{10,8},{12,10},{14,12},{3,1},{5,3},{7,5},{... | collective-permute-start | bytes 1253384 | tf_op jit(solution)/shard_map/ppermute | solution.py:314
  10.7 2.2 %copy-done = bf16[1024,2048]{1,0:T(8,128)(2,1)S(1)} copy-done((bf16[1024,2048]{1,0:T(8,128)(2,1)S(1)}, bf16[1024,2048]{1,0:T(8,128)(2,1)}, u32[]{:S(2)}) %copy-start) | copy-done | bytes 4194328
  12.9 2.7 %project.1 = (bf16[256,512]{1,0:T(8,128)(2,1)}, bf16[256,512]{1,0:T(8,128)(2,1)}, f32[512,512]{1,0:T(8,128)S(1)}) custom-call(s32[1]{0:T(128)} %bitcast.core_ref, bf16[32,2,16,2048]{3,2,1,0:T(8,128)(2,1)S(1)} %bitcast.20, bf16[2048,512]{1,0:T(8,128)(2,1)S(1)} %copy-done.1), custom_call_target="tpu_custom_call" | custom-call | flops 1 | bytes 1 | tf_op jit(solution)/shard_map/project/pallas_call | solution.py:290
  15.5 1.0 %copy-done.2 = f32[512,512]{1,0:T(8,128)} copy-done((f32[512,512]{1,0:T(8,128)}, f32[512,512]{1,0:T(8,128)S(1)}, u32[]{:S(2)}) %copy-start.2) | copy-done | bytes 1048600
  16.5 1.0 %collective-permute-start.3 = (bf16[256,512]{1,0:T(8,128)(2,1)}, bf16[256,512]{1,0:T(8,128)(2,1)S(1)}, u32[]{:S(2)}, u32[]{:S(2)}) collective-permute-start(bf16[256,512]{1,0:T(8,128)(2,1)} %get-tuple-element.25), channel_id=1, source_target_pairs={{0,1},{1,0},{2,3},{3,2},{4,5},{5,4},{6,7},{7,6},{8,9},{9,8},{10,11... | collective-permute-start | bytes 786440 | tf_op jit(solution)/shard_map/ppermute | solution.py:348
  17.6 0.9 %broadcast_in_dim.31 = f32[49,4,128]{2,1,0:T(4,128)S(1)} reshape(f32[7,7,512]{2,1,0:T(8,128)} %param.15) | data formatting | bytes 200704 | tf_op jit(solution)/shard_map/broadcast_in_dim | solution.py:411
  18.7 0.2 collective-permute-done.3.upper
  18.9 0.4 collective-permute-done.4.lower
  19.2 1.2 %copy-done.3 = f32[512,512]{1,0:T(8,128)S(1)} copy-done((f32[512,512]{1,0:T(8,128)S(1)}, f32[512,512]{1,0:T(8,128)}, u32[]{:S(2)}) %copy-start.3) | copy-done | bytes 1048600
  20.5 1.1 %combine.1 = (bf16[4,32,512]{2,1,0:T(8,128)(2,1)S(1)}, bf16[4,32,512]{2,1,0:T(8,128)(2,1)S(1)}, bf16[4,32,512]{2,1,0:T(8,128)(2,1)S(1)}, bf16[4,32,512]{2,1,0:T(8,128)(2,1)S(1)}) custom-call(s32[4]{0:T(128)S(1)} %pad_add_fusion.1.turns_ref, f32[512,512]{1,0:T(8,128)S(1)} %copy-done.3, bf16[256,512]{1,0:T(8,128)(2,1)S(1)} %collective-permute-done.3.upper, ...), custom_call_target="tpu_custom_call" | custom-call | flops 1 | bytes 1 | tf_op jit(solution)/shard_map/combine/pallas_call | solution.py:290
  21.6 4.5 %collective-permute-start.5 = (bf16[4,32,512]{2,1,0:T(8,128)(2,1)S(1)}, bf16[4,32,512]{2,1,0:T(8,128)(2,1)S(1)}, u32[]{:S(2)}, u32[]{:S(2)}) collective-permute-start(bf16[4,32,512]{2,1,0:T(8,128)(2,1)S(1)} %get-tuple-element.27), channel_id=1, source_target_pairs={{0,0},{1,8},{2,2},{3,10},{4,4},{5,12},{6,6},{7,14},{8,1},{9,9},{10... | collective-permute-start | bytes 393224 | tf_op jit(solution)/shard_map/ppermute | solution.py:373
  26.0 0.2 collective-permute-start.6
  26.2 1.6 %collective-permute-start.7 = (bf16[4,32,512]{2,1,0:T(8,128)(2,1)S(1)}, bf16[4,32,512]{2,1,0:T(8,128)(2,1)S(1)}, u32[]{:S(2)}, u32[]{:S(2)}) collective-permute-start(bf16[4,32,512]{2,1,0:T(8,128)(2,1)S(1)} %get-tuple-element.29), channel_id=1, source_target_pairs={{0,4},{1,12},{2,6},{3,14},{4,0},{5,8},{6,2},{7,10},{8,5},{9,13},{1... | collective-permute-start | bytes 393224 | tf_op jit(solution)/shard_map/ppermute | solution.py:373
  27.8 1.9 %collective-permute-start.8 = (bf16[4,32,512]{2,1,0:T(8,128)(2,1)S(1)}, bf16[4,32,512]{2,1,0:T(8,128)(2,1)S(1)}, u32[]{:S(2)}, u32[]{:S(2)}) collective-permute-start(bf16[4,32,512]{2,1,0:T(8,128)(2,1)S(1)} %get-tuple-element.30), channel_id=1, source_target_pairs={{0,6},{1,14},{2,0},{3,8},{4,2},{5,10},{6,4},{7,12},{8,7},{9,15},{1... | collective-permute-start | bytes 393224 | tf_op jit(solution)/shard_map/ppermute | solution.py:373
  29.7 0.1 broadcast_in_dim.32.taps
  29.8 1.6 %copy-done.4 = bf16[512,2048]{1,0:T(8,128)(2,1)S(1)} copy-done((bf16[512,2048]{1,0:T(8,128)(2,1)S(1)}, bf16[512,2048]{1,0:T(8,128)(2,1)}, u32[]{:S(2)}) %copy-start.4) | copy-done | bytes 2097176
  31.4 10.0 %up.1 = (f32[512,512]{1,0:T(8,128)S(1)}, f32[512,128]{1,0:T(8,128)S(1)}, bf16[512,2048]{1,0:T(8,128)(2,1)S(1)}, f32[512,2048]{1,0:T(8,128)S(1)}) custom-call(s32[1]{0:T(128)} %bitcast.core_ref, bf16[3,136,512]{2,1,0:T(8,128)(2,1)S(1)} %collective-permute-done.1.left, bf16[4,128,512]{2,1,0:T(8,128)(2,1)S(1)} %bitcast.23, ...), custom_call_target="tpu_custom_call" | custom-call | flops 4294967296 | bytes 11909120 | tf_op jit(solution)/shard_map/up/pallas_call | solution.py:290
  41.5 6.4 %back.1 = (f32[4,128,512]{2,1,0:T(8,128)S(1)}, bf16[4,128,512]{2,1,0:T(8,128)(2,1)S(1)}) custom-call(s32[4]{0:T(128)S(1)} %pad_add_fusion.places_ref, bf16[4,128,512]{2,1,0:T(8,128)(2,1)S(1)} %bitcast.24, f32[512,512]{1,0:T(8,128)S(1)} %get-tuple-element.19.normal_form, f32[512,128]{1,0:T(8,128)S(1)} %get-tuple-element.20.inv_scale, ...), custom_call_target="tpu_custom_call" | custom-call | flops 4294967296 | bytes 14424064 | tf_op jit(solution)/shard_map/back/pallas_call | solution.py:290
  47.9 2.9 %collective-permute-start.10 = (bf16[3,128,512]{2,1,0:T(8,128)(2,1)S(1)}, bf16[3,128,512]{2,1,0:T(8,128)(2,1)S(1)}, u32[]{:S(2)}, u32[]{:S(2)}) collective-permute-start(bf16[3,128,512]{2,1,0:T(8,128)(2,1)S(1)} %get-tuple-element.33), channel_id=1, source_target_pairs={{2,0},{4,2},{6,4},{8,6},{10,8},{12,10},{14,12},{3,1},{5,3},{7,5},{... | collective-permute-start | bytes 1179656 | tf_op jit(solution)/shard_map/ppermute | solution.py:323
  50.9 2.3 %collective-permute-start.9 = (bf16[3,128,512]{2,1,0:T(8,128)(2,1)S(1)}, bf16[3,128,512]{2,1,0:T(8,128)(2,1)S(1)}, u32[]{:S(2)}, u32[]{:S(2)}) collective-permute-start(bf16[3,128,512]{2,1,0:T(8,128)(2,1)S(1)} %get-tuple-element.34), channel_id=1, source_target_pairs={{0,2},{2,4},{4,6},{6,8},{8,10},{10,12},{12,14},{1,3},{3,5},{5,7},{... | collective-permute-start | bytes 1179656 | tf_op jit(solution)/shard_map/ppermute | solution.py:322
  53.3 4.2 %collective-permute-start.12 = (bf16[3,8,512]{2,1,0:T(8,128)(2,1)S(1)}, bf16[3,8,512]{2,1,0:T(8,128)(2,1)S(1)}, u32[]{:S(2)}, u32[]{:S(2)}) collective-permute-start(bf16[3,8,512]{2,1,0:T(8,128)(2,1)S(1)} %get-tuple-element.37), channel_id=1, source_target_pairs={{2,1},{3,0},{4,3},{5,2},{6,5},{7,4},{8,7},{9,6},{10,9},{11,8},{12,... | collective-permute-start | bytes 73736 | tf_op jit(solution)/shard_map/ppermute | solution.py:331
  57.5 1.9 %collective-permute-start.11 = (bf16[3,8,512]{2,1,0:T(8,128)(2,1)S(1)}, bf16[3,8,512]{2,1,0:T(8,128)(2,1)S(1)}, u32[]{:S(2)}, u32[]{:S(2)}) collective-permute-start(bf16[3,8,512]{2,1,0:T(8,128)(2,1)S(1)} %get-tuple-element.38), channel_id=1, source_target_pairs={{0,3},{1,2},{2,5},{3,4},{4,7},{5,6},{6,9},{7,8},{8,11},{9,10},{10,... | collective-permute-start | bytes 73736 | tf_op jit(solution)/shard_map/ppermute | solution.py:330
  59.5 2.7 %inner.1 = f32[4,128,512]{2,1,0:T(8,128)S(1)} custom-call(s32[1]{0:T(128)} %bitcast.core_ref, bf16[4,128,512]{2,1,0:T(8,128)(2,1)S(1)} %get-tuple-element.31.middle, bf16[4,8,512]{2,1,0:T(8,128)(2,1)S(1)} %collective-permute-done.13.edge, f32[49,4,8,128]{3,2,1,0:T(8,128)S(1)} %broadcast_in_dim.32.taps, f32[4,128,512]{2,1,0:T(8,128)S(1)} %get-tuple-element.32.mismatch), custom_call_target="tpu_custom_call" | custom-call | flops 1073741824 | bytes 3457024 | tf_op jit(solution)/shard_map/inner/pallas_call | solution.py:290
  62.2 7.4 %collective-permute-done.12.right_edge = bf16[3,8,512]{2,1,0:T(8,128)(2,1)S(1)} collective-permute-done((bf16[3,8,512]{2,1,0:T(8,128)(2,1)S(1)}, bf16[3,8,512]{2,1,0:T(8,128)(2,1)S(1)}, u32[]{:S(2)}, u32[]{:S(2)}) %collective-permute-start.12) | collective-permute-done | bytes 24608 | tf_op jit(solution)/shard_map/ppermute | solution.py:331
  69.6 2.3 %rim.1 = f32[4,128,512]{2,1,0:T(8,128)S(1)} custom-call(s32[1]{0:T(128)} %bitcast.core_ref, bf16[3,128,512]{2,1,0:T(8,128)(2,1)S(1)} %collective-permute-done.9.left, bf16[3,128,512]{2,1,0:T(8,128)(2,1)S(1)} %collective-permute-done.10.right, bf16[3,8,512]{2,1,0:T(8,128)(2,1)S(1)} %collective-permute-done.11.left_edge, ...), custom_call_target="tpu_custom_call" | custom-call | flops 1073741824 | bytes 3735552 | tf_op jit(solution)/shard_map/rim/pallas_call | solution.py:290
  71.9 1.6 %copy.14 = f32[128,4,512]{2,1,0:T(4,128)} copy(f32[128,4,512]{2,0,1:T(8,128)S(1)} %bitcast.25) | data formatting | bytes 2097152 | tf_op jit(solution)/shard_map/transpose | solution.py:474
  (42 shorter events, 0.5 us)
Async XLA Ops:
  0.0 10.7 %copy-start.1 = (bf16[2048,512]{1,0:T(8,128)(2,1)S(1)}, bf16[2048,512]{1,0:T(8,128)(2,1)}, u32[]{:S(2)}) copy-start(bf16[2048,512]{1,0:T(8,128)(2,1)} %weight) | copy-start | bytes 6291460
  1.3 1.6 %collective-permute-start = (bf16[4,8,512]{2,1,0:T(8,128)(2,1)S(1)}, bf16[4,8,512]{2,1,0:T(8,128)(2,1)S(1)}, u32[]{:S(2)}, u32[]{:S(2)}) collective-permute-start(bf16[4,8,512]{2,1,0:T(8,128)(2,1)S(1)} %slice_select_fusion), channel_id=1, source_target_pairs={{0,1},{1,0},{2,3},{3,2},{4,5},{5,4},{6,7},{7,6},{8,9},{9,8},{10,11... | collective-permute-start | bytes 98312 | tf_op jit(solution)/shard_map/ppermute | solution.py:310
  3.7 24.1 %collective-permute-start.1 = (bf16[3,136,512]{2,1,0:T(8,128)(2,1)}, bf16[3,136,512]{2,1,0:T(8,128)(2,1)S(1)}, u32[]{:S(2)}, u32[]{:S(2)}) collective-permute-start(bf16[3,136,512]{2,1,0:T(8,128)(2,1)} %pad_maximum_fusion), channel_id=1, source_target_pairs={{0,2},{2,4},{4,6},{6,8},{8,10},{10,12},{12,14},{1,3},{3,5},{5,7},{... | collective-permute-start | bytes 1253384 | tf_op jit(solution)/shard_map/ppermute | solution.py:313
  7.6 22.1 %collective-permute-start.2 = (bf16[3,136,512]{2,1,0:T(8,128)(2,1)}, bf16[3,136,512]{2,1,0:T(8,128)(2,1)S(1)}, u32[]{:S(2)}, u32[]{:S(2)}) collective-permute-start(bf16[3,136,512]{2,1,0:T(8,128)(2,1)} %pad_maximum_fusion.1), channel_id=1, source_target_pairs={{2,0},{4,2},{6,4},{8,6},{10,8},{12,10},{14,12},{3,1},{5,3},{7,5},{... | collective-permute-start | bytes 1253384 | tf_op jit(solution)/shard_map/ppermute | solution.py:314
  10.7 2.2 %copy-start = (bf16[1024,2048]{1,0:T(8,128)(2,1)S(1)}, bf16[1024,2048]{1,0:T(8,128)(2,1)}, u32[]{:S(2)}) copy-start(bf16[1024,2048]{1,0:T(8,128)(2,1)} %param.12) | copy-start | bytes 12582916
  15.5 1.0 %copy-start.2 = (f32[512,512]{1,0:T(8,128)}, f32[512,512]{1,0:T(8,128)S(1)}, u32[]{:S(2)}) copy-start(f32[512,512]{1,0:T(8,128)S(1)} %get-tuple-element.24.home) | copy-start | bytes 3145732
  16.5 13.3 %copy-start.7 = (f32[2048]{0:T(1024)S(1)}, f32[2048]{0:T(1024)}, u32[]{:S(2)}) copy-start(f32[2048]{0:T(1024)} %param.20) | copy-start | bytes 24580
  16.5 13.3 %copy-start.8 = (f32[512]{0:T(512)S(1)}, f32[512]{0:T(512)}, u32[]{:S(2)}) copy-start(f32[512]{0:T(512)} %param.16) | copy-start | bytes 6148
  16.5 13.3 %copy-start.9 = (f32[512]{0:T(512)S(1)}, f32[512]{0:T(512)}, u32[]{:S(2)}) copy-start(f32[512]{0:T(512)} %param.18) | copy-start | bytes 6148
  16.5 13.3 %copy-start.10 = (f32[512]{0:T(512)S(1)}, f32[512]{0:T(512)}, u32[]{:S(2)}) copy-start(f32[512]{0:T(512)} %param.17) | copy-start | bytes 6148
  16.5 2.3 %collective-permute-start.3 = (bf16[256,512]{1,0:T(8,128)(2,1)}, bf16[256,512]{1,0:T(8,128)(2,1)S(1)}, u32[]{:S(2)}, u32[]{:S(2)}) collective-permute-start(bf16[256,512]{1,0:T(8,128)(2,1)} %get-tuple-element.25), channel_id=1, source_target_pairs={{0,1},{1,0},{2,3},{3,2},{4,5},{5,4},{6,7},{7,6},{8,9},{9,8},{10,11... | collective-permute-start | bytes 786440 | tf_op jit(solution)/shard_map/ppermute | solution.py:348
  17.5 1.7 %collective-permute-start.4 = (bf16[256,512]{1,0:T(8,128)(2,1)}, bf16[256,512]{1,0:T(8,128)(2,1)S(1)}, u32[]{:S(2)}, u32[]{:S(2)}) collective-permute-start(bf16[256,512]{1,0:T(8,128)(2,1)} %get-tuple-element.26), channel_id=1, source_target_pairs={{0,1},{1,0},{2,3},{3,2},{4,5},{5,4},{6,7},{7,6},{8,9},{9,8},{10,11... | collective-permute-start | bytes 786440 | tf_op jit(solution)/shard_map/ppermute | solution.py:348
  19.2 1.2 %copy-start.3 = (f32[512,512]{1,0:T(8,128)S(1)}, f32[512,512]{1,0:T(8,128)}, u32[]{:S(2)}) copy-start(f32[512,512]{1,0:T(8,128)} %copy-done.2) | copy-start | bytes 3145732
  21.6 19.8 %collective-permute-start.5 = (bf16[4,32,512]{2,1,0:T(8,128)(2,1)S(1)}, bf16[4,32,512]{2,1,0:T(8,128)(2,1)S(1)}, u32[]{:S(2)}, u32[]{:S(2)}) collective-permute-start(bf16[4,32,512]{2,1,0:T(8,128)(2,1)S(1)} %get-tuple-element.27), channel_id=1, source_target_pairs={{0,0},{1,8},{2,2},{3,10},{4,4},{5,12},{6,6},{7,14},{8,1},{9,9},{10... | collective-permute-start | bytes 393224 | tf_op jit(solution)/shard_map/ppermute | solution.py:373
  26.0 15.4 %collective-permute-start.6 = (bf16[4,32,512]{2,1,0:T(8,128)(2,1)S(1)}, bf16[4,32,512]{2,1,0:T(8,128)(2,1)S(1)}, u32[]{:S(2)}, u32[]{:S(2)}) collective-permute-start(bf16[4,32,512]{2,1,0:T(8,128)(2,1)S(1)} %get-tuple-element.28), channel_id=1, source_target_pairs={{0,2},{1,10},{2,4},{3,12},{4,6},{5,14},{6,0},{7,8},{8,3},{9,11},{1... | collective-permute-start | bytes 393224 | tf_op jit(solution)/shard_map/ppermute | solution.py:373
  26.2 15.2 %collective-permute-start.7 = (bf16[4,32,512]{2,1,0:T(8,128)(2,1)S(1)}, bf16[4,32,512]{2,1,0:T(8,128)(2,1)S(1)}, u32[]{:S(2)}, u32[]{:S(2)}) collective-permute-start(bf16[4,32,512]{2,1,0:T(8,128)(2,1)S(1)} %get-tuple-element.29), channel_id=1, source_target_pairs={{0,4},{1,12},{2,6},{3,14},{4,0},{5,8},{6,2},{7,10},{8,5},{9,13},{1... | collective-permute-start | bytes 393224 | tf_op jit(solution)/shard_map/ppermute | solution.py:373
  27.8 13.7 %collective-permute-start.8 = (bf16[4,32,512]{2,1,0:T(8,128)(2,1)S(1)}, bf16[4,32,512]{2,1,0:T(8,128)(2,1)S(1)}, u32[]{:S(2)}, u32[]{:S(2)}) collective-permute-start(bf16[4,32,512]{2,1,0:T(8,128)(2,1)S(1)} %get-tuple-element.30), channel_id=1, source_target_pairs={{0,6},{1,14},{2,0},{3,8},{4,2},{5,10},{6,4},{7,12},{8,7},{9,15},{1... | collective-permute-start | bytes 393224 | tf_op jit(solution)/shard_map/ppermute | solution.py:373
  29.8 1.6 %copy-start.4 = (bf16[512,2048]{1,0:T(8,128)(2,1)S(1)}, bf16[512,2048]{1,0:T(8,128)(2,1)}, u32[]{:S(2)}) copy-start(bf16[512,2048]{1,0:T(8,128)(2,1)} %w_in.3) | copy-start | bytes 6291460
  31.4 10.0 %copy-start.5 = (bf16[512,2048]{1,0:T(8,128)(2,1)S(1)}, bf16[512,2048]{1,0:T(8,128)(2,1)}, u32[]{:S(2)}) copy-start(bf16[512,2048]{1,0:T(8,128)(2,1)} %w_in.3) | copy-start | bytes 6291460
  31.4 10.0 %copy-start.6 = (bf16[2048,512]{1,0:T(8,128)(2,1)S(1)}, bf16[2048,512]{1,0:T(8,128)(2,1)}, u32[]{:S(2)}) copy-start(bf16[2048,512]{1,0:T(8,128)(2,1)} %w_out.1) | copy-start | bytes 6291460
  31.4 10.0 %copy-start.11 = (f32[512]{0:T(512)S(1)}, f32[512]{0:T(512)}, u32[]{:S(2)}) copy-start(f32[512]{0:T(512)} %param.22) | copy-start | bytes 6148
  31.4 10.1 %copy-start.12 = (f32[512]{0:T(512)S(1)}, f32[512]{0:T(512)}, u32[]{:S(2)}) copy-start(f32[512]{0:T(512)} %param.23) | copy-start | bytes 6148
  47.9 21.7 %collective-permute-start.10 = (bf16[3,128,512]{2,1,0:T(8,128)(2,1)S(1)}, bf16[3,128,512]{2,1,0:T(8,128)(2,1)S(1)}, u32[]{:S(2)}, u32[]{:S(2)}) collective-permute-start(bf16[3,128,512]{2,1,0:T(8,128)(2,1)S(1)} %get-tuple-element.33), channel_id=1, source_target_pairs={{2,0},{4,2},{6,4},{8,6},{10,8},{12,10},{14,12},{3,1},{5,3},{7,5},{... | collective-permute-start | bytes 1179656 | tf_op jit(solution)/shard_map/ppermute | solution.py:323
  50.9 18.7 %collective-permute-start.9 = (bf16[3,128,512]{2,1,0:T(8,128)(2,1)S(1)}, bf16[3,128,512]{2,1,0:T(8,128)(2,1)S(1)}, u32[]{:S(2)}, u32[]{:S(2)}) collective-permute-start(bf16[3,128,512]{2,1,0:T(8,128)(2,1)S(1)} %get-tuple-element.34), channel_id=1, source_target_pairs={{0,2},{2,4},{4,6},{6,8},{8,10},{10,12},{12,14},{1,3},{3,5},{5,7},{... | collective-permute-start | bytes 1179656 | tf_op jit(solution)/shard_map/ppermute | solution.py:322
  53.2 6.2 %collective-permute-start.13 = (bf16[4,8,512]{2,1,0:T(8,128)(2,1)S(1)}, bf16[4,8,512]{2,1,0:T(8,128)(2,1)S(1)}, u32[]{:S(2)}, u32[]{:S(2)}) collective-permute-start(bf16[4,8,512]{2,1,0:T(8,128)(2,1)S(1)} %slice_select_fusion.1), channel_id=1, source_target_pairs={{0,1},{1,0},{2,3},{3,2},{4,5},{5,4},{6,7},{7,6},{8,9},{9,8},{10,11... | collective-permute-start | bytes 98312 | tf_op jit(solution)/shard_map/ppermute | solution.py:325
  53.3 16.3 %collective-permute-start.12 = (bf16[3,8,512]{2,1,0:T(8,128)(2,1)S(1)}, bf16[3,8,512]{2,1,0:T(8,128)(2,1)S(1)}, u32[]{:S(2)}, u32[]{:S(2)}) collective-permute-start(bf16[3,8,512]{2,1,0:T(8,128)(2,1)S(1)} %get-tuple-element.37), channel_id=1, source_target_pairs={{2,1},{3,0},{4,3},{5,2},{6,5},{7,4},{8,7},{9,6},{10,9},{11,8},{12,... | collective-permute-start | bytes 73736 | tf_op jit(solution)/shard_map/ppermute | solution.py:331
  57.5 12.1 %collective-permute-start.11 = (bf16[3,8,512]{2,1,0:T(8,128)(2,1)S(1)}, bf16[3,8,512]{2,1,0:T(8,128)(2,1)S(1)}, u32[]{:S(2)}, u32[]{:S(2)}) collective-permute-start(bf16[3,8,512]{2,1,0:T(8,128)(2,1)S(1)} %get-tuple-element.38), channel_id=1, source_target_pairs={{0,3},{1,2},{2,5},{3,4},{4,7},{5,6},{6,9},{7,8},{8,11},{9,10},{10,... | collective-permute-start | bytes 73736 | tf_op jit(solution)/shard_map/ppermute | solution.py:330

commit v3 on v2

v3 whole, which is shorter than its diff:
```python
import functools

import jax
import jax.numpy as jnp
from jax import lax
from jax.experimental import pallas as pl
from jax.experimental.pallas import tpu as pltpu
from jax.sharding import PartitionSpec as P

NORM_EPSILON = 1e-06
REACH = 3
TAPS = 2 * REACH + 1
LANES = 128
SUBLANES = 8
EDGE = 8
CHUNK = 16
COPIES = 2
MLP_TILE = 512
CONTRACT_LAST = (((1,), (1,)), ((), ()))
SWAP = [(0, 1), (1, 0)]


def aligned(start, size):
    return pl.ds(pl.multiple_of(start, size), size)


def lane_tile(tile):
    return slice(tile * LANES, (tile + 1) * LANES)


def project_kernel(other, core_ref, teacher_hbm, weight, *rest):
    *outs, rows, sems = rest
    half = 1 - core_ref[0] if other else core_ref[0]
    lines, wide, depth = rows.shape
    copies = []
    for index in range(COPIES):
        here = pl.ds(index * (lines // COPIES), lines // COPIES)
        copy = pltpu.make_async_copy(
            teacher_hbm.at[here, half], rows.at[here], sems.at[index]
        )
        copy.start()
        copies.append(copy)
    size = lines * wide // COPIES
    for index, copy in enumerate(copies):
        copy.wait()
        here = pl.ds(index * (lines // COPIES), lines // COPIES)
        product = jnp.dot(
            rows[here].reshape(size, depth), weight[...], preferred_element_type=jnp.float32
        )
        out = outs[index * len(outs) // COPIES]
        start = index * size % out.shape[0]
        out[start : start + size] = product.astype(out.dtype)


def combine_kernel(wide, turns_ref, home, upper, lower, *rest):
    *blocks, summed = rest
    half = upper.shape[0]
    for tile in range(summed.shape[0]):
        lanes = lane_tile(tile)
        for start, received in ((0, upper), (half, lower)):
            here = slice(start, start + half)
            summed[tile, here] = home[here, lanes] + received[:, lanes].astype(jnp.float32)
    for index, block in enumerate(blocks):
        tile_u, lines, _ = block.shape
        for u in range(tile_u):
            rows = pl.ds(turns_ref[index] + u, lines, stride=wide)
            for tile in range(summed.shape[0]):
                block[u, :, lane_tile(tile)] = summed[tile, rows, :].astype(jnp.bfloat16)


def spread_taps(taps, kernel):
    for row_tap in range(TAPS):
        for col_tap in range(TAPS):
            for tile in range(taps.shape[1]):
                line = kernel[row_tap, col_tap : col_tap + 1, lane_tile(tile)]
                taps[row_tap * TAPS + col_tap, tile] = jnp.broadcast_to(line, (SUBLANES, LANES))


def spread(padded, place, part, source, start, row, count):
    for tile in range(padded.shape[0]):
        padded[tile, place, pl.ds(row, count), :] = part[
            source, pl.ds(start, count), lane_tile(tile)
        ].astype(jnp.float32)


def depthwise(padded, taps, begin, store, tile_u, count, offset, sources, flip):
    tiles = padded.shape[0]
    blocks = count // (2 * SUBLANES)

    def step(index, carry):
        tile = index // blocks
        base = pl.multiple_of((index % blocks) * (2 * SUBLANES), 2 * SUBLANES)
        sums = [
            [begin(tile, u, base + half * SUBLANES) for u in range(tile_u)] for half in range(2)
        ]
        for row_tap in range(TAPS):
            weights = []
            for col_tap in range(TAPS):
                tap = row_tap * TAPS + col_tap
                weights.append(taps[TAPS * TAPS - 1 - tap if flip else tap, tile])
            for place, source in enumerate(sources):
                for half in range(2):
                    row = base + (half * SUBLANES + row_tap) + offset
                    values = padded[tile, place, pl.ds(row, SUBLANES), :]
                    for u in range(max(0, source - TAPS + 1), min(tile_u, source + 1)):
                        term = weights[source - u] * values
                        sums[half][u] = term if sums[half][u] is None else sums[half][u] + term
        for half in range(2):
            for u in range(tile_u):
                store(tile, u, base + half * SUBLANES, sums[half][u])
        return carry

    lax.fori_loop(0, tiles * blocks, step, 0)


def row_parts(rows):
    half = rows // 2 // 16 * 16
    return slice(0, half), slice(half, rows)


def begins(core, near, tile_v, count):
    top = core if near else 1 - core
    return pl.multiple_of((1 - top) * (tile_v - count), 16)


def up(core, near, count, left, middle, edge, right, kernel, bias, gain, shift, w_in, b_in, refs):
    normal_form, inv_scale, activated, slope, padded, taps, normed, wait_weights = refs
    tile_u, tile_v, channels = middle.shape
    tiles = channels // LANES
    rows = tile_u * count
    hidden = activated.shape[1]
    outside_first = core if near else 1 - core
    start = pl.multiple_of((1 - outside_first) * (tile_v - count - EDGE), EDGE)
    inside = pl.multiple_of(outside_first * EDGE, EDGE)
    outside = pl.multiple_of((1 - outside_first) * (count + EDGE), EDGE)
    spread_taps(taps, kernel)
    place = 0
    for part, rim, begin in ((left, left, tile_v), (middle, edge, 0), (right, right, tile_v)):
        for u in range(part.shape[0]):
            spread(padded, place, part, u, start, inside, count + EDGE)
            if near:
                spread(padded, place, rim, u, begin, outside, EDGE)
            else:
                for tile in range(tiles):
                    padded[tile, place, pl.ds(outside, EDGE), :] = jnp.zeros(
                        (EDGE, LANES), jnp.float32
                    )
            place += 1

    def nothing(tile, u, base):
        return None

    def store(tile, u, base, value):
        row = aligned(u * count + base, SUBLANES)
        normal_form[row, aligned(tile * LANES, LANES)] = value

    sources = range(tile_u + 2 * REACH)
    depthwise(padded, taps, nothing, store, tile_u, count, EDGE - REACH, sources, False)

    def norm_step(index, carry):
        here = aligned(index * CHUNK, CHUNK)
        conv = normal_form[here, :] + bias[...]
        centred = conv - jnp.mean(conv, axis=-1, keepdims=True)
        variance = jnp.mean(centred * centred, axis=-1, keepdims=True)
        inverse = lax.rsqrt(variance + NORM_EPSILON)
        form = centred * inverse
        normal_form[here, :] = form
        inv_scale[here, :] = jnp.broadcast_to(inverse, (CHUNK, LANES))
        normed[here, :] = (form * gain[...] + shift[...]).astype(jnp.bfloat16)
        return carry

    lax.fori_loop(0, rows // CHUNK, norm_step, 0)

    wait_weights()
    for start in range(0, hidden, MLP_TILE):
        tile = slice(start, start + MLP_TILE)
        for here in row_parts(rows):
            pre = (
                jnp.dot(normed[here, :], w_in[:, tile], preferred_element_type=jnp.float32)
                + b_in[:, tile]
            )
            phi = 0.5 * (1.0 + lax.erf(pre * 0.7071067811865476))
            activated[here, tile] = (pre * phi).astype(jnp.bfloat16)
            slope[here, tile] = phi + pre * jnp.exp(-0.5 * pre * pre) * 0.3989422804014327


def back(core, near, count, middle, gain, w_in, w_out, b_out, scale, places, targets, refs):
    (
        normal_form, inv_scale, activated, slope,
        mismatch_out, d_out, last, first, target, d_branch, d_hidden, d_normed,
    ) = refs
    tile_u, tile_v, channels = middle.shape
    rows = tile_u * count
    hidden = activated.shape[1]
    chunks = count // CHUNK
    base = begins(core, near, tile_v, count)
    for index, piece in enumerate(targets):
        target[:, aligned(places[index], piece.shape[1]), :] = piece[...]

    for here in row_parts(rows):
        d_normed[here, :] = jnp.dot(
            activated[here, :], w_out[...], preferred_element_type=jnp.float32
        )

    def mismatch_step(index, carry):
        u = index // chunks
        inside = aligned((index % chunks) * CHUNK, CHUNK)
        whole = aligned(base + (index % chunks) * CHUNK, CHUNK)
        here = aligned(index * CHUNK, CHUNK)
        mismatch = (
            middle[u, whole, :].astype(jnp.float32)
            + scale[...] * (d_normed[here, :] + b_out[...])
            - target[u, whole, :].astype(jnp.float32)
        )
        mismatch_out[u, inside, :] = mismatch
        d_branch[here, :] = (scale[...] * mismatch).astype(jnp.bfloat16)
        return carry

    lax.fori_loop(0, tile_u * chunks, mismatch_step, 0)

    for start in range(0, hidden, MLP_TILE):
        tile = slice(start, start + MLP_TILE)
        for here in row_parts(rows):
            d_activated = lax.dot_general(
                d_branch[here, :], w_out[tile, :], CONTRACT_LAST, preferred_element_type=jnp.float32
            )
            d_hidden[here, tile] = (d_activated * slope[here, tile]).astype(jnp.bfloat16)
    for here in row_parts(rows):
        d_normed[here, :] = lax.dot_general(
            d_hidden[here, :], w_in[...], CONTRACT_LAST, preferred_element_type=jnp.float32
        )

    def d_norm_step(index, carry):
        u = index // chunks
        inside = aligned((index % chunks) * CHUNK, CHUNK)
        here = aligned(index * CHUNK, CHUNK)
        scaled = d_normed[here, :] * gain[...]
        form = normal_form[here, :]
        d_conv = inv_scale[here, :1] * (
            scaled
            - jnp.mean(scaled, axis=-1, keepdims=True)
            - form * jnp.mean(scaled * form, axis=-1, keepdims=True)
        )
        d_out[u, inside, :] = d_conv.astype(jnp.bfloat16)
        return carry

    lax.fori_loop(0, tile_u * chunks, d_norm_step, 0)
    last[:, :count, :] = d_out[tile_u - REACH :]
    first[:, :count, :] = d_out[:REACH]


def near_up_kernel(
    count, core_ref, left, middle, edge, right, kernel, bias, gain, shift, w_in_hbm, b_in,
    normal_form, inv_scale, activated, slope, padded, taps, normed, w_in, sem,
):
    copy = pltpu.make_async_copy(w_in_hbm, w_in, sem)
    copy.start()
    refs = normal_form, inv_scale, activated, slope, padded, taps, normed, copy.wait
    up(
        core_ref[0], True, count, left, middle, edge, right, kernel, bias, gain, shift,
        w_in, b_in, refs,
    )


def near_back_kernel(
    pieces, count, core_ref, places_ref, middle, normal_form, inv_scale, activated, slope,
    gain, w_in, w_out, b_out, scale, *rest,
):
    targets = rest[:pieces]
    mismatch_out, d_out, last, first, own_edge, *scratch = rest[pieces:]
    core = core_ref[0]
    refs = normal_form, inv_scale, activated, slope, mismatch_out, d_out, last, first, *scratch
    back(core, True, count, middle, gain, w_in, w_out, b_out, scale, places_ref, targets, refs)
    border = pl.multiple_of((1 - core) * (count - EDGE), EDGE)
    own_edge[...] = d_out[:, pl.ds(border, EDGE), :]


def far_kernel(
    pieces, count, core_ref, places_ref, left, middle, edge, right, kernel, bias, gain, shift,
    w_in, b_in, w_out, b_out, scale, d_edge, *rest,
):
    targets = rest[:pieces]
    mismatch_out, d_out, last, first = rest[pieces : pieces + 4]
    (
        normal_form, inv_scale, activated, slope, padded, taps, normed,
        target, d_branch, d_hidden, d_normed,
    ) = rest[pieces + 4 :]
    core = core_ref[0]
    refs = normal_form, inv_scale, activated, slope, padded, taps, normed, lambda: None
    up(
        core, False, count, left, middle, edge, right, kernel, bias, gain, shift, w_in, b_in, refs
    )
    refs = (
        normal_form, inv_scale, activated, slope,
        mismatch_out, d_out, last, first, target, d_branch, d_hidden, d_normed,
    )
    back(core, False, count, middle, gain, w_in, w_out, b_out, scale, places_ref, targets, refs)
    last[:, count:, :] = d_edge[d_edge.shape[0] - REACH :]
    first[:, count:, :] = d_edge[:REACH]


def whole_rows(padded, place, near, far, edge, u, start, core, tile_v):
    near_count, far_count = near.shape[1], tile_v - near.shape[1]
    near_base = EDGE + begins(core, True, tile_v, near_count)
    far_base = EDGE + begins(core, False, tile_v, far_count)
    spread(padded, place, near, u, 0, pl.multiple_of(near_base, EDGE), near_count)
    spread(padded, place, far, u, 0, pl.multiple_of(far_base, EDGE), far_count)
    for tile in range(padded.shape[0]):
        rim = edge[u, start : start + EDGE, lane_tile(tile)].astype(jnp.float32)
        nothing = jnp.zeros_like(rim)
        padded[tile, place, 0:EDGE, :] = jnp.where(core == 1, rim, nothing)
        padded[tile, place, EDGE + tile_v : 2 * EDGE + tile_v, :] = jnp.where(
            core == 0, rim, nothing
        )


def inner_kernel(core_ref, near, far, edge, kernel, near_mismatch, far_mismatch, out, padded, taps):
    tile_u, tile_v, channels = out.shape
    core = core_ref[0]
    spread_taps(taps, kernel)
    for u in range(tile_u):
        whole_rows(padded, u, near, far, edge, u, 0, core, tile_v)
    for is_near, mismatch in ((True, near_mismatch), (False, far_mismatch)):
        count = mismatch.shape[1]
        first = begins(core, is_near, tile_v, count)

        def begin(tile, u, base):
            return mismatch[u, aligned(base, SUBLANES), aligned(tile * LANES, LANES)]

        def store(tile, u, base, value):
            out[u, aligned(first + base, SUBLANES), aligned(tile * LANES, LANES)] = value

        own = range(REACH, REACH + tile_u)
        depthwise(padded, taps, begin, store, tile_u, count, first + EDGE - REACH, own, True)


def rim_kernel(
    core_ref, near_left, near_right, far_left, far_right, kernel, inner, out, padded, taps
):
    tile_u, tile_v, channels = inner.shape
    core = core_ref[0]
    far_count = tile_v - near_left.shape[1]
    spread_taps(taps, kernel)
    place = 0
    for near, far in ((near_left, far_left), (near_right, far_right)):
        for u in range(REACH):
            whole_rows(padded, place, near, far, far, u, far_count, core, tile_v)
            place += 1

    def begin(tile, u, base):
        return inner[u, aligned(base, SUBLANES), aligned(tile * LANES, LANES)]

    def store(tile, u, base, value):
        out[aligned(base, SUBLANES), u, aligned(tile * LANES, LANES)] = value

    sides = [*range(REACH), *range(REACH + tile_u, 2 * REACH + tile_u)]
    depthwise(padded, taps, begin, store, tile_u, tile_v, EDGE - REACH, sides, True)


def call(kernel, name, outs, scratch, scalars, arrays, flops, limit, left_in_hbm=()):
    vmem = pl.BlockSpec(memory_space=pltpu.VMEM)
    smem = pl.BlockSpec(memory_space=pltpu.SMEM)
    hbm = pl.BlockSpec(memory_space=pltpu.HBM)
    moved = 1 if flops == 1 else sum(a.size * a.dtype.itemsize for a in [*arrays, *outs])
    arrays = [
        pltpu.with_memory_space_constraint(a, pltpu.HBM) if index in left_in_hbm else a
        for index, a in enumerate(arrays)
    ]
    specs = [hbm if index in left_in_hbm else vmem for index in range(len(arrays))]
    return pl.pallas_call(
        kernel,
        out_shape=tuple(outs),
        in_specs=[smem] * len(scalars) + specs,
        out_specs=(vmem,) * len(outs),
        scratch_shapes=scratch,
        compiler_params=pltpu.CompilerParams(vmem_limit_bytes=limit << 20),
        cost_estimate=pl.CostEstimate(flops=flops, bytes_accessed=moved, transcendentals=0),
        name=name,
    )(*scalars, *arrays)


def send_sides(last, first):
    row_count = lax.axis_size("row")
    forward = [(i, i + 1) for i in range(row_count - 1)]
    backward = [(b, a) for a, b in forward]
    return lax.ppermute(last, "row", forward), lax.ppermute(first, "row", backward)


def with_edge(block, edge):
    return (
        jnp.concatenate([block[-REACH:], edge[-REACH:]], axis=1),
        jnp.concatenate([block[:REACH], edge[:REACH]], axis=1),
    )


def find_target(teacher, proj_weight, core, row, tile_u, tile_v):
    row_count = lax.axis_size("row")
    halves = row_count // 2
    channels = proj_weight.shape[1]
    grid_u = tile_u * row_count
    lines = teacher.shape[0] // grid_u
    scalar = core.astype(jnp.int32)[None]
    half_line = grid_u // 2
    by_half = teacher.reshape(lines, 2, half_line, teacher.shape[1])
    size = (lines * half_line, channels)
    fourth = jax.ShapeDtypeStruct((size[0] // 2, channels), jnp.bfloat16)
    scratch = [
        pltpu.VMEM((lines, half_line, teacher.shape[1]), jnp.bfloat16),
        pltpu.SemaphoreType.DMA((COPIES,)),
    ]
    upper, lower = call(
        functools.partial(project_kernel, True),
        "project_away", [fourth] * 2, scratch, [scalar], [by_half, proj_weight], 1, 12, (0,),
    )
    (home,) = call(
        functools.partial(project_kernel, False),
        "project_home", [jax.ShapeDtypeStruct(size, jnp.float32)],
        scratch, [scalar], [by_half, proj_weight], 1, 12, (0,),
    )
    received = [lax.ppermute(away, "col", SWAP) for away in (upper, lower)]
    turns = [lax.rem(turn + row, halves) * tile_u for turn in range(halves)]
    if lines % 16:
        received = jnp.concatenate(received).astype(jnp.float32)
        summed = (home + received).astype(jnp.bfloat16)
        by_u = summed.reshape(lines, half_line, channels).transpose(1, 0, 2)
        blocks = [lax.dynamic_slice_in_dim(by_u, turn, tile_u) for turn in turns]
    else:
        blocks = call(
            functools.partial(combine_kernel, half_line),
            "combine",
            [jax.ShapeDtypeStruct((tile_u, lines, channels), jnp.bfloat16)] * halves,
            [pltpu.VMEM((channels // LANES, *size[:1], LANES), jnp.float32)],
            [jnp.stack(turns).astype(jnp.int32)],
            [home, *received],
            1,
            8,
        )
    pieces, places = [], []
    for turn in range(halves):
        pairs = []
        for r in range(row_count):
            for c in range(2):
                goal = (halves * c + (turn + r) % halves) * 2 + r // halves
                pairs.append((r * 2 + c, goal))
        pieces.append(lax.ppermute(blocks[turn], ("row", "col"), pairs))
        places.append(lax.rem(row + (halves - turn), halves) * lines)
    places = jnp.stack(places).astype(jnp.int32)
    if lines % 16:
        whole = jnp.zeros((tile_u, tile_v, channels), jnp.bfloat16)
        for index, piece in enumerate(pieces):
            whole = lax.dynamic_update_slice_in_dim(whole, piece, places[index], axis=1)
        return [whole], jnp.zeros((1,), jnp.int32)
    return pieces, places


def on_device(
    teacher,
    proj_weight,
    student,
    dw_kernel,
    dw_bias,
    norm_gain,
    norm_bias,
    w_in,
    b_in,
    w_out,
    b_out,
    layer_scale,
):
    core = lax.axis_index("col")
    row = lax.axis_index("row")
    tile_v, tile_u, channels = student.shape
    hidden = w_in.shape[1]
    tiles = channels // LANES
    wide = tile_v + 2 * EDGE
    scalar = core.astype(jnp.int32)[None]
    f32, bf16 = jnp.float32, jnp.bfloat16
    far_count = tile_v * 3 // 8 // CHUNK * CHUNK
    near_count = tile_v - far_count

    own_edge = jnp.where(core == 0, student[-EDGE:], student[:EDGE]).transpose(1, 0, 2)
    edge = lax.ppermute(own_edge, "col", SWAP)
    middle = student.transpose(1, 0, 2)
    last, first = with_edge(middle, edge)
    left, right = send_sides(last, first)
    held, _, _ = lax.optimization_barrier((proj_weight, last, first))
    targets, places = find_target(teacher, held, core, row, tile_u, tile_v)
    matmul = 2 * tile_u * tile_v * channels * hidden
    whole_tile = (tile_u, tile_v, channels)
    taps = pltpu.VMEM((TAPS * TAPS, tiles, SUBLANES, LANES), f32)

    def padded(places, count):
        return pltpu.VMEM((tiles, places, count + 2 * EDGE, LANES), f32)

    def kept(make, rows):
        return [
            make((rows, channels), f32),
            make((rows, LANES), f32),
            make((rows, hidden), bf16),
            make((rows, hidden), f32),
        ]

    def up_scratch(count):
        return [
            padded(tile_u + 2 * REACH, count), taps, pltpu.VMEM((tile_u * count, channels), bf16)
        ]

    def back_scratch(rows):
        return [
            pltpu.VMEM(whole_tile, bf16),
            pltpu.VMEM((rows, channels), bf16),
            pltpu.VMEM((rows, hidden), bf16),
            pltpu.VMEM((rows, channels), f32),
        ]

    def back_outs(count, sent):
        part, side = (tile_u, count, channels), (REACH, sent, channels)
        kinds = [(part, f32), (part, bf16), (side, bf16), (side, bf16)]
        return [jax.ShapeDtypeStruct(*kind) for kind in kinds]

    conv_args = [left, middle, edge, right, dw_kernel, dw_bias[None], norm_gain[None]]
    conv_args += [norm_bias[None], w_in, b_in[None]]
    near_rows, far_rows = tile_u * near_count, tile_u * far_count
    saved = call(
        functools.partial(near_up_kernel, near_count),
        "near_up",
        kept(jax.ShapeDtypeStruct, near_rows),
        [*up_scratch(near_count), pltpu.VMEM(w_in.shape, bf16), pltpu.SemaphoreType.DMA],
        [scalar],
        conv_args,
        2 * matmul,
        16,
        (8,),
    )
    near_mismatch, near, last, first, own_edge = call(
        functools.partial(near_back_kernel, len(targets), near_count),
        "near_back",
        back_outs(near_count, near_count)
        + [jax.ShapeDtypeStruct((tile_u, EDGE, channels), bf16)],
        back_scratch(near_rows),
        [scalar, places],
        [middle, *saved, norm_gain[None], w_in, w_out, b_out[None], layer_scale[None], *targets],
        1,
        16,
    )
    near_left, near_right = send_sides(last, first)
    d_edge = lax.ppermute(own_edge, "col", SWAP)
    far_mismatch, far, last, first = call(
        functools.partial(far_kernel, len(targets), far_count),
        "far",
        back_outs(far_count, far_count + EDGE),
        [*kept(pltpu.VMEM, far_rows), *up_scratch(far_count), *back_scratch(far_rows)],
        [scalar, places],
        [*conv_args, w_out, b_out[None], layer_scale[None], d_edge, *targets],
        1,
        24,
    )
    far_left, far_right = send_sides(last, first)
    (inner,) = call(
        inner_kernel,
        "inner",
        [jax.ShapeDtypeStruct(whole_tile, f32)],
        [padded(tile_u, tile_v), taps],
        [scalar],
        [near, far, d_edge, dw_kernel, near_mismatch, far_mismatch],
        1,
        8,
    )
    (grad,) = call(
        rim_kernel,
        "rim",
        [jax.ShapeDtypeStruct((tile_v, tile_u, channels), f32)],
        [padded(2 * REACH, tile_v), taps],
        [scalar],
        [near_left, near_right, far_left, far_right, dw_kernel, inner],
        1,
        8,
    )
    return grad


def solution(mesh):
    placed = (
        P(("groups", "row"), "col"),
        P("col", None),
        P(("groups", "col"), "row", None),
        P(),
        P(),
        P(),
        P(),
        P(),
        P(),
        P(),
        P(),
        P(),
    )
    return jax.shard_map(
        on_device,
        mesh=mesh,
        in_specs=placed,
        out_specs=P(("groups", "col"), "row", None),
        check_vma=False,
    )
```

time: 74.4 us -> 81.5 us (1.095)
  Pallas kernels: 25 us -> 41 us
  local copies, waits for them, and re-layouts: 10.1 us -> 1.39 us
  starting transfers between devices: 27.5 us -> 31.2 us
  waiting for transfers between devices: 8.85 us -> 5.44 us
    pallas_call x6 -> x8, Pallas kernels: 25 us -> 41 us  [call(): pl.pallas_call(kernel, out_shape=tuple(outs), in_specs=[smem] * len(scala...]
    unnamed x27 -> x21, local copies, waits for them, and re-layouts: 7.28 us -> 1.33 us
    ppermute x8, waiting for transfers between devices: 8.27 us -> 5.42 us  [the longest x3 3.75 us: send_sides(): lax.ppermute(first, 'row', backward)]
    ppermute x4, starting transfers between devices: 8.12 us -> 10 us  [find_target(): pieces.append(lax.ppermute(blocks[turn], ('row', 'col'), pairs))]
    ppermute x8, starting transfers between devices: 18.4 us -> 20.1 us  [the longest x3 11.6 us: send_sides(): lax.ppermute(first, 'row', backward)]
    transpose x1 -> x0, local copies, waits for them, and re-layouts: 1.65 us -> none  [on_device(): return grad.transpose(1, 0, 2)]
    broadcast_in_dim x2 -> x0, local copies, waits for them, and re-layouts: 1.02 us -> none  [on_device(): jnp.broadcast_to(dw_kernel.reshape(TAPS * TAPS, tiles, 1, LANES), (TAPS *...]
  transfers between devices with their start and end apart: 14 -> 14, of which waited for: 4 -> 3; matrix products, arithmetic and copies ran while one was open for 3% -> 1% of each run, Pallas kernels for 22% -> 37%
where the time goes in v3:
time: 81.5 us; the launch traced here: 81.1 us
  Pallas kernels  41 us (50%)
  starting transfers between devices  31.2 us (38%)
  waiting for transfers between devices  5.44 us (7%)
  other arithmetic  1.74 us (2%)
  local copies, waits for them, and re-layouts  1.39 us (2%)
    pallas_call x8, Pallas kernels, call(): pl.pallas_call(kernel, out_shape=tuple(outs), in_specs=[smem] * len(scala...  41 us
    ppermute x3, starting transfers between devices, send_sides(): lax.ppermute(first, 'row', backward)  11.6 us
    ppermute x4, starting transfers between devices, find_target(): pieces.append(lax.ppermute(blocks[turn], ('row', 'col'), pairs))  10 us
    ppermute x3, starting transfers between devices, send_sides(): lax.ppermute(last, 'row', forward)  6.95 us
    ppermute x3, waiting for transfers between devices, send_sides(): lax.ppermute(first, 'row', backward)  3.75 us
  transfers between devices with their start and end apart: 14, of which 3 were waited for; matrix products, arithmetic and copies ran while one was open for 1% of the time, Pallas kernels for 37%

profile of v3, /device:TPU:13, one launch (start us, length us, event | category | flops | bytes accessed | tf_op | source)
XLA Modules:
  0.0 81.1 jit_solution(3848178031137657375)
XLA Ops:
  0.0 1.3 %copy.18 = bf16[128,4,512]{2,0,1:T(8,128)(2,1)S(1)} copy(bf16[128,4,512]{2,1,0:T(4,128)(2,1)} %param.14) | data formatting | bytes 1048576 | tf_op args[2]
  1.3 0.7 collective-permute-start
  2.0 0.1 fusion.1
  2.1 0.8 collective-permute-done.edge
  2.9 0.8 pad_maximum_fusion
  3.7 3.1 %collective-permute-start.1 = (bf16[3,136,512]{2,1,0:T(8,128)(2,1)}, bf16[3,136,512]{2,1,0:T(8,128)(2,1)S(1)}, u32[]{:S(2)}, u32[]{:S(2)}) collective-permute-start(bf16[3,136,512]{2,1,0:T(8,128)(2,1)} %pad_maximum_fusion), channel_id=1, source_target_pairs={{0,2},{2,4},{4,6},{6,8},{8,10},{10,12},{12,14},{1,3},{3,5},{5,7},{... | collective-permute-start | bytes 1253384 | tf_op jit(solution)/shard_map/ppermute | solution.py:386
  6.8 0.8 pad_maximum_fusion.1
  7.6 3.0 %collective-permute-start.2 = (bf16[3,136,512]{2,1,0:T(8,128)(2,1)}, bf16[3,136,512]{2,1,0:T(8,128)(2,1)S(1)}, u32[]{:S(2)}, u32[]{:S(2)}) collective-permute-start(bf16[3,136,512]{2,1,0:T(8,128)(2,1)} %pad_maximum_fusion.1), channel_id=1, source_target_pairs={{2,0},{4,2},{6,4},{8,6},{10,8},{12,10},{14,12},{3,1},{5,3},{7,5},{... | collective-permute-start | bytes 1253384 | tf_op jit(solution)/shard_map/ppermute | solution.py:386
  10.7 3.4 %project_away.1 = (bf16[256,512]{1,0:T(8,128)(2,1)}, bf16[256,512]{1,0:T(8,128)(2,1)}) custom-call(s32[1]{0:T(128)} %bitcast.core_ref, bf16[32,2,16,2048]{3,2,1,0:T(8,128)(2,1)} %bitcast.37, bf16[2048,512]{1,0:T(8,128)(2,1)S(1)} %copy-done), custom_call_target="tpu_custom_call" | custom-call | flops 1 | bytes 1 | tf_op jit(solution)/shard_map/project_away/pallas_call | solution.py:370
  14.1 1.0 %collective-permute-start.3 = (bf16[256,512]{1,0:T(8,128)(2,1)}, bf16[256,512]{1,0:T(8,128)(2,1)}, u32[]{:S(2)}, u32[]{:S(2)}) collective-permute-start(bf16[256,512]{1,0:T(8,128)(2,1)} %get-tuple-element.30), channel_id=1, source_target_pairs={{0,1},{1,0},{2,3},{3,2},{4,5},{5,4},{6,7},{7,6},{8,9},{9,8},{10,11... | collective-permute-start | bytes 786440 | tf_op jit(solution)/shard_map/ppermute | solution.py:420
  15.0 0.1 collective-permute-start.4
  15.1 0.1 pad_add_fusion.places_ref
  15.2 0.1 pad_add_fusion.1.turns_ref
  15.3 2.7 %project_home.1.home = f32[512,512]{1,0:T(8,128)S(1)} custom-call(s32[1]{0:T(128)} %bitcast.core_ref, bf16[32,2,16,2048]{3,2,1,0:T(8,128)(2,1)} %bitcast.38, bf16[2048,512]{1,0:T(8,128)(2,1)S(1)} %copy-done), custom_call_target="tpu_custom_call" | custom-call | flops 1 | bytes 1 | tf_op jit(solution)/shard_map/project_home/pallas_call | solution.py:370
  18.1 1.6 %combine.1 = (bf16[4,32,512]{2,1,0:T(8,128)(2,1)S(1)}, bf16[4,32,512]{2,1,0:T(8,128)(2,1)S(1)}, bf16[4,32,512]{2,1,0:T(8,128)(2,1)S(1)}, bf16[4,32,512]{2,1,0:T(8,128)(2,1)S(1)}) custom-call(s32[4]{0:T(128)S(1)} %pad_add_fusion.1.turns_ref, f32[512,512]{1,0:T(8,128)S(1)} %project_home.1.home, bf16[256,512]{1,0:T(8,128)(2,1)} %collective-permute-done.3.upper, ...), custom_call_target="tpu_custom_call" | custom-call | flops 1 | bytes 1 | tf_op jit(solution)/shard_map/combine/pallas_call | solution.py:370
  19.7 4.5 %collective-permute-start.5 = (bf16[4,32,512]{2,1,0:T(8,128)(2,1)S(1)}, bf16[4,32,512]{2,1,0:T(8,128)(2,1)S(1)}, u32[]{:S(2)}, u32[]{:S(2)}) collective-permute-start(bf16[4,32,512]{2,1,0:T(8,128)(2,1)S(1)} %get-tuple-element.32), channel_id=1, source_target_pairs={{0,0},{1,8},{2,2},{3,10},{4,4},{5,12},{6,6},{7,14},{8,1},{9,9},{10... | collective-permute-start | bytes 393224 | tf_op jit(solution)/shard_map/ppermute | solution.py:445
  24.2 0.1 collective-permute-start.6
  24.3 1.6 %collective-permute-start.7 = (bf16[4,32,512]{2,1,0:T(8,128)(2,1)S(1)}, bf16[4,32,512]{2,1,0:T(8,128)(2,1)S(1)}, u32[]{:S(2)}, u32[]{:S(2)}) collective-permute-start(bf16[4,32,512]{2,1,0:T(8,128)(2,1)S(1)} %get-tuple-element.34), channel_id=1, source_target_pairs={{0,4},{1,12},{2,6},{3,14},{4,0},{5,8},{6,2},{7,10},{8,5},{9,13},{1... | collective-permute-start | bytes 393224 | tf_op jit(solution)/shard_map/ppermute | solution.py:445
  25.9 3.8 %collective-permute-start.8 = (bf16[4,32,512]{2,1,0:T(8,128)(2,1)S(1)}, bf16[4,32,512]{2,1,0:T(8,128)(2,1)S(1)}, u32[]{:S(2)}, u32[]{:S(2)}) collective-permute-start(bf16[4,32,512]{2,1,0:T(8,128)(2,1)S(1)} %get-tuple-element.35), channel_id=1, source_target_pairs={{0,6},{1,14},{2,0},{3,8},{4,2},{5,10},{6,4},{7,12},{8,7},{9,15},{1... | collective-permute-start | bytes 393224 | tf_op jit(solution)/shard_map/ppermute | solution.py:445
  29.7 0.0 copy-start.1
  29.8 8.5 %near_up.1 = (f32[320,512]{1,0:T(8,128)S(1)}, f32[320,128]{1,0:T(8,128)S(1)}, bf16[320,2048]{1,0:T(8,128)(2,1)S(1)}, f32[320,2048]{1,0:T(8,128)S(1)}) custom-call(s32[1]{0:T(128)} %bitcast.core_ref, bf16[3,136,512]{2,1,0:T(8,128)(2,1)S(1)} %collective-permute-done.1.left, bf16[4,128,512]{2,1,0:T(8,128)(2,1)S(1)} %bitcast.21, ...), custom_call_target="tpu_custom_call" | custom-call | flops 2147483648 | bytes 8355840 | tf_op jit(solution)/shard_map/near_up/pallas_call | solution.py:370
  38.3 7.0 %near_back.1 = (f32[4,80,512]{2,1,0:T(8,128)S(1)}, bf16[4,80,512]{2,1,0:T(8,128)(2,1)S(1)}, bf16[3,80,512]{2,1,0:T(8,128)(2,1)S(1)}, bf16[3,80,512]{2,1,0:T(8,128)(2,1)S(1)}, bf16[4,8,512]{2,1,0:T(8,128)(2,1)S(1)}) custom-call(s32[1]{0:T(128)} %bitcast.core_ref, s32[4]{0:T(128)S(1)} %pad_add_fusion.places_ref, bf16[4,128,512]{2,1,0:T(8,128)(2,1)S(1)} %bitcast.22, ...), custom_call_target="tpu_custom_call" | custom-call | flops 1 | bytes 1 | tf_op jit(solution)/shard_map/near_back/pallas_call | solution.py:370
  45.3 1.9 %collective-permute-start.9 = (bf16[3,80,512]{2,1,0:T(8,128)(2,1)S(1)}, bf16[3,80,512]{2,1,0:T(8,128)(2,1)S(1)}, u32[]{:S(2)}, u32[]{:S(2)}) collective-permute-start(bf16[3,80,512]{2,1,0:T(8,128)(2,1)S(1)} %get-tuple-element.36), channel_id=1, source_target_pairs={{0,2},{2,4},{4,6},{6,8},{8,10},{10,12},{12,14},{1,3},{3,5},{5,7},{... | collective-permute-start | bytes 737288 | tf_op jit(solution)/shard_map/ppermute | solution.py:386
  47.3 4.3 %collective-permute-start.10 = (bf16[3,80,512]{2,1,0:T(8,128)(2,1)S(1)}, bf16[3,80,512]{2,1,0:T(8,128)(2,1)S(1)}, u32[]{:S(2)}, u32[]{:S(2)}) collective-permute-start(bf16[3,80,512]{2,1,0:T(8,128)(2,1)S(1)} %get-tuple-element.37), channel_id=1, source_target_pairs={{2,0},{4,2},{6,4},{8,6},{10,8},{12,10},{14,12},{3,1},{5,3},{7,5},{... | collective-permute-start | bytes 737288 | tf_op jit(solution)/shard_map/ppermute | solution.py:386
  51.5 0.9 %collective-permute-start.11 = (bf16[4,8,512]{2,1,0:T(8,128)(2,1)S(1)}, bf16[4,8,512]{2,1,0:T(8,128)(2,1)S(1)}, u32[]{:S(2)}, u32[]{:S(2)}) collective-permute-start(bf16[4,8,512]{2,1,0:T(8,128)(2,1)S(1)} %get-tuple-element.38), channel_id=1, source_target_pairs={{0,1},{1,0},{2,3},{3,2},{4,5},{5,4},{6,7},{7,6},{8,9},{9,8},{10,11... | collective-permute-start | bytes 98312 | tf_op jit(solution)/shard_map/ppermute | solution.py:547
  52.4 0.9 %collective-permute-done.11.d_edge.edge = bf16[4,8,512]{2,1,0:T(8,128)(2,1)S(1)} collective-permute-done((bf16[4,8,512]{2,1,0:T(8,128)(2,1)S(1)}, bf16[4,8,512]{2,1,0:T(8,128)(2,1)S(1)}, u32[]{:S(2)}, u32[]{:S(2)}) %collective-permute-start.11) | collective-permute-done | bytes 32800 | tf_op jit(solution)/shard_map/ppermute | solution.py:547
  53.3 10.6 %far.1 = (f32[4,48,512]{2,1,0:T(8,128)S(1)}, bf16[4,48,512]{2,1,0:T(8,128)(2,1)S(1)}, bf16[3,56,512]{2,1,0:T(8,128)(2,1)S(1)}, bf16[3,56,512]{2,1,0:T(8,128)(2,1)S(1)}) custom-call(s32[1]{0:T(128)} %bitcast.core_ref, s32[4]{0:T(128)S(1)} %pad_add_fusion.places_ref, bf16[3,136,512]{2,1,0:T(8,128)(2,1)S(1)} %collective-permute-done.1.left, ...), custom_call_target="tpu_custom_call" | custom-call | flops 1 | bytes 1 | tf_op jit(solution)/shard_map/far/pallas_call | solution.py:370
  63.9 1.9 %collective-permute-start.12 = (bf16[3,56,512]{2,1,0:T(8,128)(2,1)S(1)}, bf16[3,56,512]{2,1,0:T(8,128)(2,1)S(1)}, u32[]{:S(2)}, u32[]{:S(2)}) collective-permute-start(bf16[3,56,512]{2,1,0:T(8,128)(2,1)S(1)} %get-tuple-element.39), channel_id=1, source_target_pairs={{0,2},{2,4},{4,6},{6,8},{8,10},{10,12},{12,14},{1,3},{3,5},{5,7},{... | collective-permute-start | bytes 516104 | tf_op jit(solution)/shard_map/ppermute | solution.py:386
  65.8 4.3 %collective-permute-start.13 = (bf16[3,56,512]{2,1,0:T(8,128)(2,1)S(1)}, bf16[3,56,512]{2,1,0:T(8,128)(2,1)S(1)}, u32[]{:S(2)}, u32[]{:S(2)}) collective-permute-start(bf16[3,56,512]{2,1,0:T(8,128)(2,1)S(1)} %get-tuple-element.40), channel_id=1, source_target_pairs={{2,0},{4,2},{6,4},{8,6},{10,8},{12,10},{14,12},{3,1},{5,3},{7,5},{... | collective-permute-start | bytes 516104 | tf_op jit(solution)/shard_map/ppermute | solution.py:386
  70.1 2.8 %inner.1 = f32[4,128,512]{2,1,0:T(8,128)S(1)} custom-call(s32[1]{0:T(128)} %bitcast.core_ref, bf16[4,80,512]{2,1,0:T(8,128)(2,1)S(1)} %get-tuple-element.41.near, bf16[4,48,512]{2,1,0:T(8,128)(2,1)S(1)} %get-tuple-element.42.far, bf16[4,8,512]{2,1,0:T(8,128)(2,1)S(1)} %collective-permute-done.11.d_edge.edge, f32[7,7,512]{2,1,0:T(8,128)S(1)} %copy-done.3, ...), custom_call_target="tpu_custom_call" | custom-call | flops 1 | bytes 1 | tf_op jit(solution)/shard_map/inner/pallas_call | solution.py:370
  72.9 3.7 %collective-permute-done.13.far_right = bf16[3,56,512]{2,1,0:T(8,128)(2,1)S(1)} collective-permute-done((bf16[3,56,512]{2,1,0:T(8,128)(2,1)S(1)}, bf16[3,56,512]{2,1,0:T(8,128)(2,1)S(1)}, u32[]{:S(2)}, u32[]{:S(2)}) %collective-permute-start.13) | collective-permute-done | bytes 172064 | tf_op jit(solution)/shard_map/ppermute | solution.py:386
  76.7 4.4 %rim.1 = f32[128,4,512]{2,1,0:T(4,128)} custom-call(s32[1]{0:T(128)} %bitcast.core_ref, bf16[3,80,512]{2,1,0:T(8,128)(2,1)S(1)} %collective-permute-done.9.near_left, bf16[3,80,512]{2,1,0:T(8,128)(2,1)S(1)} %collective-permute-done.10.near_right, bf16[3,56,512]{2,1,0:T(8,128)(2,1)S(1)} %collective-permute-done.12.far_left, ...), custom_call_target="tpu_custom_call" | custom-call | flops 1 | bytes 1 | tf_op jit(solution)/shard_map/rim/pallas_call | solution.py:370
  (32 shorter events, 0.1 us)
Async XLA Ops:
  0.0 10.7 %copy-start = (bf16[2048,512]{1,0:T(8,128)(2,1)S(1)}, bf16[2048,512]{1,0:T(8,128)(2,1)}, u32[]{:S(2)}) copy-start(bf16[2048,512]{1,0:T(8,128)(2,1)} %weight.1) | copy-start | bytes 6291460
  1.3 1.6 %collective-permute-start = (bf16[4,8,512]{2,1,0:T(8,128)(2,1)S(1)}, bf16[4,8,512]{2,1,0:T(8,128)(2,1)S(1)}, u32[]{:S(2)}, u32[]{:S(2)}) collective-permute-start(bf16[4,8,512]{2,1,0:T(8,128)(2,1)S(1)} %fusion), channel_id=1, source_target_pairs={{0,1},{1,0},{2,3},{3,2},{4,5},{5,4},{6,7},{7,6},{8,9},{9,8},{10,11... | collective-permute-start | bytes 98312 | tf_op jit(solution)/shard_map/ppermute | solution.py:482
  3.7 22.2 %collective-permute-start.1 = (bf16[3,136,512]{2,1,0:T(8,128)(2,1)}, bf16[3,136,512]{2,1,0:T(8,128)(2,1)S(1)}, u32[]{:S(2)}, u32[]{:S(2)}) collective-permute-start(bf16[3,136,512]{2,1,0:T(8,128)(2,1)} %pad_maximum_fusion), channel_id=1, source_target_pairs={{0,2},{2,4},{4,6},{6,8},{8,10},{10,12},{12,14},{1,3},{3,5},{5,7},{... | collective-permute-start | bytes 1253384 | tf_op jit(solution)/shard_map/ppermute | solution.py:386
  7.6 22.1 %collective-permute-start.2 = (bf16[3,136,512]{2,1,0:T(8,128)(2,1)}, bf16[3,136,512]{2,1,0:T(8,128)(2,1)S(1)}, u32[]{:S(2)}, u32[]{:S(2)}) collective-permute-start(bf16[3,136,512]{2,1,0:T(8,128)(2,1)} %pad_maximum_fusion.1), channel_id=1, source_target_pairs={{2,0},{4,2},{6,4},{8,6},{10,8},{12,10},{14,12},{3,1},{5,3},{7,5},{... | collective-permute-start | bytes 1253384 | tf_op jit(solution)/shard_map/ppermute | solution.py:386
  14.1 4.0 %collective-permute-start.3 = (bf16[256,512]{1,0:T(8,128)(2,1)}, bf16[256,512]{1,0:T(8,128)(2,1)}, u32[]{:S(2)}, u32[]{:S(2)}) collective-permute-start(bf16[256,512]{1,0:T(8,128)(2,1)} %get-tuple-element.30), channel_id=1, source_target_pairs={{0,1},{1,0},{2,3},{3,2},{4,5},{5,4},{6,7},{7,6},{8,9},{9,8},{10,11... | collective-permute-start | bytes 786440 | tf_op jit(solution)/shard_map/ppermute | solution.py:420
  15.0 3.0 %collective-permute-start.4 = (bf16[256,512]{1,0:T(8,128)(2,1)}, bf16[256,512]{1,0:T(8,128)(2,1)}, u32[]{:S(2)}, u32[]{:S(2)}) collective-permute-start(bf16[256,512]{1,0:T(8,128)(2,1)} %get-tuple-element.31), channel_id=1, source_target_pairs={{0,1},{1,0},{2,3},{3,2},{4,5},{5,4},{6,7},{7,6},{8,9},{9,8},{10,11... | collective-permute-start | bytes 786440 | tf_op jit(solution)/shard_map/ppermute | solution.py:420
  15.3 14.4 %copy-start.3 = (f32[7,7,512]{2,1,0:T(8,128)S(1)}, f32[7,7,512]{2,1,0:T(8,128)}, u32[]{:S(2)}) copy-start(f32[7,7,512]{2,1,0:T(8,128)} %kernel.7) | copy-start | bytes 301060
  15.3 14.4 %copy-start.4 = (f32[2048]{0:T(1024)S(1)}, f32[2048]{0:T(1024)}, u32[]{:S(2)}) copy-start(f32[2048]{0:T(1024)} %param.20) | copy-start | bytes 24580
  15.3 14.4 %copy-start.5 = (f32[512]{0:T(512)S(1)}, f32[512]{0:T(512)}, u32[]{:S(2)}) copy-start(f32[512]{0:T(512)} %param.17) | copy-start | bytes 6148
  15.3 14.4 %copy-start.8 = (f32[512]{0:T(512)S(1)}, f32[512]{0:T(512)}, u32[]{:S(2)}) copy-start(f32[512]{0:T(512)} %param.16) | copy-start | bytes 6148
  15.3 14.4 %copy-start.9 = (f32[512]{0:T(512)S(1)}, f32[512]{0:T(512)}, u32[]{:S(2)}) copy-start(f32[512]{0:T(512)} %param.18) | copy-start | bytes 6148
  19.7 18.6 %collective-permute-start.5 = (bf16[4,32,512]{2,1,0:T(8,128)(2,1)S(1)}, bf16[4,32,512]{2,1,0:T(8,128)(2,1)S(1)}, u32[]{:S(2)}, u32[]{:S(2)}) collective-permute-start(bf16[4,32,512]{2,1,0:T(8,128)(2,1)S(1)} %get-tuple-element.32), channel_id=1, source_target_pairs={{0,0},{1,8},{2,2},{3,10},{4,4},{5,12},{6,6},{7,14},{8,1},{9,9},{10... | collective-permute-start | bytes 393224 | tf_op jit(solution)/shard_map/ppermute | solution.py:445
  24.2 14.1 %collective-permute-start.6 = (bf16[4,32,512]{2,1,0:T(8,128)(2,1)S(1)}, bf16[4,32,512]{2,1,0:T(8,128)(2,1)S(1)}, u32[]{:S(2)}, u32[]{:S(2)}) collective-permute-start(bf16[4,32,512]{2,1,0:T(8,128)(2,1)S(1)} %get-tuple-element.33), channel_id=1, source_target_pairs={{0,2},{1,10},{2,4},{3,12},{4,6},{5,14},{6,0},{7,8},{8,3},{9,11},{1... | collective-permute-start | bytes 393224 | tf_op jit(solution)/shard_map/ppermute | solution.py:445
  24.3 14.0 %collective-permute-start.7 = (bf16[4,32,512]{2,1,0:T(8,128)(2,1)S(1)}, bf16[4,32,512]{2,1,0:T(8,128)(2,1)S(1)}, u32[]{:S(2)}, u32[]{:S(2)}) collective-permute-start(bf16[4,32,512]{2,1,0:T(8,128)(2,1)S(1)} %get-tuple-element.34), channel_id=1, source_target_pairs={{0,4},{1,12},{2,6},{3,14},{4,0},{5,8},{6,2},{7,10},{8,5},{9,13},{1... | collective-permute-start | bytes 393224 | tf_op jit(solution)/shard_map/ppermute | solution.py:445
  25.9 12.4 %collective-permute-start.8 = (bf16[4,32,512]{2,1,0:T(8,128)(2,1)S(1)}, bf16[4,32,512]{2,1,0:T(8,128)(2,1)S(1)}, u32[]{:S(2)}, u32[]{:S(2)}) collective-permute-start(bf16[4,32,512]{2,1,0:T(8,128)(2,1)S(1)} %get-tuple-element.35), channel_id=1, source_target_pairs={{0,6},{1,14},{2,0},{3,8},{4,2},{5,10},{6,4},{7,12},{8,7},{9,15},{1... | collective-permute-start | bytes 393224 | tf_op jit(solution)/shard_map/ppermute | solution.py:445
  29.7 8.6 %copy-start.1 = (bf16[512,2048]{1,0:T(8,128)(2,1)S(1)}, bf16[512,2048]{1,0:T(8,128)(2,1)}, u32[]{:S(2)}) copy-start(bf16[512,2048]{1,0:T(8,128)(2,1)} %w_in.3) | copy-start | bytes 6291460
  29.7 8.6 %copy-start.2 = (bf16[2048,512]{1,0:T(8,128)(2,1)S(1)}, bf16[2048,512]{1,0:T(8,128)(2,1)}, u32[]{:S(2)}) copy-start(bf16[2048,512]{1,0:T(8,128)(2,1)} %w_out.3) | copy-start | bytes 6291460
  29.8 8.6 %copy-start.6 = (f32[512]{0:T(512)S(1)}, f32[512]{0:T(512)}, u32[]{:S(2)}) copy-start(f32[512]{0:T(512)} %param.22) | copy-start | bytes 6148
  29.8 8.6 %copy-start.7 = (f32[512]{0:T(512)S(1)}, f32[512]{0:T(512)}, u32[]{:S(2)}) copy-start(f32[512]{0:T(512)} %param.23) | copy-start | bytes 6148
  45.3 31.3 %collective-permute-start.9 = (bf16[3,80,512]{2,1,0:T(8,128)(2,1)S(1)}, bf16[3,80,512]{2,1,0:T(8,128)(2,1)S(1)}, u32[]{:S(2)}, u32[]{:S(2)}) collective-permute-start(bf16[3,80,512]{2,1,0:T(8,128)(2,1)S(1)} %get-tuple-element.36), channel_id=1, source_target_pairs={{0,2},{2,4},{4,6},{6,8},{8,10},{10,12},{12,14},{1,3},{3,5},{5,7},{... | collective-permute-start | bytes 737288 | tf_op jit(solution)/shard_map/ppermute | solution.py:386
  47.3 29.4 %collective-permute-start.10 = (bf16[3,80,512]{2,1,0:T(8,128)(2,1)S(1)}, bf16[3,80,512]{2,1,0:T(8,128)(2,1)S(1)}, u32[]{:S(2)}, u32[]{:S(2)}) collective-permute-start(bf16[3,80,512]{2,1,0:T(8,128)(2,1)S(1)} %get-tuple-element.37), channel_id=1, source_target_pairs={{2,0},{4,2},{6,4},{8,6},{10,8},{12,10},{14,12},{3,1},{5,3},{7,5},{... | collective-permute-start | bytes 737288 | tf_op jit(solution)/shard_map/ppermute | solution.py:386
  51.5 1.7 %collective-permute-start.11 = (bf16[4,8,512]{2,1,0:T(8,128)(2,1)S(1)}, bf16[4,8,512]{2,1,0:T(8,128)(2,1)S(1)}, u32[]{:S(2)}, u32[]{:S(2)}) collective-permute-start(bf16[4,8,512]{2,1,0:T(8,128)(2,1)S(1)} %get-tuple-element.38), channel_id=1, source_target_pairs={{0,1},{1,0},{2,3},{3,2},{4,5},{5,4},{6,7},{7,6},{8,9},{9,8},{10,11... | collective-permute-start | bytes 98312 | tf_op jit(solution)/shard_map/ppermute | solution.py:547
  63.9 9.0 %collective-permute-start.12 = (bf16[3,56,512]{2,1,0:T(8,128)(2,1)S(1)}, bf16[3,56,512]{2,1,0:T(8,128)(2,1)S(1)}, u32[]{:S(2)}, u32[]{:S(2)}) collective-permute-start(bf16[3,56,512]{2,1,0:T(8,128)(2,1)S(1)} %get-tuple-element.39), channel_id=1, source_target_pairs={{0,2},{2,4},{4,6},{6,8},{8,10},{10,12},{12,14},{1,3},{3,5},{5,7},{... | collective-permute-start | bytes 516104 | tf_op jit(solution)/shard_map/ppermute | solution.py:386
  65.8 10.9 %collective-permute-start.13 = (bf16[3,56,512]{2,1,0:T(8,128)(2,1)S(1)}, bf16[3,56,512]{2,1,0:T(8,128)(2,1)S(1)}, u32[]{:S(2)}, u32[]{:S(2)}) collective-permute-start(bf16[3,56,512]{2,1,0:T(8,128)(2,1)S(1)} %get-tuple-element.40), channel_id=1, source_target_pairs={{2,0},{4,2},{6,4},{8,6},{10,8},{12,10},{14,12},{3,1},{5,3},{7,5},{... | collective-permute-start | bytes 516104 | tf_op jit(solution)/shard_map/ppermute | solution.py:386

commit v4 on v3

v4 whole, which is shorter than its diff:
```python
import functools

import jax
import jax.numpy as jnp
from jax import lax
from jax.experimental import pallas as pl
from jax.experimental.pallas import tpu as pltpu
from jax.sharding import PartitionSpec as P

NORM_EPSILON = 1e-06
REACH = 3
TAPS = 2 * REACH + 1
LANES = 128
SUBLANES = 8
EDGE = 8
CHUNK = 16
UNROLL = 16
COPIES = 2
MLP_TILE = 512
CONTRACT_LAST = (((1,), (1,)), ((), ()))
SWAP = [(0, 1), (1, 0)]


def aligned(start, size):
    return pl.ds(pl.multiple_of(start, size), size)


def lane_tile(tile):
    return slice(tile * LANES, (tile + 1) * LANES)


def project_kernel(other, core_ref, teacher_hbm, weight, *rest):
    *outs, rows, sems = rest
    half = 1 - core_ref[0] if other else core_ref[0]
    lines, wide, depth = rows.shape
    copies = []
    for index in range(COPIES):
        here = pl.ds(index * (lines // COPIES), lines // COPIES)
        copy = pltpu.make_async_copy(
            teacher_hbm.at[here, half], rows.at[here], sems.at[index]
        )
        copy.start()
        copies.append(copy)
    size = lines * wide // COPIES
    for index, copy in enumerate(copies):
        copy.wait()
        here = pl.ds(index * (lines // COPIES), lines // COPIES)
        product = jnp.dot(
            rows[here].reshape(size, depth), weight[...], preferred_element_type=jnp.float32
        )
        out = outs[index * len(outs) // COPIES]
        start = index * size % out.shape[0]
        out[start : start + size] = product.astype(out.dtype)


def combine_kernel(wide, turns_ref, home, upper, lower, *rest):
    *blocks, summed = rest
    half = upper.shape[0]
    for tile in range(summed.shape[0]):
        lanes = lane_tile(tile)
        for start, received in ((0, upper), (half, lower)):
            here = slice(start, start + half)
            summed[tile, here] = home[here, lanes] + received[:, lanes].astype(jnp.float32)
    for index, block in enumerate(blocks):
        tile_u, lines, _ = block.shape
        for u in range(tile_u):
            rows = pl.ds(turns_ref[index] + u, lines, stride=wide)
            for tile in range(summed.shape[0]):
                block[u, :, lane_tile(tile)] = summed[tile, rows, :].astype(jnp.bfloat16)


def spread_taps(taps, kernel):
    for row_tap in range(TAPS):
        for col_tap in range(TAPS):
            for tile in range(taps.shape[1]):
                line = kernel[row_tap, col_tap : col_tap + 1, lane_tile(tile)]
                taps[row_tap * TAPS + col_tap, tile] = jnp.broadcast_to(line, (SUBLANES, LANES))


def spread(padded, place, part, source, start, row, count):
    for tile in range(padded.shape[0]):
        padded[tile, place, pl.ds(row, count), :] = part[
            source, pl.ds(start, count), lane_tile(tile)
        ].astype(jnp.float32)


def depthwise(padded, taps, begin, store, tile_u, count, offset, sources, flip):
    tiles = padded.shape[0]
    blocks = count // (2 * SUBLANES)

    def step(index, carry):
        tile = index // blocks
        base = pl.multiple_of((index % blocks) * (2 * SUBLANES), 2 * SUBLANES)
        sums = [
            [begin(tile, u, base + half * SUBLANES) for u in range(tile_u)] for half in range(2)
        ]
        for row_tap in range(TAPS):
            weights = []
            for col_tap in range(TAPS):
                tap = row_tap * TAPS + col_tap
                weights.append(taps[TAPS * TAPS - 1 - tap if flip else tap, tile])
            for place, source in enumerate(sources):
                for half in range(2):
                    row = base + (half * SUBLANES + row_tap) + offset
                    values = padded[tile, place, pl.ds(row, SUBLANES), :]
                    for u in range(max(0, source - TAPS + 1), min(tile_u, source + 1)):
                        term = weights[source - u] * values
                        sums[half][u] = term if sums[half][u] is None else sums[half][u] + term
        for half in range(2):
            for u in range(tile_u):
                store(tile, u, base + half * SUBLANES, sums[half][u])
        return carry

    lax.fori_loop(0, tiles * blocks, step, 0)


def row_parts(rows):
    half = rows // 2 // 16 * 16
    return slice(0, half), slice(half, rows)


def repeat(count, step):
    unroll = max(n for n in range(1, UNROLL + 1) if count % n == 0)

    def body(index, carry):
        step(index)
        return carry

    lax.fori_loop(0, count, body, 0, unroll=unroll)


def fill(padded, parts, core, tile_v):
    place = 0
    for part, edge, start in parts:
        for u in range(part.shape[0]):
            spread(padded, place, part, u, 0, EDGE, tile_v)
            for tile in range(padded.shape[0]):
                rim = edge[u, start : start + EDGE, lane_tile(tile)].astype(jnp.float32)
                nothing = jnp.zeros_like(rim)
                padded[tile, place, 0:EDGE, :] = jnp.where(core == 1, rim, nothing)
                padded[tile, place, EDGE + tile_v : 2 * EDGE + tile_v, :] = jnp.where(
                    core == 0, rim, nothing
                )
            place += 1


def inner_kernel(flip, core_ref, middle, edge, kernel, base_value, out, padded, taps):
    tile_u, tile_v, channels = middle.shape
    spread_taps(taps, kernel)
    fill(padded, [(middle, edge, 0)], core_ref[0], tile_v)

    def place(tile, u, base):
        return aligned(u * tile_v + base, SUBLANES), aligned(tile * LANES, LANES)

    def begin(tile, u, base):
        rows, lanes = place(tile, u, base)
        if base_value.shape[0] == 1:
            return jnp.broadcast_to(base_value[:, lanes], (SUBLANES, LANES))
        return base_value[rows, lanes]

    def store(tile, u, base, value):
        out[place(tile, u, base)] = value

    own = range(REACH, REACH + tile_u)
    depthwise(padded, taps, begin, store, tile_u, tile_v, EDGE - REACH, own, flip)


def rim_conv(flip, core, left, right, left_edge, right_edge, kernel, inner, store, padded, taps):
    sides, tile_v = padded.shape[1], padded.shape[2] - 2 * EDGE
    tile_u = inner.shape[0] // tile_v
    spread_taps(taps, kernel)
    fill(padded, [(left, *left_edge), (right, *right_edge)], core, tile_v)

    def begin(tile, u, base):
        return inner[aligned(u * tile_v + base, SUBLANES), aligned(tile * LANES, LANES)]

    sources = [*range(REACH), *range(REACH + tile_u, 2 * REACH + tile_u)]
    depthwise(padded, taps, begin, store, tile_u, tile_v, EDGE - REACH, sources, flip)


def up_kernel(
    core_ref, left, right, kernel, inner, gain, shift, w_in_hbm, b_in,
    normal_form, inv_scale, activated, slope, padded, taps, normed, w_in, sem,
):
    copy = pltpu.make_async_copy(w_in_hbm, w_in, sem)
    copy.start()
    rows, hidden = activated.shape
    tile_v = padded.shape[2] - 2 * EDGE

    def store(tile, u, base, value):
        row = aligned(u * tile_v + base, SUBLANES)
        normal_form[row, aligned(tile * LANES, LANES)] = value

    left_edge, right_edge = (left, tile_v), (right, tile_v)
    rim_conv(
        False, core_ref[0], left, right, left_edge, right_edge, kernel, inner, store, padded, taps
    )

    def norm_step(index):
        here = aligned(index * CHUNK, CHUNK)
        conv = normal_form[here, :]
        centred = conv - jnp.mean(conv, axis=-1, keepdims=True)
        variance = jnp.mean(centred * centred, axis=-1, keepdims=True)
        inverse = lax.rsqrt(variance + NORM_EPSILON)
        form = centred * inverse
        normal_form[here, :] = form
        inv_scale[here, :] = jnp.broadcast_to(inverse, (CHUNK, LANES))
        normed[here, :] = (form * gain[...] + shift[...]).astype(jnp.bfloat16)

    repeat(rows // CHUNK, norm_step)

    copy.wait()
    for start in range(0, hidden, MLP_TILE):
        tile = slice(start, start + MLP_TILE)
        for here in row_parts(rows):
            pre = (
                jnp.dot(normed[here, :], w_in[:, tile], preferred_element_type=jnp.float32)
                + b_in[:, tile]
            )
            phi = 0.5 * (1.0 + lax.erf(pre * 0.7071067811865476))
            activated[here, tile] = (pre * phi).astype(jnp.bfloat16)
            slope[here, tile] = phi + pre * jnp.exp(-0.5 * pre * pre) * 0.3989422804014327


def back_kernel(
    pieces, places_ref, middle, normal_form, inv_scale, activated, slope,
    gain, w_in, w_out, b_out, scale, *rest,
):
    targets = rest[:pieces]
    mismatch_out, d_out, target, d_branch, d_hidden, d_normed = rest[pieces:]
    tile_u, tile_v, channels = middle.shape
    rows, hidden = activated.shape
    chunks = tile_v // CHUNK
    for index, piece in enumerate(targets):
        target[:, aligned(places_ref[index], piece.shape[1]), :] = piece[...]

    for here in row_parts(rows):
        d_normed[here, :] = jnp.dot(
            activated[here, :], w_out[...], preferred_element_type=jnp.float32
        )

    def mismatch_step(index):
        u = index // chunks
        inside = aligned((index % chunks) * CHUNK, CHUNK)
        here = aligned(index * CHUNK, CHUNK)
        mismatch = (
            middle[u, inside, :].astype(jnp.float32)
            + scale[...] * (d_normed[here, :] + b_out[...])
            - target[u, inside, :].astype(jnp.float32)
        )
        mismatch_out[here, :] = mismatch
        d_branch[here, :] = (scale[...] * mismatch).astype(jnp.bfloat16)

    repeat(tile_u * chunks, mismatch_step)

    for start in range(0, hidden, MLP_TILE):
        tile = slice(start, start + MLP_TILE)
        for here in row_parts(rows):
            d_activated = lax.dot_general(
                d_branch[here, :], w_out[tile, :], CONTRACT_LAST, preferred_element_type=jnp.float32
            )
            d_hidden[here, tile] = (d_activated * slope[here, tile]).astype(jnp.bfloat16)
    for here in row_parts(rows):
        d_normed[here, :] = lax.dot_general(
            d_hidden[here, :], w_in[...], CONTRACT_LAST, preferred_element_type=jnp.float32
        )

    def d_norm_step(index):
        u = index // chunks
        inside = aligned((index % chunks) * CHUNK, CHUNK)
        here = aligned(index * CHUNK, CHUNK)
        scaled = d_normed[here, :] * gain[...]
        form = normal_form[here, :]
        d_conv = inv_scale[here, :1] * (
            scaled
            - jnp.mean(scaled, axis=-1, keepdims=True)
            - form * jnp.mean(scaled * form, axis=-1, keepdims=True)
        )
        d_out[u, inside, :] = d_conv.astype(jnp.bfloat16)

    repeat(tile_u * chunks, d_norm_step)


def last_kernel(
    core_ref, left, right, left_edge, right_edge, kernel, inner, out, padded, taps, turned
):
    tile_v, tile_u, channels = out.shape

    def store(tile, u, base, value):
        turned[tile, aligned(u * tile_v + base, SUBLANES), :] = value

    edges = (left_edge, 0), (right_edge, 0)
    rim_conv(True, core_ref[0], left, right, *edges, kernel, inner, store, padded, taps)

    def turn_step(line):
        for tile in range(turned.shape[0]):
            out[line, :, lane_tile(tile)] = turned[tile, pl.ds(line, tile_u, stride=tile_v), :]

    repeat(tile_v, turn_step)


def call(kernel, name, outs, scratch, scalars, arrays, flops, limit, left_in_hbm=()):
    vmem = pl.BlockSpec(memory_space=pltpu.VMEM)
    smem = pl.BlockSpec(memory_space=pltpu.SMEM)
    hbm = pl.BlockSpec(memory_space=pltpu.HBM)
    moved = 1 if flops == 1 else sum(a.size * a.dtype.itemsize for a in [*arrays, *outs])
    arrays = [
        pltpu.with_memory_space_constraint(a, pltpu.HBM) if index in left_in_hbm else a
        for index, a in enumerate(arrays)
    ]
    specs = [hbm if index in left_in_hbm else vmem for index in range(len(arrays))]
    return pl.pallas_call(
        kernel,
        out_shape=tuple(outs),
        in_specs=[smem] * len(scalars) + specs,
        out_specs=(vmem,) * len(outs),
        scratch_shapes=scratch,
        compiler_params=pltpu.CompilerParams(vmem_limit_bytes=limit << 20),
        cost_estimate=pl.CostEstimate(flops=flops, bytes_accessed=moved, transcendentals=0),
        name=name,
    )(*scalars, *arrays)


def send_sides(last, first):
    row_count = lax.axis_size("row")
    forward = [(i, i + 1) for i in range(row_count - 1)]
    backward = [(b, a) for a, b in forward]
    return lax.ppermute(last, "row", forward), lax.ppermute(first, "row", backward)


def with_edge(block, edge):
    return (
        jnp.concatenate([block[-REACH:], edge[-REACH:]], axis=1),
        jnp.concatenate([block[:REACH], edge[:REACH]], axis=1),
    )


def send_edges(tile, core):
    row_count = lax.axis_size("row")
    own = jnp.where(core == 0, tile[:, -EDGE:], tile[:, :EDGE])
    forward = [(i * 2 + c, i * 2 + 3 - c) for i in range(row_count - 1) for c in range(2)]
    backward = [(b, a) for a, b in forward]
    return (
        lax.ppermute(own[-REACH:], ("row", "col"), forward),
        lax.ppermute(own, "col", SWAP),
        lax.ppermute(own[:REACH], ("row", "col"), backward),
    )


def find_target(teacher, proj_weight, core, row, tile_u, tile_v):
    row_count = lax.axis_size("row")
    halves = row_count // 2
    channels = proj_weight.shape[1]
    grid_u = tile_u * row_count
    lines = teacher.shape[0] // grid_u
    scalar = core.astype(jnp.int32)[None]
    half_line = grid_u // 2
    by_half = teacher.reshape(lines, 2, half_line, teacher.shape[1])
    size = (lines * half_line, channels)
    fourth = jax.ShapeDtypeStruct((size[0] // 2, channels), jnp.bfloat16)
    scratch = [
        pltpu.VMEM((lines, half_line, teacher.shape[1]), jnp.bfloat16),
        pltpu.SemaphoreType.DMA((COPIES,)),
    ]
    upper, lower = call(
        functools.partial(project_kernel, True),
        "project_away", [fourth] * 2, scratch, [scalar], [by_half, proj_weight], 1, 12, (0,),
    )
    (home,) = call(
        functools.partial(project_kernel, False),
        "project_home", [jax.ShapeDtypeStruct(size, jnp.float32)],
        scratch, [scalar], [by_half, proj_weight], 1, 12, (0,),
    )
    received = [lax.ppermute(away, "col", SWAP) for away in (upper, lower)]
    turns = [lax.rem(turn + row, halves) * tile_u for turn in range(halves)]
    if lines % 16:
        received = jnp.concatenate(received).astype(jnp.float32)
        summed = (home + received).astype(jnp.bfloat16)
        by_u = summed.reshape(lines, half_line, channels).transpose(1, 0, 2)
        blocks = [lax.dynamic_slice_in_dim(by_u, turn, tile_u) for turn in turns]
    else:
        blocks = call(
            functools.partial(combine_kernel, half_line),
            "combine",
            [jax.ShapeDtypeStruct((tile_u, lines, channels), jnp.bfloat16)] * halves,
            [pltpu.VMEM((channels // LANES, *size[:1], LANES), jnp.float32)],
            [jnp.stack(turns).astype(jnp.int32)],
            [home, *received],
            1,
            8,
        )
    pieces, places = [], []
    for turn in range(halves):
        pairs = []
        for r in range(row_count):
            for c in range(2):
                goal = (halves * c + (turn + r) % halves) * 2 + r // halves
                pairs.append((r * 2 + c, goal))
        pieces.append(lax.ppermute(blocks[turn], ("row", "col"), pairs))
        places.append(lax.rem(row + (halves - turn), halves) * lines)
    places = jnp.stack(places).astype(jnp.int32)
    if lines % 16:
        whole = jnp.zeros((tile_u, tile_v, channels), jnp.bfloat16)
        for index, piece in enumerate(pieces):
            whole = lax.dynamic_update_slice_in_dim(whole, piece, places[index], axis=1)
        return [whole], jnp.zeros((1,), jnp.int32), blocks[0]
    return pieces, places, blocks[0]


def on_device(
    teacher,
    proj_weight,
    student,
    dw_kernel,
    dw_bias,
    norm_gain,
    norm_bias,
    w_in,
    b_in,
    w_out,
    b_out,
    layer_scale,
):
    core = lax.axis_index("col")
    row = lax.axis_index("row")
    tile_v, tile_u, channels = student.shape
    hidden = w_in.shape[1]
    tiles = channels // LANES
    wide = tile_v + 2 * EDGE
    scalar = core.astype(jnp.int32)[None]
    f32, bf16 = jnp.float32, jnp.bfloat16
    rows = tile_u * tile_v
    own_edge = jnp.where(core == 0, student[-EDGE:], student[:EDGE])
    edge = lax.ppermute(own_edge, "col", SWAP).transpose(1, 0, 2)
    after_edge, _ = lax.optimization_barrier((student, own_edge))
    middle = after_edge.transpose(1, 0, 2)
    last, first = with_edge(middle, edge)
    left, right = send_sides(last, first)
    held, _, _ = lax.optimization_barrier((proj_weight, last, first))
    targets, places, block = find_target(teacher, held, core, row, tile_u, tile_v)
    later, _ = lax.optimization_barrier((dw_bias, block))
    matmul = 2 * rows * channels * hidden
    flat = jax.ShapeDtypeStruct((rows, channels), f32)
    taps = pltpu.VMEM((TAPS * TAPS, tiles, SUBLANES, LANES), f32)
    own_pad, side_pad = (
        pltpu.VMEM((tiles, count, tile_v + 2 * EDGE, LANES), f32) for count in (tile_u, 2 * REACH)
    )
    (inner,) = call(
        functools.partial(inner_kernel, False),
        "inner_up", [flat], [own_pad, taps], [scalar],
        [middle, edge, dw_kernel, later[None]], 1, 8,
    )
    saved = call(
        up_kernel,
        "up",
        [
            flat,
            jax.ShapeDtypeStruct((rows, LANES), f32),
            jax.ShapeDtypeStruct((rows, hidden), bf16),
            jax.ShapeDtypeStruct((rows, hidden), f32),
        ],
        [side_pad, taps, pltpu.VMEM((rows, channels), bf16), pltpu.VMEM(w_in.shape, bf16)]
        + [pltpu.SemaphoreType.DMA],
        [scalar],
        [left, right, dw_kernel, inner, norm_gain[None], norm_bias[None], w_in, b_in[None]],
        4 * matmul,
        16,
        (6,),
    )
    mismatch, d_conv = call(
        functools.partial(back_kernel, len(targets)),
        "back",
        [flat, jax.ShapeDtypeStruct((tile_u, tile_v, channels), bf16)],
        [
            pltpu.VMEM((tile_u, tile_v, channels), bf16),
            pltpu.VMEM((rows, channels), bf16),
            pltpu.VMEM((rows, hidden), bf16),
            pltpu.VMEM((rows, channels), f32),
        ],
        [places],
        [middle, *saved, norm_gain[None], w_in, w_out, b_out[None], layer_scale[None], *targets],
        4 * matmul,
        16,
    )
    left, right = send_sides(d_conv[-REACH:], d_conv[:REACH])
    left_edge, edge, right_edge = send_edges(d_conv, core)
    (inner,) = call(
        functools.partial(inner_kernel, True),
        "inner_last", [flat], [own_pad, taps], [scalar],
        [d_conv, edge, dw_kernel, mismatch], matmul, 8,
    )
    (grad,) = call(
        last_kernel,
        "last",
        [jax.ShapeDtypeStruct((tile_v, tile_u, channels), f32)],
        [side_pad, taps, pltpu.VMEM((tiles, rows, LANES), f32)],
        [scalar],
        [left, right, left_edge, right_edge, dw_kernel, inner],
        matmul,
        8,
    )
    return grad


def solution(mesh):
    placed = (
        P(("groups", "row"), "col"),
        P("col", None),
        P(("groups", "col"), "row", None),
        P(),
        P(),
        P(),
        P(),
        P(),
        P(),
        P(),
        P(),
        P(),
    )
    return jax.shard_map(
        on_device,
        mesh=mesh,
        in_specs=placed,
        out_specs=P(("groups", "col"), "row", None),
        check_vma=False,
    )
```

time: 81.5 us -> 74.5 us (0.914)
  Pallas kernels: 41 us -> 34.8 us
  starting transfers between devices: 31.2 us -> 27.9 us
  waiting for transfers between devices: 5.44 us -> 6.89 us
    ppermute x3 -> x2, starting transfers between devices: 11.6 us -> 5.07 us  [send_sides(): lax.ppermute(first, 'row', backward)]
    pallas_call x8, Pallas kernels: 41 us -> 34.8 us  [call(): pl.pallas_call(kernel, out_shape=tuple(outs), in_specs=[smem] * len(scala...]
    ppermute x2 -> x4, starting transfers between devices: 1.6 us -> 6.37 us  [the longest x1 3.28 us: send_edges(): lax.ppermute(own[:REACH], ('row', 'col'), backward)]
    ppermute x2 -> x4, waiting for transfers between devices: 1.66 us -> 6.3 us  [the longest x1 6.29 us: send_edges(): lax.ppermute(own[:REACH], ('row', 'col'), backward)]
    ppermute x3 -> x2, waiting for transfers between devices: 3.75 us -> 0.57 us  [send_sides(): lax.ppermute(first, 'row', backward)]
    unnamed x21 -> x20, local copies, waits for them, and re-layouts: 1.33 us -> 0.06 us
    optimization_barrier x0 -> x1, local copies, waits for them, and re-layouts: none -> 1.13 us  [on_device(): after_edge, _ = lax.optimization_barrier((student, own_edge))]
    slice x0 -> x3, local copies, waits for them, and re-layouts: none -> 0.87 us  [the longest x1 0.8 us: on_device(): own_edge = jnp.where(core == 0, student[-EDGE:], student[:EDGE])]
  transfers between devices with their start and end apart: 14 -> 14, of which waited for: 3 -> 2; matrix products, arithmetic and copies ran while one was open for 1% -> 3% of each run, Pallas kernels for 37% -> 34%
where the time goes in v4:
time: 74.5 us; the launch traced here: 73.8 us
  Pallas kernels  34.8 us (47%)
  starting transfers between devices  27.9 us (37%)
  waiting for transfers between devices  6.89 us (9%)
  local copies, waits for them, and re-layouts  2.13 us (3%)
  other arithmetic  1.78 us (2%)
    pallas_call x8, Pallas kernels, call(): pl.pallas_call(kernel, out_shape=tuple(outs), in_specs=[smem] * len(scala...  34.8 us
    ppermute x4, starting transfers between devices, find_target(): pieces.append(lax.ppermute(blocks[turn], ('row', 'col'), pairs))  9.17 us
    ppermute x2, starting transfers between devices, send_sides(): lax.ppermute(last, 'row', forward)  6.37 us
    ppermute x1, waiting for transfers between devices, send_edges(): lax.ppermute(own[:REACH], ('row', 'col'), backward)  6.29 us
    ppermute x2, starting transfers between devices, send_sides(): lax.ppermute(first, 'row', backward)  5.07 us
    ppermute x1, starting transfers between devices, send_edges(): lax.ppermute(own[:REACH], ('row', 'col'), backward)  3.28 us
    ppermute x1, starting transfers between devices, send_edges(): lax.ppermute(own[-REACH:], ('row', 'col'), forward)  2.29 us
  transfers between devices with their start and end apart: 14, of which 2 were waited for; matrix products, arithmetic and copies ran while one was open for 3% of the time, Pallas kernels for 34%

profile of v4, /device:TPU:13, one launch (start us, length us, event | category | flops | bytes accessed | tf_op | source)
XLA Modules:
  0.0 73.8 jit_solution(12160687170246969961)
XLA Ops:
  0.0 0.8 %fusion.2 = (bf16[8,4,512]{2,1,0:T(4,128)(2,1)S(1)}, bf16[8,4,512]{2,1,0:T(4,128)(2,1)S(1)}) fusion(bf16[128,4,512]{2,1,0:T(4,128)(2,1)} %param.14), kind=kLoop, calls=%fused_computation.9 | loop fusion | bytes 131072 | tf_op jit(solution)/shard_map/slice | solution.py:433
  0.8 0.7 %collective-permute-start = (bf16[8,4,512]{2,0,1:T(8,128)(2,1)S(1)}, bf16[8,4,512]{2,0,1:T(8,128)(2,1)S(1)}, u32[]{:S(2)}, u32[]{:S(2)}) collective-permute-start(bf16[8,4,512]{2,0,1:T(8,128)(2,1)S(1)} %copy_select_fusion), channel_id=1, source_target_pairs={{0,1},{1,0},{2,3},{3,2},{4,5},{5,4},{6,7},{7,6},{8,9},{9,8},{10,11... | collective-permute-start | bytes 98312 | tf_op jit(solution)/shard_map/ppermute | solution.py:434
  1.6 1.1 %copy.21 = bf16[128,4,512]{2,0,1:T(8,128)(2,1)S(1)} copy(bf16[128,4,512]{2,1,0:T(4,128)(2,1)} %param.14) | data formatting | bytes 1048576 | tf_op jit(solution)/shard_map/optimization_barrier | solution.py:435
  2.7 0.1 fusion.1
  2.8 0.8 %pad_maximum_fusion = bf16[3,136,512]{2,1,0:T(8,128)(2,1)} fusion(bf16[3,8,512]{2,1,0:T(8,128)(2,1)S(1)} %get-tuple-element.44, bf16[3,128,512]{2,1,0:T(8,128)(2,1)S(1)} %get-tuple-element.38), kind=kLoop, calls=%fused_computation.1 | loop fusion | flops 835584 | bytes 835584 | tf_op jit(solution)/shard_map/concatenate | solution.py:333
  3.6 3.1 %collective-permute-start.1 = (bf16[3,136,512]{2,1,0:T(8,128)(2,1)}, bf16[3,136,512]{2,1,0:T(8,128)(2,1)}, u32[]{:S(2)}, u32[]{:S(2)}) collective-permute-start(bf16[3,136,512]{2,1,0:T(8,128)(2,1)} %pad_maximum_fusion), channel_id=1, source_target_pairs={{0,2},{2,4},{4,6},{6,8},{8,10},{10,12},{12,14},{1,3},{3,5},{5,7},{... | collective-permute-start | bytes 1253384 | tf_op jit(solution)/shard_map/ppermute | solution.py:328
  6.7 0.8 %pad_maximum_fusion.1 = bf16[3,136,512]{2,1,0:T(8,128)(2,1)} fusion(bf16[3,8,512]{2,1,0:T(8,128)(2,1)S(1)} %get-tuple-element.43, bf16[3,128,512]{2,1,0:T(8,128)(2,1)S(1)} %get-tuple-element.37), kind=kLoop, calls=%fused_computation.2 | loop fusion | flops 835584 | bytes 835584 | tf_op jit(solution)/shard_map/concatenate | solution.py:334
  7.5 3.1 %collective-permute-start.2 = (bf16[3,136,512]{2,1,0:T(8,128)(2,1)}, bf16[3,136,512]{2,1,0:T(8,128)(2,1)}, u32[]{:S(2)}, u32[]{:S(2)}) collective-permute-start(bf16[3,136,512]{2,1,0:T(8,128)(2,1)} %pad_maximum_fusion.1), channel_id=1, source_target_pairs={{2,0},{4,2},{6,4},{8,6},{10,8},{12,10},{14,12},{3,1},{5,3},{7,5},{... | collective-permute-start | bytes 1253384 | tf_op jit(solution)/shard_map/ppermute | solution.py:328
  10.6 3.1 %project_away.1 = (bf16[256,512]{1,0:T(8,128)(2,1)}, bf16[256,512]{1,0:T(8,128)(2,1)S(1)}) custom-call(s32[1]{0:T(128)} %bitcast.core_ref, bf16[32,2,16,2048]{3,2,1,0:T(8,128)(2,1)} %bitcast.32, bf16[2048,512]{1,0:T(8,128)(2,1)S(1)} %copy-done), custom_call_target="tpu_custom_call" | custom-call | flops 1 | bytes 1 | tf_op jit(solution)/shard_map/project_away/pallas_call | solution.py:312
  13.8 0.8 %collective-permute-start.3 = (bf16[256,512]{1,0:T(8,128)(2,1)}, bf16[256,512]{1,0:T(8,128)(2,1)S(1)}, u32[]{:S(2)}, u32[]{:S(2)}) collective-permute-start(bf16[256,512]{1,0:T(8,128)(2,1)} %get-tuple-element.22), channel_id=1, source_target_pairs={{0,1},{1,0},{2,3},{3,2},{4,5},{5,4},{6,7},{7,6},{8,9},{9,8},{10,11... | collective-permute-start | bytes 786440 | tf_op jit(solution)/shard_map/ppermute | solution.py:374
  14.5 0.1 collective-permute-start.4
  14.6 0.1 pad_add_fusion.places_ref
  14.7 0.1 pad_add_fusion.1.turns_ref
  14.8 2.7 %project_home.1.home = f32[512,512]{1,0:T(8,128)S(1)} custom-call(s32[1]{0:T(128)} %bitcast.core_ref, bf16[32,2,16,2048]{3,2,1,0:T(8,128)(2,1)} %bitcast.33, bf16[2048,512]{1,0:T(8,128)(2,1)S(1)} %copy-done), custom_call_target="tpu_custom_call" | custom-call | flops 1 | bytes 1 | tf_op jit(solution)/shard_map/project_home/pallas_call | solution.py:312
  17.5 1.1 %combine.1 = (bf16[4,32,512]{2,1,0:T(8,128)(2,1)S(1)}, bf16[4,32,512]{2,1,0:T(8,128)(2,1)S(1)}, bf16[4,32,512]{2,1,0:T(8,128)(2,1)S(1)}, bf16[4,32,512]{2,1,0:T(8,128)(2,1)S(1)}) custom-call(s32[4]{0:T(128)S(1)} %pad_add_fusion.1.turns_ref, f32[512,512]{1,0:T(8,128)S(1)} %project_home.1.home, bf16[256,512]{1,0:T(8,128)(2,1)S(1)} %collective-permute-done.3.upper, ...), custom_call_target="tpu_custom_call" | custom-call | flops 1 | bytes 1 | tf_op jit(solution)/shard_map/combine/pallas_call | solution.py:312
  18.6 4.5 %collective-permute-start.5 = (bf16[4,32,512]{2,1,0:T(8,128)(2,1)S(1)}, bf16[4,32,512]{2,1,0:T(8,128)(2,1)S(1)}, u32[]{:S(2)}, u32[]{:S(2)}) collective-permute-start(bf16[4,32,512]{2,1,0:T(8,128)(2,1)S(1)} %get-tuple-element.24), channel_id=1, source_target_pairs={{0,0},{1,8},{2,2},{3,10},{4,4},{5,12},{6,6},{7,14},{8,1},{9,9},{10... | collective-permute-start | bytes 393224 | tf_op jit(solution)/shard_map/ppermute | solution.py:399
  23.2 0.8 %collective-permute-start.6 = (bf16[4,32,512]{2,1,0:T(8,128)(2,1)S(1)}, bf16[4,32,512]{2,1,0:T(8,128)(2,1)S(1)}, u32[]{:S(2)}, u32[]{:S(2)}) collective-permute-start(bf16[4,32,512]{2,1,0:T(8,128)(2,1)S(1)} %get-tuple-element.30), channel_id=1, source_target_pairs={{0,2},{1,10},{2,4},{3,12},{4,6},{5,14},{6,0},{7,8},{8,3},{9,11},{1... | collective-permute-start | bytes 393224 | tf_op jit(solution)/shard_map/ppermute | solution.py:399
  24.0 0.9 %collective-permute-start.7 = (bf16[4,32,512]{2,1,0:T(8,128)(2,1)S(1)}, bf16[4,32,512]{2,1,0:T(8,128)(2,1)S(1)}, u32[]{:S(2)}, u32[]{:S(2)}) collective-permute-start(bf16[4,32,512]{2,1,0:T(8,128)(2,1)S(1)} %get-tuple-element.31), channel_id=1, source_target_pairs={{0,4},{1,12},{2,6},{3,14},{4,0},{5,8},{6,2},{7,10},{8,5},{9,13},{1... | collective-permute-start | bytes 393224 | tf_op jit(solution)/shard_map/ppermute | solution.py:399
  24.9 3.0 %inner_up.1.inner = f32[512,512]{1,0:T(8,128)S(1)} custom-call(s32[1]{0:T(128)} %bitcast.core_ref, bf16[4,128,512]{2,1,0:T(8,128)(2,1)S(1)} %bitcast.21, bf16[4,8,512]{2,1,0:T(8,128)(2,1)S(1)} %bitcast.24, f32[7,7,512]{2,1,0:T(8,128)S(1)} %copy-done.1, f32[1,512]{1,0:T(1,128)S(1)} %bitcast.25), custom_call_target="tpu_custom_call" | custom-call | flops 1 | bytes 1 | tf_op jit(solution)/shard_map/inner_up/pallas_call | solution.py:312
  28.0 2.9 %collective-permute-start.8 = (bf16[4,32,512]{2,1,0:T(8,128)(2,1)S(1)}, bf16[4,32,512]{2,1,0:T(8,128)(2,1)S(1)}, u32[]{:S(2)}, u32[]{:S(2)}) collective-permute-start(bf16[4,32,512]{2,1,0:T(8,128)(2,1)S(1)} %get-tuple-element.32), channel_id=1, source_target_pairs={{0,6},{1,14},{2,0},{3,8},{4,2},{5,10},{6,4},{7,12},{8,7},{9,15},{1... | collective-permute-start | bytes 393224 | tf_op jit(solution)/shard_map/ppermute | solution.py:399
  31.0 12.0 %up.1 = (f32[512,512]{1,0:T(8,128)S(1)}, f32[512,128]{1,0:T(8,128)S(1)}, bf16[512,2048]{1,0:T(8,128)(2,1)S(1)}, f32[512,2048]{1,0:T(8,128)S(1)}) custom-call(s32[1]{0:T(128)} %bitcast.core_ref, bf16[3,136,512]{2,1,0:T(8,128)(2,1)} %collective-permute-done.1.left, bf16[3,136,512]{2,1,0:T(8,128)(2,1)} %collective-permute-done.2.right, ...), custom_call_target="tpu_custom_call" | custom-call | flops 4294967296 | bytes 11696128 | tf_op jit(solution)/shard_map/up/pallas_call | solution.py:312
  43.1 5.2 %back.1 = (f32[512,512]{1,0:T(8,128)S(1)}, bf16[4,128,512]{2,1,0:T(8,128)(2,1)S(1)}) custom-call(s32[4]{0:T(128)S(1)} %pad_add_fusion.places_ref, bf16[4,128,512]{2,1,0:T(8,128)(2,1)S(1)} %bitcast.22, f32[512,512]{1,0:T(8,128)S(1)} %get-tuple-element.26.normal_form, f32[512,128]{1,0:T(8,128)S(1)} %get-tuple-element.27.inv_scale, ...), custom_call_target="tpu_custom_call" | custom-call | flops 4294967296 | bytes 14424064 | tf_op jit(solution)/shard_map/back/pallas_call | solution.py:312
  48.3 0.1 fusion
  48.4 2.0 %collective-permute-start.10 = (bf16[3,128,512]{2,1,0:T(8,128)(2,1)S(1)}, bf16[3,128,512]{2,1,0:T(8,128)(2,1)S(1)}, u32[]{:S(2)}, u32[]{:S(2)}) collective-permute-start(bf16[3,128,512]{2,1,0:T(8,128)(2,1)S(1)} %get-tuple-element.35), channel_id=1, source_target_pairs={{2,0},{4,2},{6,4},{8,6},{10,8},{12,10},{14,12},{3,1},{5,3},{7,5},{... | collective-permute-start | bytes 1179656 | tf_op jit(solution)/shard_map/ppermute | solution.py:328
  50.4 3.3 %collective-permute-start.9 = (bf16[3,128,512]{2,1,0:T(8,128)(2,1)S(1)}, bf16[3,128,512]{2,1,0:T(8,128)(2,1)S(1)}, u32[]{:S(2)}, u32[]{:S(2)}) collective-permute-start(bf16[3,128,512]{2,1,0:T(8,128)(2,1)S(1)} %get-tuple-element.36), channel_id=1, source_target_pairs={{0,2},{2,4},{4,6},{6,8},{8,10},{10,12},{12,14},{1,3},{3,5},{5,7},{... | collective-permute-start | bytes 1179656 | tf_op jit(solution)/shard_map/ppermute | solution.py:328
  53.7 0.1 collective-permute-start.13
  53.8 3.3 %collective-permute-start.12 = (bf16[3,8,512]{2,1,0:T(8,128)(2,1)S(1)}, bf16[3,8,512]{2,1,0:T(8,128)(2,1)S(1)}, u32[]{:S(2)}, u32[]{:S(2)}) collective-permute-start(bf16[3,8,512]{2,1,0:T(8,128)(2,1)S(1)} %get-tuple-element.41), channel_id=1, source_target_pairs={{3,0},{2,1},{5,2},{4,3},{7,4},{6,5},{9,6},{8,7},{11,8},{10,9},{13,... | collective-permute-start | bytes 73736 | tf_op jit(solution)/shard_map/ppermute | solution.py:346
  57.1 2.3 %collective-permute-start.11 = (bf16[3,8,512]{2,1,0:T(8,128)(2,1)S(1)}, bf16[3,8,512]{2,1,0:T(8,128)(2,1)S(1)}, u32[]{:S(2)}, u32[]{:S(2)}) collective-permute-start(bf16[3,8,512]{2,1,0:T(8,128)(2,1)S(1)} %get-tuple-element.42), channel_id=1, source_target_pairs={{0,3},{1,2},{2,5},{3,4},{4,7},{5,6},{6,9},{7,8},{8,11},{9,10},{10,... | collective-permute-start | bytes 73736 | tf_op jit(solution)/shard_map/ppermute | solution.py:344
  59.4 3.2 %inner_last.1.inner = f32[512,512]{1,0:T(8,128)S(1)} custom-call(s32[1]{0:T(128)} %bitcast.core_ref, bf16[4,128,512]{2,1,0:T(8,128)(2,1)S(1)} %get-tuple-element.33.middle, bf16[4,8,512]{2,1,0:T(8,128)(2,1)S(1)} %collective-permute-done.13.edge, f32[7,7,512]{2,1,0:T(8,128)S(1)} %copy-done.1, f32[512,512]{1,0:T(8,128)S(1)} %get-tuple-element.34.base_value), custom_call_target="tpu_custom_call" | custom-call | flops 1073741824 | bytes 2754560 | tf_op jit(solution)/shard_map/inner_last/pallas_call | solution.py:312
  62.6 6.3 %collective-permute-done.12.right_edge = bf16[3,8,512]{2,1,0:T(8,128)(2,1)S(1)} collective-permute-done((bf16[3,8,512]{2,1,0:T(8,128)(2,1)S(1)}, bf16[3,8,512]{2,1,0:T(8,128)(2,1)S(1)}, u32[]{:S(2)}, u32[]{:S(2)}) %collective-permute-start.12) | collective-permute-done | bytes 24608 | tf_op jit(solution)/shard_map/ppermute | solution.py:346
  68.9 0.6 collective-permute-done.10.right
  69.5 4.4 %last.1 = f32[128,4,512]{2,1,0:T(4,128)} custom-call(s32[1]{0:T(128)} %bitcast.core_ref, bf16[3,128,512]{2,1,0:T(8,128)(2,1)S(1)} %collective-permute-done.9.left, bf16[3,128,512]{2,1,0:T(8,128)(2,1)S(1)} %collective-permute-done.10.right, bf16[3,8,512]{2,1,0:T(8,128)(2,1)S(1)} %collective-permute-done.11.left_edge, ...), custom_call_target="tpu_custom_call" | custom-call | flops 1073741824 | bytes 3033088 | tf_op jit(solution)/shard_map/last/pallas_call | solution.py:312
  (36 shorter events, 0.1 us)
Async XLA Ops:
  0.8 9.8 %copy-start = (bf16[2048,512]{1,0:T(8,128)(2,1)S(1)}, bf16[2048,512]{1,0:T(8,128)(2,1)}, u32[]{:S(2)}) copy-start(bf16[2048,512]{1,0:T(8,128)(2,1)} %weight.1) | copy-start | bytes 6291460
  0.8 2.0 %collective-permute-start = (bf16[8,4,512]{2,0,1:T(8,128)(2,1)S(1)}, bf16[8,4,512]{2,0,1:T(8,128)(2,1)S(1)}, u32[]{:S(2)}, u32[]{:S(2)}) collective-permute-start(bf16[8,4,512]{2,0,1:T(8,128)(2,1)S(1)} %copy_select_fusion), channel_id=1, source_target_pairs={{0,1},{1,0},{2,3},{3,2},{4,5},{5,4},{6,7},{7,6},{8,9},{9,8},{10,11... | collective-permute-start | bytes 98312 | tf_op jit(solution)/shard_map/ppermute | solution.py:434
  3.6 24.4 %collective-permute-start.1 = (bf16[3,136,512]{2,1,0:T(8,128)(2,1)}, bf16[3,136,512]{2,1,0:T(8,128)(2,1)}, u32[]{:S(2)}, u32[]{:S(2)}) collective-permute-start(bf16[3,136,512]{2,1,0:T(8,128)(2,1)} %pad_maximum_fusion), channel_id=1, source_target_pairs={{0,2},{2,4},{4,6},{6,8},{8,10},{10,12},{12,14},{1,3},{3,5},{5,7},{... | collective-permute-start | bytes 1253384 | tf_op jit(solution)/shard_map/ppermute | solution.py:328
  7.5 23.4 %collective-permute-start.2 = (bf16[3,136,512]{2,1,0:T(8,128)(2,1)}, bf16[3,136,512]{2,1,0:T(8,128)(2,1)}, u32[]{:S(2)}, u32[]{:S(2)}) collective-permute-start(bf16[3,136,512]{2,1,0:T(8,128)(2,1)} %pad_maximum_fusion.1), channel_id=1, source_target_pairs={{2,0},{4,2},{6,4},{8,6},{10,8},{12,10},{14,12},{3,1},{5,3},{7,5},{... | collective-permute-start | bytes 1253384 | tf_op jit(solution)/shard_map/ppermute | solution.py:328
  13.8 3.8 %collective-permute-start.3 = (bf16[256,512]{1,0:T(8,128)(2,1)}, bf16[256,512]{1,0:T(8,128)(2,1)S(1)}, u32[]{:S(2)}, u32[]{:S(2)}) collective-permute-start(bf16[256,512]{1,0:T(8,128)(2,1)} %get-tuple-element.22), channel_id=1, source_target_pairs={{0,1},{1,0},{2,3},{3,2},{4,5},{5,4},{6,7},{7,6},{8,9},{9,8},{10,11... | collective-permute-start | bytes 786440 | tf_op jit(solution)/shard_map/ppermute | solution.py:374
  14.5 3.0 %collective-permute-start.4 = (bf16[256,512]{1,0:T(8,128)(2,1)S(1)}, bf16[256,512]{1,0:T(8,128)(2,1)S(1)}, u32[]{:S(2)}, u32[]{:S(2)}) collective-permute-start(bf16[256,512]{1,0:T(8,128)(2,1)S(1)} %get-tuple-element.23), channel_id=1, source_target_pairs={{0,1},{1,0},{2,3},{3,2},{4,5},{5,4},{6,7},{7,6},{8,9},{9,8},{10,11... | collective-permute-start | bytes 786440 | tf_op jit(solution)/shard_map/ppermute | solution.py:374
  14.8 10.1 %copy-start.1 = (f32[7,7,512]{2,1,0:T(8,128)S(1)}, f32[7,7,512]{2,1,0:T(8,128)}, u32[]{:S(2)}) copy-start(f32[7,7,512]{2,1,0:T(8,128)} %kernel.7) | copy-start | bytes 301060
  14.8 10.1 %copy-start.2 = (f32[512]{0:T(512)S(1)}, f32[512]{0:T(512)}, u32[]{:S(2)}) copy-start(f32[512]{0:T(512)} %param.16) | copy-start | bytes 6148
  17.5 13.4 %copy-start.5 = (f32[2048]{0:T(1024)S(1)}, f32[2048]{0:T(1024)}, u32[]{:S(2)}) copy-start(f32[2048]{0:T(1024)} %param.20) | copy-start | bytes 24580
  17.5 13.4 %copy-start.6 = (f32[512]{0:T(512)S(1)}, f32[512]{0:T(512)}, u32[]{:S(2)}) copy-start(f32[512]{0:T(512)} %param.18) | copy-start | bytes 6148
  17.5 13.4 %copy-start.7 = (f32[512]{0:T(512)S(1)}, f32[512]{0:T(512)}, u32[]{:S(2)}) copy-start(f32[512]{0:T(512)} %param.17) | copy-start | bytes 6148
  18.6 24.4 %collective-permute-start.5 = (bf16[4,32,512]{2,1,0:T(8,128)(2,1)S(1)}, bf16[4,32,512]{2,1,0:T(8,128)(2,1)S(1)}, u32[]{:S(2)}, u32[]{:S(2)}) collective-permute-start(bf16[4,32,512]{2,1,0:T(8,128)(2,1)S(1)} %get-tuple-element.24), channel_id=1, source_target_pairs={{0,0},{1,8},{2,2},{3,10},{4,4},{5,12},{6,6},{7,14},{8,1},{9,9},{10... | collective-permute-start | bytes 393224 | tf_op jit(solution)/shard_map/ppermute | solution.py:399
  23.2 19.8 %collective-permute-start.6 = (bf16[4,32,512]{2,1,0:T(8,128)(2,1)S(1)}, bf16[4,32,512]{2,1,0:T(8,128)(2,1)S(1)}, u32[]{:S(2)}, u32[]{:S(2)}) collective-permute-start(bf16[4,32,512]{2,1,0:T(8,128)(2,1)S(1)} %get-tuple-element.30), channel_id=1, source_target_pairs={{0,2},{1,10},{2,4},{3,12},{4,6},{5,14},{6,0},{7,8},{8,3},{9,11},{1... | collective-permute-start | bytes 393224 | tf_op jit(solution)/shard_map/ppermute | solution.py:399
  24.0 19.0 %collective-permute-start.7 = (bf16[4,32,512]{2,1,0:T(8,128)(2,1)S(1)}, bf16[4,32,512]{2,1,0:T(8,128)(2,1)S(1)}, u32[]{:S(2)}, u32[]{:S(2)}) collective-permute-start(bf16[4,32,512]{2,1,0:T(8,128)(2,1)S(1)} %get-tuple-element.31), channel_id=1, source_target_pairs={{0,4},{1,12},{2,6},{3,14},{4,0},{5,8},{6,2},{7,10},{8,5},{9,13},{1... | collective-permute-start | bytes 393224 | tf_op jit(solution)/shard_map/ppermute | solution.py:399
  28.0 15.1 %collective-permute-start.8 = (bf16[4,32,512]{2,1,0:T(8,128)(2,1)S(1)}, bf16[4,32,512]{2,1,0:T(8,128)(2,1)S(1)}, u32[]{:S(2)}, u32[]{:S(2)}) collective-permute-start(bf16[4,32,512]{2,1,0:T(8,128)(2,1)S(1)} %get-tuple-element.32), channel_id=1, source_target_pairs={{0,6},{1,14},{2,0},{3,8},{4,2},{5,10},{6,4},{7,12},{8,7},{9,15},{1... | collective-permute-start | bytes 393224 | tf_op jit(solution)/shard_map/ppermute | solution.py:399
  30.9 12.1 %copy-start.3 = (bf16[512,2048]{1,0:T(8,128)(2,1)S(1)}, bf16[512,2048]{1,0:T(8,128)(2,1)}, u32[]{:S(2)}) copy-start(bf16[512,2048]{1,0:T(8,128)(2,1)} %w_in.1) | copy-start | bytes 6291460
  30.9 12.1 %copy-start.4 = (bf16[2048,512]{1,0:T(8,128)(2,1)S(1)}, bf16[2048,512]{1,0:T(8,128)(2,1)}, u32[]{:S(2)}) copy-start(bf16[2048,512]{1,0:T(8,128)(2,1)} %w_out.1) | copy-start | bytes 6291460
  30.9 12.1 %copy-start.8 = (f32[512]{0:T(512)S(1)}, f32[512]{0:T(512)}, u32[]{:S(2)}) copy-start(f32[512]{0:T(512)} %param.22) | copy-start | bytes 6148
  30.9 12.1 %copy-start.9 = (f32[512]{0:T(512)S(1)}, f32[512]{0:T(512)}, u32[]{:S(2)}) copy-start(f32[512]{0:T(512)} %param.23) | copy-start | bytes 6148
  48.4 21.1 %collective-permute-start.10 = (bf16[3,128,512]{2,1,0:T(8,128)(2,1)S(1)}, bf16[3,128,512]{2,1,0:T(8,128)(2,1)S(1)}, u32[]{:S(2)}, u32[]{:S(2)}) collective-permute-start(bf16[3,128,512]{2,1,0:T(8,128)(2,1)S(1)} %get-tuple-element.35), channel_id=1, source_target_pairs={{2,0},{4,2},{6,4},{8,6},{10,8},{12,10},{14,12},{3,1},{5,3},{7,5},{... | collective-permute-start | bytes 1179656 | tf_op jit(solution)/shard_map/ppermute | solution.py:328
  50.4 19.1 %collective-permute-start.9 = (bf16[3,128,512]{2,1,0:T(8,128)(2,1)S(1)}, bf16[3,128,512]{2,1,0:T(8,128)(2,1)S(1)}, u32[]{:S(2)}, u32[]{:S(2)}) collective-permute-start(bf16[3,128,512]{2,1,0:T(8,128)(2,1)S(1)} %get-tuple-element.36), channel_id=1, source_target_pairs={{0,2},{2,4},{4,6},{6,8},{8,10},{10,12},{12,14},{1,3},{3,5},{5,7},{... | collective-permute-start | bytes 1179656 | tf_op jit(solution)/shard_map/ppermute | solution.py:328
  53.7 5.7 %collective-permute-start.13 = (bf16[4,8,512]{2,1,0:T(8,128)(2,1)S(1)}, bf16[4,8,512]{2,1,0:T(8,128)(2,1)S(1)}, u32[]{:S(2)}, u32[]{:S(2)}) collective-permute-start(bf16[4,8,512]{2,1,0:T(8,128)(2,1)S(1)} %slice_select_fusion), channel_id=1, source_target_pairs={{0,1},{1,0},{2,3},{3,2},{4,5},{5,4},{6,7},{7,6},{8,9},{9,8},{10,11... | collective-permute-start | bytes 98312 | tf_op jit(solution)/shard_map/ppermute | solution.py:345
  53.8 15.1 %collective-permute-start.12 = (bf16[3,8,512]{2,1,0:T(8,128)(2,1)S(1)}, bf16[3,8,512]{2,1,0:T(8,128)(2,1)S(1)}, u32[]{:S(2)}, u32[]{:S(2)}) collective-permute-start(bf16[3,8,512]{2,1,0:T(8,128)(2,1)S(1)} %get-tuple-element.41), channel_id=1, source_target_pairs={{3,0},{2,1},{5,2},{4,3},{7,4},{6,5},{9,6},{8,7},{11,8},{10,9},{13,... | collective-permute-start | bytes 73736 | tf_op jit(solution)/shard_map/ppermute | solution.py:346
  57.1 11.8 %collective-permute-start.11 = (bf16[3,8,512]{2,1,0:T(8,128)(2,1)S(1)}, bf16[3,8,512]{2,1,0:T(8,128)(2,1)S(1)}, u32[]{:S(2)}, u32[]{:S(2)}) collective-permute-start(bf16[3,8,512]{2,1,0:T(8,128)(2,1)S(1)} %get-tuple-element.42), channel_id=1, source_target_pairs={{0,3},{1,2},{2,5},{3,4},{4,7},{5,6},{6,9},{7,8},{8,11},{9,10},{10,... | collective-permute-start | bytes 73736 | tf_op jit(solution)/shard_map/ppermute | solution.py:344

commit v5 on v4

--- a/solution.py
+++ b/solution.py
@@ -150,13 +150,13 @@
     fill(padded, [(middle, edge, 0)], core_ref[0], tile_v)
 
     def place(tile, u, base):
-        return aligned(u * tile_v + base, SUBLANES), aligned(tile * LANES, LANES)
+        return u, aligned(base, SUBLANES), aligned(tile * LANES, LANES)
 
     def begin(tile, u, base):
-        rows, lanes = place(tile, u, base)
-        if base_value.shape[0] == 1:
-            return jnp.broadcast_to(base_value[:, lanes], (SUBLANES, LANES))
-        return base_value[rows, lanes]
+        here = place(tile, u, base)
+        if len(base_value.shape) == 2:
+            return jnp.broadcast_to(base_value[:, here[2]], (SUBLANES, LANES))
+        return base_value[here]
 
     def store(tile, u, base, value):
         out[place(tile, u, base)] = value
@@ -166,13 +166,12 @@
 
 
 def rim_conv(flip, core, left, right, left_edge, right_edge, kernel, inner, store, padded, taps):
-    sides, tile_v = padded.shape[1], padded.shape[2] - 2 * EDGE
-    tile_u = inner.shape[0] // tile_v
+    tile_u, tile_v, _ = inner.shape
     spread_taps(taps, kernel)
     fill(padded, [(left, *left_edge), (right, *right_edge)], core, tile_v)
 
     def begin(tile, u, base):
-        return inner[aligned(u * tile_v + base, SUBLANES), aligned(tile * LANES, LANES)]
+        return inner[u, aligned(base, SUBLANES), aligned(tile * LANES, LANES)]
 
     sources = [*range(REACH), *range(REACH + tile_u, 2 * REACH + tile_u)]
     depthwise(padded, taps, begin, store, tile_u, tile_v, EDGE - REACH, sources, flip)
@@ -180,16 +179,16 @@
 
 def up_kernel(
     core_ref, left, right, kernel, inner, gain, shift, w_in_hbm, b_in,
-    normal_form, inv_scale, activated, slope, padded, taps, normed, w_in, sem,
+    normal_form, inv_scale, activated, slope, padded, taps, summed, normed, w_in, sem,
 ):
     copy = pltpu.make_async_copy(w_in_hbm, w_in, sem)
     copy.start()
     rows, hidden = activated.shape
-    tile_v = padded.shape[2] - 2 * EDGE
+    _, tile_v, _ = inner.shape
+    chunks = tile_v // CHUNK
 
     def store(tile, u, base, value):
-        row = aligned(u * tile_v + base, SUBLANES)
-        normal_form[row, aligned(tile * LANES, LANES)] = value
+        summed[u, aligned(base, SUBLANES), aligned(tile * LANES, LANES)] = value
 
     left_edge, right_edge = (left, tile_v), (right, tile_v)
     rim_conv(
@@ -198,7 +197,7 @@
 
     def norm_step(index):
         here = aligned(index * CHUNK, CHUNK)
-        conv = normal_form[here, :]
+        conv = summed[index // chunks, aligned((index % chunks) * CHUNK, CHUNK), :]
         centred = conv - jnp.mean(conv, axis=-1, keepdims=True)
         variance = jnp.mean(centred * centred, axis=-1, keepdims=True)
         inverse = lax.rsqrt(variance + NORM_EPSILON)
@@ -219,7 +218,8 @@
             )
             phi = 0.5 * (1.0 + lax.erf(pre * 0.7071067811865476))
             activated[here, tile] = (pre * phi).astype(jnp.bfloat16)
-            slope[here, tile] = phi + pre * jnp.exp(-0.5 * pre * pre) * 0.3989422804014327
+            rise = phi + pre * jnp.exp(-0.5 * pre * pre) * 0.3989422804014327
+            slope[here, tile] = rise.astype(jnp.bfloat16)
 
 
 def back_kernel(
@@ -248,7 +248,7 @@
             + scale[...] * (d_normed[here, :] + b_out[...])
             - target[u, inside, :].astype(jnp.float32)
         )
-        mismatch_out[here, :] = mismatch
+        mismatch_out[u, inside, :] = mismatch
         d_branch[here, :] = (scale[...] * mismatch).astype(jnp.bfloat16)
 
     repeat(tile_u * chunks, mismatch_step)
@@ -259,7 +259,9 @@
             d_activated = lax.dot_general(
                 d_branch[here, :], w_out[tile, :], CONTRACT_LAST, preferred_element_type=jnp.float32
             )
-            d_hidden[here, tile] = (d_activated * slope[here, tile]).astype(jnp.bfloat16)
+            d_hidden[here, tile] = (
+                d_activated * slope[here, tile].astype(jnp.float32)
+            ).astype(jnp.bfloat16)
     for here in row_parts(rows):
         d_normed[here, :] = lax.dot_general(
             d_hidden[here, :], w_in[...], CONTRACT_LAST, preferred_element_type=jnp.float32
@@ -287,16 +289,13 @@
     tile_v, tile_u, channels = out.shape
 
     def store(tile, u, base, value):
-        turned[tile, aligned(u * tile_v + base, SUBLANES), :] = value
+        turned[u, aligned(base, SUBLANES), aligned(tile * LANES, LANES)] = value
 
     edges = (left_edge, 0), (right_edge, 0)
     rim_conv(True, core_ref[0], left, right, *edges, kernel, inner, store, padded, taps)
 
-    def turn_step(line):
-        for tile in range(turned.shape[0]):
-            out[line, :, lane_tile(tile)] = turned[tile, pl.ds(line, tile_u, stride=tile_v), :]
-
-    repeat(tile_v, turn_step)
+    for u in range(tile_u):
+        out[:, u, :] = turned[u]
 
 
 def call(kernel, name, outs, scratch, scalars, arrays, flops, limit, left_in_hbm=()):
@@ -440,27 +439,28 @@
     targets, places, block = find_target(teacher, held, core, row, tile_u, tile_v)
     later, _ = lax.optimization_barrier((dw_bias, block))
     matmul = 2 * rows * channels * hidden
-    flat = jax.ShapeDtypeStruct((rows, channels), f32)
+    whole = (tile_u, tile_v, channels)
+    summed = jax.ShapeDtypeStruct(whole, f32)
     taps = pltpu.VMEM((TAPS * TAPS, tiles, SUBLANES, LANES), f32)
     own_pad, side_pad = (
         pltpu.VMEM((tiles, count, tile_v + 2 * EDGE, LANES), f32) for count in (tile_u, 2 * REACH)
     )
     (inner,) = call(
         functools.partial(inner_kernel, False),
-        "inner_up", [flat], [own_pad, taps], [scalar],
+        "inner_up", [summed], [own_pad, taps], [scalar],
         [middle, edge, dw_kernel, later[None]], 1, 8,
     )
     saved = call(
         up_kernel,
         "up",
         [
-            flat,
+            jax.ShapeDtypeStruct((rows, channels), f32),
             jax.ShapeDtypeStruct((rows, LANES), f32),
             jax.ShapeDtypeStruct((rows, hidden), bf16),
-            jax.ShapeDtypeStruct((rows, hidden), f32),
+            jax.ShapeDtypeStruct((rows, hidden), bf16),
         ],
-        [side_pad, taps, pltpu.VMEM((rows, channels), bf16), pltpu.VMEM(w_in.shape, bf16)]
-        + [pltpu.SemaphoreType.DMA],
+        [side_pad, taps, pltpu.VMEM(whole, f32), pltpu.VMEM((rows, channels), bf16)]
+        + [pltpu.VMEM(w_in.shape, bf16), pltpu.SemaphoreType.DMA],
         [scalar],
         [left, right, dw_kernel, inner, norm_gain[None], norm_bias[None], w_in, b_in[None]],
         4 * matmul,
@@ -470,9 +470,9 @@
     mismatch, d_conv = call(
         functools.partial(back_kernel, len(targets)),
         "back",
-        [flat, jax.ShapeDtypeStruct((tile_u, tile_v, channels), bf16)],
+        [summed, jax.ShapeDtypeStruct(whole, bf16)],
         [
-            pltpu.VMEM((tile_u, tile_v, channels), bf16),
+            pltpu.VMEM(whole, bf16),
             pltpu.VMEM((rows, channels), bf16),
             pltpu.VMEM((rows, hidden), bf16),
             pltpu.VMEM((rows, channels), f32),
@@ -486,14 +486,14 @@
     left_edge, edge, right_edge = send_edges(d_conv, core)
     (inner,) = call(
         functools.partial(inner_kernel, True),
-        "inner_last", [flat], [own_pad, taps], [scalar],
+        "inner_last", [summed], [own_pad, taps], [scalar],
         [d_conv, edge, dw_kernel, mismatch], matmul, 8,
     )
     (grad,) = call(
         last_kernel,
         "last",
         [jax.ShapeDtypeStruct((tile_v, tile_u, channels), f32)],
-        [side_pad, taps, pltpu.VMEM((tiles, rows, LANES), f32)],
+        [side_pad, taps, pltpu.VMEM(whole, f32)],
         [scalar],
         [left, right, left_edge, right_edge, dw_kernel, inner],
         matmul,

time: 74.5 us -> 68.3 us (0.917)
  Pallas kernels: 34.8 us -> 27.7 us
    pallas_call x8, Pallas kernels: 34.8 us -> 27.7 us  [call(): pl.pallas_call(kernel, out_shape=tuple(outs), in_specs=[smem] * len(scala...]
  transfers between devices with their start and end apart: 14 -> 14, of which waited for: 2 -> 2; matrix products, arithmetic and copies ran while one was open for 3% -> 3% of each run, Pallas kernels for 34% -> 28%
where the time goes in v5:
time: 68.3 us; the launch traced here: 67.5 us
  starting transfers between devices  28.1 us (41%)
  Pallas kernels  27.7 us (41%)
  waiting for transfers between devices  7.39 us (11%)
  local copies, waits for them, and re-layouts  2.13 us (3%)
  other arithmetic  1.78 us (3%)
    pallas_call x8, Pallas kernels, call(): pl.pallas_call(kernel, out_shape=tuple(outs), in_specs=[smem] * len(scala...  27.7 us
    ppermute x4, starting transfers between devices, find_target(): pieces.append(lax.ppermute(blocks[turn], ('row', 'col'), pairs))  9.46 us
    ppermute x1, waiting for transfers between devices, send_edges(): lax.ppermute(own[:REACH], ('row', 'col'), backward)  6.75 us
    ppermute x2, starting transfers between devices, send_sides(): lax.ppermute(last, 'row', forward)  6.47 us
    ppermute x2, starting transfers between devices, send_sides(): lax.ppermute(first, 'row', backward)  4.98 us
    ppermute x1, starting transfers between devices, send_edges(): lax.ppermute(own[:REACH], ('row', 'col'), backward)  3.18 us
    ppermute x1, starting transfers between devices, send_edges(): lax.ppermute(own[-REACH:], ('row', 'col'), forward)  2.38 us
  transfers between devices with their start and end apart: 14, of which 2 were waited for; matrix products, arithmetic and copies ran while one was open for 3% of the time, Pallas kernels for 28%

profile of v5, /device:TPU:13, one launch (start us, length us, event | category | flops | bytes accessed | tf_op | source)
XLA Modules:
  0.0 67.5 jit_solution(14393952856757003563)
XLA Ops:
  0.0 0.8 %fusion.2 = (bf16[8,4,512]{2,1,0:T(4,128)(2,1)S(1)}, bf16[8,4,512]{2,1,0:T(4,128)(2,1)S(1)}) fusion(bf16[128,4,512]{2,1,0:T(4,128)(2,1)} %param.14), kind=kLoop, calls=%fused_computation.9 | loop fusion | bytes 131072 | tf_op jit(solution)/shard_map/slice | solution.py:432
  0.8 0.7 %collective-permute-start = (bf16[8,4,512]{2,0,1:T(8,128)(2,1)S(1)}, bf16[8,4,512]{2,0,1:T(8,128)(2,1)S(1)}, u32[]{:S(2)}, u32[]{:S(2)}) collective-permute-start(bf16[8,4,512]{2,0,1:T(8,128)(2,1)S(1)} %copy_select_fusion), channel_id=1, source_target_pairs={{0,1},{1,0},{2,3},{3,2},{4,5},{5,4},{6,7},{7,6},{8,9},{9,8},{10,11... | collective-permute-start | bytes 98312 | tf_op jit(solution)/shard_map/ppermute | solution.py:433
  1.6 1.1 %copy.21 = bf16[128,4,512]{2,0,1:T(8,128)(2,1)S(1)} copy(bf16[128,4,512]{2,1,0:T(4,128)(2,1)} %param.14) | data formatting | bytes 1048576 | tf_op jit(solution)/shard_map/optimization_barrier | solution.py:434
  2.7 0.1 fusion.1
  2.8 0.8 %pad_maximum_fusion = bf16[3,136,512]{2,1,0:T(8,128)(2,1)} fusion(bf16[3,8,512]{2,1,0:T(8,128)(2,1)S(1)} %get-tuple-element.44, bf16[3,128,512]{2,1,0:T(8,128)(2,1)S(1)} %get-tuple-element.38), kind=kLoop, calls=%fused_computation.1 | loop fusion | flops 835584 | bytes 835584 | tf_op jit(solution)/shard_map/concatenate | solution.py:332
  3.6 3.1 %collective-permute-start.1 = (bf16[3,136,512]{2,1,0:T(8,128)(2,1)}, bf16[3,136,512]{2,1,0:T(8,128)(2,1)}, u32[]{:S(2)}, u32[]{:S(2)}) collective-permute-start(bf16[3,136,512]{2,1,0:T(8,128)(2,1)} %pad_maximum_fusion), channel_id=1, source_target_pairs={{0,2},{2,4},{4,6},{6,8},{8,10},{10,12},{12,14},{1,3},{3,5},{5,7},{... | collective-permute-start | bytes 1253384 | tf_op jit(solution)/shard_map/ppermute | solution.py:327
  6.7 0.8 %pad_maximum_fusion.1 = bf16[3,136,512]{2,1,0:T(8,128)(2,1)} fusion(bf16[3,8,512]{2,1,0:T(8,128)(2,1)S(1)} %get-tuple-element.43, bf16[3,128,512]{2,1,0:T(8,128)(2,1)S(1)} %get-tuple-element.37), kind=kLoop, calls=%fused_computation.2 | loop fusion | flops 835584 | bytes 835584 | tf_op jit(solution)/shard_map/concatenate | solution.py:333
  7.5 3.1 %collective-permute-start.2 = (bf16[3,136,512]{2,1,0:T(8,128)(2,1)}, bf16[3,136,512]{2,1,0:T(8,128)(2,1)}, u32[]{:S(2)}, u32[]{:S(2)}) collective-permute-start(bf16[3,136,512]{2,1,0:T(8,128)(2,1)} %pad_maximum_fusion.1), channel_id=1, source_target_pairs={{2,0},{4,2},{6,4},{8,6},{10,8},{12,10},{14,12},{3,1},{5,3},{7,5},{... | collective-permute-start | bytes 1253384 | tf_op jit(solution)/shard_map/ppermute | solution.py:327
  10.6 3.1 %project_away.1 = (bf16[256,512]{1,0:T(8,128)(2,1)}, bf16[256,512]{1,0:T(8,128)(2,1)S(1)}) custom-call(s32[1]{0:T(128)} %bitcast.core_ref, bf16[32,2,16,2048]{3,2,1,0:T(8,128)(2,1)} %bitcast.32, bf16[2048,512]{1,0:T(8,128)(2,1)S(1)} %copy-done), custom_call_target="tpu_custom_call" | custom-call | flops 1 | bytes 1 | tf_op jit(solution)/shard_map/project_away/pallas_call | solution.py:311
  13.8 0.8 %collective-permute-start.3 = (bf16[256,512]{1,0:T(8,128)(2,1)}, bf16[256,512]{1,0:T(8,128)(2,1)S(1)}, u32[]{:S(2)}, u32[]{:S(2)}) collective-permute-start(bf16[256,512]{1,0:T(8,128)(2,1)} %get-tuple-element.22), channel_id=1, source_target_pairs={{0,1},{1,0},{2,3},{3,2},{4,5},{5,4},{6,7},{7,6},{8,9},{9,8},{10,11... | collective-permute-start | bytes 786440 | tf_op jit(solution)/shard_map/ppermute | solution.py:373
  14.5 0.1 collective-permute-start.4
  14.6 0.1 pad_add_fusion.places_ref
  14.7 0.1 pad_add_fusion.1.turns_ref
  14.8 2.7 %project_home.1.home = f32[512,512]{1,0:T(8,128)S(1)} custom-call(s32[1]{0:T(128)} %bitcast.core_ref, bf16[32,2,16,2048]{3,2,1,0:T(8,128)(2,1)} %bitcast.33, bf16[2048,512]{1,0:T(8,128)(2,1)S(1)} %copy-done), custom_call_target="tpu_custom_call" | custom-call | flops 1 | bytes 1 | tf_op jit(solution)/shard_map/project_home/pallas_call | solution.py:311
  17.5 1.1 %combine.1 = (bf16[4,32,512]{2,1,0:T(8,128)(2,1)S(1)}, bf16[4,32,512]{2,1,0:T(8,128)(2,1)S(1)}, bf16[4,32,512]{2,1,0:T(8,128)(2,1)S(1)}, bf16[4,32,512]{2,1,0:T(8,128)(2,1)S(1)}) custom-call(s32[4]{0:T(128)S(1)} %pad_add_fusion.1.turns_ref, f32[512,512]{1,0:T(8,128)S(1)} %project_home.1.home, bf16[256,512]{1,0:T(8,128)(2,1)S(1)} %collective-permute-done.3.upper, ...), custom_call_target="tpu_custom_call" | custom-call | flops 1 | bytes 1 | tf_op jit(solution)/shard_map/combine/pallas_call | solution.py:311
  18.6 4.5 %collective-permute-start.5 = (bf16[4,32,512]{2,1,0:T(8,128)(2,1)S(1)}, bf16[4,32,512]{2,1,0:T(8,128)(2,1)S(1)}, u32[]{:S(2)}, u32[]{:S(2)}) collective-permute-start(bf16[4,32,512]{2,1,0:T(8,128)(2,1)S(1)} %get-tuple-element.24), channel_id=1, source_target_pairs={{0,0},{1,8},{2,2},{3,10},{4,4},{5,12},{6,6},{7,14},{8,1},{9,9},{10... | collective-permute-start | bytes 393224 | tf_op jit(solution)/shard_map/ppermute | solution.py:398
  23.2 0.8 %collective-permute-start.6 = (bf16[4,32,512]{2,1,0:T(8,128)(2,1)S(1)}, bf16[4,32,512]{2,1,0:T(8,128)(2,1)S(1)}, u32[]{:S(2)}, u32[]{:S(2)}) collective-permute-start(bf16[4,32,512]{2,1,0:T(8,128)(2,1)S(1)} %get-tuple-element.30), channel_id=1, source_target_pairs={{0,2},{1,10},{2,4},{3,12},{4,6},{5,14},{6,0},{7,8},{8,3},{9,11},{1... | collective-permute-start | bytes 393224 | tf_op jit(solution)/shard_map/ppermute | solution.py:398
  24.0 0.9 %collective-permute-start.7 = (bf16[4,32,512]{2,1,0:T(8,128)(2,1)S(1)}, bf16[4,32,512]{2,1,0:T(8,128)(2,1)S(1)}, u32[]{:S(2)}, u32[]{:S(2)}) collective-permute-start(bf16[4,32,512]{2,1,0:T(8,128)(2,1)S(1)} %get-tuple-element.31), channel_id=1, source_target_pairs={{0,4},{1,12},{2,6},{3,14},{4,0},{5,8},{6,2},{7,10},{8,5},{9,13},{1... | collective-permute-start | bytes 393224 | tf_op jit(solution)/shard_map/ppermute | solution.py:398
  24.9 2.8 %inner_up.1.inner = f32[4,128,512]{2,1,0:T(8,128)S(1)} custom-call(s32[1]{0:T(128)} %bitcast.core_ref, bf16[4,128,512]{2,1,0:T(8,128)(2,1)S(1)} %bitcast.21, bf16[4,8,512]{2,1,0:T(8,128)(2,1)S(1)} %bitcast.24, f32[7,7,512]{2,1,0:T(8,128)S(1)} %copy-done.1, f32[1,512]{1,0:T(1,128)S(1)} %bitcast.25), custom_call_target="tpu_custom_call" | custom-call | flops 1 | bytes 1 | tf_op jit(solution)/shard_map/inner_up/pallas_call | solution.py:311
  27.7 3.2 %collective-permute-start.8 = (bf16[4,32,512]{2,1,0:T(8,128)(2,1)S(1)}, bf16[4,32,512]{2,1,0:T(8,128)(2,1)S(1)}, u32[]{:S(2)}, u32[]{:S(2)}) collective-permute-start(bf16[4,32,512]{2,1,0:T(8,128)(2,1)S(1)} %get-tuple-element.32), channel_id=1, source_target_pairs={{0,6},{1,14},{2,0},{3,8},{4,2},{5,10},{6,4},{7,12},{8,7},{9,15},{1... | collective-permute-start | bytes 393224 | tf_op jit(solution)/shard_map/ppermute | solution.py:398
  31.0 6.7 %up.1 = (f32[512,512]{1,0:T(8,128)S(1)}, f32[512,128]{1,0:T(8,128)S(1)}, bf16[512,2048]{1,0:T(8,128)(2,1)S(1)}, bf16[512,2048]{1,0:T(8,128)(2,1)S(1)}) custom-call(s32[1]{0:T(128)} %bitcast.core_ref, bf16[3,136,512]{2,1,0:T(8,128)(2,1)} %collective-permute-done.1.left, bf16[3,136,512]{2,1,0:T(8,128)(2,1)} %collective-permute-done.2.right, ...), custom_call_target="tpu_custom_call" | custom-call | flops 4294967296 | bytes 9598976 | tf_op jit(solution)/shard_map/up/pallas_call | solution.py:311
  37.8 5.2 %back.1 = (f32[4,128,512]{2,1,0:T(8,128)S(1)}, bf16[4,128,512]{2,1,0:T(8,128)(2,1)S(1)}) custom-call(s32[4]{0:T(128)S(1)} %pad_add_fusion.places_ref, bf16[4,128,512]{2,1,0:T(8,128)(2,1)S(1)} %bitcast.22, f32[512,512]{1,0:T(8,128)S(1)} %get-tuple-element.26.normal_form, f32[512,128]{1,0:T(8,128)S(1)} %get-tuple-element.27.inv_scale, ...), custom_call_target="tpu_custom_call" | custom-call | flops 4294967296 | bytes 12326912 | tf_op jit(solution)/shard_map/back/pallas_call | solution.py:311
  42.9 0.1 fusion
  43.0 1.9 %collective-permute-start.10 = (bf16[3,128,512]{2,1,0:T(8,128)(2,1)S(1)}, bf16[3,128,512]{2,1,0:T(8,128)(2,1)S(1)}, u32[]{:S(2)}, u32[]{:S(2)}) collective-permute-start(bf16[3,128,512]{2,1,0:T(8,128)(2,1)S(1)} %get-tuple-element.35), channel_id=1, source_target_pairs={{2,0},{4,2},{6,4},{8,6},{10,8},{12,10},{14,12},{3,1},{5,3},{7,5},{... | collective-permute-start | bytes 1179656 | tf_op jit(solution)/shard_map/ppermute | solution.py:327
  44.9 3.4 %collective-permute-start.9 = (bf16[3,128,512]{2,1,0:T(8,128)(2,1)S(1)}, bf16[3,128,512]{2,1,0:T(8,128)(2,1)S(1)}, u32[]{:S(2)}, u32[]{:S(2)}) collective-permute-start(bf16[3,128,512]{2,1,0:T(8,128)(2,1)S(1)} %get-tuple-element.36), channel_id=1, source_target_pairs={{0,2},{2,4},{4,6},{6,8},{8,10},{10,12},{12,14},{1,3},{3,5},{5,7},{... | collective-permute-start | bytes 1179656 | tf_op jit(solution)/shard_map/ppermute | solution.py:327
  48.3 0.1 collective-permute-start.13
  48.4 3.2 %collective-permute-start.12 = (bf16[3,8,512]{2,1,0:T(8,128)(2,1)S(1)}, bf16[3,8,512]{2,1,0:T(8,128)(2,1)S(1)}, u32[]{:S(2)}, u32[]{:S(2)}) collective-permute-start(bf16[3,8,512]{2,1,0:T(8,128)(2,1)S(1)} %get-tuple-element.41), channel_id=1, source_target_pairs={{3,0},{2,1},{5,2},{4,3},{7,4},{6,5},{9,6},{8,7},{11,8},{10,9},{13,... | collective-permute-start | bytes 73736 | tf_op jit(solution)/shard_map/ppermute | solution.py:345
  51.6 2.4 %collective-permute-start.11 = (bf16[3,8,512]{2,1,0:T(8,128)(2,1)S(1)}, bf16[3,8,512]{2,1,0:T(8,128)(2,1)S(1)}, u32[]{:S(2)}, u32[]{:S(2)}) collective-permute-start(bf16[3,8,512]{2,1,0:T(8,128)(2,1)S(1)} %get-tuple-element.42), channel_id=1, source_target_pairs={{0,3},{1,2},{2,5},{3,4},{4,7},{5,6},{6,9},{7,8},{8,11},{9,10},{10,... | collective-permute-start | bytes 73736 | tf_op jit(solution)/shard_map/ppermute | solution.py:343
  54.0 2.7 %inner_last.1.inner = f32[4,128,512]{2,1,0:T(8,128)S(1)} custom-call(s32[1]{0:T(128)} %bitcast.core_ref, bf16[4,128,512]{2,1,0:T(8,128)(2,1)S(1)} %get-tuple-element.33.middle, bf16[4,8,512]{2,1,0:T(8,128)(2,1)S(1)} %collective-permute-done.13.edge, f32[7,7,512]{2,1,0:T(8,128)S(1)} %copy-done.1, f32[4,128,512]{2,1,0:T(8,128)S(1)} %get-tuple-element.34.base_value), custom_call_target="tpu_custom_call" | custom-call | flops 1073741824 | bytes 2754560 | tf_op jit(solution)/shard_map/inner_last/pallas_call | solution.py:311
  56.7 6.8 %collective-permute-done.12.right_edge = bf16[3,8,512]{2,1,0:T(8,128)(2,1)S(1)} collective-permute-done((bf16[3,8,512]{2,1,0:T(8,128)(2,1)S(1)}, bf16[3,8,512]{2,1,0:T(8,128)(2,1)S(1)}, u32[]{:S(2)}, u32[]{:S(2)}) %collective-permute-start.12) | collective-permute-done | bytes 24608 | tf_op jit(solution)/shard_map/ppermute | solution.py:345
  63.5 0.6 collective-permute-done.10.right
  64.1 3.5 %last.1 = f32[128,4,512]{2,1,0:T(4,128)} custom-call(s32[1]{0:T(128)} %bitcast.core_ref, bf16[3,128,512]{2,1,0:T(8,128)(2,1)S(1)} %collective-permute-done.9.left, bf16[3,128,512]{2,1,0:T(8,128)(2,1)S(1)} %collective-permute-done.10.right, bf16[3,8,512]{2,1,0:T(8,128)(2,1)S(1)} %collective-permute-done.11.left_edge, ...), custom_call_target="tpu_custom_call" | custom-call | flops 1073741824 | bytes 3033088 | tf_op jit(solution)/shard_map/last/pallas_call | solution.py:311
  (36 shorter events, 0.1 us)
Async XLA Ops:
  0.8 9.8 %copy-start = (bf16[2048,512]{1,0:T(8,128)(2,1)S(1)}, bf16[2048,512]{1,0:T(8,128)(2,1)}, u32[]{:S(2)}) copy-start(bf16[2048,512]{1,0:T(8,128)(2,1)} %weight.1) | copy-start | bytes 6291460
  0.8 2.0 %collective-permute-start = (bf16[8,4,512]{2,0,1:T(8,128)(2,1)S(1)}, bf16[8,4,512]{2,0,1:T(8,128)(2,1)S(1)}, u32[]{:S(2)}, u32[]{:S(2)}) collective-permute-start(bf16[8,4,512]{2,0,1:T(8,128)(2,1)S(1)} %copy_select_fusion), channel_id=1, source_target_pairs={{0,1},{1,0},{2,3},{3,2},{4,5},{5,4},{6,7},{7,6},{8,9},{9,8},{10,11... | collective-permute-start | bytes 98312 | tf_op jit(solution)/shard_map/ppermute | solution.py:433
  3.6 24.1 %collective-permute-start.1 = (bf16[3,136,512]{2,1,0:T(8,128)(2,1)}, bf16[3,136,512]{2,1,0:T(8,128)(2,1)}, u32[]{:S(2)}, u32[]{:S(2)}) collective-permute-start(bf16[3,136,512]{2,1,0:T(8,128)(2,1)} %pad_maximum_fusion), channel_id=1, source_target_pairs={{0,2},{2,4},{4,6},{6,8},{8,10},{10,12},{12,14},{1,3},{3,5},{5,7},{... | collective-permute-start | bytes 1253384 | tf_op jit(solution)/shard_map/ppermute | solution.py:327
  7.5 23.4 %collective-permute-start.2 = (bf16[3,136,512]{2,1,0:T(8,128)(2,1)}, bf16[3,136,512]{2,1,0:T(8,128)(2,1)}, u32[]{:S(2)}, u32[]{:S(2)}) collective-permute-start(bf16[3,136,512]{2,1,0:T(8,128)(2,1)} %pad_maximum_fusion.1), channel_id=1, source_target_pairs={{2,0},{4,2},{6,4},{8,6},{10,8},{12,10},{14,12},{3,1},{5,3},{7,5},{... | collective-permute-start | bytes 1253384 | tf_op jit(solution)/shard_map/ppermute | solution.py:327
  13.8 3.8 %collective-permute-start.3 = (bf16[256,512]{1,0:T(8,128)(2,1)}, bf16[256,512]{1,0:T(8,128)(2,1)S(1)}, u32[]{:S(2)}, u32[]{:S(2)}) collective-permute-start(bf16[256,512]{1,0:T(8,128)(2,1)} %get-tuple-element.22), channel_id=1, source_target_pairs={{0,1},{1,0},{2,3},{3,2},{4,5},{5,4},{6,7},{7,6},{8,9},{9,8},{10,11... | collective-permute-start | bytes 786440 | tf_op jit(solution)/shard_map/ppermute | solution.py:373
  14.5 3.0 %collective-permute-start.4 = (bf16[256,512]{1,0:T(8,128)(2,1)S(1)}, bf16[256,512]{1,0:T(8,128)(2,1)S(1)}, u32[]{:S(2)}, u32[]{:S(2)}) collective-permute-start(bf16[256,512]{1,0:T(8,128)(2,1)S(1)} %get-tuple-element.23), channel_id=1, source_target_pairs={{0,1},{1,0},{2,3},{3,2},{4,5},{5,4},{6,7},{7,6},{8,9},{9,8},{10,11... | collective-permute-start | bytes 786440 | tf_op jit(solution)/shard_map/ppermute | solution.py:373
  14.8 10.1 %copy-start.1 = (f32[7,7,512]{2,1,0:T(8,128)S(1)}, f32[7,7,512]{2,1,0:T(8,128)}, u32[]{:S(2)}) copy-start(f32[7,7,512]{2,1,0:T(8,128)} %kernel.7) | copy-start | bytes 301060
  14.8 10.1 %copy-start.2 = (f32[512]{0:T(512)S(1)}, f32[512]{0:T(512)}, u32[]{:S(2)}) copy-start(f32[512]{0:T(512)} %param.16) | copy-start | bytes 6148
  17.5 13.4 %copy-start.5 = (f32[2048]{0:T(1024)S(1)}, f32[2048]{0:T(1024)}, u32[]{:S(2)}) copy-start(f32[2048]{0:T(1024)} %param.20) | copy-start | bytes 24580
  17.5 13.4 %copy-start.6 = (f32[512]{0:T(512)S(1)}, f32[512]{0:T(512)}, u32[]{:S(2)}) copy-start(f32[512]{0:T(512)} %param.18) | copy-start | bytes 6148
  17.5 13.4 %copy-start.7 = (f32[512]{0:T(512)S(1)}, f32[512]{0:T(512)}, u32[]{:S(2)}) copy-start(f32[512]{0:T(512)} %param.17) | copy-start | bytes 6148
  18.6 19.1 %collective-permute-start.5 = (bf16[4,32,512]{2,1,0:T(8,128)(2,1)S(1)}, bf16[4,32,512]{2,1,0:T(8,128)(2,1)S(1)}, u32[]{:S(2)}, u32[]{:S(2)}) collective-permute-start(bf16[4,32,512]{2,1,0:T(8,128)(2,1)S(1)} %get-tuple-element.24), channel_id=1, source_target_pairs={{0,0},{1,8},{2,2},{3,10},{4,4},{5,12},{6,6},{7,14},{8,1},{9,9},{10... | collective-permute-start | bytes 393224 | tf_op jit(solution)/shard_map/ppermute | solution.py:398
  23.2 14.5 %collective-permute-start.6 = (bf16[4,32,512]{2,1,0:T(8,128)(2,1)S(1)}, bf16[4,32,512]{2,1,0:T(8,128)(2,1)S(1)}, u32[]{:S(2)}, u32[]{:S(2)}) collective-permute-start(bf16[4,32,512]{2,1,0:T(8,128)(2,1)S(1)} %get-tuple-element.30), channel_id=1, source_target_pairs={{0,2},{1,10},{2,4},{3,12},{4,6},{5,14},{6,0},{7,8},{8,3},{9,11},{1... | collective-permute-start | bytes 393224 | tf_op jit(solution)/shard_map/ppermute | solution.py:398
  24.0 13.7 %collective-permute-start.7 = (bf16[4,32,512]{2,1,0:T(8,128)(2,1)S(1)}, bf16[4,32,512]{2,1,0:T(8,128)(2,1)S(1)}, u32[]{:S(2)}, u32[]{:S(2)}) collective-permute-start(bf16[4,32,512]{2,1,0:T(8,128)(2,1)S(1)} %get-tuple-element.31), channel_id=1, source_target_pairs={{0,4},{1,12},{2,6},{3,14},{4,0},{5,8},{6,2},{7,10},{8,5},{9,13},{1... | collective-permute-start | bytes 393224 | tf_op jit(solution)/shard_map/ppermute | solution.py:398
  27.7 10.0 %collective-permute-start.8 = (bf16[4,32,512]{2,1,0:T(8,128)(2,1)S(1)}, bf16[4,32,512]{2,1,0:T(8,128)(2,1)S(1)}, u32[]{:S(2)}, u32[]{:S(2)}) collective-permute-start(bf16[4,32,512]{2,1,0:T(8,128)(2,1)S(1)} %get-tuple-element.32), channel_id=1, source_target_pairs={{0,6},{1,14},{2,0},{3,8},{4,2},{5,10},{6,4},{7,12},{8,7},{9,15},{1... | collective-permute-start | bytes 393224 | tf_op jit(solution)/shard_map/ppermute | solution.py:398
  30.9 6.8 %copy-start.3 = (bf16[512,2048]{1,0:T(8,128)(2,1)S(1)}, bf16[512,2048]{1,0:T(8,128)(2,1)}, u32[]{:S(2)}) copy-start(bf16[512,2048]{1,0:T(8,128)(2,1)} %w_in.1) | copy-start | bytes 6291460
  30.9 6.8 %copy-start.4 = (bf16[2048,512]{1,0:T(8,128)(2,1)S(1)}, bf16[2048,512]{1,0:T(8,128)(2,1)}, u32[]{:S(2)}) copy-start(bf16[2048,512]{1,0:T(8,128)(2,1)} %w_out.1) | copy-start | bytes 6291460
  30.9 6.8 %copy-start.8 = (f32[512]{0:T(512)S(1)}, f32[512]{0:T(512)}, u32[]{:S(2)}) copy-start(f32[512]{0:T(512)} %param.22) | copy-start | bytes 6148
  30.9 6.8 %copy-start.9 = (f32[512]{0:T(512)S(1)}, f32[512]{0:T(512)}, u32[]{:S(2)}) copy-start(f32[512]{0:T(512)} %param.23) | copy-start | bytes 6148
  43.0 21.1 %collective-permute-start.10 = (bf16[3,128,512]{2,1,0:T(8,128)(2,1)S(1)}, bf16[3,128,512]{2,1,0:T(8,128)(2,1)S(1)}, u32[]{:S(2)}, u32[]{:S(2)}) collective-permute-start(bf16[3,128,512]{2,1,0:T(8,128)(2,1)S(1)} %get-tuple-element.35), channel_id=1, source_target_pairs={{2,0},{4,2},{6,4},{8,6},{10,8},{12,10},{14,12},{3,1},{5,3},{7,5},{... | collective-permute-start | bytes 1179656 | tf_op jit(solution)/shard_map/ppermute | solution.py:327
  44.9 19.1 %collective-permute-start.9 = (bf16[3,128,512]{2,1,0:T(8,128)(2,1)S(1)}, bf16[3,128,512]{2,1,0:T(8,128)(2,1)S(1)}, u32[]{:S(2)}, u32[]{:S(2)}) collective-permute-start(bf16[3,128,512]{2,1,0:T(8,128)(2,1)S(1)} %get-tuple-element.36), channel_id=1, source_target_pairs={{0,2},{2,4},{4,6},{6,8},{8,10},{10,12},{12,14},{1,3},{3,5},{5,7},{... | collective-permute-start | bytes 1179656 | tf_op jit(solution)/shard_map/ppermute | solution.py:327
  48.3 5.7 %collective-permute-start.13 = (bf16[4,8,512]{2,1,0:T(8,128)(2,1)S(1)}, bf16[4,8,512]{2,1,0:T(8,128)(2,1)S(1)}, u32[]{:S(2)}, u32[]{:S(2)}) collective-permute-start(bf16[4,8,512]{2,1,0:T(8,128)(2,1)S(1)} %slice_select_fusion), channel_id=1, source_target_pairs={{0,1},{1,0},{2,3},{3,2},{4,5},{5,4},{6,7},{7,6},{8,9},{9,8},{10,11... | collective-permute-start | bytes 98312 | tf_op jit(solution)/shard_map/ppermute | solution.py:344
  48.4 15.0 %collective-permute-start.12 = (bf16[3,8,512]{2,1,0:T(8,128)(2,1)S(1)}, bf16[3,8,512]{2,1,0:T(8,128)(2,1)S(1)}, u32[]{:S(2)}, u32[]{:S(2)}) collective-permute-start(bf16[3,8,512]{2,1,0:T(8,128)(2,1)S(1)} %get-tuple-element.41), channel_id=1, source_target_pairs={{3,0},{2,1},{5,2},{4,3},{7,4},{6,5},{9,6},{8,7},{11,8},{10,9},{13,... | collective-permute-start | bytes 73736 | tf_op jit(solution)/shard_map/ppermute | solution.py:345
  51.6 11.9 %collective-permute-start.11 = (bf16[3,8,512]{2,1,0:T(8,128)(2,1)S(1)}, bf16[3,8,512]{2,1,0:T(8,128)(2,1)S(1)}, u32[]{:S(2)}, u32[]{:S(2)}) collective-permute-start(bf16[3,8,512]{2,1,0:T(8,128)(2,1)S(1)} %get-tuple-element.42), channel_id=1, source_target_pairs={{0,3},{1,2},{2,5},{3,4},{4,7},{5,6},{6,9},{7,8},{8,11},{9,10},{10,... | collective-permute-start | bytes 73736 | tf_op jit(solution)/shard_map/ppermute | solution.py:343

commit v6 on v5

--- a/solution.py
+++ b/solution.py
@@ -15,7 +15,8 @@
 EDGE = 8
 CHUNK = 16
 UNROLL = 16
-COPIES = 2
+COPIES = 8
+DOTS = 2
 MLP_TILE = 512
 CONTRACT_LAST = (((1,), (1,)), ((), ()))
 SWAP = [(0, 1), (1, 0)]
@@ -33,22 +34,22 @@
     *outs, rows, sems = rest
     half = 1 - core_ref[0] if other else core_ref[0]
     lines, wide, depth = rows.shape
+    count = next(n for n in (COPIES, 4, 2) if lines % n == 0)
     copies = []
-    for index in range(COPIES):
-        here = pl.ds(index * (lines // COPIES), lines // COPIES)
-        copy = pltpu.make_async_copy(
-            teacher_hbm.at[here, half], rows.at[here], sems.at[index]
-        )
+    for index in range(count):
+        here = pl.ds(index * (lines // count), lines // count)
+        copy = pltpu.make_async_copy(teacher_hbm.at[here, half], rows.at[here], sems.at[index])
         copy.start()
         copies.append(copy)
-    size = lines * wide // COPIES
-    for index, copy in enumerate(copies):
-        copy.wait()
-        here = pl.ds(index * (lines // COPIES), lines // COPIES)
+    size = lines * wide // DOTS
+    for index in range(DOTS):
+        for copy in copies[index * count // DOTS : (index + 1) * count // DOTS]:
+            copy.wait()
+        here = pl.ds(index * (lines // DOTS), lines // DOTS)
         product = jnp.dot(
             rows[here].reshape(size, depth), weight[...], preferred_element_type=jnp.float32
         )
-        out = outs[index * len(outs) // COPIES]
+        out = outs[index * len(outs) // DOTS]
         start = index * size % out.shape[0]
         out[start : start + size] = product.astype(out.dtype)
 
@@ -165,20 +166,36 @@
     depthwise(padded, taps, begin, store, tile_u, tile_v, EDGE - REACH, own, flip)
 
 
-def rim_conv(flip, core, left, right, left_edge, right_edge, kernel, inner, store, padded, taps):
+def side_conv(flip, core, on_left, side, edge, kernel, inner, store, padded, taps):
     tile_u, tile_v, _ = inner.shape
     spread_taps(taps, kernel)
-    fill(padded, [(left, *left_edge), (right, *right_edge)], core, tile_v)
+    fill(padded, [(side, *edge)], core, tile_v)
 
     def begin(tile, u, base):
         return inner[u, aligned(base, SUBLANES), aligned(tile * LANES, LANES)]
 
-    sources = [*range(REACH), *range(REACH + tile_u, 2 * REACH + tile_u)]
-    depthwise(padded, taps, begin, store, tile_u, tile_v, EDGE - REACH, sources, flip)
+    for is_left, first in ((True, 0), (False, REACH + tile_u)):
+        sources = range(first, first + REACH)
+
+        @pl.when(on_left == is_left)
+        def _(sources=sources):
+            depthwise(padded, taps, begin, store, tile_u, tile_v, EDGE - REACH, sources, flip)
+
+
+def side_kernel(flip, place_ref, side, edge, kernel, inner, out, padded, taps):
+    tile_v = inner.shape[1]
+
+    def store(tile, u, base, value):
+        out[u, aligned(base, SUBLANES), aligned(tile * LANES, LANES)] = value
+
+    start = edge.shape[1] - EDGE
+    side_conv(
+        flip, place_ref[0], place_ref[1] == 0, side, (edge, start), kernel, inner, store, padded, taps
+    )
 
 
 def up_kernel(
-    core_ref, left, right, kernel, inner, gain, shift, w_in_hbm, b_in,
+    place_ref, side, kernel, inner, gain, shift, w_in_hbm, b_in,
     normal_form, inv_scale, activated, slope, padded, taps, summed, normed, w_in, sem,
 ):
     copy = pltpu.make_async_copy(w_in_hbm, w_in, sem)
@@ -190,9 +207,8 @@
     def store(tile, u, base, value):
         summed[u, aligned(base, SUBLANES), aligned(tile * LANES, LANES)] = value
 
-    left_edge, right_edge = (left, tile_v), (right, tile_v)
-    rim_conv(
-        False, core_ref[0], left, right, left_edge, right_edge, kernel, inner, store, padded, taps
+    side_conv(
+        False, place_ref[0], place_ref[1] == 1, side, (side, tile_v), kernel, inner, store, padded, taps
     )
 
     def norm_step(index):
@@ -283,17 +299,15 @@
     repeat(tile_u * chunks, d_norm_step)
 
 
-def last_kernel(
-    core_ref, left, right, left_edge, right_edge, kernel, inner, out, padded, taps, turned
-):
+def last_kernel(place_ref, side, edge, kernel, inner, out, padded, taps, turned):
     tile_v, tile_u, channels = out.shape
 
     def store(tile, u, base, value):
         turned[u, aligned(base, SUBLANES), aligned(tile * LANES, LANES)] = value
 
-    edges = (left_edge, 0), (right_edge, 0)
-    rim_conv(True, core_ref[0], left, right, *edges, kernel, inner, store, padded, taps)
-
+    side_conv(
+        True, place_ref[0], place_ref[1] == 1, side, (edge, 0), kernel, inner, store, padded, taps
+    )
     for u in range(tile_u):
         out[:, u, :] = turned[u]
 
@@ -320,29 +334,22 @@
     )(*scalars, *arrays)
 
 
-def send_sides(last, first):
+def row_pairs(odd):
     row_count = lax.axis_size("row")
-    forward = [(i, i + 1) for i in range(row_count - 1)]
-    backward = [(b, a) for a, b in forward]
-    return lax.ppermute(last, "row", forward), lax.ppermute(first, "row", backward)
-
-
-def with_edge(block, edge):
-    return (
-        jnp.concatenate([block[-REACH:], edge[-REACH:]], axis=1),
-        jnp.concatenate([block[:REACH], edge[:REACH]], axis=1),
-    )
-
-
-def send_edges(tile, core):
-    row_count = lax.axis_size("row")
-    own = jnp.where(core == 0, tile[:, -EDGE:], tile[:, :EDGE])
-    forward = [(i * 2 + c, i * 2 + 3 - c) for i in range(row_count - 1) for c in range(2)]
-    backward = [(b, a) for a, b in forward]
-    return (
-        lax.ppermute(own[-REACH:], ("row", "col"), forward),
-        lax.ppermute(own, "col", SWAP),
-        lax.ppermute(own[:REACH], ("row", "col"), backward),
+    lower = range(1 if odd else 0, row_count - 1, 2)
+    return [pair for r in lower for pair in ((r, r + 1), (r + 1, r))]
+
+
+def facing(tile, row, odd):
+    to_right = (row % 2 == 1) if odd else (row % 2 == 0)
+    return lax.dynamic_slice_in_dim(
+        tile, jnp.where(to_right, tile.shape[0] - REACH, 0), REACH
+    )
+
+
+def edge_lines(tile, core):
+    return lax.dynamic_slice_in_dim(
+        tile, jnp.where(core == 0, tile.shape[1] - EDGE, 0), EDGE, axis=1
     )
 
 
@@ -433,9 +440,13 @@
     edge = lax.ppermute(own_edge, "col", SWAP).transpose(1, 0, 2)
     after_edge, _ = lax.optimization_barrier((student, own_edge))
     middle = after_edge.transpose(1, 0, 2)
-    last, first = with_edge(middle, edge)
-    left, right = send_sides(last, first)
-    held, _, _ = lax.optimization_barrier((proj_weight, last, first))
+    blocks = []
+    for odd in (True, False):
+        pieces = [facing(middle, row, odd), facing(edge, row, odd)]
+        blocks.append(jnp.concatenate(pieces, axis=1))
+    first_side = lax.ppermute(blocks[0], "row", row_pairs(True))
+    second_side = lax.ppermute(blocks[1], "row", row_pairs(False))
+    held, *_ = lax.optimization_barrier((proj_weight, *blocks))
     targets, places, block = find_target(teacher, held, core, row, tile_u, tile_v)
     later, _ = lax.optimization_barrier((dw_bias, block))
     matmul = 2 * rows * channels * hidden
@@ -443,12 +454,18 @@
     summed = jax.ShapeDtypeStruct(whole, f32)
     taps = pltpu.VMEM((TAPS * TAPS, tiles, SUBLANES, LANES), f32)
     own_pad, side_pad = (
-        pltpu.VMEM((tiles, count, tile_v + 2 * EDGE, LANES), f32) for count in (tile_u, 2 * REACH)
-    )
+        pltpu.VMEM((tiles, count, tile_v + 2 * EDGE, LANES), f32) for count in (tile_u, REACH)
+    )
+    place = jnp.stack([core, row % 2]).astype(jnp.int32)
     (inner,) = call(
         functools.partial(inner_kernel, False),
         "inner_up", [summed], [own_pad, taps], [scalar],
         [middle, edge, dw_kernel, later[None]], 1, 8,
+    )
+    (inner,) = call(
+        functools.partial(side_kernel, False),
+        "side_up", [summed], [side_pad, taps], [place],
+        [first_side, first_side, dw_kernel, inner], 1, 8,
     )
     saved = call(
         up_kernel,
@@ -461,11 +478,11 @@
         ],
         [side_pad, taps, pltpu.VMEM(whole, f32), pltpu.VMEM((rows, channels), bf16)]
         + [pltpu.VMEM(w_in.shape, bf16), pltpu.SemaphoreType.DMA],
-        [scalar],
-        [left, right, dw_kernel, inner, norm_gain[None], norm_bias[None], w_in, b_in[None]],
+        [place],
+        [second_side, dw_kernel, inner, norm_gain[None], norm_bias[None], w_in, b_in[None]],
         4 * matmul,
         16,
-        (6,),
+        (5,),
     )
     mismatch, d_conv = call(
         functools.partial(back_kernel, len(targets)),
@@ -482,21 +499,31 @@
         4 * matmul,
         16,
     )
-    left, right = send_sides(d_conv[-REACH:], d_conv[:REACH])
-    left_edge, edge, right_edge = send_edges(d_conv, core)
+    first_side = lax.ppermute(facing(d_conv, row, True), "row", row_pairs(True))
+    second_side = lax.ppermute(facing(d_conv, row, False), "row", row_pairs(False))
+    own_edge = edge_lines(d_conv, core)
+    edge = lax.ppermute(own_edge, "col", SWAP)
+    across = [(a * 2 + c, b * 2 + 1 - c) for a, b in row_pairs(False) for c in range(2)]
+    second_edge = lax.ppermute(facing(own_edge, row, False), ("row", "col"), across)
+    first_edge = lax.ppermute(edge_lines(first_side, core), "col", SWAP)
     (inner,) = call(
         functools.partial(inner_kernel, True),
         "inner_last", [summed], [own_pad, taps], [scalar],
         [d_conv, edge, dw_kernel, mismatch], matmul, 8,
+    )
+    (inner,) = call(
+        functools.partial(side_kernel, True),
+        "side_last", [summed], [side_pad, taps], [place],
+        [first_side, first_edge, dw_kernel, inner], 1, 8,
     )
     (grad,) = call(
         last_kernel,
         "last",
         [jax.ShapeDtypeStruct((tile_v, tile_u, channels), f32)],
         [side_pad, taps, pltpu.VMEM(whole, f32)],
-        [scalar],
-        [left, right, left_edge, right_edge, dw_kernel, inner],
-        matmul,
+        [place],
+        [second_side, second_edge, dw_kernel, inner],
+        1,
         8,
     )
     return grad

time: 68.3 us -> 68.9 us (level)
  starting transfers between devices: 28.1 us -> 18.8 us
  waiting for transfers between devices: 7.39 us -> 11.9 us
  Pallas kernels: 27.7 us -> 30.8 us
  local copies, waits for them, and re-layouts: 2.13 us -> 4.42 us
    ppermute x7, starting transfers between devices: 17.1 us -> 11 us  [the longest x1 3.25 us: on_device(): first_side = lax.ppermute(facing(d_conv, row, True), 'row', row_pairs(True))]
    ppermute x7, waiting for transfers between devices: 7.37 us -> 11.9 us  [the longest x1 7.72 us: on_device(): first_side = lax.ppermute(facing(d_conv, row, True), 'row', row_pairs(True))]
    ppermute x4, starting transfers between devices: 9.46 us -> 6.29 us  [find_target(): pieces.append(lax.ppermute(blocks[turn], ('row', 'col'), pairs))]
    pallas_call x8 -> x10, Pallas kernels: 27.7 us -> 30.8 us  [call(): pl.pallas_call(kernel, out_shape=tuple(outs), in_specs=[smem] * len(scala...]
    unnamed x20 -> x24, local copies, waits for them, and re-layouts: 0.06 us -> 2.16 us
  transfers between devices with their start and end apart: 14 -> 14, of which waited for: 2 -> 3; matrix products, arithmetic and copies ran while one was open for 3% -> 4% of each run, Pallas kernels for 28% -> 33%
where the time goes in v6:
time: 68.9 us; the launch traced here: 68.1 us
  Pallas kernels  30.8 us (45%)
  starting transfers between devices  18.8 us (27%)
  waiting for transfers between devices  11.9 us (17%)
  local copies, waits for them, and re-layouts  4.42 us (6%)
  other arithmetic  1.82 us (3%)
    pallas_call x10, Pallas kernels, call(): pl.pallas_call(kernel, out_shape=tuple(outs), in_specs=[smem] * len(scala...  30.8 us
    ppermute x1, waiting for transfers between devices, on_device(): first_side = lax.ppermute(facing(d_conv, row, True), 'row', row_pairs(True))  7.72 us
    ppermute x4, starting transfers between devices, find_target(): pieces.append(lax.ppermute(blocks[turn], ('row', 'col'), pairs))  6.29 us
    ppermute x1, starting transfers between devices, on_device(): first_side = lax.ppermute(facing(d_conv, row, True), 'row', row_pairs(True))  3.25 us
    ppermute x1, starting transfers between devices, on_device(): first_side = lax.ppermute(blocks[0], 'row', row_pairs(True))  2.99 us
    ppermute x1, waiting for transfers between devices, on_device(): lax.ppermute(facing(own_edge, row, False), ('row', 'col'), across)  2.53 us
    unnamed x24, local copies, waits for them, and re-layouts  2.16 us
    ppermute x1, waiting for transfers between devices, on_device(): second_side = lax.ppermute(blocks[1], 'row', row_pairs(False))  1.63 us
  transfers between devices with their start and end apart: 14, of which 3 were waited for; matrix products, arithmetic and copies ran while one was open for 4% of the time, Pallas kernels for 33%

profile of v6, /device:TPU:13, one launch (start us, length us, event | category | flops | bytes accessed | tf_op | source)
XLA Modules:
  0.0 68.1 jit_solution(12782131457885491658)
XLA Ops:
  0.0 0.8 %fusion.1 = (bf16[8,4,512]{2,1,0:T(4,128)(2,1)S(1)}, bf16[8,4,512]{2,1,0:T(4,128)(2,1)S(1)}) fusion(bf16[128,4,512]{2,1,0:T(4,128)(2,1)} %param.14), kind=kLoop, calls=%fused_computation.17 | loop fusion | bytes 131072 | tf_op jit(solution)/shard_map/slice | solution.py:439
  0.8 0.7 %collective-permute-start = (bf16[8,4,512]{2,0,1:T(8,128)(2,1)S(1)}, bf16[8,4,512]{2,0,1:T(8,128)(2,1)S(1)}, u32[]{:S(2)}, u32[]{:S(2)}) collective-permute-start(bf16[8,4,512]{2,0,1:T(8,128)(2,1)S(1)} %copy_select_fusion), channel_id=1, source_target_pairs={{0,1},{1,0},{2,3},{3,2},{4,5},{5,4},{6,7},{7,6},{8,9},{9,8},{10,11... | collective-permute-start | bytes 98312 | tf_op jit(solution)/shard_map/ppermute | solution.py:440
  1.6 1.3 %copy.24 = bf16[128,4,512]{2,0,1:T(8,128)(2,1)S(1)} copy(bf16[128,4,512]{2,1,0:T(4,128)(2,1)} %param.14) | data formatting | bytes 1048576 | tf_op jit(solution)/shard_map/optimization_barrier | solution.py:441
  3.0 0.8 %pad_maximum_fusion.1 = bf16[3,136,512]{2,1,0:T(8,128)(2,1)} fusion(bf16[3,8,512]{2,1,0:T(8,128)(2,1)S(1)} %get-tuple-element.43, bf16[3,128,512]{2,1,0:T(8,128)(2,1)S(1)} %get-tuple-element.37), kind=kLoop, calls=%fused_computation.1 | loop fusion | flops 835584 | bytes 835584 | tf_op jit(solution)/shard_map/concatenate | solution.py:446
  3.8 3.0 %collective-permute-start.2 = (bf16[3,136,512]{2,1,0:T(8,128)(2,1)}, bf16[3,136,512]{2,1,0:T(8,128)(2,1)S(1)}, u32[]{:S(2)}, u32[]{:S(2)}) collective-permute-start(bf16[3,136,512]{2,1,0:T(8,128)(2,1)} %pad_maximum_fusion.1), channel_id=1, source_target_pairs={{2,4},{4,2},{6,8},{8,6},{10,12},{12,10},{3,5},{5,3},{7,9},{9,7},{1... | collective-permute-start | bytes 1253384 | tf_op jit(solution)/shard_map/ppermute | solution.py:447
  6.8 0.8 %pad_maximum_fusion = bf16[3,136,512]{2,1,0:T(8,128)(2,1)} fusion(bf16[3,8,512]{2,1,0:T(8,128)(2,1)S(1)} %get-tuple-element.44, bf16[3,128,512]{2,1,0:T(8,128)(2,1)S(1)} %get-tuple-element.38), kind=kLoop, calls=%fused_computation | loop fusion | flops 835584 | bytes 835584 | tf_op jit(solution)/shard_map/concatenate | solution.py:446
  7.5 1.4 %collective-permute-start.1 = (bf16[3,136,512]{2,1,0:T(8,128)(2,1)}, bf16[3,136,512]{2,1,0:T(8,128)(2,1)}, u32[]{:S(2)}, u32[]{:S(2)}) collective-permute-start(bf16[3,136,512]{2,1,0:T(8,128)(2,1)} %pad_maximum_fusion), channel_id=1, source_target_pairs={{0,2},{2,0},{4,6},{6,4},{8,10},{10,8},{12,14},{14,12},{1,3},{3,1},... | collective-permute-start | bytes 1253384 | tf_op jit(solution)/shard_map/ppermute | solution.py:448
  8.9 3.4 %project_away.1 = (bf16[256,512]{1,0:T(8,128)(2,1)}, bf16[256,512]{1,0:T(8,128)(2,1)}) custom-call(s32[1]{0:T(128)} %bitcast.core_ref, bf16[32,2,16,2048]{3,2,1,0:T(8,128)(2,1)} %bitcast.38, bf16[2048,512]{1,0:T(8,128)(2,1)S(1)} %copy-done), custom_call_target="tpu_custom_call" | custom-call | flops 1 | bytes 1 | tf_op jit(solution)/shard_map/project_away/pallas_call | solution.py:325
  12.3 0.7 collective-permute-start.3
  13.3 2.7 %project_home.1.home = f32[512,512]{1,0:T(8,128)S(1)} custom-call(s32[1]{0:T(128)} %bitcast.core_ref, bf16[32,2,16,2048]{3,2,1,0:T(8,128)(2,1)} %bitcast.39, bf16[2048,512]{1,0:T(8,128)(2,1)S(1)} %copy-done), custom_call_target="tpu_custom_call" | custom-call | flops 1 | bytes 1 | tf_op jit(solution)/shard_map/project_home/pallas_call | solution.py:325
  16.0 1.5 %combine.1 = (bf16[4,32,512]{2,1,0:T(8,128)(2,1)S(1)}, bf16[4,32,512]{2,1,0:T(8,128)(2,1)S(1)}, bf16[4,32,512]{2,1,0:T(8,128)(2,1)S(1)}, bf16[4,32,512]{2,1,0:T(8,128)(2,1)S(1)}) custom-call(s32[4]{0:T(128)S(1)} %pad_add_fusion.2.turns_ref, f32[512,512]{1,0:T(8,128)S(1)} %project_home.1.home, bf16[256,512]{1,0:T(8,128)(2,1)S(1)} %collective-permute-done.3.upper, ...), custom_call_target="tpu_custom_call" | custom-call | flops 1 | bytes 1 | tf_op jit(solution)/shard_map/combine/pallas_call | solution.py:325
  17.6 2.9 %collective-permute-start.5 = (bf16[4,32,512]{2,1,0:T(8,128)(2,1)S(1)}, bf16[4,32,512]{2,1,0:T(8,128)(2,1)S(1)}, u32[]{:S(2)}, u32[]{:S(2)}) collective-permute-start(bf16[4,32,512]{2,1,0:T(8,128)(2,1)S(1)} %get-tuple-element.24), channel_id=1, source_target_pairs={{0,0},{1,8},{2,2},{3,10},{4,4},{5,12},{6,6},{7,14},{8,1},{9,9},{10... | collective-permute-start | bytes 393224 | tf_op jit(solution)/shard_map/ppermute | solution.py:405
  20.4 1.5 %collective-permute-start.6 = (bf16[4,32,512]{2,1,0:T(8,128)(2,1)S(1)}, bf16[4,32,512]{2,1,0:T(8,128)(2,1)S(1)}, u32[]{:S(2)}, u32[]{:S(2)}) collective-permute-start(bf16[4,32,512]{2,1,0:T(8,128)(2,1)S(1)} %get-tuple-element.30), channel_id=1, source_target_pairs={{0,2},{1,10},{2,4},{3,12},{4,6},{5,14},{6,0},{7,8},{8,3},{9,11},{1... | collective-permute-start | bytes 393224 | tf_op jit(solution)/shard_map/ppermute | solution.py:405
  22.0 1.6 %collective-permute-start.7 = (bf16[4,32,512]{2,1,0:T(8,128)(2,1)S(1)}, bf16[4,32,512]{2,1,0:T(8,128)(2,1)S(1)}, u32[]{:S(2)}, u32[]{:S(2)}) collective-permute-start(bf16[4,32,512]{2,1,0:T(8,128)(2,1)S(1)} %get-tuple-element.31), channel_id=1, source_target_pairs={{0,4},{1,12},{2,6},{3,14},{4,0},{5,8},{6,2},{7,10},{8,5},{9,13},{1... | collective-permute-start | bytes 393224 | tf_op jit(solution)/shard_map/ppermute | solution.py:405
  23.6 2.8 %inner_up.1.inner = f32[4,128,512]{2,1,0:T(8,128)S(1)} custom-call(s32[1]{0:T(128)} %bitcast.core_ref, bf16[4,128,512]{2,1,0:T(8,128)(2,1)S(1)} %bitcast.28, bf16[4,8,512]{2,1,0:T(8,128)(2,1)S(1)} %bitcast.30, f32[7,7,512]{2,1,0:T(8,128)S(1)} %copy-done.1, f32[1,512]{1,0:T(1,128)S(1)} %bitcast.31), custom_call_target="tpu_custom_call" | custom-call | flops 1 | bytes 1 | tf_op jit(solution)/shard_map/inner_up/pallas_call | solution.py:325
  26.4 0.3 collective-permute-start.8
  26.7 1.9 %side_up.1.inner = f32[4,128,512]{2,1,0:T(8,128)S(1)} custom-call(s32[2]{0:T(128)S(1)} %pad_add_fusion.place_ref, bf16[3,136,512]{2,1,0:T(8,128)(2,1)S(1)} %collective-permute-done.2.side.edge, bf16[3,136,512]{2,1,0:T(8,128)(2,1)S(1)} %collective-permute-done.2.side.edge, f32[7,7,512]{2,1,0:T(8,128)S(1)} %copy-done.1, f32[4,128,512]{2,1,0:T(8,128)S(1)} %inner_up.1.inner), custom_call_target="tpu_custom_call" | custom-call | flops 1 | bytes 1 | tf_op jit(solution)/shard_map/side_up/pallas_call | solution.py:325
  28.6 1.6 %collective-permute-done.1.side = bf16[3,136,512]{2,1,0:T(8,128)(2,1)} collective-permute-done((bf16[3,136,512]{2,1,0:T(8,128)(2,1)}, bf16[3,136,512]{2,1,0:T(8,128)(2,1)}, u32[]{:S(2)}, u32[]{:S(2)}) %collective-permute-start.1) | collective-permute-done | bytes 417824 | tf_op jit(solution)/shard_map/ppermute | solution.py:448
  30.3 5.7 %up.1 = (f32[512,512]{1,0:T(8,128)S(1)}, f32[512,128]{1,0:T(8,128)S(1)}, bf16[512,2048]{1,0:T(8,128)(2,1)S(1)}, bf16[512,2048]{1,0:T(8,128)(2,1)S(1)}) custom-call(s32[2]{0:T(128)S(1)} %pad_add_fusion.place_ref, bf16[3,136,512]{2,1,0:T(8,128)(2,1)} %collective-permute-done.1.side, f32[7,7,512]{2,1,0:T(8,128)S(1)} %copy-done.1, ...), custom_call_target="tpu_custom_call" | custom-call | flops 4294967296 | bytes 9181184 | tf_op jit(solution)/shard_map/up/pallas_call | solution.py:325
  36.1 5.2 %back.1 = (f32[4,128,512]{2,1,0:T(8,128)S(1)}, bf16[4,128,512]{2,1,0:T(8,128)(2,1)S(1)}) custom-call(s32[4]{0:T(128)S(1)} %pad_add_fusion.1.places_ref, bf16[4,128,512]{2,1,0:T(8,128)(2,1)S(1)} %bitcast.29, f32[512,512]{1,0:T(8,128)S(1)} %get-tuple-element.26.normal_form, f32[512,128]{1,0:T(8,128)S(1)} %get-tuple-element.27.inv_scale, ...), custom_call_target="tpu_custom_call" | custom-call | flops 4294967296 | bytes 12326912 | tf_op jit(solution)/shard_map/back/pallas_call | solution.py:325
  41.3 0.9 %copy-done.10 = f32[4,128,512]{2,1,0:T(8,128)} copy-done((f32[4,128,512]{2,1,0:T(8,128)}, f32[4,128,512]{2,1,0:T(8,128)S(1)}, u32[]{:S(2)}) %copy-start.10) | copy-done | bytes 1048600
  42.2 3.3 %collective-permute-start.11 = (bf16[3,128,512]{2,1,0:T(8,128)(2,1)S(1)}, bf16[3,128,512]{2,1,0:T(8,128)(2,1)S(1)}, u32[]{:S(2)}, u32[]{:S(2)}) collective-permute-start(bf16[3,128,512]{2,1,0:T(8,128)(2,1)S(1)} %get-tuple-element.35), channel_id=1, source_target_pairs={{2,4},{4,2},{6,8},{8,6},{10,12},{12,10},{3,5},{5,3},{7,9},{9,7},{1... | collective-permute-start | bytes 1179656 | tf_op jit(solution)/shard_map/ppermute | solution.py:502
  45.5 0.8 %collective-permute-start.9 = (bf16[3,128,512]{2,1,0:T(8,128)(2,1)S(1)}, bf16[3,128,512]{2,1,0:T(8,128)(2,1)S(1)}, u32[]{:S(2)}, u32[]{:S(2)}) collective-permute-start(bf16[3,128,512]{2,1,0:T(8,128)(2,1)S(1)} %get-tuple-element.36), channel_id=1, source_target_pairs={{0,2},{2,0},{4,6},{6,4},{8,10},{10,8},{12,14},{14,12},{1,3},{3,1},... | collective-permute-start | bytes 1179656 | tf_op jit(solution)/shard_map/ppermute | solution.py:503
  46.2 1.1 %collective-permute-start.13 = (bf16[4,8,512]{2,1,0:T(8,128)(2,1)S(1)}, bf16[4,8,512]{2,1,0:T(8,128)(2,1)S(1)}, u32[]{:S(2)}, u32[]{:S(2)}) collective-permute-start(bf16[4,8,512]{2,1,0:T(8,128)(2,1)S(1)} %constant_dynamic-slice_fusion), channel_id=1, source_target_pairs={{0,1},{1,0},{2,3},{3,2},{4,5},{5,4},{6,7},{7,6},{8,9},{9,8},{10,11... | collective-permute-start | bytes 98312 | tf_op jit(solution)/shard_map/ppermute | solution.py:505
  47.3 0.2 collective-permute-start.10
  47.5 7.7 %collective-permute-done.11.side = bf16[3,128,512]{2,1,0:T(8,128)(2,1)S(1)} collective-permute-done((bf16[3,128,512]{2,1,0:T(8,128)(2,1)S(1)}, bf16[3,128,512]{2,1,0:T(8,128)(2,1)S(1)}, u32[]{:S(2)}, u32[]{:S(2)}) %collective-permute-start.11) | collective-permute-done | bytes 393248 | tf_op jit(solution)/shard_map/ppermute | solution.py:502
  55.2 1.4 %collective-permute-start.12 = (bf16[3,8,512]{2,1,0:T(8,128)(2,1)S(1)}, bf16[3,8,512]{2,1,0:T(8,128)(2,1)S(1)}, u32[]{:S(2)}, u32[]{:S(2)}) collective-permute-start(bf16[3,8,512]{2,1,0:T(8,128)(2,1)S(1)} %constant_dynamic-slice_fusion.1), channel_id=1, source_target_pairs={{0,1},{1,0},{2,3},{3,2},{4,5},{5,4},{6,7},{7,6},{8,9},{9,8},{10,11... | collective-permute-start | bytes 73736 | tf_op jit(solution)/shard_map/ppermute | solution.py:508
  56.6 1.2 %copy-done.11 = f32[4,128,512]{2,1,0:T(8,128)S(1)} copy-done((f32[4,128,512]{2,1,0:T(8,128)S(1)}, f32[4,128,512]{2,1,0:T(8,128)}, u32[]{:S(2)}) %copy-start.11) | copy-done | bytes 1048600
  57.8 2.7 %inner_last.1.inner = f32[4,128,512]{2,1,0:T(8,128)S(1)} custom-call(s32[1]{0:T(128)} %bitcast.core_ref, bf16[4,128,512]{2,1,0:T(8,128)(2,1)S(1)} %get-tuple-element.33.middle, bf16[4,8,512]{2,1,0:T(8,128)(2,1)S(1)} %collective-permute-done.13.edge, f32[7,7,512]{2,1,0:T(8,128)S(1)} %copy-done.1, f32[4,128,512]{2,1,0:T(8,128)S(1)} %copy-done.11), custom_call_target="tpu_custom_call" | custom-call | flops 1073741824 | bytes 2754560 | tf_op jit(solution)/shard_map/inner_last/pallas_call | solution.py:325
  60.5 1.9 %side_last.1.inner = f32[4,128,512]{2,1,0:T(8,128)S(1)} custom-call(s32[2]{0:T(128)S(1)} %pad_add_fusion.place_ref, bf16[3,128,512]{2,1,0:T(8,128)(2,1)S(1)} %collective-permute-done.11.side, bf16[3,8,512]{2,1,0:T(8,128)(2,1)S(1)} %collective-permute-done.12.edge, f32[7,7,512]{2,1,0:T(8,128)S(1)} %copy-done.1, f32[4,128,512]{2,1,0:T(8,128)S(1)} %inner_last.1.inner), custom_call_target="tpu_custom_call" | custom-call | flops 1 | bytes 1 | tf_op jit(solution)/shard_map/side_last/pallas_call | solution.py:325
  62.5 2.5 %collective-permute-done.10.edge = bf16[3,8,512]{2,1,0:T(8,128)(2,1)S(1)} collective-permute-done((bf16[3,8,512]{2,1,0:T(8,128)(2,1)S(1)}, bf16[3,8,512]{2,1,0:T(8,128)(2,1)S(1)}, u32[]{:S(2)}, u32[]{:S(2)}) %collective-permute-start.10) | collective-permute-done | bytes 24608 | tf_op jit(solution)/shard_map/ppermute | solution.py:507
  65.0 3.1 %last.1 = f32[128,4,512]{2,1,0:T(4,128)} custom-call(s32[2]{0:T(128)S(1)} %pad_add_fusion.place_ref, bf16[3,128,512]{2,1,0:T(8,128)(2,1)S(1)} %collective-permute-done.9.side, bf16[3,8,512]{2,1,0:T(8,128)(2,1)S(1)} %collective-permute-done.10.edge, f32[7,7,512]{2,1,0:T(8,128)S(1)} %copy-done.1, f32[4,128,512]{2,1,0:T(8,128)S(1)} %side_last.1.inner), custom_call_target="tpu_custom_call" | custom-call | flops 1 | bytes 1 | tf_op jit(solution)/shard_map/last/pallas_call | solution.py:325
  (44 shorter events, 0.6 us)
Async XLA Ops:
  0.8 2.1 %collective-permute-start = (bf16[8,4,512]{2,0,1:T(8,128)(2,1)S(1)}, bf16[8,4,512]{2,0,1:T(8,128)(2,1)S(1)}, u32[]{:S(2)}, u32[]{:S(2)}) collective-permute-start(bf16[8,4,512]{2,0,1:T(8,128)(2,1)S(1)} %copy_select_fusion), channel_id=1, source_target_pairs={{0,1},{1,0},{2,3},{3,2},{4,5},{5,4},{6,7},{7,6},{8,9},{9,8},{10,11... | collective-permute-start | bytes 98312 | tf_op jit(solution)/shard_map/ppermute | solution.py:440
  1.6 7.4 %copy-start = (bf16[2048,512]{1,0:T(8,128)(2,1)S(1)}, bf16[2048,512]{1,0:T(8,128)(2,1)}, u32[]{:S(2)}) copy-start(bf16[2048,512]{1,0:T(8,128)(2,1)} %weight.1) | copy-start | bytes 6291460
  3.8 22.6 %collective-permute-start.2 = (bf16[3,136,512]{2,1,0:T(8,128)(2,1)}, bf16[3,136,512]{2,1,0:T(8,128)(2,1)S(1)}, u32[]{:S(2)}, u32[]{:S(2)}) collective-permute-start(bf16[3,136,512]{2,1,0:T(8,128)(2,1)} %pad_maximum_fusion.1), channel_id=1, source_target_pairs={{2,4},{4,2},{6,8},{8,6},{10,12},{12,10},{3,5},{5,3},{7,9},{9,7},{1... | collective-permute-start | bytes 1253384 | tf_op jit(solution)/shard_map/ppermute | solution.py:447
  7.5 22.7 %collective-permute-start.1 = (bf16[3,136,512]{2,1,0:T(8,128)(2,1)}, bf16[3,136,512]{2,1,0:T(8,128)(2,1)}, u32[]{:S(2)}, u32[]{:S(2)}) collective-permute-start(bf16[3,136,512]{2,1,0:T(8,128)(2,1)} %pad_maximum_fusion), channel_id=1, source_target_pairs={{0,2},{2,0},{4,6},{6,4},{8,10},{10,8},{12,14},{14,12},{1,3},{3,1},... | collective-permute-start | bytes 1253384 | tf_op jit(solution)/shard_map/ppermute | solution.py:448
  12.3 3.7 %collective-permute-start.3 = (bf16[256,512]{1,0:T(8,128)(2,1)}, bf16[256,512]{1,0:T(8,128)(2,1)S(1)}, u32[]{:S(2)}, u32[]{:S(2)}) collective-permute-start(bf16[256,512]{1,0:T(8,128)(2,1)} %get-tuple-element.22), channel_id=1, source_target_pairs={{0,1},{1,0},{2,3},{3,2},{4,5},{5,4},{6,7},{7,6},{8,9},{9,8},{10,11... | collective-permute-start | bytes 786440 | tf_op jit(solution)/shard_map/ppermute | solution.py:380
  13.0 3.0 %collective-permute-start.4 = (bf16[256,512]{1,0:T(8,128)(2,1)}, bf16[256,512]{1,0:T(8,128)(2,1)}, u32[]{:S(2)}, u32[]{:S(2)}) collective-permute-start(bf16[256,512]{1,0:T(8,128)(2,1)} %get-tuple-element.23), channel_id=1, source_target_pairs={{0,1},{1,0},{2,3},{3,2},{4,5},{5,4},{6,7},{7,6},{8,9},{9,8},{10,11... | collective-permute-start | bytes 786440 | tf_op jit(solution)/shard_map/ppermute | solution.py:380
  13.3 10.3 %copy-start.1 = (f32[7,7,512]{2,1,0:T(8,128)S(1)}, f32[7,7,512]{2,1,0:T(8,128)}, u32[]{:S(2)}) copy-start(f32[7,7,512]{2,1,0:T(8,128)} %kernel.11) | copy-start | bytes 301060
  13.3 10.3 %copy-start.2 = (f32[512]{0:T(512)S(1)}, f32[512]{0:T(512)}, u32[]{:S(2)}) copy-start(f32[512]{0:T(512)} %param.16) | copy-start | bytes 6148
  17.6 18.4 %collective-permute-start.5 = (bf16[4,32,512]{2,1,0:T(8,128)(2,1)S(1)}, bf16[4,32,512]{2,1,0:T(8,128)(2,1)S(1)}, u32[]{:S(2)}, u32[]{:S(2)}) collective-permute-start(bf16[4,32,512]{2,1,0:T(8,128)(2,1)S(1)} %get-tuple-element.24), channel_id=1, source_target_pairs={{0,0},{1,8},{2,2},{3,10},{4,4},{5,12},{6,6},{7,14},{8,1},{9,9},{10... | collective-permute-start | bytes 393224 | tf_op jit(solution)/shard_map/ppermute | solution.py:405
  20.4 15.5 %collective-permute-start.6 = (bf16[4,32,512]{2,1,0:T(8,128)(2,1)S(1)}, bf16[4,32,512]{2,1,0:T(8,128)(2,1)S(1)}, u32[]{:S(2)}, u32[]{:S(2)}) collective-permute-start(bf16[4,32,512]{2,1,0:T(8,128)(2,1)S(1)} %get-tuple-element.30), channel_id=1, source_target_pairs={{0,2},{1,10},{2,4},{3,12},{4,6},{5,14},{6,0},{7,8},{8,3},{9,11},{1... | collective-permute-start | bytes 393224 | tf_op jit(solution)/shard_map/ppermute | solution.py:405
  22.0 14.0 %collective-permute-start.7 = (bf16[4,32,512]{2,1,0:T(8,128)(2,1)S(1)}, bf16[4,32,512]{2,1,0:T(8,128)(2,1)S(1)}, u32[]{:S(2)}, u32[]{:S(2)}) collective-permute-start(bf16[4,32,512]{2,1,0:T(8,128)(2,1)S(1)} %get-tuple-element.31), channel_id=1, source_target_pairs={{0,4},{1,12},{2,6},{3,14},{4,0},{5,8},{6,2},{7,10},{8,5},{9,13},{1... | collective-permute-start | bytes 393224 | tf_op jit(solution)/shard_map/ppermute | solution.py:405
  23.6 6.6 %copy-start.5 = (f32[2048]{0:T(1024)S(1)}, f32[2048]{0:T(1024)}, u32[]{:S(2)}) copy-start(f32[2048]{0:T(1024)} %param.20) | copy-start | bytes 24580
  23.6 6.6 %copy-start.6 = (f32[512]{0:T(512)S(1)}, f32[512]{0:T(512)}, u32[]{:S(2)}) copy-start(f32[512]{0:T(512)} %param.18) | copy-start | bytes 6148
  23.6 6.6 %copy-start.7 = (f32[512]{0:T(512)S(1)}, f32[512]{0:T(512)}, u32[]{:S(2)}) copy-start(f32[512]{0:T(512)} %param.17) | copy-start | bytes 6148
  26.4 9.6 %collective-permute-start.8 = (bf16[4,32,512]{2,1,0:T(8,128)(2,1)S(1)}, bf16[4,32,512]{2,1,0:T(8,128)(2,1)S(1)}, u32[]{:S(2)}, u32[]{:S(2)}) collective-permute-start(bf16[4,32,512]{2,1,0:T(8,128)(2,1)S(1)} %get-tuple-element.32), channel_id=1, source_target_pairs={{0,6},{1,14},{2,0},{3,8},{4,2},{5,10},{6,4},{7,12},{8,7},{9,15},{1... | collective-permute-start | bytes 393224 | tf_op jit(solution)/shard_map/ppermute | solution.py:405
  30.2 5.8 %copy-start.3 = (bf16[512,2048]{1,0:T(8,128)(2,1)S(1)}, bf16[512,2048]{1,0:T(8,128)(2,1)}, u32[]{:S(2)}) copy-start(bf16[512,2048]{1,0:T(8,128)(2,1)} %w_in.1) | copy-start | bytes 6291460
  30.2 5.8 %copy-start.4 = (bf16[2048,512]{1,0:T(8,128)(2,1)S(1)}, bf16[2048,512]{1,0:T(8,128)(2,1)}, u32[]{:S(2)}) copy-start(bf16[2048,512]{1,0:T(8,128)(2,1)} %w_out.1) | copy-start | bytes 6291460
  30.2 5.8 %copy-start.8 = (f32[512]{0:T(512)S(1)}, f32[512]{0:T(512)}, u32[]{:S(2)}) copy-start(f32[512]{0:T(512)} %param.22) | copy-start | bytes 6148
  30.2 5.8 %copy-start.9 = (f32[512]{0:T(512)S(1)}, f32[512]{0:T(512)}, u32[]{:S(2)}) copy-start(f32[512]{0:T(512)} %param.23) | copy-start | bytes 6148
  41.2 1.0 %copy-start.10 = (f32[4,128,512]{2,1,0:T(8,128)}, f32[4,128,512]{2,1,0:T(8,128)S(1)}, u32[]{:S(2)}) copy-start(f32[4,128,512]{2,1,0:T(8,128)S(1)} %get-tuple-element.34.base_value) | copy-start | bytes 3145732
  42.2 13.0 %collective-permute-start.11 = (bf16[3,128,512]{2,1,0:T(8,128)(2,1)S(1)}, bf16[3,128,512]{2,1,0:T(8,128)(2,1)S(1)}, u32[]{:S(2)}, u32[]{:S(2)}) collective-permute-start(bf16[3,128,512]{2,1,0:T(8,128)(2,1)S(1)} %get-tuple-element.35), channel_id=1, source_target_pairs={{2,4},{4,2},{6,8},{8,6},{10,12},{12,10},{3,5},{5,3},{7,9},{9,7},{1... | collective-permute-start | bytes 1179656 | tf_op jit(solution)/shard_map/ppermute | solution.py:502
  45.5 19.5 %collective-permute-start.9 = (bf16[3,128,512]{2,1,0:T(8,128)(2,1)S(1)}, bf16[3,128,512]{2,1,0:T(8,128)(2,1)S(1)}, u32[]{:S(2)}, u32[]{:S(2)}) collective-permute-start(bf16[3,128,512]{2,1,0:T(8,128)(2,1)S(1)} %get-tuple-element.36), channel_id=1, source_target_pairs={{0,2},{2,0},{4,6},{6,4},{8,10},{10,8},{12,14},{14,12},{1,3},{3,1},... | collective-permute-start | bytes 1179656 | tf_op jit(solution)/shard_map/ppermute | solution.py:503
  46.2 10.4 %collective-permute-start.13 = (bf16[4,8,512]{2,1,0:T(8,128)(2,1)S(1)}, bf16[4,8,512]{2,1,0:T(8,128)(2,1)S(1)}, u32[]{:S(2)}, u32[]{:S(2)}) collective-permute-start(bf16[4,8,512]{2,1,0:T(8,128)(2,1)S(1)} %constant_dynamic-slice_fusion), channel_id=1, source_target_pairs={{0,1},{1,0},{2,3},{3,2},{4,5},{5,4},{6,7},{7,6},{8,9},{9,8},{10,11... | collective-permute-start | bytes 98312 | tf_op jit(solution)/shard_map/ppermute | solution.py:505
  47.3 17.6 %collective-permute-start.10 = (bf16[3,8,512]{2,1,0:T(8,128)(2,1)S(1)}, bf16[3,8,512]{2,1,0:T(8,128)(2,1)S(1)}, u32[]{:S(2)}, u32[]{:S(2)}) collective-permute-start(bf16[3,8,512]{2,1,0:T(8,128)(2,1)S(1)} %constant_dynamic-slice_fusion.3), channel_id=1, source_target_pairs={{0,3},{1,2},{2,1},{3,0},{4,7},{5,6},{6,5},{7,4},{8,11},{9,10},{10,... | collective-permute-start | bytes 73736 | tf_op jit(solution)/shard_map/ppermute | solution.py:507
  55.2 5.3 %collective-permute-start.12 = (bf16[3,8,512]{2,1,0:T(8,128)(2,1)S(1)}, bf16[3,8,512]{2,1,0:T(8,128)(2,1)S(1)}, u32[]{:S(2)}, u32[]{:S(2)}) collective-permute-start(bf16[3,8,512]{2,1,0:T(8,128)(2,1)S(1)} %constant_dynamic-slice_fusion.1), channel_id=1, source_target_pairs={{0,1},{1,0},{2,3},{3,2},{4,5},{5,4},{6,7},{7,6},{8,9},{9,8},{10,11... | collective-permute-start | bytes 73736 | tf_op jit(solution)/shard_map/ppermute | solution.py:508
  56.6 1.2 %copy-start.11 = (f32[4,128,512]{2,1,0:T(8,128)S(1)}, f32[4,128,512]{2,1,0:T(8,128)}, u32[]{:S(2)}) copy-start(f32[4,128,512]{2,1,0:T(8,128)} %copy-done.10) | copy-start | bytes 3145732

commit v7 on v6

--- a/solution.py
+++ b/solution.py
@@ -145,8 +145,13 @@
             place += 1
 
 
-def inner_kernel(flip, core_ref, middle, edge, kernel, base_value, out, padded, taps):
+def inner_kernel(flip, core_ref, middle, edge, kernel, base_value, out, padded, taps, *fetch):
     tile_u, tile_v, channels = middle.shape
+    copies = []
+    if fetch:
+        copies.append(pltpu.make_async_copy(base_value, *fetch))
+        copies[0].start()
+        base_value = fetch[0]
     spread_taps(taps, kernel)
     fill(padded, [(middle, edge, 0)], core_ref[0], tile_v)
 
@@ -162,6 +167,8 @@
     def store(tile, u, base, value):
         out[place(tile, u, base)] = value
 
+    for copy in copies:
+        copy.wait()
     own = range(REACH, REACH + tile_u)
     depthwise(padded, taps, begin, store, tile_u, tile_v, EDGE - REACH, own, flip)
 
@@ -243,7 +250,7 @@
     gain, w_in, w_out, b_out, scale, *rest,
 ):
     targets = rest[:pieces]
-    mismatch_out, d_out, target, d_branch, d_hidden, d_normed = rest[pieces:]
+    mismatch_hbm, d_out, mismatch_out, sem, target, d_branch, d_hidden, d_normed = rest[pieces:]
     tile_u, tile_v, channels = middle.shape
     rows, hidden = activated.shape
     chunks = tile_v // CHUNK
@@ -268,6 +275,8 @@
         d_branch[here, :] = (scale[...] * mismatch).astype(jnp.bfloat16)
 
     repeat(tile_u * chunks, mismatch_step)
+    copy = pltpu.make_async_copy(mismatch_out, mismatch_hbm, sem)
+    copy.start()
 
     for start in range(0, hidden, MLP_TILE):
         tile = slice(start, start + MLP_TILE)
@@ -297,6 +306,7 @@
         d_out[u, inside, :] = d_conv.astype(jnp.bfloat16)
 
     repeat(tile_u * chunks, d_norm_step)
+    copy.wait()
 
 
 def last_kernel(place_ref, side, edge, kernel, inner, out, padded, taps, turned):
@@ -312,7 +322,9 @@
         out[:, u, :] = turned[u]
 
 
-def call(kernel, name, outs, scratch, scalars, arrays, flops, limit, left_in_hbm=()):
+def call(
+    kernel, name, outs, scratch, scalars, arrays, flops, limit, left_in_hbm=(), out_in_hbm=()
+):
     vmem = pl.BlockSpec(memory_space=pltpu.VMEM)
     smem = pl.BlockSpec(memory_space=pltpu.SMEM)
     hbm = pl.BlockSpec(memory_space=pltpu.HBM)
@@ -326,7 +338,7 @@
         kernel,
         out_shape=tuple(outs),
         in_specs=[smem] * len(scalars) + specs,
-        out_specs=(vmem,) * len(outs),
+        out_specs=tuple(hbm if index in out_in_hbm else vmem for index in range(len(outs))),
         scratch_shapes=scratch,
         compiler_params=pltpu.CompilerParams(vmem_limit_bytes=limit << 20),
         cost_estimate=pl.CostEstimate(flops=flops, bytes_accessed=moved, transcendentals=0),
@@ -351,6 +363,17 @@
     return lax.dynamic_slice_in_dim(
         tile, jnp.where(core == 0, tile.shape[1] - EDGE, 0), EDGE, axis=1
     )
+
+
+def around(tile, core, row):
+    first_side = lax.ppermute(facing(tile, row, True), "row", row_pairs(True))
+    second_side = lax.ppermute(facing(tile, row, False), "row", row_pairs(False))
+    own_edge = edge_lines(tile, core)
+    edge = lax.ppermute(own_edge, "col", SWAP)
+    across = [(a * 2 + c, b * 2 + 1 - c) for a, b in row_pairs(False) for c in range(2)]
+    second_edge = lax.ppermute(facing(own_edge, row, False), ("row", "col"), across)
+    first_edge = lax.ppermute(edge_lines(first_side, core), "col", SWAP)
+    return first_side, second_side, edge, first_edge, second_edge
 
 
 def find_target(teacher, proj_weight, core, row, tile_u, tile_v):
@@ -436,17 +459,15 @@
     scalar = core.astype(jnp.int32)[None]
     f32, bf16 = jnp.float32, jnp.bfloat16
     rows = tile_u * tile_v
-    own_edge = jnp.where(core == 0, student[-EDGE:], student[:EDGE])
-    edge = lax.ppermute(own_edge, "col", SWAP).transpose(1, 0, 2)
-    after_edge, _ = lax.optimization_barrier((student, own_edge))
-    middle = after_edge.transpose(1, 0, 2)
-    blocks = []
-    for odd in (True, False):
-        pieces = [facing(middle, row, odd), facing(edge, row, odd)]
-        blocks.append(jnp.concatenate(pieces, axis=1))
-    first_side = lax.ppermute(blocks[0], "row", row_pairs(True))
-    second_side = lax.ppermute(blocks[1], "row", row_pairs(False))
-    held, *_ = lax.optimization_barrier((proj_weight, *blocks))
+    middle = student.transpose(1, 0, 2)
+    first_block = facing(middle, row, True)
+    first_side = lax.ppermute(first_block, "row", row_pairs(True))
+    edge = lax.ppermute(edge_lines(middle, core), "col", SWAP)
+    second_block = jnp.concatenate(
+        [facing(middle, row, False), facing(edge, row, False)], axis=1
+    )
+    second_side = lax.ppermute(second_block, "row", row_pairs(False))
+    held, *_ = lax.optimization_barrier((proj_weight, first_block, second_block))
     targets, places, block = find_target(teacher, held, core, row, tile_u, tile_v)
     later, _ = lax.optimization_barrier((dw_bias, block))
     matmul = 2 * rows * channels * hidden
@@ -462,10 +483,12 @@
         "inner_up", [summed], [own_pad, taps], [scalar],
         [middle, edge, dw_kernel, later[None]], 1, 8,
     )
+    arrived, _ = lax.optimization_barrier((first_side, inner))
+    first_edge = lax.ppermute(edge_lines(arrived, core), "col", SWAP)
     (inner,) = call(
         functools.partial(side_kernel, False),
         "side_up", [summed], [side_pad, taps], [place],
-        [first_side, first_side, dw_kernel, inner], 1, 8,
+        [first_side, first_edge, dw_kernel, inner], 1, 8,
     )
     saved = call(
         up_kernel,
@@ -489,6 +512,8 @@
         "back",
         [summed, jax.ShapeDtypeStruct(whole, bf16)],
         [
+            pltpu.VMEM(whole, f32),
+            pltpu.SemaphoreType.DMA,
             pltpu.VMEM(whole, bf16),
             pltpu.VMEM((rows, channels), bf16),
             pltpu.VMEM((rows, hidden), bf16),
@@ -498,18 +523,14 @@
         [middle, *saved, norm_gain[None], w_in, w_out, b_out[None], layer_scale[None], *targets],
         4 * matmul,
         16,
-    )
-    first_side = lax.ppermute(facing(d_conv, row, True), "row", row_pairs(True))
-    second_side = lax.ppermute(facing(d_conv, row, False), "row", row_pairs(False))
-    own_edge = edge_lines(d_conv, core)
-    edge = lax.ppermute(own_edge, "col", SWAP)
-    across = [(a * 2 + c, b * 2 + 1 - c) for a, b in row_pairs(False) for c in range(2)]
-    second_edge = lax.ppermute(facing(own_edge, row, False), ("row", "col"), across)
-    first_edge = lax.ppermute(edge_lines(first_side, core), "col", SWAP)
+        out_in_hbm=(0,),
+    )
+    first_side, second_side, edge, first_edge, second_edge = around(d_conv, core, row)
     (inner,) = call(
         functools.partial(inner_kernel, True),
-        "inner_last", [summed], [own_pad, taps], [scalar],
-        [d_conv, edge, dw_kernel, mismatch], matmul, 8,
+        "inner_last", [summed],
+        [own_pad, taps, pltpu.VMEM(whole, f32), pltpu.SemaphoreType.DMA], [scalar],
+        [d_conv, edge, dw_kernel, mismatch], matmul, 8, (3,),
     )
     (inner,) = call(
         functools.partial(side_kernel, True),

time: 68.9 us -> 67.3 us (0.977)
  local copies, waits for them, and re-layouts: 4.42 us -> 3.32 us
  starting transfers between devices: 18.8 us -> 17.9 us
  other arithmetic: 1.82 us -> 1.01 us
    dynamic_slice x4, local copies, waits for them, and re-layouts: 0.17 us -> 1.8 us  [facing(): lax.dynamic_slice_in_dim(tile, jnp.where(to_right, tile.shape[0] - REACH,...]
    optimization_barrier x1 -> x0, local copies, waits for them, and re-layouts: 1.28 us -> none  [on_device(): after_edge, _ = lax.optimization_barrier((student, own_edge))]
    ppermute x4, waiting for transfers between devices: 0.01 us -> 1.26 us  [find_target(): pieces.append(lax.ppermute(blocks[turn], ('row', 'col'), pairs))]
    ppermute x8 -> x9, waiting for transfers between devices: 11.9 us -> 11 us  [the longest x1 7.64 us: around(): first_side = lax.ppermute(facing(tile, row, True), 'row', row_pairs(True))]
    slice x1 -> x0, local copies, waits for them, and re-layouts: 0.8 us -> none  [on_device(): own_edge = jnp.where(core == 0, student[-EDGE:], student[:EDGE])]
    concatenate x2 -> x1, other arithmetic: 1.57 us -> 0.78 us  [on_device(): jnp.concatenate([facing(middle, row, False), facing(edge, row, False)], a...]
    ppermute x8 -> x9, starting transfers between devices: 11.8 us -> 11.1 us  [the longest x1 3.28 us: around(): first_side = lax.ppermute(facing(tile, row, True), 'row', row_pairs(True))]
    unnamed x24 -> x23, local copies, waits for them, and re-layouts: 2.16 us -> 1.5 us
  transfers between devices with their start and end apart: 14 -> 15, of which waited for: 3 -> 3; matrix products, arithmetic and copies ran while one was open for 4% -> 3% of each run, Pallas kernels for 33% -> 35%
where the time goes in v7:
time: 67.3 us; the launch traced here: 66.2 us
  Pallas kernels  31.4 us (47%)
  starting transfers between devices  17.9 us (27%)
  waiting for transfers between devices  12.3 us (18%)
  local copies, waits for them, and re-layouts  3.32 us (5%)
  other arithmetic  1.01 us (2%)
    pallas_call x10, Pallas kernels, call(): pl.pallas_call(kernel, out_shape=tuple(outs), in_specs=[smem] * len(scala...  31.4 us
    ppermute x1, waiting for transfers between devices, around(): first_side = lax.ppermute(facing(tile, row, True), 'row', row_pairs(True))  7.64 us
    ppermute x4, starting transfers between devices, find_target(): pieces.append(lax.ppermute(blocks[turn], ('row', 'col'), pairs))  6.23 us
    ppermute x1, waiting for transfers between devices, around(): lax.ppermute(facing(own_edge, row, False), ('row', 'col'), across)  3.37 us
    ppermute x1, starting transfers between devices, around(): first_side = lax.ppermute(facing(tile, row, True), 'row', row_pairs(True))  3.28 us
    ppermute x1, starting transfers between devices, on_device(): first_side = lax.ppermute(first_block, 'row', row_pairs(True))  2.99 us
    dynamic_slice x4, local copies, waits for them, and re-layouts, facing(): lax.dynamic_slice_in_dim(tile, jnp.where(to_right, tile.shape[0] - REACH,...  1.8 us
    unnamed x23, local copies, waits for them, and re-layouts  1.5 us
  transfers between devices with their start and end apart: 15, of which 3 were waited for; matrix products, arithmetic and copies ran while one was open for 3% of the time, Pallas kernels for 35%

profile of v7, /device:TPU:13, one launch (start us, length us, event | category | flops | bytes accessed | tf_op | source)
XLA Modules:
  0.0 66.2 jit_solution(13456348921058193868)
XLA Ops:
  0.0 1.3 %copy.19 = bf16[128,4,512]{2,0,1:T(8,128)(2,1)S(1)} copy(bf16[128,4,512]{2,1,0:T(4,128)(2,1)} %param.14) | data formatting | bytes 1048576 | tf_op args[2]
  1.3 0.7 %collective-permute-start = (bf16[4,8,512]{2,1,0:T(8,128)(2,1)S(1)}, bf16[4,8,512]{2,1,0:T(8,128)(2,1)S(1)}, u32[]{:S(2)}, u32[]{:S(2)}) collective-permute-start(bf16[4,8,512]{2,1,0:T(8,128)(2,1)S(1)} %dynamic-slice_bitcast_fusion.2), channel_id=1, source_target_pairs={{0,1},{1,0},{2,3},{3,2},{4,5},{5,4},{6,7},{7,6},{8,9},{9,8},{10,11... | collective-permute-start | bytes 98312 | tf_op jit(solution)/shard_map/ppermute | solution.py:465
  2.1 0.8 %dynamic-slice_bitcast_fusion = (bf16[3,128,512]{2,1,0:T(8,128)(2,1)}, bf16[3,128,512]{2,1,0:T(8,128)(2,1)S(1)}) fusion(bf16[128,4,512]{2,0,1:T(8,128)(2,1)S(1)} %copy.19, s32[]{:T(128)S(6)} %select_n.53, s32[]{:T(128)S(6)} %select_n.51), kind=kLoop, calls=%fused_computation.1 | loop fusion | bytes 1572872 | tf_op jit(solution)/shard_map/dynamic_slice | solution.py:357
  2.9 3.0 %collective-permute-start.2 = (bf16[3,128,512]{2,1,0:T(8,128)(2,1)}, bf16[3,128,512]{2,1,0:T(8,128)(2,1)S(1)}, u32[]{:S(2)}, u32[]{:S(2)}) collective-permute-start(bf16[3,128,512]{2,1,0:T(8,128)(2,1)} %get-tuple-element.37), channel_id=1, source_target_pairs={{2,4},{4,2},{6,8},{8,6},{10,12},{12,10},{3,5},{5,3},{7,9},{9,7},{1... | collective-permute-start | bytes 1179656 | tf_op jit(solution)/shard_map/ppermute | solution.py:464
  5.9 0.8 %pad_maximum_fusion = bf16[3,136,512]{2,1,0:T(8,128)(2,1)} fusion(bf16[3,8,512]{2,1,0:T(8,128)(2,1)S(1)} %constant_dynamic-slice_fusion.6, bf16[3,128,512]{2,1,0:T(8,128)(2,1)S(1)} %get-tuple-element.38), kind=kLoop, calls=%fused_computation | loop fusion | flops 835584 | bytes 835584 | tf_op jit(solution)/shard_map/concatenate | solution.py:466
  6.7 3.4 %project_away.1 = (bf16[256,512]{1,0:T(8,128)(2,1)}, bf16[256,512]{1,0:T(8,128)(2,1)}) custom-call(s32[1]{0:T(128)} %bitcast.core_ref, bf16[32,2,16,2048]{3,2,1,0:T(8,128)(2,1)} %bitcast.34, bf16[2048,512]{1,0:T(8,128)(2,1)S(1)} %copy-done), custom_call_target="tpu_custom_call" | custom-call | flops 1 | bytes 1 | tf_op jit(solution)/shard_map/project_away/pallas_call | solution.py:337
  10.1 0.4 collective-permute-start.3
  10.5 0.2 collective-permute-start.4
  10.7 1.4 %collective-permute-start.1 = (bf16[3,136,512]{2,1,0:T(8,128)(2,1)}, bf16[3,136,512]{2,1,0:T(8,128)(2,1)S(1)}, u32[]{:S(2)}, u32[]{:S(2)}) collective-permute-start(bf16[3,136,512]{2,1,0:T(8,128)(2,1)} %pad_maximum_fusion), channel_id=1, source_target_pairs={{0,2},{2,0},{4,6},{6,4},{8,10},{10,8},{12,14},{14,12},{1,3},{3,1},... | collective-permute-start | bytes 1253384 | tf_op jit(solution)/shard_map/ppermute | solution.py:469
  12.2 2.7 %project_home.1.home = f32[512,512]{1,0:T(8,128)S(1)} custom-call(s32[1]{0:T(128)} %bitcast.core_ref, bf16[32,2,16,2048]{3,2,1,0:T(8,128)(2,1)} %bitcast.35, bf16[2048,512]{1,0:T(8,128)(2,1)S(1)} %copy-done), custom_call_target="tpu_custom_call" | custom-call | flops 1 | bytes 1 | tf_op jit(solution)/shard_map/project_home/pallas_call | solution.py:337
  14.9 1.5 %combine.1 = (bf16[4,32,512]{2,1,0:T(8,128)(2,1)S(1)}, bf16[4,32,512]{2,1,0:T(8,128)(2,1)S(1)}, bf16[4,32,512]{2,1,0:T(8,128)(2,1)S(1)}, bf16[4,32,512]{2,1,0:T(8,128)(2,1)S(1)}) custom-call(s32[4]{0:T(128)S(1)} %pad_add_fusion.2.turns_ref, f32[512,512]{1,0:T(8,128)S(1)} %project_home.1.home, bf16[256,512]{1,0:T(8,128)(2,1)S(1)} %collective-permute-done.3.upper, ...), custom_call_target="tpu_custom_call" | custom-call | flops 1 | bytes 1 | tf_op jit(solution)/shard_map/combine/pallas_call | solution.py:337
  16.5 2.8 %inner_up.1.inner = f32[4,128,512]{2,1,0:T(8,128)S(1)} custom-call(s32[1]{0:T(128)} %bitcast.core_ref, bf16[4,128,512]{2,1,0:T(8,128)(2,1)S(1)} %bitcast.25, bf16[4,8,512]{2,1,0:T(8,128)(2,1)S(1)} %collective-permute-done.edge, f32[7,7,512]{2,1,0:T(8,128)S(1)} %copy-done.1, f32[1,512]{1,0:T(1,128)S(1)} %bitcast.27), custom_call_target="tpu_custom_call" | custom-call | flops 1 | bytes 1 | tf_op jit(solution)/shard_map/inner_up/pallas_call | solution.py:337
  19.3 0.7 %collective-permute-start.5 = (bf16[3,8,512]{2,1,0:T(8,128)(2,1)S(1)}, bf16[3,8,512]{2,1,0:T(8,128)(2,1)S(1)}, u32[]{:S(2)}, u32[]{:S(2)}) collective-permute-start(bf16[3,8,512]{2,1,0:T(8,128)(2,1)S(1)} %constant_dynamic-slice_fusion.5), channel_id=1, source_target_pairs={{0,1},{1,0},{2,3},{3,2},{4,5},{5,4},{6,7},{7,6},{8,9},{9,8},{10,11... | collective-permute-start | bytes 73736 | tf_op jit(solution)/shard_map/ppermute | solution.py:487
  20.1 2.6 %collective-permute-start.6 = (bf16[4,32,512]{2,1,0:T(8,128)(2,1)S(1)}, bf16[4,32,512]{2,1,0:T(8,128)(2,1)S(1)}, u32[]{:S(2)}, u32[]{:S(2)}) collective-permute-start(bf16[4,32,512]{2,1,0:T(8,128)(2,1)S(1)} %get-tuple-element.23), channel_id=1, source_target_pairs={{0,0},{1,8},{2,2},{3,10},{4,4},{5,12},{6,6},{7,14},{8,1},{9,9},{10... | collective-permute-start | bytes 393224 | tf_op jit(solution)/shard_map/ppermute | solution.py:428
  22.7 1.8 %collective-permute-start.7 = (bf16[4,32,512]{2,1,0:T(8,128)(2,1)S(1)}, bf16[4,32,512]{2,1,0:T(8,128)(2,1)S(1)}, u32[]{:S(2)}, u32[]{:S(2)}) collective-permute-start(bf16[4,32,512]{2,1,0:T(8,128)(2,1)S(1)} %get-tuple-element.30), channel_id=1, source_target_pairs={{0,2},{1,10},{2,4},{3,12},{4,6},{5,14},{6,0},{7,8},{8,3},{9,11},{1... | collective-permute-start | bytes 393224 | tf_op jit(solution)/shard_map/ppermute | solution.py:428
  24.5 1.2 %collective-permute-start.8 = (bf16[4,32,512]{2,1,0:T(8,128)(2,1)S(1)}, bf16[4,32,512]{2,1,0:T(8,128)(2,1)S(1)}, u32[]{:S(2)}, u32[]{:S(2)}) collective-permute-start(bf16[4,32,512]{2,1,0:T(8,128)(2,1)S(1)} %get-tuple-element.31), channel_id=1, source_target_pairs={{0,4},{1,12},{2,6},{3,14},{4,0},{5,8},{6,2},{7,10},{8,5},{9,13},{1... | collective-permute-start | bytes 393224 | tf_op jit(solution)/shard_map/ppermute | solution.py:428
  25.7 0.6 collective-permute-start.9
  26.3 1.9 %side_up.1.inner = f32[4,128,512]{2,1,0:T(8,128)S(1)} custom-call(s32[2]{0:T(128)S(1)} %pad_add_fusion.place_ref, bf16[3,128,512]{2,1,0:T(8,128)(2,1)S(1)} %collective-permute-done.2.side, bf16[3,8,512]{2,1,0:T(8,128)(2,1)S(1)} %collective-permute-done.5.edge, f32[7,7,512]{2,1,0:T(8,128)S(1)} %copy-done.1, f32[4,128,512]{2,1,0:T(8,128)S(1)} %inner_up.1.inner), custom_call_target="tpu_custom_call" | custom-call | flops 1 | bytes 1 | tf_op jit(solution)/shard_map/side_up/pallas_call | solution.py:337
  28.3 5.1 %up.1 = (f32[512,512]{1,0:T(8,128)S(1)}, f32[512,128]{1,0:T(8,128)S(1)}, bf16[512,2048]{1,0:T(8,128)(2,1)S(1)}, bf16[512,2048]{1,0:T(8,128)(2,1)S(1)}) custom-call(s32[2]{0:T(128)S(1)} %pad_add_fusion.place_ref, bf16[3,136,512]{2,1,0:T(8,128)(2,1)S(1)} %collective-permute-done.1.side, f32[7,7,512]{2,1,0:T(8,128)S(1)} %copy-done.1, ...), custom_call_target="tpu_custom_call" | custom-call | flops 4294967296 | bytes 9181184 | tf_op jit(solution)/shard_map/up/pallas_call | solution.py:337
  33.4 1.2 %collective-permute-done.8.rest_2_ = bf16[4,32,512]{2,1,0:T(8,128)(2,1)S(1)} collective-permute-done((bf16[4,32,512]{2,1,0:T(8,128)(2,1)S(1)}, bf16[4,32,512]{2,1,0:T(8,128)(2,1)S(1)}, u32[]{:S(2)}, u32[]{:S(2)}) %collective-permute-start.8) | collective-permute-done | bytes 131104 | tf_op jit(solution)/shard_map/ppermute | solution.py:428
  34.7 5.2 %back.1 = (f32[4,128,512]{2,1,0:T(8,128)S(1)}, bf16[4,128,512]{2,1,0:T(8,128)(2,1)S(1)}) custom-call(s32[4]{0:T(128)S(1)} %pad_add_fusion.1.places_ref, bf16[4,128,512]{2,1,0:T(8,128)(2,1)S(1)} %bitcast.26, f32[512,512]{1,0:T(8,128)S(1)} %get-tuple-element.26.normal_form, f32[512,128]{1,0:T(8,128)S(1)} %get-tuple-element.27.inv_scale, ...), custom_call_target="tpu_custom_call" | custom-call | flops 4294967296 | bytes 12326912 | tf_op jit(solution)/shard_map/back/pallas_call | solution.py:337
  39.9 0.9 %constant_dynamic-slice_fusion.2 = (bf16[3,128,512]{2,1,0:T(8,128)(2,1)S(1)}, bf16[3,128,512]{2,1,0:T(8,128)(2,1)}) fusion(bf16[4,128,512]{2,1,0:T(8,128)(2,1)S(1)} %get-tuple-element.33.middle, s32[]{:T(128)S(6)} %select_n.53, s32[]{:T(128)S(6)} %select_n.51), kind=kLoop, calls=%fused_computation.6 | loop fusion | bytes 1572872 | tf_op jit(solution)/shard_map/dynamic_slice | solution.py:357
  40.8 0.2 copy-done.10
  41.0 3.3 %collective-permute-start.12 = (bf16[3,128,512]{2,1,0:T(8,128)(2,1)S(1)}, bf16[3,128,512]{2,1,0:T(8,128)(2,1)S(1)}, u32[]{:S(2)}, u32[]{:S(2)}) collective-permute-start(bf16[3,128,512]{2,1,0:T(8,128)(2,1)S(1)} %get-tuple-element.35), channel_id=1, source_target_pairs={{2,4},{4,2},{6,8},{8,6},{10,12},{12,10},{3,5},{5,3},{7,9},{9,7},{1... | collective-permute-start | bytes 1179656 | tf_op jit(solution)/shard_map/ppermute | solution.py:369
  44.3 1.3 %collective-permute-start.10 = (bf16[3,128,512]{2,1,0:T(8,128)(2,1)}, bf16[3,128,512]{2,1,0:T(8,128)(2,1)S(1)}, u32[]{:S(2)}, u32[]{:S(2)}) collective-permute-start(bf16[3,128,512]{2,1,0:T(8,128)(2,1)} %get-tuple-element.36), channel_id=1, source_target_pairs={{0,2},{2,0},{4,6},{6,4},{8,10},{10,8},{12,14},{14,12},{1,3},{3,1},... | collective-permute-start | bytes 1179656 | tf_op jit(solution)/shard_map/ppermute | solution.py:370
  45.6 0.5 collective-permute-start.14
  46.1 0.2 collective-permute-start.11
  46.3 7.6 %collective-permute-done.12.side = bf16[3,128,512]{2,1,0:T(8,128)(2,1)S(1)} collective-permute-done((bf16[3,128,512]{2,1,0:T(8,128)(2,1)S(1)}, bf16[3,128,512]{2,1,0:T(8,128)(2,1)S(1)}, u32[]{:S(2)}, u32[]{:S(2)}) %collective-permute-start.12) | collective-permute-done | bytes 393248 | tf_op jit(solution)/shard_map/ppermute | solution.py:369
  54.0 3.8 %inner_last.1.inner = f32[4,128,512]{2,1,0:T(8,128)S(1)} custom-call(s32[1]{0:T(128)} %bitcast.core_ref, bf16[4,128,512]{2,1,0:T(8,128)(2,1)S(1)} %get-tuple-element.33.middle, bf16[4,8,512]{2,1,0:T(8,128)(2,1)S(1)} %collective-permute-done.14.edge, f32[7,7,512]{2,1,0:T(8,128)S(1)} %copy-done.1, f32[4,128,512]{2,1,0:T(8,128)} %copy-done.10), custom_call_target="tpu_custom_call" | custom-call | flops 1073741824 | bytes 2754560 | tf_op jit(solution)/shard_map/inner_last/pallas_call | solution.py:337
  57.8 1.9 %side_last.1.inner = f32[4,128,512]{2,1,0:T(8,128)S(1)} custom-call(s32[2]{0:T(128)S(1)} %pad_add_fusion.place_ref, bf16[3,128,512]{2,1,0:T(8,128)(2,1)S(1)} %collective-permute-done.12.side, bf16[3,8,512]{2,1,0:T(8,128)(2,1)S(1)} %collective-permute-done.13.edge, f32[7,7,512]{2,1,0:T(8,128)S(1)} %copy-done.1, f32[4,128,512]{2,1,0:T(8,128)S(1)} %inner_last.1.inner), custom_call_target="tpu_custom_call" | custom-call | flops 1 | bytes 1 | tf_op jit(solution)/shard_map/side_last/pallas_call | solution.py:337
  59.7 3.4 %collective-permute-done.11.edge = bf16[3,8,512]{2,1,0:T(8,128)(2,1)S(1)} collective-permute-done((bf16[3,8,512]{2,1,0:T(8,128)(2,1)S(1)}, bf16[3,8,512]{2,1,0:T(8,128)(2,1)S(1)}, u32[]{:S(2)}, u32[]{:S(2)}) %collective-permute-start.11) | collective-permute-done | bytes 24608 | tf_op jit(solution)/shard_map/ppermute | solution.py:374
  63.1 3.1 %last.1 = f32[128,4,512]{2,1,0:T(4,128)} custom-call(s32[2]{0:T(128)S(1)} %pad_add_fusion.place_ref, bf16[3,128,512]{2,1,0:T(8,128)(2,1)S(1)} %collective-permute-done.10.side, bf16[3,8,512]{2,1,0:T(8,128)(2,1)S(1)} %collective-permute-done.11.edge, f32[7,7,512]{2,1,0:T(8,128)S(1)} %copy-done.1, f32[4,128,512]{2,1,0:T(8,128)S(1)} %side_last.1.inner), custom_call_target="tpu_custom_call" | custom-call | flops 1 | bytes 1 | tf_op jit(solution)/shard_map/last/pallas_call | solution.py:337
  (43 shorter events, 0.4 us)
Async XLA Ops:
  0.0 6.7 %copy-start = (bf16[2048,512]{1,0:T(8,128)(2,1)S(1)}, bf16[2048,512]{1,0:T(8,128)(2,1)}, u32[]{:S(2)}) copy-start(bf16[2048,512]{1,0:T(8,128)(2,1)} %weight.1) | copy-start | bytes 6291460
  1.3 4.6 %collective-permute-start = (bf16[4,8,512]{2,1,0:T(8,128)(2,1)S(1)}, bf16[4,8,512]{2,1,0:T(8,128)(2,1)S(1)}, u32[]{:S(2)}, u32[]{:S(2)}) collective-permute-start(bf16[4,8,512]{2,1,0:T(8,128)(2,1)S(1)} %dynamic-slice_bitcast_fusion.2), channel_id=1, source_target_pairs={{0,1},{1,0},{2,3},{3,2},{4,5},{5,4},{6,7},{7,6},{8,9},{9,8},{10,11... | collective-permute-start | bytes 98312 | tf_op jit(solution)/shard_map/ppermute | solution.py:465
  2.9 16.4 %collective-permute-start.2 = (bf16[3,128,512]{2,1,0:T(8,128)(2,1)}, bf16[3,128,512]{2,1,0:T(8,128)(2,1)S(1)}, u32[]{:S(2)}, u32[]{:S(2)}) collective-permute-start(bf16[3,128,512]{2,1,0:T(8,128)(2,1)} %get-tuple-element.37), channel_id=1, source_target_pairs={{2,4},{4,2},{6,8},{8,6},{10,12},{12,10},{3,5},{5,3},{7,9},{9,7},{1... | collective-permute-start | bytes 1179656 | tf_op jit(solution)/shard_map/ppermute | solution.py:464
  10.1 4.8 %collective-permute-start.3 = (bf16[256,512]{1,0:T(8,128)(2,1)}, bf16[256,512]{1,0:T(8,128)(2,1)S(1)}, u32[]{:S(2)}, u32[]{:S(2)}) collective-permute-start(bf16[256,512]{1,0:T(8,128)(2,1)} %get-tuple-element.21), channel_id=1, source_target_pairs={{0,1},{1,0},{2,3},{3,2},{4,5},{5,4},{6,7},{7,6},{8,9},{9,8},{10,11... | collective-permute-start | bytes 786440 | tf_op jit(solution)/shard_map/ppermute | solution.py:403
  10.5 4.5 %collective-permute-start.4 = (bf16[256,512]{1,0:T(8,128)(2,1)}, bf16[256,512]{1,0:T(8,128)(2,1)}, u32[]{:S(2)}, u32[]{:S(2)}) collective-permute-start(bf16[256,512]{1,0:T(8,128)(2,1)} %get-tuple-element.22), channel_id=1, source_target_pairs={{0,1},{1,0},{2,3},{3,2},{4,5},{5,4},{6,7},{7,6},{8,9},{9,8},{10,11... | collective-permute-start | bytes 786440 | tf_op jit(solution)/shard_map/ppermute | solution.py:403
  10.7 17.5 %collective-permute-start.1 = (bf16[3,136,512]{2,1,0:T(8,128)(2,1)}, bf16[3,136,512]{2,1,0:T(8,128)(2,1)S(1)}, u32[]{:S(2)}, u32[]{:S(2)}) collective-permute-start(bf16[3,136,512]{2,1,0:T(8,128)(2,1)} %pad_maximum_fusion), channel_id=1, source_target_pairs={{0,2},{2,0},{4,6},{6,4},{8,10},{10,8},{12,14},{14,12},{1,3},{3,1},... | collective-permute-start | bytes 1253384 | tf_op jit(solution)/shard_map/ppermute | solution.py:469
  12.2 4.3 %copy-start.1 = (f32[7,7,512]{2,1,0:T(8,128)S(1)}, f32[7,7,512]{2,1,0:T(8,128)}, u32[]{:S(2)}) copy-start(f32[7,7,512]{2,1,0:T(8,128)} %kernel.11) | copy-start | bytes 301060
  12.2 4.3 %copy-start.2 = (f32[512]{0:T(512)S(1)}, f32[512]{0:T(512)}, u32[]{:S(2)}) copy-start(f32[512]{0:T(512)} %param.16) | copy-start | bytes 6148
  16.5 11.7 %copy-start.5 = (f32[2048]{0:T(1024)S(1)}, f32[2048]{0:T(1024)}, u32[]{:S(2)}) copy-start(f32[2048]{0:T(1024)} %param.20) | copy-start | bytes 24580
  16.5 11.7 %copy-start.6 = (f32[512]{0:T(512)S(1)}, f32[512]{0:T(512)}, u32[]{:S(2)}) copy-start(f32[512]{0:T(512)} %param.18) | copy-start | bytes 6148
  16.5 11.7 %copy-start.7 = (f32[512]{0:T(512)S(1)}, f32[512]{0:T(512)}, u32[]{:S(2)}) copy-start(f32[512]{0:T(512)} %param.17) | copy-start | bytes 6148
  19.3 6.4 %collective-permute-start.5 = (bf16[3,8,512]{2,1,0:T(8,128)(2,1)S(1)}, bf16[3,8,512]{2,1,0:T(8,128)(2,1)S(1)}, u32[]{:S(2)}, u32[]{:S(2)}) collective-permute-start(bf16[3,8,512]{2,1,0:T(8,128)(2,1)S(1)} %constant_dynamic-slice_fusion.5), channel_id=1, source_target_pairs={{0,1},{1,0},{2,3},{3,2},{4,5},{5,4},{6,7},{7,6},{8,9},{9,8},{10,11... | collective-permute-start | bytes 73736 | tf_op jit(solution)/shard_map/ppermute | solution.py:487
  20.1 13.3 %collective-permute-start.6 = (bf16[4,32,512]{2,1,0:T(8,128)(2,1)S(1)}, bf16[4,32,512]{2,1,0:T(8,128)(2,1)S(1)}, u32[]{:S(2)}, u32[]{:S(2)}) collective-permute-start(bf16[4,32,512]{2,1,0:T(8,128)(2,1)S(1)} %get-tuple-element.23), channel_id=1, source_target_pairs={{0,0},{1,8},{2,2},{3,10},{4,4},{5,12},{6,6},{7,14},{8,1},{9,9},{10... | collective-permute-start | bytes 393224 | tf_op jit(solution)/shard_map/ppermute | solution.py:428
  22.7 10.7 %collective-permute-start.7 = (bf16[4,32,512]{2,1,0:T(8,128)(2,1)S(1)}, bf16[4,32,512]{2,1,0:T(8,128)(2,1)S(1)}, u32[]{:S(2)}, u32[]{:S(2)}) collective-permute-start(bf16[4,32,512]{2,1,0:T(8,128)(2,1)S(1)} %get-tuple-element.30), channel_id=1, source_target_pairs={{0,2},{1,10},{2,4},{3,12},{4,6},{5,14},{6,0},{7,8},{8,3},{9,11},{1... | collective-permute-start | bytes 393224 | tf_op jit(solution)/shard_map/ppermute | solution.py:428
  24.5 10.2 %collective-permute-start.8 = (bf16[4,32,512]{2,1,0:T(8,128)(2,1)S(1)}, bf16[4,32,512]{2,1,0:T(8,128)(2,1)S(1)}, u32[]{:S(2)}, u32[]{:S(2)}) collective-permute-start(bf16[4,32,512]{2,1,0:T(8,128)(2,1)S(1)} %get-tuple-element.31), channel_id=1, source_target_pairs={{0,4},{1,12},{2,6},{3,14},{4,0},{5,8},{6,2},{7,10},{8,5},{9,13},{1... | collective-permute-start | bytes 393224 | tf_op jit(solution)/shard_map/ppermute | solution.py:428
  25.7 9.0 %collective-permute-start.9 = (bf16[4,32,512]{2,1,0:T(8,128)(2,1)S(1)}, bf16[4,32,512]{2,1,0:T(8,128)(2,1)S(1)}, u32[]{:S(2)}, u32[]{:S(2)}) collective-permute-start(bf16[4,32,512]{2,1,0:T(8,128)(2,1)S(1)} %get-tuple-element.32), channel_id=1, source_target_pairs={{0,6},{1,14},{2,0},{3,8},{4,2},{5,10},{6,4},{7,12},{8,7},{9,15},{1... | collective-permute-start | bytes 393224 | tf_op jit(solution)/shard_map/ppermute | solution.py:428
  28.3 6.4 %copy-start.3 = (bf16[512,2048]{1,0:T(8,128)(2,1)S(1)}, bf16[512,2048]{1,0:T(8,128)(2,1)}, u32[]{:S(2)}) copy-start(bf16[512,2048]{1,0:T(8,128)(2,1)} %w_in.1) | copy-start | bytes 6291460
  28.3 6.4 %copy-start.4 = (bf16[2048,512]{1,0:T(8,128)(2,1)S(1)}, bf16[2048,512]{1,0:T(8,128)(2,1)}, u32[]{:S(2)}) copy-start(bf16[2048,512]{1,0:T(8,128)(2,1)} %w_out.1) | copy-start | bytes 6291460
  28.3 6.4 %copy-start.8 = (f32[512]{0:T(512)S(1)}, f32[512]{0:T(512)}, u32[]{:S(2)}) copy-start(f32[512]{0:T(512)} %param.22) | copy-start | bytes 6148
  28.3 6.4 %copy-start.9 = (f32[512]{0:T(512)S(1)}, f32[512]{0:T(512)}, u32[]{:S(2)}) copy-start(f32[512]{0:T(512)} %param.23) | copy-start | bytes 6148
  39.9 1.1 %copy-start.10 = (f32[4,128,512]{2,1,0:T(8,128)}, f32[4,128,512]{2,1,0:T(8,128)S(1)}, u32[]{:S(2)}) copy-start(f32[4,128,512]{2,1,0:T(8,128)S(1)} %get-tuple-element.34.base_value) | copy-start | bytes 3145732
  41.0 13.0 %collective-permute-start.12 = (bf16[3,128,512]{2,1,0:T(8,128)(2,1)S(1)}, bf16[3,128,512]{2,1,0:T(8,128)(2,1)S(1)}, u32[]{:S(2)}, u32[]{:S(2)}) collective-permute-start(bf16[3,128,512]{2,1,0:T(8,128)(2,1)S(1)} %get-tuple-element.35), channel_id=1, source_target_pairs={{2,4},{4,2},{6,8},{8,6},{10,12},{12,10},{3,5},{5,3},{7,9},{9,7},{1... | collective-permute-start | bytes 1179656 | tf_op jit(solution)/shard_map/ppermute | solution.py:369
  44.3 18.8 %collective-permute-start.10 = (bf16[3,128,512]{2,1,0:T(8,128)(2,1)}, bf16[3,128,512]{2,1,0:T(8,128)(2,1)S(1)}, u32[]{:S(2)}, u32[]{:S(2)}) collective-permute-start(bf16[3,128,512]{2,1,0:T(8,128)(2,1)} %get-tuple-element.36), channel_id=1, source_target_pairs={{0,2},{2,0},{4,6},{6,4},{8,10},{10,8},{12,14},{14,12},{1,3},{3,1},... | collective-permute-start | bytes 1179656 | tf_op jit(solution)/shard_map/ppermute | solution.py:370
  45.6 8.4 %collective-permute-start.14 = (bf16[4,8,512]{2,1,0:T(8,128)(2,1)S(1)}, bf16[4,8,512]{2,1,0:T(8,128)(2,1)S(1)}, u32[]{:S(2)}, u32[]{:S(2)}) collective-permute-start(bf16[4,8,512]{2,1,0:T(8,128)(2,1)S(1)} %constant_dynamic-slice_fusion), channel_id=1, source_target_pairs={{0,1},{1,0},{2,3},{3,2},{4,5},{5,4},{6,7},{7,6},{8,9},{9,8},{10,11... | collective-permute-start | bytes 98312 | tf_op jit(solution)/shard_map/ppermute | solution.py:372
  46.1 17.0 %collective-permute-start.11 = (bf16[3,8,512]{2,1,0:T(8,128)(2,1)S(1)}, bf16[3,8,512]{2,1,0:T(8,128)(2,1)S(1)}, u32[]{:S(2)}, u32[]{:S(2)}) collective-permute-start(bf16[3,8,512]{2,1,0:T(8,128)(2,1)S(1)} %constant_dynamic-slice_fusion.3), channel_id=1, source_target_pairs={{0,3},{1,2},{2,1},{3,0},{4,7},{5,6},{6,5},{7,4},{8,11},{9,10},{10,... | collective-permute-start | bytes 73736 | tf_op jit(solution)/shard_map/ppermute | solution.py:374
  54.0 3.8 %collective-permute-start.13 = (bf16[3,8,512]{2,1,0:T(8,128)(2,1)S(1)}, bf16[3,8,512]{2,1,0:T(8,128)(2,1)S(1)}, u32[]{:S(2)}, u32[]{:S(2)}) collective-permute-start(bf16[3,8,512]{2,1,0:T(8,128)(2,1)S(1)} %constant_dynamic-slice_fusion.1), channel_id=1, source_target_pairs={{0,1},{1,0},{2,3},{3,2},{4,5},{5,4},{6,7},{7,6},{8,9},{9,8},{10,11... | collective-permute-start | bytes 73736 | tf_op jit(solution)/shard_map/ppermute | solution.py:375

commit v8 on v7

--- a/solution.py
+++ b/solution.py
@@ -246,11 +246,12 @@
 
 
 def back_kernel(
-    pieces, places_ref, middle, normal_form, inv_scale, activated, slope,
+    pieces, place_ref, places_ref, middle, normal_form, inv_scale, activated, slope,
     gain, w_in, w_out, b_out, scale, *rest,
 ):
     targets = rest[:pieces]
-    mismatch_hbm, d_out, mismatch_out, sem, target, d_branch, d_hidden, d_normed = rest[pieces:]
+    mismatch_hbm, d_out, even, odd, edge, even_edge, odd_edge, *scratch = rest[pieces:]
+    mismatch_out, sem, target, d_branch, d_hidden, d_normed = scratch
     tile_u, tile_v, channels = middle.shape
     rows, hidden = activated.shape
     chunks = tile_v // CHUNK
@@ -306,24 +307,40 @@
         d_out[u, inside, :] = d_conv.astype(jnp.bfloat16)
 
     repeat(tile_u * chunks, d_norm_step)
+    edge[...] = d_out[:, pl.ds(pl.multiple_of((1 - place_ref[0]) * (tile_v - EDGE), EDGE), EDGE), :]
+    for block, block_edge, from_left in ((even, even_edge, place_ref[1]), (odd, odd_edge, 1 - place_ref[1])):
+        columns = pl.ds((1 - from_left) * (tile_u - REACH), REACH)
+        block[...] = d_out[columns]
+        block_edge[...] = edge[columns]
     copy.wait()
 
 
-def last_kernel(place_ref, side, edge, kernel, inner, out, padded, taps, turned):
+def last_kernel(
+    place_ref, even, odd, even_edge, odd_edge, kernel, inner, out, padded, taps, turned
+):
     tile_v, tile_u, channels = out.shape
+    spread_taps(taps, kernel)
+    sides = (even, even_edge, 0), (odd, odd_edge, 0)
+    for parity in range(2):
+
+        @pl.when(place_ref[1] == parity)
+        def _(left=sides[1 - parity], right=sides[parity]):
+            fill(padded, [left, right], place_ref[0], tile_v)
+
+    def begin(tile, u, base):
+        return inner[u, aligned(base, SUBLANES), aligned(tile * LANES, LANES)]
 
     def store(tile, u, base, value):
         turned[u, aligned(base, SUBLANES), aligned(tile * LANES, LANES)] = value
 
-    side_conv(
-        True, place_ref[0], place_ref[1] == 1, side, (edge, 0), kernel, inner, store, padded, taps
-    )
+    sources = [*range(REACH), *range(REACH + tile_u, 2 * REACH + tile_u)]
+    depthwise(padded, taps, begin, store, tile_u, tile_v, EDGE - REACH, sources, True)
     for u in range(tile_u):
         out[:, u, :] = turned[u]
 
 
 def call(
-    kernel, name, outs, scratch, scalars, arrays, flops, limit, left_in_hbm=(), out_in_hbm=()
+    kernel, name, outs, scratch, scalars, arrays, flops, limit, left_in_hbm=(), anywhere=(), out_anywhere=()
 ):
     vmem = pl.BlockSpec(memory_space=pltpu.VMEM)
     smem = pl.BlockSpec(memory_space=pltpu.SMEM)
@@ -333,12 +350,16 @@
         pltpu.with_memory_space_constraint(a, pltpu.HBM) if index in left_in_hbm else a
         for index, a in enumerate(arrays)
     ]
-    specs = [hbm if index in left_in_hbm else vmem for index in range(len(arrays))]
+    free = pl.BlockSpec(memory_space=pl.ANY)
+    specs = [
+        hbm if index in left_in_hbm else free if index in anywhere else vmem
+        for index in range(len(arrays))
+    ]
     return pl.pallas_call(
         kernel,
         out_shape=tuple(outs),
         in_specs=[smem] * len(scalars) + specs,
-        out_specs=tuple(hbm if index in out_in_hbm else vmem for index in range(len(outs))),
+        out_specs=tuple(free if index in out_anywhere else vmem for index in range(len(outs))),
         scratch_shapes=scratch,
         compiler_params=pltpu.CompilerParams(vmem_limit_bytes=limit << 20),
         cost_estimate=pl.CostEstimate(flops=flops, bytes_accessed=moved, transcendentals=0),
@@ -365,15 +386,8 @@
     )
 
 
-def around(tile, core, row):
-    first_side = lax.ppermute(facing(tile, row, True), "row", row_pairs(True))
-    second_side = lax.ppermute(facing(tile, row, False), "row", row_pairs(False))
-    own_edge = edge_lines(tile, core)
-    edge = lax.ppermute(own_edge, "col", SWAP)
-    across = [(a * 2 + c, b * 2 + 1 - c) for a, b in row_pairs(False) for c in range(2)]
-    second_edge = lax.ppermute(facing(own_edge, row, False), ("row", "col"), across)
-    first_edge = lax.ppermute(edge_lines(first_side, core), "col", SWAP)
-    return first_side, second_side, edge, first_edge, second_edge
+def across(pairs):
+    return [(a * 2 + c, b * 2 + 1 - c) for a, b in pairs for c in range(2)]
 
 
 def find_target(teacher, proj_weight, core, row, tile_u, tile_v):
@@ -474,8 +488,9 @@
     whole = (tile_u, tile_v, channels)
     summed = jax.ShapeDtypeStruct(whole, f32)
     taps = pltpu.VMEM((TAPS * TAPS, tiles, SUBLANES, LANES), f32)
-    own_pad, side_pad = (
-        pltpu.VMEM((tiles, count, tile_v + 2 * EDGE, LANES), f32) for count in (tile_u, REACH)
+    own_pad, side_pad, rim_pad = (
+        pltpu.VMEM((tiles, count, tile_v + 2 * EDGE, LANES), f32)
+        for count in (tile_u, REACH, 2 * REACH)
     )
     place = jnp.stack([core, row % 2]).astype(jnp.int32)
     (inner,) = call(
@@ -507,10 +522,12 @@
         16,
         (5,),
     )
-    mismatch, d_conv = call(
+    side, rim = (REACH, tile_v, channels), (REACH, EDGE, channels)
+    sent = [side, side, (tile_u, EDGE, channels), rim, rim]
+    mismatch, d_conv, even, odd, edge, even_edge, odd_edge = call(
         functools.partial(back_kernel, len(targets)),
         "back",
-        [summed, jax.ShapeDtypeStruct(whole, bf16)],
+        [summed] + [jax.ShapeDtypeStruct(shape, bf16) for shape in (whole, *sent)],
         [
             pltpu.VMEM(whole, f32),
             pltpu.SemaphoreType.DMA,
@@ -519,31 +536,30 @@
             pltpu.VMEM((rows, hidden), bf16),
             pltpu.VMEM((rows, channels), f32),
         ],
-        [places],
+        [place, places],
         [middle, *saved, norm_gain[None], w_in, w_out, b_out[None], layer_scale[None], *targets],
         4 * matmul,
         16,
-        out_in_hbm=(0,),
-    )
-    first_side, second_side, edge, first_edge, second_edge = around(d_conv, core, row)
+        out_anywhere=(0,),
+    )
+    even = lax.ppermute(even, "row", row_pairs(False))
+    odd = lax.ppermute(odd, "row", row_pairs(True))
+    edge = lax.ppermute(edge, "col", SWAP)
+    even_edge = lax.ppermute(even_edge, ("row", "col"), across(row_pairs(False)))
+    odd_edge = lax.ppermute(odd_edge, ("row", "col"), across(row_pairs(True)))
     (inner,) = call(
         functools.partial(inner_kernel, True),
         "inner_last", [summed],
         [own_pad, taps, pltpu.VMEM(whole, f32), pltpu.SemaphoreType.DMA], [scalar],
-        [d_conv, edge, dw_kernel, mismatch], matmul, 8, (3,),
-    )
-    (inner,) = call(
-        functools.partial(side_kernel, True),
-        "side_last", [summed], [side_pad, taps], [place],
-        [first_side, first_edge, dw_kernel, inner], 1, 8,
+        [d_conv, edge, dw_kernel, mismatch], matmul, 8, anywhere=(3,),
     )
     (grad,) = call(
         last_kernel,
         "last",
         [jax.ShapeDtypeStruct((tile_v, tile_u, channels), f32)],
-        [side_pad, taps, pltpu.VMEM(whole, f32)],
+        [rim_pad, taps, pltpu.VMEM(whole, f32)],
         [place],
-        [second_side, second_edge, dw_kernel, inner],
+        [even, odd, even_edge, odd_edge, dw_kernel, inner],
         1,
         8,
     )

time: 67.3 us -> 64.4 us (0.957)
  starting transfers between devices: 17.9 us -> 21.9 us
  waiting for transfers between devices: 12.3 us -> 9.33 us
  Pallas kernels: 31.4 us -> 29.1 us
  local copies, waits for them, and re-layouts: 3.32 us -> 2.22 us
    ppermute x5, starting transfers between devices: 5.27 us -> 9.3 us  [the longest x1 3.28 us: on_device(): odd = lax.ppermute(odd, 'row', row_pairs(True))]
    ppermute x5, waiting for transfers between devices: 11 us -> 8.02 us  [the longest x1 7.2 us: on_device(): lax.ppermute(even_edge, ('row', 'col'), across(row_pairs(False)))]
    pallas_call x10 -> x9, Pallas kernels: 31.4 us -> 29.1 us  [call(): pl.pallas_call(kernel, out_shape=tuple(outs), in_specs=[smem] * len(scala...]
    dynamic_slice x4 -> x2, local copies, waits for them, and re-layouts: 1.8 us -> 0.85 us  [facing(): lax.dynamic_slice_in_dim(tile, jnp.where(to_right, tile.shape[0] - REACH,...]
    unnamed x23 -> x25, local copies, waits for them, and re-layouts: 1.5 us -> 1.34 us
  transfers between devices with their start and end apart: 15 -> 15, of which waited for: 3 -> 4; matrix products, arithmetic and copies ran while one was open for 3% -> 3% of each run, Pallas kernels for 35% -> 31%
where the time goes in v8:
time: 64.4 us; the launch traced here: 63.9 us
  Pallas kernels  29.1 us (45%)
  starting transfers between devices  21.9 us (34%)
  waiting for transfers between devices  9.33 us (14%)
  local copies, waits for them, and re-layouts  2.22 us (3%)
  other arithmetic  1.01 us (2%)
    pallas_call x9, Pallas kernels, call(): pl.pallas_call(kernel, out_shape=tuple(outs), in_specs=[smem] * len(scala...  29.1 us
    ppermute x1, waiting for transfers between devices, on_device(): lax.ppermute(even_edge, ('row', 'col'), across(row_pairs(False)))  7.2 us
    ppermute x4, starting transfers between devices, find_target(): pieces.append(lax.ppermute(blocks[turn], ('row', 'col'), pairs))  6.23 us
    ppermute x1, starting transfers between devices, on_device(): odd = lax.ppermute(odd, 'row', row_pairs(True))  3.28 us
    ppermute x1, starting transfers between devices, on_device(): first_side = lax.ppermute(first_block, 'row', row_pairs(True))  2.99 us
    ppermute x1, starting transfers between devices, on_device(): even = lax.ppermute(even, 'row', row_pairs(False))  2.64 us
    ppermute x1, starting transfers between devices, on_device(): odd_edge = lax.ppermute(odd_edge, ('row', 'col'), across(row_pairs(True)))  1.91 us
    ppermute x1, starting transfers between devices, on_device(): lax.ppermute(even_edge, ('row', 'col'), across(row_pairs(False)))  1.4 us
  transfers between devices with their start and end apart: 15, of which 4 were waited for; matrix products, arithmetic and copies ran while one was open for 3% of the time, Pallas kernels for 31%

profile of v8, /device:TPU:13, one launch (start us, length us, event | category | flops | bytes accessed | tf_op | source)
XLA Modules:
  0.0 63.9 jit_solution(13821174131964719830)
XLA Ops:
  0.0 1.3 %copy.19 = bf16[128,4,512]{2,0,1:T(8,128)(2,1)S(1)} copy(bf16[128,4,512]{2,1,0:T(4,128)(2,1)} %param.14) | data formatting | bytes 1048576 | tf_op args[2]
  1.3 0.7 %collective-permute-start = (bf16[4,8,512]{2,1,0:T(8,128)(2,1)S(1)}, bf16[4,8,512]{2,1,0:T(8,128)(2,1)S(1)}, u32[]{:S(2)}, u32[]{:S(2)}) collective-permute-start(bf16[4,8,512]{2,1,0:T(8,128)(2,1)S(1)} %dynamic-slice_bitcast_fusion.2), channel_id=1, source_target_pairs={{0,1},{1,0},{2,3},{3,2},{4,5},{5,4},{6,7},{7,6},{8,9},{9,8},{10,11... | collective-permute-start | bytes 98312 | tf_op jit(solution)/shard_map/ppermute | solution.py:479
  2.1 0.8 %dynamic-slice_bitcast_fusion = (bf16[3,128,512]{2,1,0:T(8,128)(2,1)}, bf16[3,128,512]{2,1,0:T(8,128)(2,1)S(1)}) fusion(bf16[128,4,512]{2,0,1:T(8,128)(2,1)S(1)} %copy.19, s32[]{:T(128)S(6)} %select_n.33, s32[]{:T(128)S(6)} %select_n.31), kind=kLoop, calls=%fused_computation.1 | loop fusion | bytes 1572872 | tf_op jit(solution)/shard_map/dynamic_slice | solution.py:378
  2.9 3.0 %collective-permute-start.2 = (bf16[3,128,512]{2,1,0:T(8,128)(2,1)}, bf16[3,128,512]{2,1,0:T(8,128)(2,1)S(1)}, u32[]{:S(2)}, u32[]{:S(2)}) collective-permute-start(bf16[3,128,512]{2,1,0:T(8,128)(2,1)} %get-tuple-element.45), channel_id=1, source_target_pairs={{2,4},{4,2},{6,8},{8,6},{10,12},{12,10},{3,5},{5,3},{7,9},{9,7},{1... | collective-permute-start | bytes 1179656 | tf_op jit(solution)/shard_map/ppermute | solution.py:478
  5.9 0.8 %pad_maximum_fusion = bf16[3,136,512]{2,1,0:T(8,128)(2,1)} fusion(bf16[3,8,512]{2,1,0:T(8,128)(2,1)S(1)} %constant_dynamic-slice_fusion.1, bf16[3,128,512]{2,1,0:T(8,128)(2,1)S(1)} %get-tuple-element.46), kind=kLoop, calls=%fused_computation | loop fusion | flops 835584 | bytes 835584 | tf_op jit(solution)/shard_map/concatenate | solution.py:480
  6.7 3.4 %project_away.1 = (bf16[256,512]{1,0:T(8,128)(2,1)}, bf16[256,512]{1,0:T(8,128)(2,1)}) custom-call(s32[1]{0:T(128)} %bitcast.core_ref, bf16[32,2,16,2048]{3,2,1,0:T(8,128)(2,1)} %bitcast.34, bf16[2048,512]{1,0:T(8,128)(2,1)S(1)} %copy-done), custom_call_target="tpu_custom_call" | custom-call | flops 1 | bytes 1 | tf_op jit(solution)/shard_map/project_away/pallas_call | solution.py:358
  10.1 0.4 collective-permute-start.3
  10.5 0.2 collective-permute-start.4
  10.7 1.4 %collective-permute-start.1 = (bf16[3,136,512]{2,1,0:T(8,128)(2,1)}, bf16[3,136,512]{2,1,0:T(8,128)(2,1)S(1)}, u32[]{:S(2)}, u32[]{:S(2)}) collective-permute-start(bf16[3,136,512]{2,1,0:T(8,128)(2,1)} %pad_maximum_fusion), channel_id=1, source_target_pairs={{0,2},{2,0},{4,6},{6,4},{8,10},{10,8},{12,14},{14,12},{1,3},{3,1},... | collective-permute-start | bytes 1253384 | tf_op jit(solution)/shard_map/ppermute | solution.py:483
  12.1 0.1 pad_add_fusion.2.turns_ref
  12.2 2.7 %project_home.1.home = f32[512,512]{1,0:T(8,128)S(1)} custom-call(s32[1]{0:T(128)} %bitcast.core_ref, bf16[32,2,16,2048]{3,2,1,0:T(8,128)(2,1)} %bitcast.35, bf16[2048,512]{1,0:T(8,128)(2,1)S(1)} %copy-done), custom_call_target="tpu_custom_call" | custom-call | flops 1 | bytes 1 | tf_op jit(solution)/shard_map/project_home/pallas_call | solution.py:358
  15.0 1.1 %combine.1 = (bf16[4,32,512]{2,1,0:T(8,128)(2,1)S(1)}, bf16[4,32,512]{2,1,0:T(8,128)(2,1)S(1)}, bf16[4,32,512]{2,1,0:T(8,128)(2,1)S(1)}, bf16[4,32,512]{2,1,0:T(8,128)(2,1)S(1)}) custom-call(s32[4]{0:T(128)S(1)} %pad_add_fusion.2.turns_ref, f32[512,512]{1,0:T(8,128)S(1)} %project_home.1.home, bf16[256,512]{1,0:T(8,128)(2,1)S(1)} %collective-permute-done.3.upper, ...), custom_call_target="tpu_custom_call" | custom-call | flops 1 | bytes 1 | tf_op jit(solution)/shard_map/combine/pallas_call | solution.py:358
  16.1 2.8 %inner_up.1.inner = f32[4,128,512]{2,1,0:T(8,128)S(1)} custom-call(s32[1]{0:T(128)} %bitcast.core_ref, bf16[4,128,512]{2,1,0:T(8,128)(2,1)S(1)} %bitcast.25, bf16[4,8,512]{2,1,0:T(8,128)(2,1)S(1)} %copy-done.3, f32[7,7,512]{2,1,0:T(8,128)S(1)} %copy-done.1, f32[1,512]{1,0:T(1,128)S(1)} %bitcast.27), custom_call_target="tpu_custom_call" | custom-call | flops 1 | bytes 1 | tf_op jit(solution)/shard_map/inner_up/pallas_call | solution.py:358
  18.9 0.7 %collective-permute-start.5 = (bf16[3,8,512]{2,1,0:T(8,128)(2,1)S(1)}, bf16[3,8,512]{2,1,0:T(8,128)(2,1)S(1)}, u32[]{:S(2)}, u32[]{:S(2)}) collective-permute-start(bf16[3,8,512]{2,1,0:T(8,128)(2,1)S(1)} %constant_dynamic-slice_fusion), channel_id=1, source_target_pairs={{0,1},{1,0},{2,3},{3,2},{4,5},{5,4},{6,7},{7,6},{8,9},{9,8},{10,11... | collective-permute-start | bytes 73736 | tf_op jit(solution)/shard_map/ppermute | solution.py:502
  19.6 0.1 pad_add_fusion.1.places_ref
  19.6 2.6 %collective-permute-start.6 = (bf16[4,32,512]{2,1,0:T(8,128)(2,1)S(1)}, bf16[4,32,512]{2,1,0:T(8,128)(2,1)S(1)}, u32[]{:S(2)}, u32[]{:S(2)}) collective-permute-start(bf16[4,32,512]{2,1,0:T(8,128)(2,1)S(1)} %get-tuple-element.28), channel_id=1, source_target_pairs={{0,0},{1,8},{2,2},{3,10},{4,4},{5,12},{6,6},{7,14},{8,1},{9,9},{10... | collective-permute-start | bytes 393224 | tf_op jit(solution)/shard_map/ppermute | solution.py:442
  22.3 1.8 %collective-permute-start.7 = (bf16[4,32,512]{2,1,0:T(8,128)(2,1)S(1)}, bf16[4,32,512]{2,1,0:T(8,128)(2,1)S(1)}, u32[]{:S(2)}, u32[]{:S(2)}) collective-permute-start(bf16[4,32,512]{2,1,0:T(8,128)(2,1)S(1)} %get-tuple-element.35), channel_id=1, source_target_pairs={{0,2},{1,10},{2,4},{3,12},{4,6},{5,14},{6,0},{7,8},{8,3},{9,11},{1... | collective-permute-start | bytes 393224 | tf_op jit(solution)/shard_map/ppermute | solution.py:442
  24.0 1.2 %collective-permute-start.8 = (bf16[4,32,512]{2,1,0:T(8,128)(2,1)S(1)}, bf16[4,32,512]{2,1,0:T(8,128)(2,1)S(1)}, u32[]{:S(2)}, u32[]{:S(2)}) collective-permute-start(bf16[4,32,512]{2,1,0:T(8,128)(2,1)S(1)} %get-tuple-element.36), channel_id=1, source_target_pairs={{0,4},{1,12},{2,6},{3,14},{4,0},{5,8},{6,2},{7,10},{8,5},{9,13},{1... | collective-permute-start | bytes 393224 | tf_op jit(solution)/shard_map/ppermute | solution.py:442
  25.3 0.6 collective-permute-start.9
  25.9 1.9 %side_up.1.inner = f32[4,128,512]{2,1,0:T(8,128)S(1)} custom-call(s32[2]{0:T(128)S(1)} %pad_add_fusion.place_ref, bf16[3,128,512]{2,1,0:T(8,128)(2,1)S(1)} %collective-permute-done.2.side, bf16[3,8,512]{2,1,0:T(8,128)(2,1)S(1)} %collective-permute-done.5.edge, f32[7,7,512]{2,1,0:T(8,128)S(1)} %copy-done.1, f32[4,128,512]{2,1,0:T(8,128)S(1)} %inner_up.1.inner), custom_call_target="tpu_custom_call" | custom-call | flops 1 | bytes 1 | tf_op jit(solution)/shard_map/side_up/pallas_call | solution.py:358
  27.8 0.3 collective-permute-done.1.side
  28.2 5.1 %up.1 = (f32[512,512]{1,0:T(8,128)S(1)}, f32[512,128]{1,0:T(8,128)S(1)}, bf16[512,2048]{1,0:T(8,128)(2,1)S(1)}, bf16[512,2048]{1,0:T(8,128)(2,1)S(1)}) custom-call(s32[2]{0:T(128)S(1)} %pad_add_fusion.place_ref, bf16[3,136,512]{2,1,0:T(8,128)(2,1)S(1)} %collective-permute-done.1.side, f32[7,7,512]{2,1,0:T(8,128)S(1)} %copy-done.1, ...), custom_call_target="tpu_custom_call" | custom-call | flops 4294967296 | bytes 9181184 | tf_op jit(solution)/shard_map/up/pallas_call | solution.py:358
  33.2 1.0 %collective-permute-done.8.rest_2_ = bf16[4,32,512]{2,1,0:T(8,128)(2,1)S(1)} collective-permute-done((bf16[4,32,512]{2,1,0:T(8,128)(2,1)S(1)}, bf16[4,32,512]{2,1,0:T(8,128)(2,1)S(1)}, u32[]{:S(2)}, u32[]{:S(2)}) %collective-permute-start.8) | collective-permute-done | bytes 131104 | tf_op jit(solution)/shard_map/ppermute | solution.py:442
  34.3 5.4 %back.1 = (f32[4,128,512]{2,1,0:T(8,128)S(1)}, bf16[4,128,512]{2,1,0:T(8,128)(2,1)S(1)}, bf16[3,128,512]{2,1,0:T(8,128)(2,1)S(1)}, bf16[3,128,512]{2,1,0:T(8,128...) custom-call(s32[2]{0:T(128)S(1)} %pad_add_fusion.place_ref, ...), custom_call_target="tpu_custom_call" | custom-call | flops 4294967296 | bytes 13195264 | tf_op jit(solution)/shard_map/back/pallas_call | solution.py:358
  39.7 2.6 %collective-permute-start.10 = (bf16[3,128,512]{2,1,0:T(8,128)(2,1)S(1)}, bf16[3,128,512]{2,1,0:T(8,128)(2,1)S(1)}, u32[]{:S(2)}, u32[]{:S(2)}) collective-permute-start(bf16[3,128,512]{2,1,0:T(8,128)(2,1)S(1)} %get-tuple-element.38), channel_id=1, source_target_pairs={{0,2},{2,0},{4,6},{6,4},{8,10},{10,8},{12,14},{14,12},{1,3},{3,1},... | collective-permute-start | bytes 1179656 | tf_op jit(solution)/shard_map/ppermute | solution.py:545
  42.3 3.3 %collective-permute-start.11 = (bf16[3,128,512]{2,1,0:T(8,128)(2,1)S(1)}, bf16[3,128,512]{2,1,0:T(8,128)(2,1)S(1)}, u32[]{:S(2)}, u32[]{:S(2)}) collective-permute-start(bf16[3,128,512]{2,1,0:T(8,128)(2,1)S(1)} %get-tuple-element.39), channel_id=1, source_target_pairs={{2,4},{4,2},{6,8},{8,6},{10,12},{12,10},{3,5},{5,3},{7,9},{9,7},{1... | collective-permute-start | bytes 1179656 | tf_op jit(solution)/shard_map/ppermute | solution.py:546
  45.7 1.4 %collective-permute-start.12 = (bf16[3,8,512]{2,1,0:T(8,128)(2,1)S(1)}, bf16[3,8,512]{2,1,0:T(8,128)(2,1)S(1)}, u32[]{:S(2)}, u32[]{:S(2)}) collective-permute-start(bf16[3,8,512]{2,1,0:T(8,128)(2,1)S(1)} %get-tuple-element.40), channel_id=1, source_target_pairs={{0,3},{1,2},{2,1},{3,0},{4,7},{5,6},{6,5},{7,4},{8,11},{9,10},{10,... | collective-permute-start | bytes 73736 | tf_op jit(solution)/shard_map/ppermute | solution.py:548
  47.1 1.9 %collective-permute-start.13 = (bf16[3,8,512]{2,1,0:T(8,128)(2,1)S(1)}, bf16[3,8,512]{2,1,0:T(8,128)(2,1)S(1)}, u32[]{:S(2)}, u32[]{:S(2)}) collective-permute-start(bf16[3,8,512]{2,1,0:T(8,128)(2,1)S(1)} %get-tuple-element.41), channel_id=1, source_target_pairs={{2,5},{3,4},{4,3},{5,2},{6,9},{7,8},{8,7},{9,6},{10,13},{11,12},{1... | collective-permute-start | bytes 73736 | tf_op jit(solution)/shard_map/ppermute | solution.py:549
  49.0 2.8 %inner_last.1.inner = f32[4,128,512]{2,1,0:T(8,128)S(1)} custom-call(s32[1]{0:T(128)} %bitcast.core_ref, bf16[4,128,512]{2,1,0:T(8,128)(2,1)S(1)} %get-tuple-element.42.middle, bf16[4,8,512]{2,1,0:T(8,128)(2,1)S(1)} %collective-permute-done.14.edge, f32[7,7,512]{2,1,0:T(8,128)S(1)} %copy-done.1, f32[4,128,512]{2,1,0:T(8,128)S(1)} %get-tuple-element.44.base_value), custom_call_target="tpu_custom_call" | custom-call | flops 1073741824 | bytes 2754560 | tf_op jit(solution)/shard_map/inner_last/pallas_call | solution.py:358
  51.8 7.2 %collective-permute-done.12.even_edge = bf16[3,8,512]{2,1,0:T(8,128)(2,1)S(1)} collective-permute-done((bf16[3,8,512]{2,1,0:T(8,128)(2,1)S(1)}, bf16[3,8,512]{2,1,0:T(8,128)(2,1)S(1)}, u32[]{:S(2)}, u32[]{:S(2)}) %collective-permute-start.12) | collective-permute-done | bytes 24608 | tf_op jit(solution)/shard_map/ppermute | solution.py:548
  59.0 0.8 %collective-permute-done.10.even = bf16[3,128,512]{2,1,0:T(8,128)(2,1)S(1)} collective-permute-done((bf16[3,128,512]{2,1,0:T(8,128)(2,1)S(1)}, bf16[3,128,512]{2,1,0:T(8,128)(2,1)S(1)}, u32[]{:S(2)}, u32[]{:S(2)}) %collective-permute-start.10) | collective-permute-done | bytes 393248 | tf_op jit(solution)/shard_map/ppermute | solution.py:545
  59.8 4.0 %last.1 = f32[128,4,512]{2,1,0:T(4,128)} custom-call(s32[2]{0:T(128)S(1)} %pad_add_fusion.place_ref, bf16[3,128,512]{2,1,0:T(8,128)(2,1)S(1)} %collective-permute-done.10.even, bf16[3,128,512]{2,1,0:T(8,128)(2,1)S(1)} %collective-permute-done.11.odd, bf16[3,8,512]{2,1,0:T(8,128)(2,1)S(1)} %collective-permute-done.12.even_edge, ...), custom_call_target="tpu_custom_call" | custom-call | flops 1 | bytes 1 | tf_op jit(solution)/shard_map/last/pallas_call | solution.py:358
  (40 shorter events, 0.3 us)
Async XLA Ops:
  0.0 6.7 %copy-start = (bf16[2048,512]{1,0:T(8,128)(2,1)S(1)}, bf16[2048,512]{1,0:T(8,128)(2,1)}, u32[]{:S(2)}) copy-start(bf16[2048,512]{1,0:T(8,128)(2,1)} %weight.1) | copy-start | bytes 6291460
  1.3 4.6 %collective-permute-start = (bf16[4,8,512]{2,1,0:T(8,128)(2,1)S(1)}, bf16[4,8,512]{2,1,0:T(8,128)(2,1)S(1)}, u32[]{:S(2)}, u32[]{:S(2)}) collective-permute-start(bf16[4,8,512]{2,1,0:T(8,128)(2,1)S(1)} %dynamic-slice_bitcast_fusion.2), channel_id=1, source_target_pairs={{0,1},{1,0},{2,3},{3,2},{4,5},{5,4},{6,7},{7,6},{8,9},{9,8},{10,11... | collective-permute-start | bytes 98312 | tf_op jit(solution)/shard_map/ppermute | solution.py:479
  2.9 16.0 %collective-permute-start.2 = (bf16[3,128,512]{2,1,0:T(8,128)(2,1)}, bf16[3,128,512]{2,1,0:T(8,128)(2,1)S(1)}, u32[]{:S(2)}, u32[]{:S(2)}) collective-permute-start(bf16[3,128,512]{2,1,0:T(8,128)(2,1)} %get-tuple-element.45), channel_id=1, source_target_pairs={{2,4},{4,2},{6,8},{8,6},{10,12},{12,10},{3,5},{5,3},{7,9},{9,7},{1... | collective-permute-start | bytes 1179656 | tf_op jit(solution)/shard_map/ppermute | solution.py:478
  5.9 4.2 %copy-start.2 = (bf16[4,8,512]{2,1,0:T(8,128)(2,1)}, bf16[4,8,512]{2,1,0:T(8,128)(2,1)S(1)}, u32[]{:S(2)}) copy-start(bf16[4,8,512]{2,1,0:T(8,128)(2,1)S(1)} %collective-permute-done.edge) | copy-start | bytes 98308
  10.1 4.8 %collective-permute-start.3 = (bf16[256,512]{1,0:T(8,128)(2,1)}, bf16[256,512]{1,0:T(8,128)(2,1)S(1)}, u32[]{:S(2)}, u32[]{:S(2)}) collective-permute-start(bf16[256,512]{1,0:T(8,128)(2,1)} %get-tuple-element.26), channel_id=1, source_target_pairs={{0,1},{1,0},{2,3},{3,2},{4,5},{5,4},{6,7},{7,6},{8,9},{9,8},{10,11... | collective-permute-start | bytes 786440 | tf_op jit(solution)/shard_map/ppermute | solution.py:417
  10.5 4.5 %collective-permute-start.4 = (bf16[256,512]{1,0:T(8,128)(2,1)}, bf16[256,512]{1,0:T(8,128)(2,1)S(1)}, u32[]{:S(2)}, u32[]{:S(2)}) collective-permute-start(bf16[256,512]{1,0:T(8,128)(2,1)} %get-tuple-element.27), channel_id=1, source_target_pairs={{0,1},{1,0},{2,3},{3,2},{4,5},{5,4},{6,7},{7,6},{8,9},{9,8},{10,11... | collective-permute-start | bytes 786440 | tf_op jit(solution)/shard_map/ppermute | solution.py:417
  10.7 17.4 %collective-permute-start.1 = (bf16[3,136,512]{2,1,0:T(8,128)(2,1)}, bf16[3,136,512]{2,1,0:T(8,128)(2,1)S(1)}, u32[]{:S(2)}, u32[]{:S(2)}) collective-permute-start(bf16[3,136,512]{2,1,0:T(8,128)(2,1)} %pad_maximum_fusion), channel_id=1, source_target_pairs={{0,2},{2,0},{4,6},{6,4},{8,10},{10,8},{12,14},{14,12},{1,3},{3,1},... | collective-permute-start | bytes 1253384 | tf_op jit(solution)/shard_map/ppermute | solution.py:483
  12.2 3.8 %copy-start.1 = (f32[7,7,512]{2,1,0:T(8,128)S(1)}, f32[7,7,512]{2,1,0:T(8,128)}, u32[]{:S(2)}) copy-start(f32[7,7,512]{2,1,0:T(8,128)} %kernel.9) | copy-start | bytes 301060
  12.2 3.8 %copy-start.3 = (bf16[4,8,512]{2,1,0:T(8,128)(2,1)S(1)}, bf16[4,8,512]{2,1,0:T(8,128)(2,1)}, u32[]{:S(2)}) copy-start(bf16[4,8,512]{2,1,0:T(8,128)(2,1)} %copy-done.2) | copy-start | bytes 98308
  12.2 3.8 %copy-start.4 = (f32[512]{0:T(512)S(1)}, f32[512]{0:T(512)}, u32[]{:S(2)}) copy-start(f32[512]{0:T(512)} %param.16) | copy-start | bytes 6148
  16.1 12.0 %copy-start.7 = (f32[2048]{0:T(1024)S(1)}, f32[2048]{0:T(1024)}, u32[]{:S(2)}) copy-start(f32[2048]{0:T(1024)} %param.20) | copy-start | bytes 24580
  16.1 12.0 %copy-start.8 = (f32[512]{0:T(512)S(1)}, f32[512]{0:T(512)}, u32[]{:S(2)}) copy-start(f32[512]{0:T(512)} %param.18) | copy-start | bytes 6148
  16.1 12.0 %copy-start.9 = (f32[512]{0:T(512)S(1)}, f32[512]{0:T(512)}, u32[]{:S(2)}) copy-start(f32[512]{0:T(512)} %param.17) | copy-start | bytes 6148
  18.9 6.3 %collective-permute-start.5 = (bf16[3,8,512]{2,1,0:T(8,128)(2,1)S(1)}, bf16[3,8,512]{2,1,0:T(8,128)(2,1)S(1)}, u32[]{:S(2)}, u32[]{:S(2)}) collective-permute-start(bf16[3,8,512]{2,1,0:T(8,128)(2,1)S(1)} %constant_dynamic-slice_fusion), channel_id=1, source_target_pairs={{0,1},{1,0},{2,3},{3,2},{4,5},{5,4},{6,7},{7,6},{8,9},{9,8},{10,11... | collective-permute-start | bytes 73736 | tf_op jit(solution)/shard_map/ppermute | solution.py:502
  19.6 14.6 %collective-permute-start.6 = (bf16[4,32,512]{2,1,0:T(8,128)(2,1)S(1)}, bf16[4,32,512]{2,1,0:T(8,128)(2,1)S(1)}, u32[]{:S(2)}, u32[]{:S(2)}) collective-permute-start(bf16[4,32,512]{2,1,0:T(8,128)(2,1)S(1)} %get-tuple-element.28), channel_id=1, source_target_pairs={{0,0},{1,8},{2,2},{3,10},{4,4},{5,12},{6,6},{7,14},{8,1},{9,9},{10... | collective-permute-start | bytes 393224 | tf_op jit(solution)/shard_map/ppermute | solution.py:442
  22.3 11.0 %collective-permute-start.7 = (bf16[4,32,512]{2,1,0:T(8,128)(2,1)S(1)}, bf16[4,32,512]{2,1,0:T(8,128)(2,1)S(1)}, u32[]{:S(2)}, u32[]{:S(2)}) collective-permute-start(bf16[4,32,512]{2,1,0:T(8,128)(2,1)S(1)} %get-tuple-element.35), channel_id=1, source_target_pairs={{0,2},{1,10},{2,4},{3,12},{4,6},{5,14},{6,0},{7,8},{8,3},{9,11},{1... | collective-permute-start | bytes 393224 | tf_op jit(solution)/shard_map/ppermute | solution.py:442
  24.0 10.2 %collective-permute-start.8 = (bf16[4,32,512]{2,1,0:T(8,128)(2,1)S(1)}, bf16[4,32,512]{2,1,0:T(8,128)(2,1)S(1)}, u32[]{:S(2)}, u32[]{:S(2)}) collective-permute-start(bf16[4,32,512]{2,1,0:T(8,128)(2,1)S(1)} %get-tuple-element.36), channel_id=1, source_target_pairs={{0,4},{1,12},{2,6},{3,14},{4,0},{5,8},{6,2},{7,10},{8,5},{9,13},{1... | collective-permute-start | bytes 393224 | tf_op jit(solution)/shard_map/ppermute | solution.py:442
  25.3 9.0 %collective-permute-start.9 = (bf16[4,32,512]{2,1,0:T(8,128)(2,1)S(1)}, bf16[4,32,512]{2,1,0:T(8,128)(2,1)S(1)}, u32[]{:S(2)}, u32[]{:S(2)}) collective-permute-start(bf16[4,32,512]{2,1,0:T(8,128)(2,1)S(1)} %get-tuple-element.37), channel_id=1, source_target_pairs={{0,6},{1,14},{2,0},{3,8},{4,2},{5,10},{6,4},{7,12},{8,7},{9,15},{1... | collective-permute-start | bytes 393224 | tf_op jit(solution)/shard_map/ppermute | solution.py:442
  28.1 6.1 %copy-start.5 = (bf16[512,2048]{1,0:T(8,128)(2,1)S(1)}, bf16[512,2048]{1,0:T(8,128)(2,1)}, u32[]{:S(2)}) copy-start(bf16[512,2048]{1,0:T(8,128)(2,1)} %w_in.1) | copy-start | bytes 6291460
  28.1 6.1 %copy-start.6 = (bf16[2048,512]{1,0:T(8,128)(2,1)S(1)}, bf16[2048,512]{1,0:T(8,128)(2,1)}, u32[]{:S(2)}) copy-start(bf16[2048,512]{1,0:T(8,128)(2,1)} %w_out.1) | copy-start | bytes 6291460
  28.1 6.1 %copy-start.10 = (f32[512]{0:T(512)S(1)}, f32[512]{0:T(512)}, u32[]{:S(2)}) copy-start(f32[512]{0:T(512)} %param.22) | copy-start | bytes 6148
  28.1 6.1 %copy-start.11 = (f32[512]{0:T(512)S(1)}, f32[512]{0:T(512)}, u32[]{:S(2)}) copy-start(f32[512]{0:T(512)} %param.23) | copy-start | bytes 6148
  39.7 20.2 %collective-permute-start.10 = (bf16[3,128,512]{2,1,0:T(8,128)(2,1)S(1)}, bf16[3,128,512]{2,1,0:T(8,128)(2,1)S(1)}, u32[]{:S(2)}, u32[]{:S(2)}) collective-permute-start(bf16[3,128,512]{2,1,0:T(8,128)(2,1)S(1)} %get-tuple-element.38), channel_id=1, source_target_pairs={{0,2},{2,0},{4,6},{6,4},{8,10},{10,8},{12,14},{14,12},{1,3},{3,1},... | collective-permute-start | bytes 1179656 | tf_op jit(solution)/shard_map/ppermute | solution.py:545
  42.3 17.5 %collective-permute-start.11 = (bf16[3,128,512]{2,1,0:T(8,128)(2,1)S(1)}, bf16[3,128,512]{2,1,0:T(8,128)(2,1)S(1)}, u32[]{:S(2)}, u32[]{:S(2)}) collective-permute-start(bf16[3,128,512]{2,1,0:T(8,128)(2,1)S(1)} %get-tuple-element.39), channel_id=1, source_target_pairs={{2,4},{4,2},{6,8},{8,6},{10,12},{12,10},{3,5},{5,3},{7,9},{9,7},{1... | collective-permute-start | bytes 1179656 | tf_op jit(solution)/shard_map/ppermute | solution.py:546
  45.6 3.4 %collective-permute-start.14 = (bf16[4,8,512]{2,1,0:T(8,128)(2,1)S(1)}, bf16[4,8,512]{2,1,0:T(8,128)(2,1)S(1)}, u32[]{:S(2)}, u32[]{:S(2)}) collective-permute-start(bf16[4,8,512]{2,1,0:T(8,128)(2,1)S(1)} %get-tuple-element.43), channel_id=1, source_target_pairs={{0,1},{1,0},{2,3},{3,2},{4,5},{5,4},{6,7},{7,6},{8,9},{9,8},{10,11... | collective-permute-start | bytes 98312 | tf_op jit(solution)/shard_map/ppermute | solution.py:547
  45.7 13.3 %collective-permute-start.12 = (bf16[3,8,512]{2,1,0:T(8,128)(2,1)S(1)}, bf16[3,8,512]{2,1,0:T(8,128)(2,1)S(1)}, u32[]{:S(2)}, u32[]{:S(2)}) collective-permute-start(bf16[3,8,512]{2,1,0:T(8,128)(2,1)S(1)} %get-tuple-element.40), channel_id=1, source_target_pairs={{0,3},{1,2},{2,1},{3,0},{4,7},{5,6},{6,5},{7,4},{8,11},{9,10},{10,... | collective-permute-start | bytes 73736 | tf_op jit(solution)/shard_map/ppermute | solution.py:548
  47.1 11.9 %collective-permute-start.13 = (bf16[3,8,512]{2,1,0:T(8,128)(2,1)S(1)}, bf16[3,8,512]{2,1,0:T(8,128)(2,1)S(1)}, u32[]{:S(2)}, u32[]{:S(2)}) collective-permute-start(bf16[3,8,512]{2,1,0:T(8,128)(2,1)S(1)} %get-tuple-element.41), channel_id=1, source_target_pairs={{2,5},{3,4},{4,3},{5,2},{6,9},{7,8},{8,7},{9,6},{10,13},{11,12},{1... | collective-permute-start | bytes 73736 | tf_op jit(solution)/shard_map/ppermute | solution.py:549

commit v9 on v8

--- a/solution.py
+++ b/solution.py
@@ -197,7 +197,7 @@
 
     start = edge.shape[1] - EDGE
     side_conv(
-        flip, place_ref[0], place_ref[1] == 0, side, (edge, start), kernel, inner, store, padded, taps
+        flip, place_ref[0], place_ref[1] == 1, side, (edge, start), kernel, inner, store, padded, taps
     )
 
 
@@ -215,7 +215,7 @@
         summed[u, aligned(base, SUBLANES), aligned(tile * LANES, LANES)] = value
 
     side_conv(
-        False, place_ref[0], place_ref[1] == 1, side, (side, tile_v), kernel, inner, store, padded, taps
+        False, place_ref[0], place_ref[1] == 0, side, (side, tile_v), kernel, inner, store, padded, taps
     )
 
     def norm_step(index):
@@ -474,13 +474,13 @@
     f32, bf16 = jnp.float32, jnp.bfloat16
     rows = tile_u * tile_v
     middle = student.transpose(1, 0, 2)
-    first_block = facing(middle, row, True)
-    first_side = lax.ppermute(first_block, "row", row_pairs(True))
+    first_block = facing(middle, row, False)
+    first_side = lax.ppermute(first_block, "row", row_pairs(False))
     edge = lax.ppermute(edge_lines(middle, core), "col", SWAP)
     second_block = jnp.concatenate(
-        [facing(middle, row, False), facing(edge, row, False)], axis=1
-    )
-    second_side = lax.ppermute(second_block, "row", row_pairs(False))
+        [facing(middle, row, True), facing(edge, row, True)], axis=1
+    )
+    second_side = lax.ppermute(second_block, "row", row_pairs(True))
     held, *_ = lax.optimization_barrier((proj_weight, first_block, second_block))
     targets, places, block = find_target(teacher, held, core, row, tile_u, tile_v)
     later, _ = lax.optimization_barrier((dw_bias, block))

time: 64.4 us -> 65.8 us (1.022)
  starting transfers between devices: 21.9 us -> 26.4 us
  waiting for transfers between devices: 9.33 us -> 5.81 us
    ppermute x1, starting transfers between devices: 0.67 us -> 4.99 us  [on_device(): first_edge = lax.ppermute(edge_lines(arrived, core), 'col', SWAP)]
    ppermute x1, waiting for transfers between devices: 7.2 us -> 4.74 us  [on_device(): lax.ppermute(even_edge, ('row', 'col'), across(row_pairs(False)))]
    ppermute x4, starting transfers between devices: 6.23 us -> 7.56 us  [find_target(): pieces.append(lax.ppermute(blocks[turn], ('row', 'col'), pairs))]
    ppermute x2, starting transfers between devices: 4.37 us -> 3.25 us  [the longest x1 2.04 us: on_device(): second_side = lax.ppermute(second_block, 'row', row_pairs(True))]
    ppermute x1, starting transfers between devices: 1.4 us -> 0.58 us  [on_device(): lax.ppermute(even_edge, ('row', 'col'), across(row_pairs(False)))]
    ppermute x1, starting transfers between devices: 3.28 us -> 3.96 us  [on_device(): odd = lax.ppermute(odd, 'row', row_pairs(True))]
  transfers between devices with their start and end apart: 15 -> 15, of which waited for: 4 -> 4; matrix products, arithmetic and copies ran while one was open for 3% -> 3% of each run, Pallas kernels for 31% -> 30%
where the time goes in v9:
time: 65.8 us; the launch traced here: 64.8 us
  Pallas kernels  29.1 us (44%)
  starting transfers between devices  26.4 us (40%)
  waiting for transfers between devices  5.81 us (9%)
  local copies, waits for them, and re-layouts  2.21 us (3%)
  other arithmetic  1.01 us (2%)
    pallas_call x9, Pallas kernels, call(): pl.pallas_call(kernel, out_shape=tuple(outs), in_specs=[smem] * len(scala...  29.1 us
    ppermute x4, starting transfers between devices, find_target(): pieces.append(lax.ppermute(blocks[turn], ('row', 'col'), pairs))  7.56 us
    ppermute x1, starting transfers between devices, on_device(): first_edge = lax.ppermute(edge_lines(arrived, core), 'col', SWAP)  4.99 us
    ppermute x1, waiting for transfers between devices, on_device(): lax.ppermute(even_edge, ('row', 'col'), across(row_pairs(False)))  4.74 us
    ppermute x1, starting transfers between devices, on_device(): odd = lax.ppermute(odd, 'row', row_pairs(True))  3.96 us
    ppermute x1, starting transfers between devices, on_device(): even = lax.ppermute(even, 'row', row_pairs(False))  2.64 us
    ppermute x1, starting transfers between devices, on_device(): second_side = lax.ppermute(second_block, 'row', row_pairs(True))  2.04 us
    ppermute x1, starting transfers between devices, on_device(): odd_edge = lax.ppermute(odd_edge, ('row', 'col'), across(row_pairs(True)))  2.01 us
  transfers between devices with their start and end apart: 15, of which 4 were waited for; matrix products, arithmetic and copies ran while one was open for 3% of the time, Pallas kernels for 30%

profile of v9, /device:TPU:13, one launch (start us, length us, event | category | flops | bytes accessed | tf_op | source)
XLA Modules:
  0.0 64.8 jit_solution(14860002617794737678)
XLA Ops:
  0.0 1.3 %copy.19 = bf16[128,4,512]{2,0,1:T(8,128)(2,1)S(1)} copy(bf16[128,4,512]{2,1,0:T(4,128)(2,1)} %param.14) | data formatting | bytes 1048576 | tf_op args[2]
  1.3 0.7 %collective-permute-start = (bf16[4,8,512]{2,1,0:T(8,128)(2,1)S(1)}, bf16[4,8,512]{2,1,0:T(8,128)(2,1)S(1)}, u32[]{:S(2)}, u32[]{:S(2)}) collective-permute-start(bf16[4,8,512]{2,1,0:T(8,128)(2,1)S(1)} %dynamic-slice_bitcast_fusion.2), channel_id=1, source_target_pairs={{0,1},{1,0},{2,3},{3,2},{4,5},{5,4},{6,7},{7,6},{8,9},{9,8},{10,11... | collective-permute-start | bytes 98312 | tf_op jit(solution)/shard_map/ppermute | solution.py:479
  2.1 0.8 %dynamic-slice_bitcast_fusion = (bf16[3,128,512]{2,1,0:T(8,128)(2,1)}, bf16[3,128,512]{2,1,0:T(8,128)(2,1)S(1)}) fusion(bf16[128,4,512]{2,0,1:T(8,128)(2,1)S(1)} %copy.19, s32[]{:T(128)S(6)} %select_n.33, s32[]{:T(128)S(6)} %select_n.31), kind=kLoop, calls=%fused_computation.1 | loop fusion | bytes 1572872 | tf_op jit(solution)/shard_map/dynamic_slice | solution.py:378
  2.9 1.2 %collective-permute-start.2 = (bf16[3,128,512]{2,1,0:T(8,128)(2,1)}, bf16[3,128,512]{2,1,0:T(8,128)(2,1)S(1)}, u32[]{:S(2)}, u32[]{:S(2)}) collective-permute-start(bf16[3,128,512]{2,1,0:T(8,128)(2,1)} %get-tuple-element.45), channel_id=1, source_target_pairs={{0,2},{2,0},{4,6},{6,4},{8,10},{10,8},{12,14},{14,12},{1,3},{3,1},... | collective-permute-start | bytes 1179656 | tf_op jit(solution)/shard_map/ppermute | solution.py:478
  4.1 0.8 %pad_maximum_fusion = bf16[3,136,512]{2,1,0:T(8,128)(2,1)} fusion(bf16[3,8,512]{2,1,0:T(8,128)(2,1)S(1)} %constant_dynamic-slice_fusion.1, bf16[3,128,512]{2,1,0:T(8,128)(2,1)S(1)} %get-tuple-element.46), kind=kLoop, calls=%fused_computation | loop fusion | flops 835584 | bytes 835584 | tf_op jit(solution)/shard_map/concatenate | solution.py:480
  4.9 3.4 %project_away.1 = (bf16[256,512]{1,0:T(8,128)(2,1)}, bf16[256,512]{1,0:T(8,128)(2,1)}) custom-call(s32[1]{0:T(128)} %bitcast.core_ref, bf16[32,2,16,2048]{3,2,1,0:T(8,128)(2,1)} %bitcast.34, bf16[2048,512]{1,0:T(8,128)(2,1)S(1)} %copy-done), custom_call_target="tpu_custom_call" | custom-call | flops 1 | bytes 1 | tf_op jit(solution)/shard_map/project_away/pallas_call | solution.py:358
  8.3 0.4 collective-permute-start.3
  8.7 0.2 collective-permute-start.4
  8.9 2.0 %collective-permute-start.1 = (bf16[3,136,512]{2,1,0:T(8,128)(2,1)}, bf16[3,136,512]{2,1,0:T(8,128)(2,1)S(1)}, u32[]{:S(2)}, u32[]{:S(2)}) collective-permute-start(bf16[3,136,512]{2,1,0:T(8,128)(2,1)} %pad_maximum_fusion), channel_id=1, source_target_pairs={{2,4},{4,2},{6,8},{8,6},{10,12},{12,10},{3,5},{5,3},{7,9},{9,7},{1... | collective-permute-start | bytes 1253384 | tf_op jit(solution)/shard_map/ppermute | solution.py:483
  10.9 0.1 pad_add_fusion.place_ref
  11.0 0.1 pad_add_fusion.2.turns_ref
  11.1 2.7 %project_home.1.home = f32[512,512]{1,0:T(8,128)S(1)} custom-call(s32[1]{0:T(128)} %bitcast.core_ref, bf16[32,2,16,2048]{3,2,1,0:T(8,128)(2,1)} %bitcast.35, bf16[2048,512]{1,0:T(8,128)(2,1)S(1)} %copy-done), custom_call_target="tpu_custom_call" | custom-call | flops 1 | bytes 1 | tf_op jit(solution)/shard_map/project_home/pallas_call | solution.py:358
  13.8 1.1 %combine.1 = (bf16[4,32,512]{2,1,0:T(8,128)(2,1)S(1)}, bf16[4,32,512]{2,1,0:T(8,128)(2,1)S(1)}, bf16[4,32,512]{2,1,0:T(8,128)(2,1)S(1)}, bf16[4,32,512]{2,1,0:T(8,128)(2,1)S(1)}) custom-call(s32[4]{0:T(128)S(1)} %pad_add_fusion.2.turns_ref, f32[512,512]{1,0:T(8,128)S(1)} %project_home.1.home, bf16[256,512]{1,0:T(8,128)(2,1)S(1)} %collective-permute-done.3.upper, ...), custom_call_target="tpu_custom_call" | custom-call | flops 1 | bytes 1 | tf_op jit(solution)/shard_map/combine/pallas_call | solution.py:358
  15.0 2.8 %inner_up.1.inner = f32[4,128,512]{2,1,0:T(8,128)S(1)} custom-call(s32[1]{0:T(128)} %bitcast.core_ref, bf16[4,128,512]{2,1,0:T(8,128)(2,1)S(1)} %bitcast.25, bf16[4,8,512]{2,1,0:T(8,128)(2,1)S(1)} %copy-done.3, f32[7,7,512]{2,1,0:T(8,128)S(1)} %copy-done.1, f32[1,512]{1,0:T(1,128)S(1)} %bitcast.27), custom_call_target="tpu_custom_call" | custom-call | flops 1 | bytes 1 | tf_op jit(solution)/shard_map/inner_up/pallas_call | solution.py:358
  17.7 5.0 %collective-permute-start.5 = (bf16[3,8,512]{2,1,0:T(8,128)(2,1)S(1)}, bf16[3,8,512]{2,1,0:T(8,128)(2,1)S(1)}, u32[]{:S(2)}, u32[]{:S(2)}) collective-permute-start(bf16[3,8,512]{2,1,0:T(8,128)(2,1)S(1)} %constant_dynamic-slice_fusion), channel_id=1, source_target_pairs={{0,1},{1,0},{2,3},{3,2},{4,5},{5,4},{6,7},{7,6},{8,9},{9,8},{10,11... | collective-permute-start | bytes 73736 | tf_op jit(solution)/shard_map/ppermute | solution.py:502
  22.7 0.1 pad_add_fusion.1.places_ref
  22.8 1.9 %collective-permute-start.6 = (bf16[4,32,512]{2,1,0:T(8,128)(2,1)S(1)}, bf16[4,32,512]{2,1,0:T(8,128)(2,1)S(1)}, u32[]{:S(2)}, u32[]{:S(2)}) collective-permute-start(bf16[4,32,512]{2,1,0:T(8,128)(2,1)S(1)} %get-tuple-element.28), channel_id=1, source_target_pairs={{0,0},{1,8},{2,2},{3,10},{4,4},{5,12},{6,6},{7,14},{8,1},{9,9},{10... | collective-permute-start | bytes 393224 | tf_op jit(solution)/shard_map/ppermute | solution.py:442
  24.7 4.5 %collective-permute-start.7 = (bf16[4,32,512]{2,1,0:T(8,128)(2,1)S(1)}, bf16[4,32,512]{2,1,0:T(8,128)(2,1)S(1)}, u32[]{:S(2)}, u32[]{:S(2)}) collective-permute-start(bf16[4,32,512]{2,1,0:T(8,128)(2,1)S(1)} %get-tuple-element.35), channel_id=1, source_target_pairs={{0,2},{1,10},{2,4},{3,12},{4,6},{5,14},{6,0},{7,8},{8,3},{9,11},{1... | collective-permute-start | bytes 393224 | tf_op jit(solution)/shard_map/ppermute | solution.py:442
  29.2 1.2 %collective-permute-start.8 = (bf16[4,32,512]{2,1,0:T(8,128)(2,1)S(1)}, bf16[4,32,512]{2,1,0:T(8,128)(2,1)S(1)}, u32[]{:S(2)}, u32[]{:S(2)}) collective-permute-start(bf16[4,32,512]{2,1,0:T(8,128)(2,1)S(1)} %get-tuple-element.36), channel_id=1, source_target_pairs={{0,4},{1,12},{2,6},{3,14},{4,0},{5,8},{6,2},{7,10},{8,5},{9,13},{1... | collective-permute-start | bytes 393224 | tf_op jit(solution)/shard_map/ppermute | solution.py:442
  30.4 1.9 %side_up.1.inner = f32[4,128,512]{2,1,0:T(8,128)S(1)} custom-call(s32[2]{0:T(128)S(1)} %pad_add_fusion.place_ref, bf16[3,128,512]{2,1,0:T(8,128)(2,1)S(1)} %collective-permute-done.2.side, bf16[3,8,512]{2,1,0:T(8,128)(2,1)S(1)} %collective-permute-done.5.edge, f32[7,7,512]{2,1,0:T(8,128)S(1)} %copy-done.1, f32[4,128,512]{2,1,0:T(8,128)S(1)} %inner_up.1.inner), custom_call_target="tpu_custom_call" | custom-call | flops 1 | bytes 1 | tf_op jit(solution)/shard_map/side_up/pallas_call | solution.py:358
  32.4 5.1 %up.1 = (f32[512,512]{1,0:T(8,128)S(1)}, f32[512,128]{1,0:T(8,128)S(1)}, bf16[512,2048]{1,0:T(8,128)(2,1)S(1)}, bf16[512,2048]{1,0:T(8,128)(2,1)S(1)}) custom-call(s32[2]{0:T(128)S(1)} %pad_add_fusion.place_ref, bf16[3,136,512]{2,1,0:T(8,128)(2,1)S(1)} %collective-permute-done.1.side, f32[7,7,512]{2,1,0:T(8,128)S(1)} %copy-done.1, ...), custom_call_target="tpu_custom_call" | custom-call | flops 4294967296 | bytes 9181184 | tf_op jit(solution)/shard_map/up/pallas_call | solution.py:358
  37.5 0.4 collective-permute-done.7.rest_1_
  37.8 0.5 collective-permute-done.8.rest_2_
  38.4 5.4 %back.1 = (f32[4,128,512]{2,1,0:T(8,128)S(1)}, bf16[4,128,512]{2,1,0:T(8,128)(2,1)S(1)}, bf16[3,128,512]{2,1,0:T(8,128)(2,1)S(1)}, bf16[3,128,512]{2,1,0:T(8,128...) custom-call(s32[2]{0:T(128)S(1)} %pad_add_fusion.place_ref, ...), custom_call_target="tpu_custom_call" | custom-call | flops 4294967296 | bytes 13195264 | tf_op jit(solution)/shard_map/back/pallas_call | solution.py:358
  43.8 2.6 %collective-permute-start.10 = (bf16[3,128,512]{2,1,0:T(8,128)(2,1)S(1)}, bf16[3,128,512]{2,1,0:T(8,128)(2,1)S(1)}, u32[]{:S(2)}, u32[]{:S(2)}) collective-permute-start(bf16[3,128,512]{2,1,0:T(8,128)(2,1)S(1)} %get-tuple-element.38), channel_id=1, source_target_pairs={{0,2},{2,0},{4,6},{6,4},{8,10},{10,8},{12,14},{14,12},{1,3},{3,1},... | collective-permute-start | bytes 1179656 | tf_op jit(solution)/shard_map/ppermute | solution.py:545
  46.4 4.0 %collective-permute-start.11 = (bf16[3,128,512]{2,1,0:T(8,128)(2,1)S(1)}, bf16[3,128,512]{2,1,0:T(8,128)(2,1)S(1)}, u32[]{:S(2)}, u32[]{:S(2)}) collective-permute-start(bf16[3,128,512]{2,1,0:T(8,128)(2,1)S(1)} %get-tuple-element.39), channel_id=1, source_target_pairs={{2,4},{4,2},{6,8},{8,6},{10,12},{12,10},{3,5},{5,3},{7,9},{9,7},{1... | collective-permute-start | bytes 1179656 | tf_op jit(solution)/shard_map/ppermute | solution.py:546
  50.5 0.6 collective-permute-start.12
  51.0 2.0 %collective-permute-start.13 = (bf16[3,8,512]{2,1,0:T(8,128)(2,1)S(1)}, bf16[3,8,512]{2,1,0:T(8,128)(2,1)S(1)}, u32[]{:S(2)}, u32[]{:S(2)}) collective-permute-start(bf16[3,8,512]{2,1,0:T(8,128)(2,1)S(1)} %get-tuple-element.41), channel_id=1, source_target_pairs={{2,5},{3,4},{4,3},{5,2},{6,9},{7,8},{8,7},{9,6},{10,13},{11,12},{1... | collective-permute-start | bytes 73736 | tf_op jit(solution)/shard_map/ppermute | solution.py:549
  53.1 2.8 %inner_last.1.inner = f32[4,128,512]{2,1,0:T(8,128)S(1)} custom-call(s32[1]{0:T(128)} %bitcast.core_ref, bf16[4,128,512]{2,1,0:T(8,128)(2,1)S(1)} %get-tuple-element.42.middle, bf16[4,8,512]{2,1,0:T(8,128)(2,1)S(1)} %collective-permute-done.14.edge, f32[7,7,512]{2,1,0:T(8,128)S(1)} %copy-done.1, f32[4,128,512]{2,1,0:T(8,128)S(1)} %get-tuple-element.44.base_value), custom_call_target="tpu_custom_call" | custom-call | flops 1073741824 | bytes 2754560 | tf_op jit(solution)/shard_map/inner_last/pallas_call | solution.py:358
  55.9 4.7 %collective-permute-done.12.even_edge = bf16[3,8,512]{2,1,0:T(8,128)(2,1)S(1)} collective-permute-done((bf16[3,8,512]{2,1,0:T(8,128)(2,1)S(1)}, bf16[3,8,512]{2,1,0:T(8,128)(2,1)S(1)}, u32[]{:S(2)}, u32[]{:S(2)}) %collective-permute-start.12) | collective-permute-done | bytes 24608 | tf_op jit(solution)/shard_map/ppermute | solution.py:548
  60.6 0.2 collective-permute-done.10.even
  60.8 4.0 %last.1 = f32[128,4,512]{2,1,0:T(4,128)} custom-call(s32[2]{0:T(128)S(1)} %pad_add_fusion.place_ref, bf16[3,128,512]{2,1,0:T(8,128)(2,1)S(1)} %collective-permute-done.10.even, bf16[3,128,512]{2,1,0:T(8,128)(2,1)S(1)} %collective-permute-done.11.odd, bf16[3,8,512]{2,1,0:T(8,128)(2,1)S(1)} %collective-permute-done.12.even_edge, ...), custom_call_target="tpu_custom_call" | custom-call | flops 1 | bytes 1 | tf_op jit(solution)/shard_map/last/pallas_call | solution.py:358
  (40 shorter events, 0.2 us)
Async XLA Ops:
  0.0 4.9 %copy-start = (bf16[2048,512]{1,0:T(8,128)(2,1)S(1)}, bf16[2048,512]{1,0:T(8,128)(2,1)}, u32[]{:S(2)}) copy-start(bf16[2048,512]{1,0:T(8,128)(2,1)} %weight.1) | copy-start | bytes 6291460
  1.3 2.8 %collective-permute-start = (bf16[4,8,512]{2,1,0:T(8,128)(2,1)S(1)}, bf16[4,8,512]{2,1,0:T(8,128)(2,1)S(1)}, u32[]{:S(2)}, u32[]{:S(2)}) collective-permute-start(bf16[4,8,512]{2,1,0:T(8,128)(2,1)S(1)} %dynamic-slice_bitcast_fusion.2), channel_id=1, source_target_pairs={{0,1},{1,0},{2,3},{3,2},{4,5},{5,4},{6,7},{7,6},{8,9},{9,8},{10,11... | collective-permute-start | bytes 98312 | tf_op jit(solution)/shard_map/ppermute | solution.py:479
  2.9 14.8 %collective-permute-start.2 = (bf16[3,128,512]{2,1,0:T(8,128)(2,1)}, bf16[3,128,512]{2,1,0:T(8,128)(2,1)S(1)}, u32[]{:S(2)}, u32[]{:S(2)}) collective-permute-start(bf16[3,128,512]{2,1,0:T(8,128)(2,1)} %get-tuple-element.45), channel_id=1, source_target_pairs={{0,2},{2,0},{4,6},{6,4},{8,10},{10,8},{12,14},{14,12},{1,3},{3,1},... | collective-permute-start | bytes 1179656 | tf_op jit(solution)/shard_map/ppermute | solution.py:478
  4.1 4.2 %copy-start.2 = (bf16[4,8,512]{2,1,0:T(8,128)(2,1)}, bf16[4,8,512]{2,1,0:T(8,128)(2,1)S(1)}, u32[]{:S(2)}) copy-start(bf16[4,8,512]{2,1,0:T(8,128)(2,1)S(1)} %collective-permute-done.edge) | copy-start | bytes 98308
  8.3 5.5 %collective-permute-start.3 = (bf16[256,512]{1,0:T(8,128)(2,1)}, bf16[256,512]{1,0:T(8,128)(2,1)S(1)}, u32[]{:S(2)}, u32[]{:S(2)}) collective-permute-start(bf16[256,512]{1,0:T(8,128)(2,1)} %get-tuple-element.26), channel_id=1, source_target_pairs={{0,1},{1,0},{2,3},{3,2},{4,5},{5,4},{6,7},{7,6},{8,9},{9,8},{10,11... | collective-permute-start | bytes 786440 | tf_op jit(solution)/shard_map/ppermute | solution.py:417
  8.7 5.1 %collective-permute-start.4 = (bf16[256,512]{1,0:T(8,128)(2,1)}, bf16[256,512]{1,0:T(8,128)(2,1)S(1)}, u32[]{:S(2)}, u32[]{:S(2)}) collective-permute-start(bf16[256,512]{1,0:T(8,128)(2,1)} %get-tuple-element.27), channel_id=1, source_target_pairs={{0,1},{1,0},{2,3},{3,2},{4,5},{5,4},{6,7},{7,6},{8,9},{9,8},{10,11... | collective-permute-start | bytes 786440 | tf_op jit(solution)/shard_map/ppermute | solution.py:417
  8.9 23.5 %collective-permute-start.1 = (bf16[3,136,512]{2,1,0:T(8,128)(2,1)}, bf16[3,136,512]{2,1,0:T(8,128)(2,1)S(1)}, u32[]{:S(2)}, u32[]{:S(2)}) collective-permute-start(bf16[3,136,512]{2,1,0:T(8,128)(2,1)} %pad_maximum_fusion), channel_id=1, source_target_pairs={{2,4},{4,2},{6,8},{8,6},{10,12},{12,10},{3,5},{5,3},{7,9},{9,7},{1... | collective-permute-start | bytes 1253384 | tf_op jit(solution)/shard_map/ppermute | solution.py:483
  11.1 3.8 %copy-start.1 = (f32[7,7,512]{2,1,0:T(8,128)S(1)}, f32[7,7,512]{2,1,0:T(8,128)}, u32[]{:S(2)}) copy-start(f32[7,7,512]{2,1,0:T(8,128)} %kernel.9) | copy-start | bytes 301060
  11.1 3.8 %copy-start.3 = (bf16[4,8,512]{2,1,0:T(8,128)(2,1)S(1)}, bf16[4,8,512]{2,1,0:T(8,128)(2,1)}, u32[]{:S(2)}) copy-start(bf16[4,8,512]{2,1,0:T(8,128)(2,1)} %copy-done.2) | copy-start | bytes 98308
  11.1 3.8 %copy-start.4 = (f32[512]{0:T(512)S(1)}, f32[512]{0:T(512)}, u32[]{:S(2)}) copy-start(f32[512]{0:T(512)} %param.16) | copy-start | bytes 6148
  14.9 17.4 %copy-start.7 = (f32[2048]{0:T(1024)S(1)}, f32[2048]{0:T(1024)}, u32[]{:S(2)}) copy-start(f32[2048]{0:T(1024)} %param.20) | copy-start | bytes 24580
  14.9 17.4 %copy-start.8 = (f32[512]{0:T(512)S(1)}, f32[512]{0:T(512)}, u32[]{:S(2)}) copy-start(f32[512]{0:T(512)} %param.18) | copy-start | bytes 6148
  14.9 17.4 %copy-start.9 = (f32[512]{0:T(512)S(1)}, f32[512]{0:T(512)}, u32[]{:S(2)}) copy-start(f32[512]{0:T(512)} %param.17) | copy-start | bytes 6148
  17.7 12.6 %collective-permute-start.5 = (bf16[3,8,512]{2,1,0:T(8,128)(2,1)S(1)}, bf16[3,8,512]{2,1,0:T(8,128)(2,1)S(1)}, u32[]{:S(2)}, u32[]{:S(2)}) collective-permute-start(bf16[3,8,512]{2,1,0:T(8,128)(2,1)S(1)} %constant_dynamic-slice_fusion), channel_id=1, source_target_pairs={{0,1},{1,0},{2,3},{3,2},{4,5},{5,4},{6,7},{7,6},{8,9},{9,8},{10,11... | collective-permute-start | bytes 73736 | tf_op jit(solution)/shard_map/ppermute | solution.py:502
  22.8 15.5 %collective-permute-start.6 = (bf16[4,32,512]{2,1,0:T(8,128)(2,1)S(1)}, bf16[4,32,512]{2,1,0:T(8,128)(2,1)S(1)}, u32[]{:S(2)}, u32[]{:S(2)}) collective-permute-start(bf16[4,32,512]{2,1,0:T(8,128)(2,1)S(1)} %get-tuple-element.28), channel_id=1, source_target_pairs={{0,0},{1,8},{2,2},{3,10},{4,4},{5,12},{6,6},{7,14},{8,1},{9,9},{10... | collective-permute-start | bytes 393224 | tf_op jit(solution)/shard_map/ppermute | solution.py:442
  24.7 13.1 %collective-permute-start.7 = (bf16[4,32,512]{2,1,0:T(8,128)(2,1)S(1)}, bf16[4,32,512]{2,1,0:T(8,128)(2,1)S(1)}, u32[]{:S(2)}, u32[]{:S(2)}) collective-permute-start(bf16[4,32,512]{2,1,0:T(8,128)(2,1)S(1)} %get-tuple-element.35), channel_id=1, source_target_pairs={{0,2},{1,10},{2,4},{3,12},{4,6},{5,14},{6,0},{7,8},{8,3},{9,11},{1... | collective-permute-start | bytes 393224 | tf_op jit(solution)/shard_map/ppermute | solution.py:442
  29.2 9.2 %collective-permute-start.8 = (bf16[4,32,512]{2,1,0:T(8,128)(2,1)S(1)}, bf16[4,32,512]{2,1,0:T(8,128)(2,1)S(1)}, u32[]{:S(2)}, u32[]{:S(2)}) collective-permute-start(bf16[4,32,512]{2,1,0:T(8,128)(2,1)S(1)} %get-tuple-element.36), channel_id=1, source_target_pairs={{0,4},{1,12},{2,6},{3,14},{4,0},{5,8},{6,2},{7,10},{8,5},{9,13},{1... | collective-permute-start | bytes 393224 | tf_op jit(solution)/shard_map/ppermute | solution.py:442
  30.4 8.0 %collective-permute-start.9 = (bf16[4,32,512]{2,1,0:T(8,128)(2,1)S(1)}, bf16[4,32,512]{2,1,0:T(8,128)(2,1)S(1)}, u32[]{:S(2)}, u32[]{:S(2)}) collective-permute-start(bf16[4,32,512]{2,1,0:T(8,128)(2,1)S(1)} %get-tuple-element.37), channel_id=1, source_target_pairs={{0,6},{1,14},{2,0},{3,8},{4,2},{5,10},{6,4},{7,12},{8,7},{9,15},{1... | collective-permute-start | bytes 393224 | tf_op jit(solution)/shard_map/ppermute | solution.py:442
  32.4 6.0 %copy-start.5 = (bf16[512,2048]{1,0:T(8,128)(2,1)S(1)}, bf16[512,2048]{1,0:T(8,128)(2,1)}, u32[]{:S(2)}) copy-start(bf16[512,2048]{1,0:T(8,128)(2,1)} %w_in.1) | copy-start | bytes 6291460
  32.4 6.0 %copy-start.6 = (bf16[2048,512]{1,0:T(8,128)(2,1)S(1)}, bf16[2048,512]{1,0:T(8,128)(2,1)}, u32[]{:S(2)}) copy-start(bf16[2048,512]{1,0:T(8,128)(2,1)} %w_out.1) | copy-start | bytes 6291460
  32.4 6.0 %copy-start.10 = (f32[512]{0:T(512)S(1)}, f32[512]{0:T(512)}, u32[]{:S(2)}) copy-start(f32[512]{0:T(512)} %param.22) | copy-start | bytes 6148
  32.4 6.0 %copy-start.11 = (f32[512]{0:T(512)S(1)}, f32[512]{0:T(512)}, u32[]{:S(2)}) copy-start(f32[512]{0:T(512)} %param.23) | copy-start | bytes 6148
  43.8 17.0 %collective-permute-start.10 = (bf16[3,128,512]{2,1,0:T(8,128)(2,1)S(1)}, bf16[3,128,512]{2,1,0:T(8,128)(2,1)S(1)}, u32[]{:S(2)}, u32[]{:S(2)}) collective-permute-start(bf16[3,128,512]{2,1,0:T(8,128)(2,1)S(1)} %get-tuple-element.38), channel_id=1, source_target_pairs={{0,2},{2,0},{4,6},{6,4},{8,10},{10,8},{12,14},{14,12},{1,3},{3,1},... | collective-permute-start | bytes 1179656 | tf_op jit(solution)/shard_map/ppermute | solution.py:545
  46.4 14.4 %collective-permute-start.11 = (bf16[3,128,512]{2,1,0:T(8,128)(2,1)S(1)}, bf16[3,128,512]{2,1,0:T(8,128)(2,1)S(1)}, u32[]{:S(2)}, u32[]{:S(2)}) collective-permute-start(bf16[3,128,512]{2,1,0:T(8,128)(2,1)S(1)} %get-tuple-element.39), channel_id=1, source_target_pairs={{2,4},{4,2},{6,8},{8,6},{10,12},{12,10},{3,5},{5,3},{7,9},{9,7},{1... | collective-permute-start | bytes 1179656 | tf_op jit(solution)/shard_map/ppermute | solution.py:546
  50.4 2.7 %collective-permute-start.14 = (bf16[4,8,512]{2,1,0:T(8,128)(2,1)S(1)}, bf16[4,8,512]{2,1,0:T(8,128)(2,1)S(1)}, u32[]{:S(2)}, u32[]{:S(2)}) collective-permute-start(bf16[4,8,512]{2,1,0:T(8,128)(2,1)S(1)} %get-tuple-element.43), channel_id=1, source_target_pairs={{0,1},{1,0},{2,3},{3,2},{4,5},{5,4},{6,7},{7,6},{8,9},{9,8},{10,11... | collective-permute-start | bytes 98312 | tf_op jit(solution)/shard_map/ppermute | solution.py:547
  50.5 10.2 %collective-permute-start.12 = (bf16[3,8,512]{2,1,0:T(8,128)(2,1)S(1)}, bf16[3,8,512]{2,1,0:T(8,128)(2,1)S(1)}, u32[]{:S(2)}, u32[]{:S(2)}) collective-permute-start(bf16[3,8,512]{2,1,0:T(8,128)(2,1)S(1)} %get-tuple-element.40), channel_id=1, source_target_pairs={{0,3},{1,2},{2,1},{3,0},{4,7},{5,6},{6,5},{7,4},{8,11},{9,10},{10,... | collective-permute-start | bytes 73736 | tf_op jit(solution)/shard_map/ppermute | solution.py:548
  51.0 9.6 %collective-permute-start.13 = (bf16[3,8,512]{2,1,0:T(8,128)(2,1)S(1)}, bf16[3,8,512]{2,1,0:T(8,128)(2,1)S(1)}, u32[]{:S(2)}, u32[]{:S(2)}) collective-permute-start(bf16[3,8,512]{2,1,0:T(8,128)(2,1)S(1)} %get-tuple-element.41), channel_id=1, source_target_pairs={{2,5},{3,4},{4,3},{5,2},{6,9},{7,8},{8,7},{9,6},{10,13},{11,12},{1... | collective-permute-start | bytes 73736 | tf_op jit(solution)/shard_map/ppermute | solution.py:549

commit v10 on v8

--- a/solution.py
+++ b/solution.py
@@ -16,7 +16,6 @@
 CHUNK = 16
 UNROLL = 16
 COPIES = 8
-DOTS = 2
 MLP_TILE = 512
 CONTRACT_LAST = (((1,), (1,)), ((), ()))
 SWAP = [(0, 1), (1, 0)]
@@ -30,32 +29,52 @@
     return slice(tile * LANES, (tile + 1) * LANES)
 
 
-def project_kernel(other, core_ref, teacher_hbm, weight, *rest):
-    *outs, rows, sems = rest
-    half = 1 - core_ref[0] if other else core_ref[0]
-    lines, wide, depth = rows.shape
+def project_kernel(
+    core_ref, teacher_hbm, weight, upper, lower, home_anywhere, rows, sems, home, home_sems
+):
+    core = core_ref[0]
+    _, lines, wide, depth = rows.shape
     count = next(n for n in (COPIES, 4, 2) if lines % n == 0)
     copies = []
-    for index in range(count):
-        here = pl.ds(index * (lines // count), lines // count)
-        copy = pltpu.make_async_copy(teacher_hbm.at[here, half], rows.at[here], sems.at[index])
-        copy.start()
-        copies.append(copy)
-    size = lines * wide // DOTS
-    for index in range(DOTS):
-        for copy in copies[index * count // DOTS : (index + 1) * count // DOTS]:
-            copy.wait()
-        here = pl.ds(index * (lines // DOTS), lines // DOTS)
-        product = jnp.dot(
-            rows[here].reshape(size, depth), weight[...], preferred_element_type=jnp.float32
-        )
-        out = outs[index * len(outs) // DOTS]
-        start = index * size % out.shape[0]
-        out[start : start + size] = product.astype(out.dtype)
-
-
-def combine_kernel(wide, turns_ref, home, upper, lower, *rest):
-    *blocks, summed = rest
+    for slot, half in enumerate((1 - core, core)):
+        for index in range(count):
+            here = pl.ds(index * (lines // count), lines // count)
+            copy = pltpu.make_async_copy(
+                teacher_hbm.at[here, half], rows.at[slot, here], sems.at[slot, index]
+            )
+            copy.start()
+            copies.append(copy)
+    size = lines * wide // 2
+    leaving = []
+    for slot in range(2):
+        for index in range(2):
+            first = slot * count + index * count // 2
+            for copy in copies[first : first + count // 2]:
+                copy.wait()
+            here = pl.ds(index * (lines // 2), lines // 2)
+            product = jnp.dot(
+                rows[slot, here].reshape(size, depth),
+                weight[...],
+                preferred_element_type=jnp.float32,
+            )
+            if slot:
+                here = pl.ds(index * size, size)
+                home[here] = product
+                leaving.append(
+                    pltpu.make_async_copy(home.at[here], home_anywhere.at[here], home_sems.at[index])
+                )
+                leaving[-1].start()
+            else:
+                (upper, lower)[index][...] = product.astype(upper.dtype)
+    for copy in leaving:
+        copy.wait()
+
+
+def combine_kernel(wide, turns_ref, home_anywhere, upper, lower, *rest):
+    *blocks, summed, home, sem = rest
+    copy = pltpu.make_async_copy(home_anywhere, home, sem)
+    copy.start()
+    copy.wait()
     half = upper.shape[0]
     for tile in range(summed.shape[0]):
         lanes = lane_tile(tile)
@@ -145,14 +164,18 @@
             place += 1
 
 
-def inner_kernel(flip, core_ref, middle, edge, kernel, base_value, out, padded, taps, *fetch):
+def inner_kernel(flip, core_ref, middle, edge, kernel, base_value, out, *scratch):
     tile_u, tile_v, channels = middle.shape
     copies = []
-    if fetch:
+    if flip:
+        padded, *fetch = scratch
+        taps = kernel
         copies.append(pltpu.make_async_copy(base_value, *fetch))
         copies[0].start()
         base_value = fetch[0]
-    spread_taps(taps, kernel)
+    else:
+        taps, padded = scratch
+        spread_taps(taps, kernel)
     fill(padded, [(middle, edge, 0)], core_ref[0], tile_v)
 
     def place(tile, u, base):
@@ -173,9 +196,8 @@
     depthwise(padded, taps, begin, store, tile_u, tile_v, EDGE - REACH, own, flip)
 
 
-def side_conv(flip, core, on_left, side, edge, kernel, inner, store, padded, taps):
+def side_conv(flip, core, on_left, side, edge, taps, inner, store, padded):
     tile_u, tile_v, _ = inner.shape
-    spread_taps(taps, kernel)
     fill(padded, [(side, *edge)], core, tile_v)
 
     def begin(tile, u, base):
@@ -189,7 +211,7 @@
             depthwise(padded, taps, begin, store, tile_u, tile_v, EDGE - REACH, sources, flip)
 
 
-def side_kernel(flip, place_ref, side, edge, kernel, inner, out, padded, taps):
+def side_kernel(flip, place_ref, side, edge, taps, inner, out, padded):
     tile_v = inner.shape[1]
 
     def store(tile, u, base, value):
@@ -197,13 +219,13 @@
 
     start = edge.shape[1] - EDGE
     side_conv(
-        flip, place_ref[0], place_ref[1] == 0, side, (edge, start), kernel, inner, store, padded, taps
+        flip, place_ref[0], place_ref[1] == 0, side, (edge, start), taps, inner, store, padded
     )
 
 
 def up_kernel(
-    place_ref, side, kernel, inner, gain, shift, w_in_hbm, b_in,
-    normal_form, inv_scale, activated, slope, padded, taps, summed, normed, w_in, sem,
+    place_ref, side, taps, inner, gain, shift, w_in_hbm, b_in,
+    normal_form, inv_scale, activated, slope, padded, summed, normed, w_in, sem,
 ):
     copy = pltpu.make_async_copy(w_in_hbm, w_in, sem)
     copy.start()
@@ -215,7 +237,7 @@
         summed[u, aligned(base, SUBLANES), aligned(tile * LANES, LANES)] = value
 
     side_conv(
-        False, place_ref[0], place_ref[1] == 1, side, (side, tile_v), kernel, inner, store, padded, taps
+        False, place_ref[0], place_ref[1] == 1, side, (side, tile_v), taps, inner, store, padded
     )
 
     def norm_step(index):
@@ -316,10 +338,9 @@
 
 
 def last_kernel(
-    place_ref, even, odd, even_edge, odd_edge, kernel, inner, out, padded, taps, turned
+    place_ref, even, odd, even_edge, odd_edge, taps, inner, out, padded, turned
 ):
     tile_v, tile_u, channels = out.shape
-    spread_taps(taps, kernel)
     sides = (even, even_edge, 0), (odd, odd_edge, 0)
     for parity in range(2):
 
@@ -401,18 +422,17 @@
     by_half = teacher.reshape(lines, 2, half_line, teacher.shape[1])
     size = (lines * half_line, channels)
     fourth = jax.ShapeDtypeStruct((size[0] // 2, channels), jnp.bfloat16)
-    scratch = [
-        pltpu.VMEM((lines, half_line, teacher.shape[1]), jnp.bfloat16),
-        pltpu.SemaphoreType.DMA((COPIES,)),
-    ]
-    upper, lower = call(
-        functools.partial(project_kernel, True),
-        "project_away", [fourth] * 2, scratch, [scalar], [by_half, proj_weight], 1, 12, (0,),
-    )
-    (home,) = call(
-        functools.partial(project_kernel, False),
-        "project_home", [jax.ShapeDtypeStruct(size, jnp.float32)],
-        scratch, [scalar], [by_half, proj_weight], 1, 12, (0,),
+    upper, lower, home = call(
+        project_kernel,
+        "project",
+        [fourth, fourth, jax.ShapeDtypeStruct(size, jnp.float32)],
+        [
+            pltpu.VMEM((2, lines, half_line, teacher.shape[1]), jnp.bfloat16),
+            pltpu.SemaphoreType.DMA((2, COPIES)),
+            pltpu.VMEM(size, jnp.float32),
+            pltpu.SemaphoreType.DMA((2,)),
+        ],
+        [scalar], [by_half, proj_weight], 1, 16, (0,), out_anywhere=(2,),
     )
     received = [lax.ppermute(away, "col", SWAP) for away in (upper, lower)]
     turns = [lax.rem(turn + row, halves) * tile_u for turn in range(halves)]
@@ -426,11 +446,16 @@
             functools.partial(combine_kernel, half_line),
             "combine",
             [jax.ShapeDtypeStruct((tile_u, lines, channels), jnp.bfloat16)] * halves,
-            [pltpu.VMEM((channels // LANES, *size[:1], LANES), jnp.float32)],
+            [
+                pltpu.VMEM((channels // LANES, *size[:1], LANES), jnp.float32),
+                pltpu.VMEM(size, jnp.float32),
+                pltpu.SemaphoreType.DMA,
+            ],
             [jnp.stack(turns).astype(jnp.int32)],
             [home, *received],
             1,
             8,
+            anywhere=(0,),
         )
     pieces, places = [], []
     for turn in range(halves):
@@ -446,8 +471,8 @@
         whole = jnp.zeros((tile_u, tile_v, channels), jnp.bfloat16)
         for index, piece in enumerate(pieces):
             whole = lax.dynamic_update_slice_in_dim(whole, piece, places[index], axis=1)
-        return [whole], jnp.zeros((1,), jnp.int32), blocks[0]
-    return pieces, places, blocks[0]
+        return [whole], jnp.zeros((1,), jnp.int32), home
+    return pieces, places, home
 
 
 def on_device(
@@ -473,8 +498,10 @@
     scalar = core.astype(jnp.int32)[None]
     f32, bf16 = jnp.float32, jnp.bfloat16
     rows = tile_u * tile_v
-    middle = student.transpose(1, 0, 2)
-    first_block = facing(middle, row, True)
+    columns = jnp.where(row % 2 == 1, tile_u - REACH, 0)
+    first_block = lax.dynamic_slice_in_dim(student, columns, REACH, axis=1).transpose(1, 0, 2)
+    after_block, _ = lax.optimization_barrier((student, first_block))
+    middle = after_block.transpose(1, 0, 2)
     first_side = lax.ppermute(first_block, "row", row_pairs(True))
     edge = lax.ppermute(edge_lines(middle, core), "col", SWAP)
     second_block = jnp.concatenate(
@@ -482,28 +509,28 @@
     )
     second_side = lax.ppermute(second_block, "row", row_pairs(False))
     held, *_ = lax.optimization_barrier((proj_weight, first_block, second_block))
-    targets, places, block = find_target(teacher, held, core, row, tile_u, tile_v)
-    later, _ = lax.optimization_barrier((dw_bias, block))
+    targets, places, home = find_target(teacher, held, core, row, tile_u, tile_v)
+    later, _ = lax.optimization_barrier((dw_bias, home))
     matmul = 2 * rows * channels * hidden
     whole = (tile_u, tile_v, channels)
     summed = jax.ShapeDtypeStruct(whole, f32)
-    taps = pltpu.VMEM((TAPS * TAPS, tiles, SUBLANES, LANES), f32)
+    taps = jax.ShapeDtypeStruct((TAPS * TAPS, tiles, SUBLANES, LANES), f32)
     own_pad, side_pad, rim_pad = (
         pltpu.VMEM((tiles, count, tile_v + 2 * EDGE, LANES), f32)
         for count in (tile_u, REACH, 2 * REACH)
     )
     place = jnp.stack([core, row % 2]).astype(jnp.int32)
-    (inner,) = call(
+    inner, taps = call(
         functools.partial(inner_kernel, False),
-        "inner_up", [summed], [own_pad, taps], [scalar],
+        "inner_up", [summed, taps], [own_pad], [scalar],
         [middle, edge, dw_kernel, later[None]], 1, 8,
     )
     arrived, _ = lax.optimization_barrier((first_side, inner))
     first_edge = lax.ppermute(edge_lines(arrived, core), "col", SWAP)
     (inner,) = call(
         functools.partial(side_kernel, False),
-        "side_up", [summed], [side_pad, taps], [place],
-        [first_side, first_edge, dw_kernel, inner], 1, 8,
+        "side_up", [summed], [side_pad], [place],
+        [first_side, first_edge, taps, inner], 1, 8,
     )
     saved = call(
         up_kernel,
@@ -514,10 +541,10 @@
             jax.ShapeDtypeStruct((rows, hidden), bf16),
             jax.ShapeDtypeStruct((rows, hidden), bf16),
         ],
-        [side_pad, taps, pltpu.VMEM(whole, f32), pltpu.VMEM((rows, channels), bf16)]
+        [side_pad, pltpu.VMEM(whole, f32), pltpu.VMEM((rows, channels), bf16)]
         + [pltpu.VMEM(w_in.shape, bf16), pltpu.SemaphoreType.DMA],
         [place],
-        [second_side, dw_kernel, inner, norm_gain[None], norm_bias[None], w_in, b_in[None]],
+        [second_side, taps, inner, norm_gain[None], norm_bias[None], w_in, b_in[None]],
         4 * matmul,
         16,
         (5,),
@@ -550,16 +577,16 @@
     (inner,) = call(
         functools.partial(inner_kernel, True),
         "inner_last", [summed],
-        [own_pad, taps, pltpu.VMEM(whole, f32), pltpu.SemaphoreType.DMA], [scalar],
-        [d_conv, edge, dw_kernel, mismatch], matmul, 8, anywhere=(3,),
+        [own_pad, pltpu.VMEM(whole, f32), pltpu.SemaphoreType.DMA], [scalar],
+        [d_conv, edge, taps, mismatch], matmul, 8, anywhere=(3,),
     )
     (grad,) = call(
         last_kernel,
         "last",
         [jax.ShapeDtypeStruct((tile_v, tile_u, channels), f32)],
-        [rim_pad, taps, pltpu.VMEM(whole, f32)],
+        [rim_pad, pltpu.VMEM(whole, f32)],
         [place],
-        [even, odd, even_edge, odd_edge, dw_kernel, inner],
+        [even, odd, even_edge, odd_edge, taps, inner],
         1,
         8,
     )

time: 64.4 us -> 64.6 us (level)
  local copies, waits for them, and re-layouts: 2.22 us -> 4.62 us
  waiting for transfers between devices: 9.33 us -> 7.26 us
    ppermute x1, waiting for transfers between devices: 7.2 us -> 4.76 us  [on_device(): lax.ppermute(even_edge, ('row', 'col'), across(row_pairs(False)))]
    unnamed x25 -> x27, local copies, waits for them, and re-layouts: 1.34 us -> 3.09 us
    dynamic_slice x0 -> x1, local copies, waits for them, and re-layouts: none -> 1.39 us  [on_device(): lax.dynamic_slice_in_dim(student, columns, REACH, axis=1).transpose(1, 0, 2)]
    dynamic_slice x2, local copies, waits for them, and re-layouts: 0.85 us -> 0.03 us  [facing(): lax.dynamic_slice_in_dim(tile, jnp.where(to_right, tile.shape[0] - REACH,...]
    ppermute x1, waiting for transfers between devices: 0.01 us -> 0.82 us  [on_device(): edge = lax.ppermute(edge_lines(middle, core), 'col', SWAP)]
    pallas_call x9 -> x8, Pallas kernels: 29.1 us -> 28.5 us  [call(): pl.pallas_call(kernel, out_shape=tuple(outs), in_specs=[smem] * len(scala...]
  transfers between devices with their start and end apart: 15 -> 15, of which waited for: 4 -> 4; matrix products, arithmetic and copies ran while one was open for 3% -> 2% of each run, Pallas kernels for 31% -> 30%
where the time goes in v10:
time: 64.6 us; the launch traced here: 63.9 us
  Pallas kernels  28.5 us (44%)
  starting transfers between devices  22.1 us (34%)
  waiting for transfers between devices  7.26 us (11%)
  local copies, waits for them, and re-layouts  4.62 us (7%)
  other arithmetic  1.01 us (2%)
    pallas_call x8, Pallas kernels, call(): pl.pallas_call(kernel, out_shape=tuple(outs), in_specs=[smem] * len(scala...  28.5 us
    ppermute x4, starting transfers between devices, find_target(): pieces.append(lax.ppermute(blocks[turn], ('row', 'col'), pairs))  6.24 us
    ppermute x1, waiting for transfers between devices, on_device(): lax.ppermute(even_edge, ('row', 'col'), across(row_pairs(False)))  4.76 us
    ppermute x1, starting transfers between devices, on_device(): odd = lax.ppermute(odd, 'row', row_pairs(True))  3.81 us
    unnamed x27, local copies, waits for them, and re-layouts  3.09 us
    ppermute x1, starting transfers between devices, on_device(): first_side = lax.ppermute(first_block, 'row', row_pairs(True))  2.99 us
    ppermute x1, starting transfers between devices, on_device(): even = lax.ppermute(even, 'row', row_pairs(False))  2.64 us
    ppermute x1, starting transfers between devices, on_device(): odd_edge = lax.ppermute(odd_edge, ('row', 'col'), across(row_pairs(True)))  1.91 us
  transfers between devices with their start and end apart: 15, of which 4 were waited for; matrix products, arithmetic and copies ran while one was open for 2% of the time, Pallas kernels for 30%

profile of v10, /device:TPU:13, one launch (start us, length us, event | category | flops | bytes accessed | tf_op | source)
XLA Modules:
  0.0 63.9 jit_solution(6853792348544528392)
XLA Ops:
  0.0 1.4 %constant_dynamic-slice_fusion.2 = bf16[128,3,512]{2,1,0:T(4,128)(2,1)S(1)} fusion(bf16[128,4,512]{2,1,0:T(4,128)(2,1)} %param.14, s32[]{:T(128)S(6)} %select_n.31), kind=kLoop, calls=%fused_computation.6 | loop fusion | bytes 786436 | tf_op jit(solution)/shard_map/dynamic_slice | solution.py:502
  1.4 0.9 %copy.21 = bf16[128,3,512]{2,0,1:T(8,128)(2,1)} copy(bf16[128,3,512]{2,1,0:T(4,128)(2,1)S(1)} %constant_dynamic-slice_fusion.2) | data formatting | bytes 786432
  2.3 3.0 %collective-permute-start.2 = (bf16[3,128,512]{2,1,0:T(8,128)(2,1)}, bf16[3,128,512]{2,1,0:T(8,128)(2,1)S(1)}, u32[]{:S(2)}, u32[]{:S(2)}) collective-permute-start(bf16[3,128,512]{2,1,0:T(8,128)(2,1)} %bitcast.25), channel_id=1, source_target_pairs={{2,4},{4,2},{6,8},{8,6},{10,12},{12,10},{3,5},{5,3},{7,9},{9,7},{1... | collective-permute-start | bytes 1179656 | tf_op jit(solution)/shard_map/ppermute | solution.py:505
  5.3 0.1 copy.22
  5.4 1.0 %collective-permute-start = (bf16[4,8,512]{2,1,0:T(8,128)(2,1)S(1)}, bf16[4,8,512]{2,1,0:T(8,128)(2,1)S(1)}, u32[]{:S(2)}, u32[]{:S(2)}) collective-permute-start(bf16[4,8,512]{2,1,0:T(8,128)(2,1)S(1)} %dynamic-slice_bitcast_fusion.1), channel_id=1, source_target_pairs={{0,1},{1,0},{2,3},{3,2},{4,5},{5,4},{6,7},{7,6},{8,9},{9,8},{10,11... | collective-permute-start | bytes 98312 | tf_op jit(solution)/shard_map/ppermute | solution.py:506
  6.5 0.8 %collective-permute-done.edge = bf16[4,8,512]{2,1,0:T(8,128)(2,1)S(1)} collective-permute-done((bf16[4,8,512]{2,1,0:T(8,128)(2,1)S(1)}, bf16[4,8,512]{2,1,0:T(8,128)(2,1)S(1)}, u32[]{:S(2)}, u32[]{:S(2)}) %collective-permute-start) | collective-permute-done | bytes 32800 | tf_op jit(solution)/shard_map/ppermute | solution.py:506
  7.3 0.8 %pad_maximum_fusion = bf16[3,136,512]{2,1,0:T(8,128)(2,1)} fusion(bf16[3,8,512]{2,1,0:T(8,128)(2,1)S(1)} %constant_dynamic-slice_fusion.1, bf16[3,128,512]{2,1,0:T(8,128)(2,1)S(1)} %dynamic-slice_bitcast_fusion), kind=kLoop, calls=%fused_computation | loop fusion | flops 835584 | bytes 835584 | tf_op jit(solution)/shard_map/concatenate | solution.py:507
  8.1 1.4 %collective-permute-start.1 = (bf16[3,136,512]{2,1,0:T(8,128)(2,1)}, bf16[3,136,512]{2,1,0:T(8,128)(2,1)}, u32[]{:S(2)}, u32[]{:S(2)}) collective-permute-start(bf16[3,136,512]{2,1,0:T(8,128)(2,1)} %pad_maximum_fusion), channel_id=1, source_target_pairs={{0,2},{2,0},{4,6},{6,4},{8,10},{10,8},{12,14},{14,12},{1,3},{3,1},... | collective-permute-start | bytes 1253384 | tf_op jit(solution)/shard_map/ppermute | solution.py:510
  9.5 5.0 %project.1 = (bf16[256,512]{1,0:T(8,128)(2,1)}, bf16[256,512]{1,0:T(8,128)(2,1)S(1)}, f32[512,512]{1,0:T(8,128)S(1)}) custom-call(s32[1]{0:T(128)} %bitcast.core_ref, bf16[32,2,16,2048]{3,2,1,0:T(8,128)(2,1)} %bitcast.35, bf16[2048,512]{1,0:T(8,128)(2,1)S(1)} %copy-done), custom_call_target="tpu_custom_call" | custom-call | flops 1 | bytes 1 | tf_op jit(solution)/shard_map/project/pallas_call | solution.py:379
  14.6 1.0 %copy-done.1 = f32[512,512]{1,0:T(8,128)} copy-done((f32[512,512]{1,0:T(8,128)}, f32[512,512]{1,0:T(8,128)S(1)}, u32[]{:S(2)}) %copy-start.1) | copy-done | bytes 1048600
  15.5 0.6 collective-permute-start.4
  16.1 0.1 pad_add_fusion.2.turns_ref
  16.2 2.8 %inner_up.1 = (f32[4,128,512]{2,1,0:T(8,128)S(1)}, f32[49,4,8,128]{3,2,1,0:T(8,128)S(1)}) custom-call(s32[1]{0:T(128)} %bitcast.core_ref, bf16[4,128,512]{2,1,0:T(8,128)(2,1)S(1)} %bitcast.26, bf16[4,8,512]{2,1,0:T(8,128)(2,1)S(1)} %collective-permute-done.edge, f32[7,7,512]{2,1,0:T(8,128)S(1)} %copy-done.3, f32[1,512]{1,0:T(1,128)S(1)} %bitcast.28), custom_call_target="tpu_custom_call" | custom-call | flops 1 | bytes 1 | tf_op jit(solution)/shard_map/inner_up/pallas_call | solution.py:379
  19.1 0.6 collective-permute-start.3
  19.7 1.2 %copy-done.2 = f32[512,512]{1,0:T(8,128)S(1)} copy-done((f32[512,512]{1,0:T(8,128)S(1)}, f32[512,512]{1,0:T(8,128)}, u32[]{:S(2)}) %copy-start.2) | copy-done | bytes 1048600
  21.0 1.1 %combine.1 = (bf16[4,32,512]{2,1,0:T(8,128)(2,1)S(1)}, bf16[4,32,512]{2,1,0:T(8,128)(2,1)S(1)}, bf16[4,32,512]{2,1,0:T(8,128)(2,1)S(1)}, bf16[4,32,512]{2,1,0:T(8,128)(2,1)S(1)}) custom-call(s32[4]{0:T(128)S(1)} %pad_add_fusion.2.turns_ref, f32[512,512]{1,0:T(8,128)S(1)} %copy-done.2, bf16[256,512]{1,0:T(8,128)(2,1)S(1)} %collective-permute-done.4.upper, ...), custom_call_target="tpu_custom_call" | custom-call | flops 1 | bytes 1 | tf_op jit(solution)/shard_map/combine/pallas_call | solution.py:379
  22.1 2.6 %collective-permute-start.6 = (bf16[4,32,512]{2,1,0:T(8,128)(2,1)S(1)}, bf16[4,32,512]{2,1,0:T(8,128)(2,1)S(1)}, u32[]{:S(2)}, u32[]{:S(2)}) collective-permute-start(bf16[4,32,512]{2,1,0:T(8,128)(2,1)S(1)} %get-tuple-element.42), channel_id=1, source_target_pairs={{0,0},{1,8},{2,2},{3,10},{4,4},{5,12},{6,6},{7,14},{8,1},{9,9},{10... | collective-permute-start | bytes 393224 | tf_op jit(solution)/shard_map/ppermute | solution.py:467
  24.7 1.8 %collective-permute-start.7 = (bf16[4,32,512]{2,1,0:T(8,128)(2,1)S(1)}, bf16[4,32,512]{2,1,0:T(8,128)(2,1)S(1)}, u32[]{:S(2)}, u32[]{:S(2)}) collective-permute-start(bf16[4,32,512]{2,1,0:T(8,128)(2,1)S(1)} %get-tuple-element.43), channel_id=1, source_target_pairs={{0,2},{1,10},{2,4},{3,12},{4,6},{5,14},{6,0},{7,8},{8,3},{9,11},{1... | collective-permute-start | bytes 393224 | tf_op jit(solution)/shard_map/ppermute | solution.py:467
  26.5 1.2 %collective-permute-start.8 = (bf16[4,32,512]{2,1,0:T(8,128)(2,1)S(1)}, bf16[4,32,512]{2,1,0:T(8,128)(2,1)S(1)}, u32[]{:S(2)}, u32[]{:S(2)}) collective-permute-start(bf16[4,32,512]{2,1,0:T(8,128)(2,1)S(1)} %get-tuple-element.44), channel_id=1, source_target_pairs={{0,4},{1,12},{2,6},{3,14},{4,0},{5,8},{6,2},{7,10},{8,5},{9,13},{1... | collective-permute-start | bytes 393224 | tf_op jit(solution)/shard_map/ppermute | solution.py:467
  27.7 0.6 collective-permute-start.9
  28.4 1.8 %side_up.1.inner = f32[4,128,512]{2,1,0:T(8,128)S(1)} custom-call(s32[2]{0:T(128)S(1)} %pad_add_fusion.place_ref, bf16[3,128,512]{2,1,0:T(8,128)(2,1)S(1)} %collective-permute-done.2.side, bf16[3,8,512]{2,1,0:T(8,128)(2,1)S(1)} %collective-permute-done.3.edge, f32[49,4,8,128]{3,2,1,0:T(8,128)S(1)} %get-tuple-element.33.taps.kernel, ...), custom_call_target="tpu_custom_call" | custom-call | flops 1 | bytes 1 | tf_op jit(solution)/shard_map/side_up/pallas_call | solution.py:379
  30.3 5.6 %up.1 = (f32[512,512]{1,0:T(8,128)S(1)}, f32[512,128]{1,0:T(8,128)S(1)}, bf16[512,2048]{1,0:T(8,128)(2,1)S(1)}, bf16[512,2048]{1,0:T(8,128)(2,1)S(1)}) custom-call(s32[2]{0:T(128)S(1)} %pad_add_fusion.place_ref, bf16[3,136,512]{2,1,0:T(8,128)(2,1)} %collective-permute-done.1.side, f32[49,4,8,128]{3,2,1,0:T(8,128)S(1)} %get-tuple-element.33.taps.kernel, ...), custom_call_target="tpu_custom_call" | custom-call | flops 4294967296 | bytes 9883648 | tf_op jit(solution)/shard_map/up/pallas_call | solution.py:379
  36.0 0.7 %collective-permute-done.8.rest_2_ = bf16[4,32,512]{2,1,0:T(8,128)(2,1)S(1)} collective-permute-done((bf16[4,32,512]{2,1,0:T(8,128)(2,1)S(1)}, bf16[4,32,512]{2,1,0:T(8,128)(2,1)S(1)}, u32[]{:S(2)}, u32[]{:S(2)}) %collective-permute-start.8) | collective-permute-done | bytes 131104 | tf_op jit(solution)/shard_map/ppermute | solution.py:467
  36.7 5.4 %back.1 = (f32[4,128,512]{2,1,0:T(8,128)S(1)}, bf16[4,128,512]{2,1,0:T(8,128)(2,1)S(1)}, bf16[3,128,512]{2,1,0:T(8,128)(2,1)S(1)}, bf16[3,128,512]{2,1,0:T(8,128...) custom-call(s32[2]{0:T(128)S(1)} %pad_add_fusion.place_ref, ...), custom_call_target="tpu_custom_call" | custom-call | flops 4294967296 | bytes 13195264 | tf_op jit(solution)/shard_map/back/pallas_call | solution.py:379
  42.1 2.6 %collective-permute-start.10 = (bf16[3,128,512]{2,1,0:T(8,128)(2,1)S(1)}, bf16[3,128,512]{2,1,0:T(8,128)(2,1)S(1)}, u32[]{:S(2)}, u32[]{:S(2)}) collective-permute-start(bf16[3,128,512]{2,1,0:T(8,128)(2,1)S(1)} %get-tuple-element.46), channel_id=1, source_target_pairs={{0,2},{2,0},{4,6},{6,4},{8,10},{10,8},{12,14},{14,12},{1,3},{3,1},... | collective-permute-start | bytes 1179656 | tf_op jit(solution)/shard_map/ppermute | solution.py:572
  44.8 3.8 %collective-permute-start.11 = (bf16[3,128,512]{2,1,0:T(8,128)(2,1)S(1)}, bf16[3,128,512]{2,1,0:T(8,128)(2,1)S(1)}, u32[]{:S(2)}, u32[]{:S(2)}) collective-permute-start(bf16[3,128,512]{2,1,0:T(8,128)(2,1)S(1)} %get-tuple-element.47), channel_id=1, source_target_pairs={{2,4},{4,2},{6,8},{8,6},{10,12},{12,10},{3,5},{5,3},{7,9},{9,7},{1... | collective-permute-start | bytes 1179656 | tf_op jit(solution)/shard_map/ppermute | solution.py:573
  48.7 0.9 %collective-permute-start.12 = (bf16[3,8,512]{2,1,0:T(8,128)(2,1)S(1)}, bf16[3,8,512]{2,1,0:T(8,128)(2,1)S(1)}, u32[]{:S(2)}, u32[]{:S(2)}) collective-permute-start(bf16[3,8,512]{2,1,0:T(8,128)(2,1)S(1)} %get-tuple-element.48), channel_id=1, source_target_pairs={{0,3},{1,2},{2,1},{3,0},{4,7},{5,6},{6,5},{7,4},{8,11},{9,10},{10,... | collective-permute-start | bytes 73736 | tf_op jit(solution)/shard_map/ppermute | solution.py:575
  49.5 1.9 %collective-permute-start.13 = (bf16[3,8,512]{2,1,0:T(8,128)(2,1)S(1)}, bf16[3,8,512]{2,1,0:T(8,128)(2,1)S(1)}, u32[]{:S(2)}, u32[]{:S(2)}) collective-permute-start(bf16[3,8,512]{2,1,0:T(8,128)(2,1)S(1)} %get-tuple-element.49), channel_id=1, source_target_pairs={{2,5},{3,4},{4,3},{5,2},{6,9},{7,8},{8,7},{9,6},{10,13},{11,12},{1... | collective-permute-start | bytes 73736 | tf_op jit(solution)/shard_map/ppermute | solution.py:576
  51.5 2.7 %inner_last.1.inner = f32[4,128,512]{2,1,0:T(8,128)S(1)} custom-call(s32[1]{0:T(128)} %bitcast.core_ref, bf16[4,128,512]{2,1,0:T(8,128)(2,1)S(1)} %get-tuple-element.50.middle, bf16[4,8,512]{2,1,0:T(8,128)(2,1)S(1)} %collective-permute-done.14.edge, f32[49,4,8,128]{3,2,1,0:T(8,128)S(1)} %get-tuple-element.33.taps.kernel, ...), custom_call_target="tpu_custom_call" | custom-call | flops 1073741824 | bytes 3457024 | tf_op jit(solution)/shard_map/inner_last/pallas_call | solution.py:379
  54.2 4.8 %collective-permute-done.12.even_edge = bf16[3,8,512]{2,1,0:T(8,128)(2,1)S(1)} collective-permute-done((bf16[3,8,512]{2,1,0:T(8,128)(2,1)S(1)}, bf16[3,8,512]{2,1,0:T(8,128)(2,1)S(1)}, u32[]{:S(2)}, u32[]{:S(2)}) %collective-permute-start.12) | collective-permute-done | bytes 24608 | tf_op jit(solution)/shard_map/ppermute | solution.py:575
  59.0 0.9 %collective-permute-done.10.even = bf16[3,128,512]{2,1,0:T(8,128)(2,1)S(1)} collective-permute-done((bf16[3,128,512]{2,1,0:T(8,128)(2,1)S(1)}, bf16[3,128,512]{2,1,0:T(8,128)(2,1)S(1)}, u32[]{:S(2)}, u32[]{:S(2)}) %collective-permute-start.10) | collective-permute-done | bytes 393248 | tf_op jit(solution)/shard_map/ppermute | solution.py:572
  59.9 4.0 %last.1 = f32[128,4,512]{2,1,0:T(4,128)} custom-call(s32[2]{0:T(128)S(1)} %pad_add_fusion.place_ref, bf16[3,128,512]{2,1,0:T(8,128)(2,1)S(1)} %collective-permute-done.10.even, bf16[3,128,512]{2,1,0:T(8,128)(2,1)S(1)} %collective-permute-done.11.odd, bf16[3,8,512]{2,1,0:T(8,128)(2,1)S(1)} %collective-permute-done.12.even_edge, ...), custom_call_target="tpu_custom_call" | custom-call | flops 1 | bytes 1 | tf_op jit(solution)/shard_map/last/pallas_call | solution.py:379
  (43 shorter events, 0.4 us)
Async XLA Ops:
  0.0 5.3 %copy-start.12 = (bf16[128,4,512]{2,1,0:T(4,128)(2,1)S(1)}, bf16[128,4,512]{2,1,0:T(4,128)(2,1)}, u32[]{:S(2)}) copy-start(bf16[128,4,512]{2,1,0:T(4,128)(2,1)} %param.14) | copy-start | bytes 1572868
  1.4 8.1 %copy-start = (bf16[2048,512]{1,0:T(8,128)(2,1)S(1)}, bf16[2048,512]{1,0:T(8,128)(2,1)}, u32[]{:S(2)}) copy-start(bf16[2048,512]{1,0:T(8,128)(2,1)} %weight) | copy-start | bytes 6291460
  2.3 16.8 %collective-permute-start.2 = (bf16[3,128,512]{2,1,0:T(8,128)(2,1)}, bf16[3,128,512]{2,1,0:T(8,128)(2,1)S(1)}, u32[]{:S(2)}, u32[]{:S(2)}) collective-permute-start(bf16[3,128,512]{2,1,0:T(8,128)(2,1)} %bitcast.25), channel_id=1, source_target_pairs={{2,4},{4,2},{6,8},{8,6},{10,12},{12,10},{3,5},{5,3},{7,9},{9,7},{1... | collective-permute-start | bytes 1179656 | tf_op jit(solution)/shard_map/ppermute | solution.py:505
  5.4 1.9 %collective-permute-start = (bf16[4,8,512]{2,1,0:T(8,128)(2,1)S(1)}, bf16[4,8,512]{2,1,0:T(8,128)(2,1)S(1)}, u32[]{:S(2)}, u32[]{:S(2)}) collective-permute-start(bf16[4,8,512]{2,1,0:T(8,128)(2,1)S(1)} %dynamic-slice_bitcast_fusion.1), channel_id=1, source_target_pairs={{0,1},{1,0},{2,3},{3,2},{4,5},{5,4},{6,7},{7,6},{8,9},{9,8},{10,11... | collective-permute-start | bytes 98312 | tf_op jit(solution)/shard_map/ppermute | solution.py:506
  8.1 22.2 %collective-permute-start.1 = (bf16[3,136,512]{2,1,0:T(8,128)(2,1)}, bf16[3,136,512]{2,1,0:T(8,128)(2,1)}, u32[]{:S(2)}, u32[]{:S(2)}) collective-permute-start(bf16[3,136,512]{2,1,0:T(8,128)(2,1)} %pad_maximum_fusion), channel_id=1, source_target_pairs={{0,2},{2,0},{4,6},{6,4},{8,10},{10,8},{12,14},{14,12},{1,3},{3,1},... | collective-permute-start | bytes 1253384 | tf_op jit(solution)/shard_map/ppermute | solution.py:510
  9.5 6.7 %copy-start.3 = (f32[7,7,512]{2,1,0:T(8,128)S(1)}, f32[7,7,512]{2,1,0:T(8,128)}, u32[]{:S(2)}) copy-start(f32[7,7,512]{2,1,0:T(8,128)} %kernel.1) | copy-start | bytes 301060
  9.5 6.7 %copy-start.4 = (f32[512]{0:T(512)S(1)}, f32[512]{0:T(512)}, u32[]{:S(2)}) copy-start(f32[512]{0:T(512)} %param.16) | copy-start | bytes 6148
  14.5 1.0 %copy-start.1 = (f32[512,512]{1,0:T(8,128)}, f32[512,512]{1,0:T(8,128)S(1)}, u32[]{:S(2)}) copy-start(f32[512,512]{1,0:T(8,128)S(1)} %get-tuple-element.31.home_anywhere) | copy-start | bytes 3145732
  15.5 4.2 %collective-permute-start.4 = (bf16[256,512]{1,0:T(8,128)(2,1)}, bf16[256,512]{1,0:T(8,128)(2,1)S(1)}, u32[]{:S(2)}, u32[]{:S(2)}) collective-permute-start(bf16[256,512]{1,0:T(8,128)(2,1)} %get-tuple-element.40), channel_id=1, source_target_pairs={{0,1},{1,0},{2,3},{3,2},{4,5},{5,4},{6,7},{7,6},{8,9},{9,8},{10,11... | collective-permute-start | bytes 786440 | tf_op jit(solution)/shard_map/ppermute | solution.py:437
  16.1 3.6 %collective-permute-start.5 = (bf16[256,512]{1,0:T(8,128)(2,1)S(1)}, bf16[256,512]{1,0:T(8,128)(2,1)S(1)}, u32[]{:S(2)}, u32[]{:S(2)}) collective-permute-start(bf16[256,512]{1,0:T(8,128)(2,1)S(1)} %get-tuple-element.41), channel_id=1, source_target_pairs={{0,1},{1,0},{2,3},{3,2},{4,5},{5,4},{6,7},{7,6},{8,9},{9,8},{10,11... | collective-permute-start | bytes 786440 | tf_op jit(solution)/shard_map/ppermute | solution.py:437
  19.1 8.7 %collective-permute-start.3 = (bf16[3,8,512]{2,1,0:T(8,128)(2,1)S(1)}, bf16[3,8,512]{2,1,0:T(8,128)(2,1)S(1)}, u32[]{:S(2)}, u32[]{:S(2)}) collective-permute-start(bf16[3,8,512]{2,1,0:T(8,128)(2,1)S(1)} %constant_dynamic-slice_fusion), channel_id=1, source_target_pairs={{0,1},{1,0},{2,3},{3,2},{4,5},{5,4},{6,7},{7,6},{8,9},{9,8},{10,11... | collective-permute-start | bytes 73736 | tf_op jit(solution)/shard_map/ppermute | solution.py:529
  19.6 10.6 %copy-start.8 = (f32[512]{0:T(512)S(1)}, f32[512]{0:T(512)}, u32[]{:S(2)}) copy-start(f32[512]{0:T(512)} %param.18) | copy-start | bytes 6148
  19.7 1.2 %copy-start.2 = (f32[512,512]{1,0:T(8,128)S(1)}, f32[512,512]{1,0:T(8,128)}, u32[]{:S(2)}) copy-start(f32[512,512]{1,0:T(8,128)} %copy-done.1) | copy-start | bytes 3145732
  21.0 9.3 %copy-start.7 = (f32[2048]{0:T(1024)S(1)}, f32[2048]{0:T(1024)}, u32[]{:S(2)}) copy-start(f32[2048]{0:T(1024)} %param.20) | copy-start | bytes 24580
  21.0 9.3 %copy-start.9 = (f32[512]{0:T(512)S(1)}, f32[512]{0:T(512)}, u32[]{:S(2)}) copy-start(f32[512]{0:T(512)} %param.17) | copy-start | bytes 6148
  22.1 13.9 %collective-permute-start.6 = (bf16[4,32,512]{2,1,0:T(8,128)(2,1)S(1)}, bf16[4,32,512]{2,1,0:T(8,128)(2,1)S(1)}, u32[]{:S(2)}, u32[]{:S(2)}) collective-permute-start(bf16[4,32,512]{2,1,0:T(8,128)(2,1)S(1)} %get-tuple-element.42), channel_id=1, source_target_pairs={{0,0},{1,8},{2,2},{3,10},{4,4},{5,12},{6,6},{7,14},{8,1},{9,9},{10... | collective-permute-start | bytes 393224 | tf_op jit(solution)/shard_map/ppermute | solution.py:467
  24.7 11.2 %collective-permute-start.7 = (bf16[4,32,512]{2,1,0:T(8,128)(2,1)S(1)}, bf16[4,32,512]{2,1,0:T(8,128)(2,1)S(1)}, u32[]{:S(2)}, u32[]{:S(2)}) collective-permute-start(bf16[4,32,512]{2,1,0:T(8,128)(2,1)S(1)} %get-tuple-element.43), channel_id=1, source_target_pairs={{0,2},{1,10},{2,4},{3,12},{4,6},{5,14},{6,0},{7,8},{8,3},{9,11},{1... | collective-permute-start | bytes 393224 | tf_op jit(solution)/shard_map/ppermute | solution.py:467
  26.5 10.2 %collective-permute-start.8 = (bf16[4,32,512]{2,1,0:T(8,128)(2,1)S(1)}, bf16[4,32,512]{2,1,0:T(8,128)(2,1)S(1)}, u32[]{:S(2)}, u32[]{:S(2)}) collective-permute-start(bf16[4,32,512]{2,1,0:T(8,128)(2,1)S(1)} %get-tuple-element.44), channel_id=1, source_target_pairs={{0,4},{1,12},{2,6},{3,14},{4,0},{5,8},{6,2},{7,10},{8,5},{9,13},{1... | collective-permute-start | bytes 393224 | tf_op jit(solution)/shard_map/ppermute | solution.py:467
  27.7 9.0 %collective-permute-start.9 = (bf16[4,32,512]{2,1,0:T(8,128)(2,1)S(1)}, bf16[4,32,512]{2,1,0:T(8,128)(2,1)S(1)}, u32[]{:S(2)}, u32[]{:S(2)}) collective-permute-start(bf16[4,32,512]{2,1,0:T(8,128)(2,1)S(1)} %get-tuple-element.45), channel_id=1, source_target_pairs={{0,6},{1,14},{2,0},{3,8},{4,2},{5,10},{6,4},{7,12},{8,7},{9,15},{1... | collective-permute-start | bytes 393224 | tf_op jit(solution)/shard_map/ppermute | solution.py:467
  30.3 6.5 %copy-start.5 = (bf16[512,2048]{1,0:T(8,128)(2,1)S(1)}, bf16[512,2048]{1,0:T(8,128)(2,1)}, u32[]{:S(2)}) copy-start(bf16[512,2048]{1,0:T(8,128)(2,1)} %w_in.1) | copy-start | bytes 6291460
  30.3 6.5 %copy-start.6 = (bf16[2048,512]{1,0:T(8,128)(2,1)S(1)}, bf16[2048,512]{1,0:T(8,128)(2,1)}, u32[]{:S(2)}) copy-start(bf16[2048,512]{1,0:T(8,128)(2,1)} %w_out.1) | copy-start | bytes 6291460
  30.3 6.4 %copy-start.10 = (f32[512]{0:T(512)S(1)}, f32[512]{0:T(512)}, u32[]{:S(2)}) copy-start(f32[512]{0:T(512)} %param.22) | copy-start | bytes 6148
  30.3 6.4 %copy-start.11 = (f32[512]{0:T(512)S(1)}, f32[512]{0:T(512)}, u32[]{:S(2)}) copy-start(f32[512]{0:T(512)} %param.23) | copy-start | bytes 6148
  42.1 17.8 %collective-permute-start.10 = (bf16[3,128,512]{2,1,0:T(8,128)(2,1)S(1)}, bf16[3,128,512]{2,1,0:T(8,128)(2,1)S(1)}, u32[]{:S(2)}, u32[]{:S(2)}) collective-permute-start(bf16[3,128,512]{2,1,0:T(8,128)(2,1)S(1)} %get-tuple-element.46), channel_id=1, source_target_pairs={{0,2},{2,0},{4,6},{6,4},{8,10},{10,8},{12,14},{14,12},{1,3},{3,1},... | collective-permute-start | bytes 1179656 | tf_op jit(solution)/shard_map/ppermute | solution.py:572
  44.8 15.1 %collective-permute-start.11 = (bf16[3,128,512]{2,1,0:T(8,128)(2,1)S(1)}, bf16[3,128,512]{2,1,0:T(8,128)(2,1)S(1)}, u32[]{:S(2)}, u32[]{:S(2)}) collective-permute-start(bf16[3,128,512]{2,1,0:T(8,128)(2,1)S(1)} %get-tuple-element.47), channel_id=1, source_target_pairs={{2,4},{4,2},{6,8},{8,6},{10,12},{12,10},{3,5},{5,3},{7,9},{9,7},{1... | collective-permute-start | bytes 1179656 | tf_op jit(solution)/shard_map/ppermute | solution.py:573
  48.6 2.9 %collective-permute-start.14 = (bf16[4,8,512]{2,1,0:T(8,128)(2,1)S(1)}, bf16[4,8,512]{2,1,0:T(8,128)(2,1)S(1)}, u32[]{:S(2)}, u32[]{:S(2)}) collective-permute-start(bf16[4,8,512]{2,1,0:T(8,128)(2,1)S(1)} %get-tuple-element.51), channel_id=1, source_target_pairs={{0,1},{1,0},{2,3},{3,2},{4,5},{5,4},{6,7},{7,6},{8,9},{9,8},{10,11... | collective-permute-start | bytes 98312 | tf_op jit(solution)/shard_map/ppermute | solution.py:574
  48.7 10.3 %collective-permute-start.12 = (bf16[3,8,512]{2,1,0:T(8,128)(2,1)S(1)}, bf16[3,8,512]{2,1,0:T(8,128)(2,1)S(1)}, u32[]{:S(2)}, u32[]{:S(2)}) collective-permute-start(bf16[3,8,512]{2,1,0:T(8,128)(2,1)S(1)} %get-tuple-element.48), channel_id=1, source_target_pairs={{0,3},{1,2},{2,1},{3,0},{4,7},{5,6},{6,5},{7,4},{8,11},{9,10},{10,... | collective-permute-start | bytes 73736 | tf_op jit(solution)/shard_map/ppermute | solution.py:575
  49.5 9.4 %collective-permute-start.13 = (bf16[3,8,512]{2,1,0:T(8,128)(2,1)S(1)}, bf16[3,8,512]{2,1,0:T(8,128)(2,1)S(1)}, u32[]{:S(2)}, u32[]{:S(2)}) collective-permute-start(bf16[3,8,512]{2,1,0:T(8,128)(2,1)S(1)} %get-tuple-element.49), channel_id=1, source_target_pairs={{2,5},{3,4},{4,3},{5,2},{6,9},{7,8},{8,7},{9,6},{10,13},{11,12},{1... | collective-permute-start | bytes 73736 | tf_op jit(solution)/shard_map/ppermute | solution.py:576

commit v11 on v8

--- a/solution.py
+++ b/solution.py
@@ -14,7 +14,8 @@
 SUBLANES = 8
 EDGE = 8
 CHUNK = 16
-UNROLL = 16
+UNROLL = 32
+GROUP = 4
 COPIES = 8
 DOTS = 2
 MLP_TILE = 512
@@ -87,13 +88,13 @@
 
 def depthwise(padded, taps, begin, store, tile_u, count, offset, sources, flip):
     tiles = padded.shape[0]
-    blocks = count // (2 * SUBLANES)
+    blocks = count // (GROUP * SUBLANES)
 
     def step(index, carry):
         tile = index // blocks
-        base = pl.multiple_of((index % blocks) * (2 * SUBLANES), 2 * SUBLANES)
+        base = pl.multiple_of((index % blocks) * (GROUP * SUBLANES), GROUP * SUBLANES)
         sums = [
-            [begin(tile, u, base + half * SUBLANES) for u in range(tile_u)] for half in range(2)
+            [begin(tile, u, base + half * SUBLANES) for u in range(tile_u)] for half in range(GROUP)
         ]
         for row_tap in range(TAPS):
             weights = []
@@ -101,13 +102,13 @@
                 tap = row_tap * TAPS + col_tap
                 weights.append(taps[TAPS * TAPS - 1 - tap if flip else tap, tile])
             for place, source in enumerate(sources):
-                for half in range(2):
+                for half in range(GROUP):
                     row = base + (half * SUBLANES + row_tap) + offset
                     values = padded[tile, place, pl.ds(row, SUBLANES), :]
                     for u in range(max(0, source - TAPS + 1), min(tile_u, source + 1)):
                         term = weights[source - u] * values
                         sums[half][u] = term if sums[half][u] is None else sums[half][u] + term
-        for half in range(2):
+        for half in range(GROUP):
             for u in range(tile_u):
                 store(tile, u, base + half * SUBLANES, sums[half][u])
         return carry

time: 64.4 us -> 64 us (level)
  Pallas kernels: 29.1 us -> 27.4 us
  waiting for transfers between devices: 9.33 us -> 10.9 us
    ppermute x1, waiting for transfers between devices: 7.2 us -> 9.31 us  [on_device(): lax.ppermute(even_edge, ('row', 'col'), across(row_pairs(False)))]
    pallas_call x9, Pallas kernels: 29.1 us -> 27.4 us  [call(): pl.pallas_call(kernel, out_shape=tuple(outs), in_specs=[smem] * len(scala...]
    ppermute x1, waiting for transfers between devices: 0.29 us -> 1.36 us  [on_device(): second_side = lax.ppermute(second_block, 'row', row_pairs(False))]
    ppermute x1, waiting for transfers between devices: 0.81 us -> 0.01 us  [on_device(): even = lax.ppermute(even, 'row', row_pairs(False))]
    ppermute x4, waiting for transfers between devices: 1.01 us -> 0.22 us  [find_target(): pieces.append(lax.ppermute(blocks[turn], ('row', 'col'), pairs))]
  transfers between devices with their start and end apart: 15 -> 15, of which waited for: 4 -> 3; matrix products, arithmetic and copies ran while one was open for 3% -> 3% of each run, Pallas kernels for 31% -> 30%
where the time goes in v11:
time: 64 us; the launch traced here: 63.8 us
  Pallas kernels  27.4 us (43%)
  starting transfers between devices  21.9 us (34%)
  waiting for transfers between devices  10.9 us (17%)
  local copies, waits for them, and re-layouts  2.22 us (3%)
  other arithmetic  1.01 us (2%)
    pallas_call x9, Pallas kernels, call(): pl.pallas_call(kernel, out_shape=tuple(outs), in_specs=[smem] * len(scala...  27.4 us
    ppermute x1, waiting for transfers between devices, on_device(): lax.ppermute(even_edge, ('row', 'col'), across(row_pairs(False)))  9.31 us
    ppermute x4, starting transfers between devices, find_target(): pieces.append(lax.ppermute(blocks[turn], ('row', 'col'), pairs))  6.23 us
    ppermute x1, starting transfers between devices, on_device(): odd = lax.ppermute(odd, 'row', row_pairs(True))  3 us
    ppermute x1, starting transfers between devices, on_device(): first_side = lax.ppermute(first_block, 'row', row_pairs(True))  2.99 us
    ppermute x1, starting transfers between devices, on_device(): even = lax.ppermute(even, 'row', row_pairs(False))  2.65 us
    ppermute x1, starting transfers between devices, on_device(): odd_edge = lax.ppermute(odd_edge, ('row', 'col'), across(row_pairs(True)))  1.91 us
    ppermute x1, starting transfers between devices, on_device(): lax.ppermute(even_edge, ('row', 'col'), across(row_pairs(False)))  1.68 us
  transfers between devices with their start and end apart: 15, of which 3 were waited for; matrix products, arithmetic and copies ran while one was open for 3% of the time, Pallas kernels for 30%

profile of v11, /device:TPU:13, one launch (start us, length us, event | category | flops | bytes accessed | tf_op | source)
XLA Modules:
  0.0 63.8 jit_solution(15020510244785698816)
XLA Ops:
  0.0 1.3 %copy.19 = bf16[128,4,512]{2,0,1:T(8,128)(2,1)S(1)} copy(bf16[128,4,512]{2,1,0:T(4,128)(2,1)} %param.14) | data formatting | bytes 1048576 | tf_op args[2]
  1.3 0.7 %collective-permute-start = (bf16[4,8,512]{2,1,0:T(8,128)(2,1)S(1)}, bf16[4,8,512]{2,1,0:T(8,128)(2,1)S(1)}, u32[]{:S(2)}, u32[]{:S(2)}) collective-permute-start(bf16[4,8,512]{2,1,0:T(8,128)(2,1)S(1)} %dynamic-slice_bitcast_fusion.2), channel_id=1, source_target_pairs={{0,1},{1,0},{2,3},{3,2},{4,5},{5,4},{6,7},{7,6},{8,9},{9,8},{10,11... | collective-permute-start | bytes 98312 | tf_op jit(solution)/shard_map/ppermute | solution.py:480
  2.1 0.8 %dynamic-slice_bitcast_fusion = (bf16[3,128,512]{2,1,0:T(8,128)(2,1)}, bf16[3,128,512]{2,1,0:T(8,128)(2,1)S(1)}) fusion(bf16[128,4,512]{2,0,1:T(8,128)(2,1)S(1)} %copy.19, s32[]{:T(128)S(6)} %select_n.33, s32[]{:T(128)S(6)} %select_n.31), kind=kLoop, calls=%fused_computation.1 | loop fusion | bytes 1572872 | tf_op jit(solution)/shard_map/dynamic_slice | solution.py:379
  2.9 3.0 %collective-permute-start.2 = (bf16[3,128,512]{2,1,0:T(8,128)(2,1)}, bf16[3,128,512]{2,1,0:T(8,128)(2,1)S(1)}, u32[]{:S(2)}, u32[]{:S(2)}) collective-permute-start(bf16[3,128,512]{2,1,0:T(8,128)(2,1)} %get-tuple-element.45), channel_id=1, source_target_pairs={{2,4},{4,2},{6,8},{8,6},{10,12},{12,10},{3,5},{5,3},{7,9},{9,7},{1... | collective-permute-start | bytes 1179656 | tf_op jit(solution)/shard_map/ppermute | solution.py:479
  5.9 0.8 %pad_maximum_fusion = bf16[3,136,512]{2,1,0:T(8,128)(2,1)} fusion(bf16[3,8,512]{2,1,0:T(8,128)(2,1)S(1)} %constant_dynamic-slice_fusion.1, bf16[3,128,512]{2,1,0:T(8,128)(2,1)S(1)} %get-tuple-element.46), kind=kLoop, calls=%fused_computation | loop fusion | flops 835584 | bytes 835584 | tf_op jit(solution)/shard_map/concatenate | solution.py:481
  6.7 3.4 %project_away.1 = (bf16[256,512]{1,0:T(8,128)(2,1)}, bf16[256,512]{1,0:T(8,128)(2,1)}) custom-call(s32[1]{0:T(128)} %bitcast.core_ref, bf16[32,2,16,2048]{3,2,1,0:T(8,128)(2,1)} %bitcast.34, bf16[2048,512]{1,0:T(8,128)(2,1)S(1)} %copy-done), custom_call_target="tpu_custom_call" | custom-call | flops 1 | bytes 1 | tf_op jit(solution)/shard_map/project_away/pallas_call | solution.py:359
  10.1 0.4 collective-permute-start.3
  10.5 0.2 collective-permute-start.4
  10.7 1.4 %collective-permute-start.1 = (bf16[3,136,512]{2,1,0:T(8,128)(2,1)}, bf16[3,136,512]{2,1,0:T(8,128)(2,1)S(1)}, u32[]{:S(2)}, u32[]{:S(2)}) collective-permute-start(bf16[3,136,512]{2,1,0:T(8,128)(2,1)} %pad_maximum_fusion), channel_id=1, source_target_pairs={{0,2},{2,0},{4,6},{6,4},{8,10},{10,8},{12,14},{14,12},{1,3},{3,1},... | collective-permute-start | bytes 1253384 | tf_op jit(solution)/shard_map/ppermute | solution.py:484
  12.1 0.1 pad_add_fusion.place_ref
  12.1 0.1 pad_add_fusion.2.turns_ref
  12.2 2.7 %project_home.1.home = f32[512,512]{1,0:T(8,128)S(1)} custom-call(s32[1]{0:T(128)} %bitcast.core_ref, bf16[32,2,16,2048]{3,2,1,0:T(8,128)(2,1)} %bitcast.35, bf16[2048,512]{1,0:T(8,128)(2,1)S(1)} %copy-done), custom_call_target="tpu_custom_call" | custom-call | flops 1 | bytes 1 | tf_op jit(solution)/shard_map/project_home/pallas_call | solution.py:359
  15.0 1.1 %combine.1 = (bf16[4,32,512]{2,1,0:T(8,128)(2,1)S(1)}, bf16[4,32,512]{2,1,0:T(8,128)(2,1)S(1)}, bf16[4,32,512]{2,1,0:T(8,128)(2,1)S(1)}, bf16[4,32,512]{2,1,0:T(8,128)(2,1)S(1)}) custom-call(s32[4]{0:T(128)S(1)} %pad_add_fusion.2.turns_ref, f32[512,512]{1,0:T(8,128)S(1)} %project_home.1.home, bf16[256,512]{1,0:T(8,128)(2,1)S(1)} %collective-permute-done.3.upper, ...), custom_call_target="tpu_custom_call" | custom-call | flops 1 | bytes 1 | tf_op jit(solution)/shard_map/combine/pallas_call | solution.py:359
  16.1 2.5 %inner_up.1.inner = f32[4,128,512]{2,1,0:T(8,128)S(1)} custom-call(s32[1]{0:T(128)} %bitcast.core_ref, bf16[4,128,512]{2,1,0:T(8,128)(2,1)S(1)} %bitcast.25, bf16[4,8,512]{2,1,0:T(8,128)(2,1)S(1)} %copy-done.3, f32[7,7,512]{2,1,0:T(8,128)S(1)} %copy-done.1, f32[1,512]{1,0:T(1,128)S(1)} %bitcast.27), custom_call_target="tpu_custom_call" | custom-call | flops 1 | bytes 1 | tf_op jit(solution)/shard_map/inner_up/pallas_call | solution.py:359
  18.6 0.7 %collective-permute-start.5 = (bf16[3,8,512]{2,1,0:T(8,128)(2,1)S(1)}, bf16[3,8,512]{2,1,0:T(8,128)(2,1)S(1)}, u32[]{:S(2)}, u32[]{:S(2)}) collective-permute-start(bf16[3,8,512]{2,1,0:T(8,128)(2,1)S(1)} %constant_dynamic-slice_fusion), channel_id=1, source_target_pairs={{0,1},{1,0},{2,3},{3,2},{4,5},{5,4},{6,7},{7,6},{8,9},{9,8},{10,11... | collective-permute-start | bytes 73736 | tf_op jit(solution)/shard_map/ppermute | solution.py:503
  19.3 0.1 pad_add_fusion.1.places_ref
  19.3 2.6 %collective-permute-start.6 = (bf16[4,32,512]{2,1,0:T(8,128)(2,1)S(1)}, bf16[4,32,512]{2,1,0:T(8,128)(2,1)S(1)}, u32[]{:S(2)}, u32[]{:S(2)}) collective-permute-start(bf16[4,32,512]{2,1,0:T(8,128)(2,1)S(1)} %get-tuple-element.28), channel_id=1, source_target_pairs={{0,0},{1,8},{2,2},{3,10},{4,4},{5,12},{6,6},{7,14},{8,1},{9,9},{10... | collective-permute-start | bytes 393224 | tf_op jit(solution)/shard_map/ppermute | solution.py:443
  22.0 1.8 %collective-permute-start.7 = (bf16[4,32,512]{2,1,0:T(8,128)(2,1)S(1)}, bf16[4,32,512]{2,1,0:T(8,128)(2,1)S(1)}, u32[]{:S(2)}, u32[]{:S(2)}) collective-permute-start(bf16[4,32,512]{2,1,0:T(8,128)(2,1)S(1)} %get-tuple-element.35), channel_id=1, source_target_pairs={{0,2},{1,10},{2,4},{3,12},{4,6},{5,14},{6,0},{7,8},{8,3},{9,11},{1... | collective-permute-start | bytes 393224 | tf_op jit(solution)/shard_map/ppermute | solution.py:443
  23.7 1.2 %collective-permute-start.8 = (bf16[4,32,512]{2,1,0:T(8,128)(2,1)S(1)}, bf16[4,32,512]{2,1,0:T(8,128)(2,1)S(1)}, u32[]{:S(2)}, u32[]{:S(2)}) collective-permute-start(bf16[4,32,512]{2,1,0:T(8,128)(2,1)S(1)} %get-tuple-element.36), channel_id=1, source_target_pairs={{0,4},{1,12},{2,6},{3,14},{4,0},{5,8},{6,2},{7,10},{8,5},{9,13},{1... | collective-permute-start | bytes 393224 | tf_op jit(solution)/shard_map/ppermute | solution.py:443
  24.9 0.6 collective-permute-start.9
  25.6 1.8 %side_up.1.inner = f32[4,128,512]{2,1,0:T(8,128)S(1)} custom-call(s32[2]{0:T(128)S(1)} %pad_add_fusion.place_ref, bf16[3,128,512]{2,1,0:T(8,128)(2,1)S(1)} %collective-permute-done.2.side, bf16[3,8,512]{2,1,0:T(8,128)(2,1)S(1)} %collective-permute-done.5.edge, f32[7,7,512]{2,1,0:T(8,128)S(1)} %copy-done.1, f32[4,128,512]{2,1,0:T(8,128)S(1)} %inner_up.1.inner), custom_call_target="tpu_custom_call" | custom-call | flops 1 | bytes 1 | tf_op jit(solution)/shard_map/side_up/pallas_call | solution.py:359
  27.3 1.4 %collective-permute-done.1.side = bf16[3,136,512]{2,1,0:T(8,128)(2,1)S(1)} collective-permute-done((bf16[3,136,512]{2,1,0:T(8,128)(2,1)}, bf16[3,136,512]{2,1,0:T(8,128)(2,1)S(1)}, u32[]{:S(2)}, u32[]{:S(2)}) %collective-permute-start.1) | collective-permute-done | bytes 417824 | tf_op jit(solution)/shard_map/ppermute | solution.py:484
  28.8 4.9 %up.1 = (f32[512,512]{1,0:T(8,128)S(1)}, f32[512,128]{1,0:T(8,128)S(1)}, bf16[512,2048]{1,0:T(8,128)(2,1)S(1)}, bf16[512,2048]{1,0:T(8,128)(2,1)S(1)}) custom-call(s32[2]{0:T(128)S(1)} %pad_add_fusion.place_ref, bf16[3,136,512]{2,1,0:T(8,128)(2,1)S(1)} %collective-permute-done.1.side, f32[7,7,512]{2,1,0:T(8,128)S(1)} %copy-done.1, ...), custom_call_target="tpu_custom_call" | custom-call | flops 4294967296 | bytes 9181184 | tf_op jit(solution)/shard_map/up/pallas_call | solution.py:359
  33.7 0.2 collective-permute-done.8.rest_2_
  34.0 4.8 %back.1 = (f32[4,128,512]{2,1,0:T(8,128)S(1)}, bf16[4,128,512]{2,1,0:T(8,128)(2,1)S(1)}, bf16[3,128,512]{2,1,0:T(8,128)(2,1)S(1)}, bf16[3,128,512]{2,1,0:T(8,128...) custom-call(s32[2]{0:T(128)S(1)} %pad_add_fusion.place_ref, ...), custom_call_target="tpu_custom_call" | custom-call | flops 4294967296 | bytes 13195264 | tf_op jit(solution)/shard_map/back/pallas_call | solution.py:359
  38.8 2.7 %collective-permute-start.10 = (bf16[3,128,512]{2,1,0:T(8,128)(2,1)S(1)}, bf16[3,128,512]{2,1,0:T(8,128)(2,1)S(1)}, u32[]{:S(2)}, u32[]{:S(2)}) collective-permute-start(bf16[3,128,512]{2,1,0:T(8,128)(2,1)S(1)} %get-tuple-element.38), channel_id=1, source_target_pairs={{0,2},{2,0},{4,6},{6,4},{8,10},{10,8},{12,14},{14,12},{1,3},{3,1},... | collective-permute-start | bytes 1179656 | tf_op jit(solution)/shard_map/ppermute | solution.py:546
  41.4 3.0 %collective-permute-start.11 = (bf16[3,128,512]{2,1,0:T(8,128)(2,1)S(1)}, bf16[3,128,512]{2,1,0:T(8,128)(2,1)S(1)}, u32[]{:S(2)}, u32[]{:S(2)}) collective-permute-start(bf16[3,128,512]{2,1,0:T(8,128)(2,1)S(1)} %get-tuple-element.39), channel_id=1, source_target_pairs={{2,4},{4,2},{6,8},{8,6},{10,12},{12,10},{3,5},{5,3},{7,9},{9,7},{1... | collective-permute-start | bytes 1179656 | tf_op jit(solution)/shard_map/ppermute | solution.py:547
  44.5 1.7 %collective-permute-start.12 = (bf16[3,8,512]{2,1,0:T(8,128)(2,1)S(1)}, bf16[3,8,512]{2,1,0:T(8,128)(2,1)S(1)}, u32[]{:S(2)}, u32[]{:S(2)}) collective-permute-start(bf16[3,8,512]{2,1,0:T(8,128)(2,1)S(1)} %get-tuple-element.40), channel_id=1, source_target_pairs={{0,3},{1,2},{2,1},{3,0},{4,7},{5,6},{6,5},{7,4},{8,11},{9,10},{10,... | collective-permute-start | bytes 73736 | tf_op jit(solution)/shard_map/ppermute | solution.py:549
  46.2 1.9 %collective-permute-start.13 = (bf16[3,8,512]{2,1,0:T(8,128)(2,1)S(1)}, bf16[3,8,512]{2,1,0:T(8,128)(2,1)S(1)}, u32[]{:S(2)}, u32[]{:S(2)}) collective-permute-start(bf16[3,8,512]{2,1,0:T(8,128)(2,1)S(1)} %get-tuple-element.41), channel_id=1, source_target_pairs={{2,5},{3,4},{4,3},{5,2},{6,9},{7,8},{8,7},{9,6},{10,13},{11,12},{1... | collective-permute-start | bytes 73736 | tf_op jit(solution)/shard_map/ppermute | solution.py:550
  48.1 2.5 %inner_last.1.inner = f32[4,128,512]{2,1,0:T(8,128)S(1)} custom-call(s32[1]{0:T(128)} %bitcast.core_ref, bf16[4,128,512]{2,1,0:T(8,128)(2,1)S(1)} %get-tuple-element.42.middle, bf16[4,8,512]{2,1,0:T(8,128)(2,1)S(1)} %collective-permute-done.14.edge, f32[7,7,512]{2,1,0:T(8,128)S(1)} %copy-done.1, f32[4,128,512]{2,1,0:T(8,128)S(1)} %get-tuple-element.44.base_value), custom_call_target="tpu_custom_call" | custom-call | flops 1073741824 | bytes 2754560 | tf_op jit(solution)/shard_map/inner_last/pallas_call | solution.py:359
  50.7 9.3 %collective-permute-done.12.even_edge = bf16[3,8,512]{2,1,0:T(8,128)(2,1)S(1)} collective-permute-done((bf16[3,8,512]{2,1,0:T(8,128)(2,1)S(1)}, bf16[3,8,512]{2,1,0:T(8,128)(2,1)S(1)}, u32[]{:S(2)}, u32[]{:S(2)}) %collective-permute-start.12) | collective-permute-done | bytes 24608 | tf_op jit(solution)/shard_map/ppermute | solution.py:549
  60.0 3.8 %last.1 = f32[128,4,512]{2,1,0:T(4,128)} custom-call(s32[2]{0:T(128)S(1)} %pad_add_fusion.place_ref, bf16[3,128,512]{2,1,0:T(8,128)(2,1)S(1)} %collective-permute-done.10.even, bf16[3,128,512]{2,1,0:T(8,128)(2,1)S(1)} %collective-permute-done.11.odd, bf16[3,8,512]{2,1,0:T(8,128)(2,1)S(1)} %collective-permute-done.12.even_edge, ...), custom_call_target="tpu_custom_call" | custom-call | flops 1 | bytes 1 | tf_op jit(solution)/shard_map/last/pallas_call | solution.py:359
  (40 shorter events, 0.2 us)
Async XLA Ops:
  0.0 6.7 %copy-start = (bf16[2048,512]{1,0:T(8,128)(2,1)S(1)}, bf16[2048,512]{1,0:T(8,128)(2,1)}, u32[]{:S(2)}) copy-start(bf16[2048,512]{1,0:T(8,128)(2,1)} %weight.1) | copy-start | bytes 6291460
  1.3 4.6 %collective-permute-start = (bf16[4,8,512]{2,1,0:T(8,128)(2,1)S(1)}, bf16[4,8,512]{2,1,0:T(8,128)(2,1)S(1)}, u32[]{:S(2)}, u32[]{:S(2)}) collective-permute-start(bf16[4,8,512]{2,1,0:T(8,128)(2,1)S(1)} %dynamic-slice_bitcast_fusion.2), channel_id=1, source_target_pairs={{0,1},{1,0},{2,3},{3,2},{4,5},{5,4},{6,7},{7,6},{8,9},{9,8},{10,11... | collective-permute-start | bytes 98312 | tf_op jit(solution)/shard_map/ppermute | solution.py:480
  2.9 15.7 %collective-permute-start.2 = (bf16[3,128,512]{2,1,0:T(8,128)(2,1)}, bf16[3,128,512]{2,1,0:T(8,128)(2,1)S(1)}, u32[]{:S(2)}, u32[]{:S(2)}) collective-permute-start(bf16[3,128,512]{2,1,0:T(8,128)(2,1)} %get-tuple-element.45), channel_id=1, source_target_pairs={{2,4},{4,2},{6,8},{8,6},{10,12},{12,10},{3,5},{5,3},{7,9},{9,7},{1... | collective-permute-start | bytes 1179656 | tf_op jit(solution)/shard_map/ppermute | solution.py:479
  5.9 4.2 %copy-start.2 = (bf16[4,8,512]{2,1,0:T(8,128)(2,1)}, bf16[4,8,512]{2,1,0:T(8,128)(2,1)S(1)}, u32[]{:S(2)}) copy-start(bf16[4,8,512]{2,1,0:T(8,128)(2,1)S(1)} %collective-permute-done.edge) | copy-start | bytes 98308
  10.1 4.8 %collective-permute-start.3 = (bf16[256,512]{1,0:T(8,128)(2,1)}, bf16[256,512]{1,0:T(8,128)(2,1)S(1)}, u32[]{:S(2)}, u32[]{:S(2)}) collective-permute-start(bf16[256,512]{1,0:T(8,128)(2,1)} %get-tuple-element.26), channel_id=1, source_target_pairs={{0,1},{1,0},{2,3},{3,2},{4,5},{5,4},{6,7},{7,6},{8,9},{9,8},{10,11... | collective-permute-start | bytes 786440 | tf_op jit(solution)/shard_map/ppermute | solution.py:418
  10.5 4.5 %collective-permute-start.4 = (bf16[256,512]{1,0:T(8,128)(2,1)}, bf16[256,512]{1,0:T(8,128)(2,1)S(1)}, u32[]{:S(2)}, u32[]{:S(2)}) collective-permute-start(bf16[256,512]{1,0:T(8,128)(2,1)} %get-tuple-element.27), channel_id=1, source_target_pairs={{0,1},{1,0},{2,3},{3,2},{4,5},{5,4},{6,7},{7,6},{8,9},{9,8},{10,11... | collective-permute-start | bytes 786440 | tf_op jit(solution)/shard_map/ppermute | solution.py:418
  10.7 18.0 %collective-permute-start.1 = (bf16[3,136,512]{2,1,0:T(8,128)(2,1)}, bf16[3,136,512]{2,1,0:T(8,128)(2,1)S(1)}, u32[]{:S(2)}, u32[]{:S(2)}) collective-permute-start(bf16[3,136,512]{2,1,0:T(8,128)(2,1)} %pad_maximum_fusion), channel_id=1, source_target_pairs={{0,2},{2,0},{4,6},{6,4},{8,10},{10,8},{12,14},{14,12},{1,3},{3,1},... | collective-permute-start | bytes 1253384 | tf_op jit(solution)/shard_map/ppermute | solution.py:484
  12.2 3.8 %copy-start.1 = (f32[7,7,512]{2,1,0:T(8,128)S(1)}, f32[7,7,512]{2,1,0:T(8,128)}, u32[]{:S(2)}) copy-start(f32[7,7,512]{2,1,0:T(8,128)} %kernel.9) | copy-start | bytes 301060
  12.2 3.8 %copy-start.3 = (bf16[4,8,512]{2,1,0:T(8,128)(2,1)S(1)}, bf16[4,8,512]{2,1,0:T(8,128)(2,1)}, u32[]{:S(2)}) copy-start(bf16[4,8,512]{2,1,0:T(8,128)(2,1)} %copy-done.2) | copy-start | bytes 98308
  12.2 3.8 %copy-start.4 = (f32[512]{0:T(512)S(1)}, f32[512]{0:T(512)}, u32[]{:S(2)}) copy-start(f32[512]{0:T(512)} %param.16) | copy-start | bytes 6148
  16.1 12.6 %copy-start.7 = (f32[2048]{0:T(1024)S(1)}, f32[2048]{0:T(1024)}, u32[]{:S(2)}) copy-start(f32[2048]{0:T(1024)} %param.20) | copy-start | bytes 24580
  16.1 12.6 %copy-start.8 = (f32[512]{0:T(512)S(1)}, f32[512]{0:T(512)}, u32[]{:S(2)}) copy-start(f32[512]{0:T(512)} %param.18) | copy-start | bytes 6148
  16.1 12.6 %copy-start.9 = (f32[512]{0:T(512)S(1)}, f32[512]{0:T(512)}, u32[]{:S(2)}) copy-start(f32[512]{0:T(512)} %param.17) | copy-start | bytes 6148
  18.6 6.3 %collective-permute-start.5 = (bf16[3,8,512]{2,1,0:T(8,128)(2,1)S(1)}, bf16[3,8,512]{2,1,0:T(8,128)(2,1)S(1)}, u32[]{:S(2)}, u32[]{:S(2)}) collective-permute-start(bf16[3,8,512]{2,1,0:T(8,128)(2,1)S(1)} %constant_dynamic-slice_fusion), channel_id=1, source_target_pairs={{0,1},{1,0},{2,3},{3,2},{4,5},{5,4},{6,7},{7,6},{8,9},{9,8},{10,11... | collective-permute-start | bytes 73736 | tf_op jit(solution)/shard_map/ppermute | solution.py:503
  19.3 14.6 %collective-permute-start.6 = (bf16[4,32,512]{2,1,0:T(8,128)(2,1)S(1)}, bf16[4,32,512]{2,1,0:T(8,128)(2,1)S(1)}, u32[]{:S(2)}, u32[]{:S(2)}) collective-permute-start(bf16[4,32,512]{2,1,0:T(8,128)(2,1)S(1)} %get-tuple-element.28), channel_id=1, source_target_pairs={{0,0},{1,8},{2,2},{3,10},{4,4},{5,12},{6,6},{7,14},{8,1},{9,9},{10... | collective-permute-start | bytes 393224 | tf_op jit(solution)/shard_map/ppermute | solution.py:443
  22.0 11.7 %collective-permute-start.7 = (bf16[4,32,512]{2,1,0:T(8,128)(2,1)S(1)}, bf16[4,32,512]{2,1,0:T(8,128)(2,1)S(1)}, u32[]{:S(2)}, u32[]{:S(2)}) collective-permute-start(bf16[4,32,512]{2,1,0:T(8,128)(2,1)S(1)} %get-tuple-element.35), channel_id=1, source_target_pairs={{0,2},{1,10},{2,4},{3,12},{4,6},{5,14},{6,0},{7,8},{8,3},{9,11},{1... | collective-permute-start | bytes 393224 | tf_op jit(solution)/shard_map/ppermute | solution.py:443
  23.7 10.2 %collective-permute-start.8 = (bf16[4,32,512]{2,1,0:T(8,128)(2,1)S(1)}, bf16[4,32,512]{2,1,0:T(8,128)(2,1)S(1)}, u32[]{:S(2)}, u32[]{:S(2)}) collective-permute-start(bf16[4,32,512]{2,1,0:T(8,128)(2,1)S(1)} %get-tuple-element.36), channel_id=1, source_target_pairs={{0,4},{1,12},{2,6},{3,14},{4,0},{5,8},{6,2},{7,10},{8,5},{9,13},{1... | collective-permute-start | bytes 393224 | tf_op jit(solution)/shard_map/ppermute | solution.py:443
  24.9 9.0 %collective-permute-start.9 = (bf16[4,32,512]{2,1,0:T(8,128)(2,1)S(1)}, bf16[4,32,512]{2,1,0:T(8,128)(2,1)S(1)}, u32[]{:S(2)}, u32[]{:S(2)}) collective-permute-start(bf16[4,32,512]{2,1,0:T(8,128)(2,1)S(1)} %get-tuple-element.37), channel_id=1, source_target_pairs={{0,6},{1,14},{2,0},{3,8},{4,2},{5,10},{6,4},{7,12},{8,7},{9,15},{1... | collective-permute-start | bytes 393224 | tf_op jit(solution)/shard_map/ppermute | solution.py:443
  28.7 5.2 %copy-start.5 = (bf16[512,2048]{1,0:T(8,128)(2,1)S(1)}, bf16[512,2048]{1,0:T(8,128)(2,1)}, u32[]{:S(2)}) copy-start(bf16[512,2048]{1,0:T(8,128)(2,1)} %w_in.1) | copy-start | bytes 6291460
  28.7 5.2 %copy-start.6 = (bf16[2048,512]{1,0:T(8,128)(2,1)S(1)}, bf16[2048,512]{1,0:T(8,128)(2,1)}, u32[]{:S(2)}) copy-start(bf16[2048,512]{1,0:T(8,128)(2,1)} %w_out.1) | copy-start | bytes 6291460
  28.7 5.2 %copy-start.10 = (f32[512]{0:T(512)S(1)}, f32[512]{0:T(512)}, u32[]{:S(2)}) copy-start(f32[512]{0:T(512)} %param.22) | copy-start | bytes 6148
  28.8 5.2 %copy-start.11 = (f32[512]{0:T(512)S(1)}, f32[512]{0:T(512)}, u32[]{:S(2)}) copy-start(f32[512]{0:T(512)} %param.23) | copy-start | bytes 6148
  38.8 21.2 %collective-permute-start.10 = (bf16[3,128,512]{2,1,0:T(8,128)(2,1)S(1)}, bf16[3,128,512]{2,1,0:T(8,128)(2,1)S(1)}, u32[]{:S(2)}, u32[]{:S(2)}) collective-permute-start(bf16[3,128,512]{2,1,0:T(8,128)(2,1)S(1)} %get-tuple-element.38), channel_id=1, source_target_pairs={{0,2},{2,0},{4,6},{6,4},{8,10},{10,8},{12,14},{14,12},{1,3},{3,1},... | collective-permute-start | bytes 1179656 | tf_op jit(solution)/shard_map/ppermute | solution.py:546
  41.4 18.6 %collective-permute-start.11 = (bf16[3,128,512]{2,1,0:T(8,128)(2,1)S(1)}, bf16[3,128,512]{2,1,0:T(8,128)(2,1)S(1)}, u32[]{:S(2)}, u32[]{:S(2)}) collective-permute-start(bf16[3,128,512]{2,1,0:T(8,128)(2,1)S(1)} %get-tuple-element.39), channel_id=1, source_target_pairs={{2,4},{4,2},{6,8},{8,6},{10,12},{12,10},{3,5},{5,3},{7,9},{9,7},{1... | collective-permute-start | bytes 1179656 | tf_op jit(solution)/shard_map/ppermute | solution.py:547
  44.4 3.7 %collective-permute-start.14 = (bf16[4,8,512]{2,1,0:T(8,128)(2,1)S(1)}, bf16[4,8,512]{2,1,0:T(8,128)(2,1)S(1)}, u32[]{:S(2)}, u32[]{:S(2)}) collective-permute-start(bf16[4,8,512]{2,1,0:T(8,128)(2,1)S(1)} %get-tuple-element.43), channel_id=1, source_target_pairs={{0,1},{1,0},{2,3},{3,2},{4,5},{5,4},{6,7},{7,6},{8,9},{9,8},{10,11... | collective-permute-start | bytes 98312 | tf_op jit(solution)/shard_map/ppermute | solution.py:548
  44.5 15.5 %collective-permute-start.12 = (bf16[3,8,512]{2,1,0:T(8,128)(2,1)S(1)}, bf16[3,8,512]{2,1,0:T(8,128)(2,1)S(1)}, u32[]{:S(2)}, u32[]{:S(2)}) collective-permute-start(bf16[3,8,512]{2,1,0:T(8,128)(2,1)S(1)} %get-tuple-element.40), channel_id=1, source_target_pairs={{0,3},{1,2},{2,1},{3,0},{4,7},{5,6},{6,5},{7,4},{8,11},{9,10},{10,... | collective-permute-start | bytes 73736 | tf_op jit(solution)/shard_map/ppermute | solution.py:549
  46.2 13.8 %collective-permute-start.13 = (bf16[3,8,512]{2,1,0:T(8,128)(2,1)S(1)}, bf16[3,8,512]{2,1,0:T(8,128)(2,1)S(1)}, u32[]{:S(2)}, u32[]{:S(2)}) collective-permute-start(bf16[3,8,512]{2,1,0:T(8,128)(2,1)S(1)} %get-tuple-element.41), channel_id=1, source_target_pairs={{2,5},{3,4},{4,3},{5,2},{6,9},{7,8},{8,7},{9,6},{10,13},{11,12},{1... | collective-permute-start | bytes 73736 | tf_op jit(solution)/shard_map/ppermute | solution.py:550

commit v12 on v11

--- a/solution.py
+++ b/solution.py
@@ -317,7 +317,8 @@
 
 
 def last_kernel(
-    place_ref, even, odd, even_edge, odd_edge, kernel, inner, out, padded, taps, turned
+    place_ref, even, odd, even_edge, odd_edge, kernel, inner, out,
+    padded, taps, turned, staged, sems,
 ):
     tile_v, tile_u, channels = out.shape
     spread_taps(taps, kernel)
@@ -328,16 +329,31 @@
         def _(left=sides[1 - parity], right=sides[parity]):
             fill(padded, [left, right], place_ref[0], tile_v)
 
-    def begin(tile, u, base):
-        return inner[u, aligned(base, SUBLANES), aligned(tile * LANES, LANES)]
-
-    def store(tile, u, base, value):
-        turned[u, aligned(base, SUBLANES), aligned(tile * LANES, LANES)] = value
-
     sources = [*range(REACH), *range(REACH + tile_u, 2 * REACH + tile_u)]
-    depthwise(padded, taps, begin, store, tile_u, tile_v, EDGE - REACH, sources, True)
-    for u in range(tile_u):
-        out[:, u, :] = turned[u]
+    lines = GROUP * SUBLANES
+    copies = []
+    for first in range(0, tile_v, lines):
+
+        def place(tile, u, base, first=first):
+            return u, aligned(first + base, SUBLANES), aligned(tile * LANES, LANES)
+
+        def begin(tile, u, base, place=place):
+            return inner[place(tile, u, base)]
+
+        def store(tile, u, base, value, place=place):
+            turned[place(tile, u, base)] = value
+
+        offset = first + EDGE - REACH
+        depthwise(padded, taps, begin, store, tile_u, lines, offset, sources, True)
+        here = pl.ds(first, lines)
+        for u in range(tile_u):
+            staged[here, u, :] = turned[u, here, :]
+        copies.append(
+            pltpu.make_async_copy(staged.at[here], out.at[here], sems.at[first // lines])
+        )
+        copies[-1].start()
+    for copy in copies:
+        copy.wait()
 
 
 def call(
@@ -558,11 +574,13 @@
         last_kernel,
         "last",
         [jax.ShapeDtypeStruct((tile_v, tile_u, channels), f32)],
-        [rim_pad, taps, pltpu.VMEM(whole, f32)],
+        [rim_pad, taps, pltpu.VMEM(whole, f32), pltpu.VMEM((tile_v, tile_u, channels), f32)]
+        + [pltpu.SemaphoreType.DMA((tile_v // (GROUP * SUBLANES),))],
         [place],
         [even, odd, even_edge, odd_edge, dw_kernel, inner],
         1,
-        8,
+        10,
+        out_anywhere=(0,),
     )
     return grad
 

time: 64 us -> 64 us (level)
  no operation moved by 1% of the time
where the time goes in v12:
time: 64 us; the launch traced here: 63.7 us
  Pallas kernels  27.4 us (43%)
  starting transfers between devices  21.9 us (34%)
  waiting for transfers between devices  10.9 us (17%)
  local copies, waits for them, and re-layouts  2.22 us (3%)
  other arithmetic  1.01 us (2%)
    pallas_call x9, Pallas kernels, call(): pl.pallas_call(kernel, out_shape=tuple(outs), in_specs=[smem] * len(scala...  27.4 us
    ppermute x1, waiting for transfers between devices, on_device(): lax.ppermute(even_edge, ('row', 'col'), across(row_pairs(False)))  9.31 us
    ppermute x4, starting transfers between devices, find_target(): pieces.append(lax.ppermute(blocks[turn], ('row', 'col'), pairs))  6.23 us
    ppermute x1, starting transfers between devices, on_device(): odd = lax.ppermute(odd, 'row', row_pairs(True))  3 us
    ppermute x1, starting transfers between devices, on_device(): first_side = lax.ppermute(first_block, 'row', row_pairs(True))  2.99 us
    ppermute x1, starting transfers between devices, on_device(): even = lax.ppermute(even, 'row', row_pairs(False))  2.65 us
    ppermute x1, starting transfers between devices, on_device(): odd_edge = lax.ppermute(odd_edge, ('row', 'col'), across(row_pairs(True)))  1.91 us
    ppermute x1, starting transfers between devices, on_device(): lax.ppermute(even_edge, ('row', 'col'), across(row_pairs(False)))  1.68 us
  transfers between devices with their start and end apart: 15, of which 3 were waited for; matrix products, arithmetic and copies ran while one was open for 3% of the time, Pallas kernels for 30%

profile of v12, /device:TPU:13, one launch (start us, length us, event | category | flops | bytes accessed | tf_op | source)
XLA Modules:
  0.0 63.7 jit_solution(16092857185365026708)
XLA Ops:
  0.0 1.3 %copy.19 = bf16[128,4,512]{2,0,1:T(8,128)(2,1)S(1)} copy(bf16[128,4,512]{2,1,0:T(4,128)(2,1)} %param.14) | data formatting | bytes 1048576 | tf_op args[2]
  1.3 0.7 %collective-permute-start = (bf16[4,8,512]{2,1,0:T(8,128)(2,1)S(1)}, bf16[4,8,512]{2,1,0:T(8,128)(2,1)S(1)}, u32[]{:S(2)}, u32[]{:S(2)}) collective-permute-start(bf16[4,8,512]{2,1,0:T(8,128)(2,1)S(1)} %dynamic-slice_bitcast_fusion.2), channel_id=1, source_target_pairs={{0,1},{1,0},{2,3},{3,2},{4,5},{5,4},{6,7},{7,6},{8,9},{9,8},{10,11... | collective-permute-start | bytes 98312 | tf_op jit(solution)/shard_map/ppermute | solution.py:496
  2.1 0.8 %dynamic-slice_bitcast_fusion = (bf16[3,128,512]{2,1,0:T(8,128)(2,1)}, bf16[3,128,512]{2,1,0:T(8,128)(2,1)S(1)}) fusion(bf16[128,4,512]{2,0,1:T(8,128)(2,1)S(1)} %copy.19, s32[]{:T(128)S(6)} %select_n.33, s32[]{:T(128)S(6)} %select_n.31), kind=kLoop, calls=%fused_computation.1 | loop fusion | bytes 1572872 | tf_op jit(solution)/shard_map/dynamic_slice | solution.py:395
  2.9 3.0 %collective-permute-start.2 = (bf16[3,128,512]{2,1,0:T(8,128)(2,1)}, bf16[3,128,512]{2,1,0:T(8,128)(2,1)S(1)}, u32[]{:S(2)}, u32[]{:S(2)}) collective-permute-start(bf16[3,128,512]{2,1,0:T(8,128)(2,1)} %get-tuple-element.45), channel_id=1, source_target_pairs={{2,4},{4,2},{6,8},{8,6},{10,12},{12,10},{3,5},{5,3},{7,9},{9,7},{1... | collective-permute-start | bytes 1179656 | tf_op jit(solution)/shard_map/ppermute | solution.py:495
  5.9 0.8 %pad_maximum_fusion = bf16[3,136,512]{2,1,0:T(8,128)(2,1)} fusion(bf16[3,8,512]{2,1,0:T(8,128)(2,1)S(1)} %constant_dynamic-slice_fusion.1, bf16[3,128,512]{2,1,0:T(8,128)(2,1)S(1)} %get-tuple-element.46), kind=kLoop, calls=%fused_computation | loop fusion | flops 835584 | bytes 835584 | tf_op jit(solution)/shard_map/concatenate | solution.py:497
  6.7 3.4 %project_away.1 = (bf16[256,512]{1,0:T(8,128)(2,1)}, bf16[256,512]{1,0:T(8,128)(2,1)}) custom-call(s32[1]{0:T(128)} %bitcast.core_ref, bf16[32,2,16,2048]{3,2,1,0:T(8,128)(2,1)} %bitcast.34, bf16[2048,512]{1,0:T(8,128)(2,1)S(1)} %copy-done), custom_call_target="tpu_custom_call" | custom-call | flops 1 | bytes 1 | tf_op jit(solution)/shard_map/project_away/pallas_call | solution.py:375
  10.1 0.4 collective-permute-start.3
  10.5 0.2 collective-permute-start.4
  10.7 1.4 %collective-permute-start.1 = (bf16[3,136,512]{2,1,0:T(8,128)(2,1)}, bf16[3,136,512]{2,1,0:T(8,128)(2,1)S(1)}, u32[]{:S(2)}, u32[]{:S(2)}) collective-permute-start(bf16[3,136,512]{2,1,0:T(8,128)(2,1)} %pad_maximum_fusion), channel_id=1, source_target_pairs={{0,2},{2,0},{4,6},{6,4},{8,10},{10,8},{12,14},{14,12},{1,3},{3,1},... | collective-permute-start | bytes 1253384 | tf_op jit(solution)/shard_map/ppermute | solution.py:500
  12.1 0.1 pad_add_fusion.place_ref
  12.1 0.1 pad_add_fusion.2.turns_ref
  12.2 2.7 %project_home.1.home = f32[512,512]{1,0:T(8,128)S(1)} custom-call(s32[1]{0:T(128)} %bitcast.core_ref, bf16[32,2,16,2048]{3,2,1,0:T(8,128)(2,1)} %bitcast.35, bf16[2048,512]{1,0:T(8,128)(2,1)S(1)} %copy-done), custom_call_target="tpu_custom_call" | custom-call | flops 1 | bytes 1 | tf_op jit(solution)/shard_map/project_home/pallas_call | solution.py:375
  15.0 1.1 %combine.1 = (bf16[4,32,512]{2,1,0:T(8,128)(2,1)S(1)}, bf16[4,32,512]{2,1,0:T(8,128)(2,1)S(1)}, bf16[4,32,512]{2,1,0:T(8,128)(2,1)S(1)}, bf16[4,32,512]{2,1,0:T(8,128)(2,1)S(1)}) custom-call(s32[4]{0:T(128)S(1)} %pad_add_fusion.2.turns_ref, f32[512,512]{1,0:T(8,128)S(1)} %project_home.1.home, bf16[256,512]{1,0:T(8,128)(2,1)S(1)} %collective-permute-done.3.upper, ...), custom_call_target="tpu_custom_call" | custom-call | flops 1 | bytes 1 | tf_op jit(solution)/shard_map/combine/pallas_call | solution.py:375
  16.1 2.5 %inner_up.1.inner = f32[4,128,512]{2,1,0:T(8,128)S(1)} custom-call(s32[1]{0:T(128)} %bitcast.core_ref, bf16[4,128,512]{2,1,0:T(8,128)(2,1)S(1)} %bitcast.25, bf16[4,8,512]{2,1,0:T(8,128)(2,1)S(1)} %copy-done.3, f32[7,7,512]{2,1,0:T(8,128)S(1)} %copy-done.1, f32[1,512]{1,0:T(1,128)S(1)} %bitcast.27), custom_call_target="tpu_custom_call" | custom-call | flops 1 | bytes 1 | tf_op jit(solution)/shard_map/inner_up/pallas_call | solution.py:375
  18.6 0.7 %collective-permute-start.5 = (bf16[3,8,512]{2,1,0:T(8,128)(2,1)S(1)}, bf16[3,8,512]{2,1,0:T(8,128)(2,1)S(1)}, u32[]{:S(2)}, u32[]{:S(2)}) collective-permute-start(bf16[3,8,512]{2,1,0:T(8,128)(2,1)S(1)} %constant_dynamic-slice_fusion), channel_id=1, source_target_pairs={{0,1},{1,0},{2,3},{3,2},{4,5},{5,4},{6,7},{7,6},{8,9},{9,8},{10,11... | collective-permute-start | bytes 73736 | tf_op jit(solution)/shard_map/ppermute | solution.py:519
  19.3 0.1 pad_add_fusion.1.places_ref
  19.3 2.6 %collective-permute-start.6 = (bf16[4,32,512]{2,1,0:T(8,128)(2,1)S(1)}, bf16[4,32,512]{2,1,0:T(8,128)(2,1)S(1)}, u32[]{:S(2)}, u32[]{:S(2)}) collective-permute-start(bf16[4,32,512]{2,1,0:T(8,128)(2,1)S(1)} %get-tuple-element.28), channel_id=1, source_target_pairs={{0,0},{1,8},{2,2},{3,10},{4,4},{5,12},{6,6},{7,14},{8,1},{9,9},{10... | collective-permute-start | bytes 393224 | tf_op jit(solution)/shard_map/ppermute | solution.py:459
  22.0 1.8 %collective-permute-start.7 = (bf16[4,32,512]{2,1,0:T(8,128)(2,1)S(1)}, bf16[4,32,512]{2,1,0:T(8,128)(2,1)S(1)}, u32[]{:S(2)}, u32[]{:S(2)}) collective-permute-start(bf16[4,32,512]{2,1,0:T(8,128)(2,1)S(1)} %get-tuple-element.35), channel_id=1, source_target_pairs={{0,2},{1,10},{2,4},{3,12},{4,6},{5,14},{6,0},{7,8},{8,3},{9,11},{1... | collective-permute-start | bytes 393224 | tf_op jit(solution)/shard_map/ppermute | solution.py:459
  23.7 1.2 %collective-permute-start.8 = (bf16[4,32,512]{2,1,0:T(8,128)(2,1)S(1)}, bf16[4,32,512]{2,1,0:T(8,128)(2,1)S(1)}, u32[]{:S(2)}, u32[]{:S(2)}) collective-permute-start(bf16[4,32,512]{2,1,0:T(8,128)(2,1)S(1)} %get-tuple-element.36), channel_id=1, source_target_pairs={{0,4},{1,12},{2,6},{3,14},{4,0},{5,8},{6,2},{7,10},{8,5},{9,13},{1... | collective-permute-start | bytes 393224 | tf_op jit(solution)/shard_map/ppermute | solution.py:459
  24.9 0.6 collective-permute-start.9
  25.6 1.8 %side_up.1.inner = f32[4,128,512]{2,1,0:T(8,128)S(1)} custom-call(s32[2]{0:T(128)S(1)} %pad_add_fusion.place_ref, bf16[3,128,512]{2,1,0:T(8,128)(2,1)S(1)} %collective-permute-done.2.side, bf16[3,8,512]{2,1,0:T(8,128)(2,1)S(1)} %collective-permute-done.5.edge, f32[7,7,512]{2,1,0:T(8,128)S(1)} %copy-done.1, f32[4,128,512]{2,1,0:T(8,128)S(1)} %inner_up.1.inner), custom_call_target="tpu_custom_call" | custom-call | flops 1 | bytes 1 | tf_op jit(solution)/shard_map/side_up/pallas_call | solution.py:375
  27.3 1.4 %collective-permute-done.1.side = bf16[3,136,512]{2,1,0:T(8,128)(2,1)S(1)} collective-permute-done((bf16[3,136,512]{2,1,0:T(8,128)(2,1)}, bf16[3,136,512]{2,1,0:T(8,128)(2,1)S(1)}, u32[]{:S(2)}, u32[]{:S(2)}) %collective-permute-start.1) | collective-permute-done | bytes 417824 | tf_op jit(solution)/shard_map/ppermute | solution.py:500
  28.8 4.9 %up.1 = (f32[512,512]{1,0:T(8,128)S(1)}, f32[512,128]{1,0:T(8,128)S(1)}, bf16[512,2048]{1,0:T(8,128)(2,1)S(1)}, bf16[512,2048]{1,0:T(8,128)(2,1)S(1)}) custom-call(s32[2]{0:T(128)S(1)} %pad_add_fusion.place_ref, bf16[3,136,512]{2,1,0:T(8,128)(2,1)S(1)} %collective-permute-done.1.side, f32[7,7,512]{2,1,0:T(8,128)S(1)} %copy-done.1, ...), custom_call_target="tpu_custom_call" | custom-call | flops 4294967296 | bytes 9181184 | tf_op jit(solution)/shard_map/up/pallas_call | solution.py:375
  33.7 0.2 collective-permute-done.8.rest_2_
  34.0 4.8 %back.1 = (f32[4,128,512]{2,1,0:T(8,128)S(1)}, bf16[4,128,512]{2,1,0:T(8,128)(2,1)S(1)}, bf16[3,128,512]{2,1,0:T(8,128)(2,1)S(1)}, bf16[3,128,512]{2,1,0:T(8,128...) custom-call(s32[2]{0:T(128)S(1)} %pad_add_fusion.place_ref, ...), custom_call_target="tpu_custom_call" | custom-call | flops 4294967296 | bytes 13195264 | tf_op jit(solution)/shard_map/back/pallas_call | solution.py:375
  38.8 2.7 %collective-permute-start.10 = (bf16[3,128,512]{2,1,0:T(8,128)(2,1)S(1)}, bf16[3,128,512]{2,1,0:T(8,128)(2,1)S(1)}, u32[]{:S(2)}, u32[]{:S(2)}) collective-permute-start(bf16[3,128,512]{2,1,0:T(8,128)(2,1)S(1)} %get-tuple-element.38), channel_id=1, source_target_pairs={{0,2},{2,0},{4,6},{6,4},{8,10},{10,8},{12,14},{14,12},{1,3},{3,1},... | collective-permute-start | bytes 1179656 | tf_op jit(solution)/shard_map/ppermute | solution.py:562
  41.4 3.0 %collective-permute-start.11 = (bf16[3,128,512]{2,1,0:T(8,128)(2,1)S(1)}, bf16[3,128,512]{2,1,0:T(8,128)(2,1)S(1)}, u32[]{:S(2)}, u32[]{:S(2)}) collective-permute-start(bf16[3,128,512]{2,1,0:T(8,128)(2,1)S(1)} %get-tuple-element.39), channel_id=1, source_target_pairs={{2,4},{4,2},{6,8},{8,6},{10,12},{12,10},{3,5},{5,3},{7,9},{9,7},{1... | collective-permute-start | bytes 1179656 | tf_op jit(solution)/shard_map/ppermute | solution.py:563
  44.5 1.7 %collective-permute-start.12 = (bf16[3,8,512]{2,1,0:T(8,128)(2,1)S(1)}, bf16[3,8,512]{2,1,0:T(8,128)(2,1)S(1)}, u32[]{:S(2)}, u32[]{:S(2)}) collective-permute-start(bf16[3,8,512]{2,1,0:T(8,128)(2,1)S(1)} %get-tuple-element.40), channel_id=1, source_target_pairs={{0,3},{1,2},{2,1},{3,0},{4,7},{5,6},{6,5},{7,4},{8,11},{9,10},{10,... | collective-permute-start | bytes 73736 | tf_op jit(solution)/shard_map/ppermute | solution.py:565
  46.2 1.9 %collective-permute-start.13 = (bf16[3,8,512]{2,1,0:T(8,128)(2,1)S(1)}, bf16[3,8,512]{2,1,0:T(8,128)(2,1)S(1)}, u32[]{:S(2)}, u32[]{:S(2)}) collective-permute-start(bf16[3,8,512]{2,1,0:T(8,128)(2,1)S(1)} %get-tuple-element.41), channel_id=1, source_target_pairs={{2,5},{3,4},{4,3},{5,2},{6,9},{7,8},{8,7},{9,6},{10,13},{11,12},{1... | collective-permute-start | bytes 73736 | tf_op jit(solution)/shard_map/ppermute | solution.py:566
  48.1 2.5 %inner_last.1.inner = f32[4,128,512]{2,1,0:T(8,128)S(1)} custom-call(s32[1]{0:T(128)} %bitcast.core_ref, bf16[4,128,512]{2,1,0:T(8,128)(2,1)S(1)} %get-tuple-element.42.middle, bf16[4,8,512]{2,1,0:T(8,128)(2,1)S(1)} %collective-permute-done.14.edge, f32[7,7,512]{2,1,0:T(8,128)S(1)} %copy-done.1, f32[4,128,512]{2,1,0:T(8,128)S(1)} %get-tuple-element.44.base_value), custom_call_target="tpu_custom_call" | custom-call | flops 1073741824 | bytes 2754560 | tf_op jit(solution)/shard_map/inner_last/pallas_call | solution.py:375
  50.7 9.3 %collective-permute-done.12.even_edge = bf16[3,8,512]{2,1,0:T(8,128)(2,1)S(1)} collective-permute-done((bf16[3,8,512]{2,1,0:T(8,128)(2,1)S(1)}, bf16[3,8,512]{2,1,0:T(8,128)(2,1)S(1)}, u32[]{:S(2)}, u32[]{:S(2)}) %collective-permute-start.12) | collective-permute-done | bytes 24608 | tf_op jit(solution)/shard_map/ppermute | solution.py:565
  60.0 3.8 %last.1 = f32[128,4,512]{2,1,0:T(4,128)} custom-call(s32[2]{0:T(128)S(1)} %pad_add_fusion.place_ref, bf16[3,128,512]{2,1,0:T(8,128)(2,1)S(1)} %collective-permute-done.10.even, bf16[3,128,512]{2,1,0:T(8,128)(2,1)S(1)} %collective-permute-done.11.odd, bf16[3,8,512]{2,1,0:T(8,128)(2,1)S(1)} %collective-permute-done.12.even_edge, ...), custom_call_target="tpu_custom_call" | custom-call | flops 1 | bytes 1 | tf_op jit(solution)/shard_map/last/pallas_call | solution.py:375
  (40 shorter events, 0.2 us)
Async XLA Ops:
  0.0 6.7 %copy-start = (bf16[2048,512]{1,0:T(8,128)(2,1)S(1)}, bf16[2048,512]{1,0:T(8,128)(2,1)}, u32[]{:S(2)}) copy-start(bf16[2048,512]{1,0:T(8,128)(2,1)} %weight.1) | copy-start | bytes 6291460
  1.3 4.6 %collective-permute-start = (bf16[4,8,512]{2,1,0:T(8,128)(2,1)S(1)}, bf16[4,8,512]{2,1,0:T(8,128)(2,1)S(1)}, u32[]{:S(2)}, u32[]{:S(2)}) collective-permute-start(bf16[4,8,512]{2,1,0:T(8,128)(2,1)S(1)} %dynamic-slice_bitcast_fusion.2), channel_id=1, source_target_pairs={{0,1},{1,0},{2,3},{3,2},{4,5},{5,4},{6,7},{7,6},{8,9},{9,8},{10,11... | collective-permute-start | bytes 98312 | tf_op jit(solution)/shard_map/ppermute | solution.py:496
  2.9 15.7 %collective-permute-start.2 = (bf16[3,128,512]{2,1,0:T(8,128)(2,1)}, bf16[3,128,512]{2,1,0:T(8,128)(2,1)S(1)}, u32[]{:S(2)}, u32[]{:S(2)}) collective-permute-start(bf16[3,128,512]{2,1,0:T(8,128)(2,1)} %get-tuple-element.45), channel_id=1, source_target_pairs={{2,4},{4,2},{6,8},{8,6},{10,12},{12,10},{3,5},{5,3},{7,9},{9,7},{1... | collective-permute-start | bytes 1179656 | tf_op jit(solution)/shard_map/ppermute | solution.py:495
  5.9 4.2 %copy-start.2 = (bf16[4,8,512]{2,1,0:T(8,128)(2,1)}, bf16[4,8,512]{2,1,0:T(8,128)(2,1)S(1)}, u32[]{:S(2)}) copy-start(bf16[4,8,512]{2,1,0:T(8,128)(2,1)S(1)} %collective-permute-done.edge) | copy-start | bytes 98308
  10.1 4.8 %collective-permute-start.3 = (bf16[256,512]{1,0:T(8,128)(2,1)}, bf16[256,512]{1,0:T(8,128)(2,1)S(1)}, u32[]{:S(2)}, u32[]{:S(2)}) collective-permute-start(bf16[256,512]{1,0:T(8,128)(2,1)} %get-tuple-element.26), channel_id=1, source_target_pairs={{0,1},{1,0},{2,3},{3,2},{4,5},{5,4},{6,7},{7,6},{8,9},{9,8},{10,11... | collective-permute-start | bytes 786440 | tf_op jit(solution)/shard_map/ppermute | solution.py:434
  10.5 4.5 %collective-permute-start.4 = (bf16[256,512]{1,0:T(8,128)(2,1)}, bf16[256,512]{1,0:T(8,128)(2,1)S(1)}, u32[]{:S(2)}, u32[]{:S(2)}) collective-permute-start(bf16[256,512]{1,0:T(8,128)(2,1)} %get-tuple-element.27), channel_id=1, source_target_pairs={{0,1},{1,0},{2,3},{3,2},{4,5},{5,4},{6,7},{7,6},{8,9},{9,8},{10,11... | collective-permute-start | bytes 786440 | tf_op jit(solution)/shard_map/ppermute | solution.py:434
  10.7 18.0 %collective-permute-start.1 = (bf16[3,136,512]{2,1,0:T(8,128)(2,1)}, bf16[3,136,512]{2,1,0:T(8,128)(2,1)S(1)}, u32[]{:S(2)}, u32[]{:S(2)}) collective-permute-start(bf16[3,136,512]{2,1,0:T(8,128)(2,1)} %pad_maximum_fusion), channel_id=1, source_target_pairs={{0,2},{2,0},{4,6},{6,4},{8,10},{10,8},{12,14},{14,12},{1,3},{3,1},... | collective-permute-start | bytes 1253384 | tf_op jit(solution)/shard_map/ppermute | solution.py:500
  12.2 3.8 %copy-start.1 = (f32[7,7,512]{2,1,0:T(8,128)S(1)}, f32[7,7,512]{2,1,0:T(8,128)}, u32[]{:S(2)}) copy-start(f32[7,7,512]{2,1,0:T(8,128)} %kernel.9) | copy-start | bytes 301060
  12.2 3.8 %copy-start.3 = (bf16[4,8,512]{2,1,0:T(8,128)(2,1)S(1)}, bf16[4,8,512]{2,1,0:T(8,128)(2,1)}, u32[]{:S(2)}) copy-start(bf16[4,8,512]{2,1,0:T(8,128)(2,1)} %copy-done.2) | copy-start | bytes 98308
  12.2 3.8 %copy-start.4 = (f32[512]{0:T(512)S(1)}, f32[512]{0:T(512)}, u32[]{:S(2)}) copy-start(f32[512]{0:T(512)} %param.16) | copy-start | bytes 6148
  16.1 12.6 %copy-start.7 = (f32[2048]{0:T(1024)S(1)}, f32[2048]{0:T(1024)}, u32[]{:S(2)}) copy-start(f32[2048]{0:T(1024)} %param.20) | copy-start | bytes 24580
  16.1 12.6 %copy-start.8 = (f32[512]{0:T(512)S(1)}, f32[512]{0:T(512)}, u32[]{:S(2)}) copy-start(f32[512]{0:T(512)} %param.18) | copy-start | bytes 6148
  16.1 12.6 %copy-start.9 = (f32[512]{0:T(512)S(1)}, f32[512]{0:T(512)}, u32[]{:S(2)}) copy-start(f32[512]{0:T(512)} %param.17) | copy-start | bytes 6148
  18.6 6.3 %collective-permute-start.5 = (bf16[3,8,512]{2,1,0:T(8,128)(2,1)S(1)}, bf16[3,8,512]{2,1,0:T(8,128)(2,1)S(1)}, u32[]{:S(2)}, u32[]{:S(2)}) collective-permute-start(bf16[3,8,512]{2,1,0:T(8,128)(2,1)S(1)} %constant_dynamic-slice_fusion), channel_id=1, source_target_pairs={{0,1},{1,0},{2,3},{3,2},{4,5},{5,4},{6,7},{7,6},{8,9},{9,8},{10,11... | collective-permute-start | bytes 73736 | tf_op jit(solution)/shard_map/ppermute | solution.py:519
  19.3 14.6 %collective-permute-start.6 = (bf16[4,32,512]{2,1,0:T(8,128)(2,1)S(1)}, bf16[4,32,512]{2,1,0:T(8,128)(2,1)S(1)}, u32[]{:S(2)}, u32[]{:S(2)}) collective-permute-start(bf16[4,32,512]{2,1,0:T(8,128)(2,1)S(1)} %get-tuple-element.28), channel_id=1, source_target_pairs={{0,0},{1,8},{2,2},{3,10},{4,4},{5,12},{6,6},{7,14},{8,1},{9,9},{10... | collective-permute-start | bytes 393224 | tf_op jit(solution)/shard_map/ppermute | solution.py:459
  22.0 11.7 %collective-permute-start.7 = (bf16[4,32,512]{2,1,0:T(8,128)(2,1)S(1)}, bf16[4,32,512]{2,1,0:T(8,128)(2,1)S(1)}, u32[]{:S(2)}, u32[]{:S(2)}) collective-permute-start(bf16[4,32,512]{2,1,0:T(8,128)(2,1)S(1)} %get-tuple-element.35), channel_id=1, source_target_pairs={{0,2},{1,10},{2,4},{3,12},{4,6},{5,14},{6,0},{7,8},{8,3},{9,11},{1... | collective-permute-start | bytes 393224 | tf_op jit(solution)/shard_map/ppermute | solution.py:459
  23.7 10.2 %collective-permute-start.8 = (bf16[4,32,512]{2,1,0:T(8,128)(2,1)S(1)}, bf16[4,32,512]{2,1,0:T(8,128)(2,1)S(1)}, u32[]{:S(2)}, u32[]{:S(2)}) collective-permute-start(bf16[4,32,512]{2,1,0:T(8,128)(2,1)S(1)} %get-tuple-element.36), channel_id=1, source_target_pairs={{0,4},{1,12},{2,6},{3,14},{4,0},{5,8},{6,2},{7,10},{8,5},{9,13},{1... | collective-permute-start | bytes 393224 | tf_op jit(solution)/shard_map/ppermute | solution.py:459
  24.9 9.0 %collective-permute-start.9 = (bf16[4,32,512]{2,1,0:T(8,128)(2,1)S(1)}, bf16[4,32,512]{2,1,0:T(8,128)(2,1)S(1)}, u32[]{:S(2)}, u32[]{:S(2)}) collective-permute-start(bf16[4,32,512]{2,1,0:T(8,128)(2,1)S(1)} %get-tuple-element.37), channel_id=1, source_target_pairs={{0,6},{1,14},{2,0},{3,8},{4,2},{5,10},{6,4},{7,12},{8,7},{9,15},{1... | collective-permute-start | bytes 393224 | tf_op jit(solution)/shard_map/ppermute | solution.py:459
  28.7 5.2 %copy-start.5 = (bf16[512,2048]{1,0:T(8,128)(2,1)S(1)}, bf16[512,2048]{1,0:T(8,128)(2,1)}, u32[]{:S(2)}) copy-start(bf16[512,2048]{1,0:T(8,128)(2,1)} %w_in.1) | copy-start | bytes 6291460
  28.7 5.2 %copy-start.6 = (bf16[2048,512]{1,0:T(8,128)(2,1)S(1)}, bf16[2048,512]{1,0:T(8,128)(2,1)}, u32[]{:S(2)}) copy-start(bf16[2048,512]{1,0:T(8,128)(2,1)} %w_out.1) | copy-start | bytes 6291460
  28.7 5.2 %copy-start.10 = (f32[512]{0:T(512)S(1)}, f32[512]{0:T(512)}, u32[]{:S(2)}) copy-start(f32[512]{0:T(512)} %param.22) | copy-start | bytes 6148
  28.8 5.2 %copy-start.11 = (f32[512]{0:T(512)S(1)}, f32[512]{0:T(512)}, u32[]{:S(2)}) copy-start(f32[512]{0:T(512)} %param.23) | copy-start | bytes 6148
  38.8 21.2 %collective-permute-start.10 = (bf16[3,128,512]{2,1,0:T(8,128)(2,1)S(1)}, bf16[3,128,512]{2,1,0:T(8,128)(2,1)S(1)}, u32[]{:S(2)}, u32[]{:S(2)}) collective-permute-start(bf16[3,128,512]{2,1,0:T(8,128)(2,1)S(1)} %get-tuple-element.38), channel_id=1, source_target_pairs={{0,2},{2,0},{4,6},{6,4},{8,10},{10,8},{12,14},{14,12},{1,3},{3,1},... | collective-permute-start | bytes 1179656 | tf_op jit(solution)/shard_map/ppermute | solution.py:562
  41.4 18.6 %collective-permute-start.11 = (bf16[3,128,512]{2,1,0:T(8,128)(2,1)S(1)}, bf16[3,128,512]{2,1,0:T(8,128)(2,1)S(1)}, u32[]{:S(2)}, u32[]{:S(2)}) collective-permute-start(bf16[3,128,512]{2,1,0:T(8,128)(2,1)S(1)} %get-tuple-element.39), channel_id=1, source_target_pairs={{2,4},{4,2},{6,8},{8,6},{10,12},{12,10},{3,5},{5,3},{7,9},{9,7},{1... | collective-permute-start | bytes 1179656 | tf_op jit(solution)/shard_map/ppermute | solution.py:563
  44.4 3.7 %collective-permute-start.14 = (bf16[4,8,512]{2,1,0:T(8,128)(2,1)S(1)}, bf16[4,8,512]{2,1,0:T(8,128)(2,1)S(1)}, u32[]{:S(2)}, u32[]{:S(2)}) collective-permute-start(bf16[4,8,512]{2,1,0:T(8,128)(2,1)S(1)} %get-tuple-element.43), channel_id=1, source_target_pairs={{0,1},{1,0},{2,3},{3,2},{4,5},{5,4},{6,7},{7,6},{8,9},{9,8},{10,11... | collective-permute-start | bytes 98312 | tf_op jit(solution)/shard_map/ppermute | solution.py:564
  44.5 15.5 %collective-permute-start.12 = (bf16[3,8,512]{2,1,0:T(8,128)(2,1)S(1)}, bf16[3,8,512]{2,1,0:T(8,128)(2,1)S(1)}, u32[]{:S(2)}, u32[]{:S(2)}) collective-permute-start(bf16[3,8,512]{2,1,0:T(8,128)(2,1)S(1)} %get-tuple-element.40), channel_id=1, source_target_pairs={{0,3},{1,2},{2,1},{3,0},{4,7},{5,6},{6,5},{7,4},{8,11},{9,10},{10,... | collective-permute-start | bytes 73736 | tf_op jit(solution)/shard_map/ppermute | solution.py:565
  46.2 13.8 %collective-permute-start.13 = (bf16[3,8,512]{2,1,0:T(8,128)(2,1)S(1)}, bf16[3,8,512]{2,1,0:T(8,128)(2,1)S(1)}, u32[]{:S(2)}, u32[]{:S(2)}) collective-permute-start(bf16[3,8,512]{2,1,0:T(8,128)(2,1)S(1)} %get-tuple-element.41), channel_id=1, source_target_pairs={{2,5},{3,4},{4,3},{5,2},{6,9},{7,8},{8,7},{9,6},{10,13},{11,12},{1... | collective-permute-start | bytes 73736 | tf_op jit(solution)/shard_map/ppermute | solution.py:566

commit v13 on v12

--- a/solution.py
+++ b/solution.py
@@ -17,7 +17,6 @@
 UNROLL = 32
 GROUP = 4
 COPIES = 8
-DOTS = 2
 MLP_TILE = 512
 CONTRACT_LAST = (((1,), (1,)), ((), ()))
 SWAP = [(0, 1), (1, 0)]
@@ -42,26 +41,31 @@
         copy = pltpu.make_async_copy(teacher_hbm.at[here, half], rows.at[here], sems.at[index])
         copy.start()
         copies.append(copy)
-    size = lines * wide // DOTS
-    for index in range(DOTS):
-        for copy in copies[index * count // DOTS : (index + 1) * count // DOTS]:
-            copy.wait()
-        here = pl.ds(index * (lines // DOTS), lines // DOTS)
-        product = jnp.dot(
-            rows[here].reshape(size, depth), weight[...], preferred_element_type=jnp.float32
-        )
-        out = outs[index * len(outs) // DOTS]
-        start = index * size % out.shape[0]
-        out[start : start + size] = product.astype(out.dtype)
-
-
-def combine_kernel(wide, turns_ref, home, upper, lower, *rest):
+    done = 0
+    for out in outs:
+        taken = out.shape[0] // wide
+        parts = 2 if len(outs) == 1 else 1
+        for part in range(parts):
+            here = pl.ds(done + part * (taken // parts), taken // parts)
+            last = pl.cdiv((done + (part + 1) * (taken // parts)) * count, lines)
+            while copies and len(copies) > count - last:
+                copies.pop(0).wait()
+            size = taken // parts * wide
+            product = jnp.dot(
+                rows[here].reshape(size, depth), weight[...], preferred_element_type=jnp.float32
+            )
+            out[part * size : (part + 1) * size] = product.astype(out.dtype)
+        done += taken
+
+
+def combine_kernel(wide, turns_ref, home, first, second, third, *rest):
     *blocks, summed = rest
-    half = upper.shape[0]
     for tile in range(summed.shape[0]):
         lanes = lane_tile(tile)
-        for start, received in ((0, upper), (half, lower)):
-            here = slice(start, start + half)
+        start = 0
+        for received in (first, second, third):
+            here = slice(start, start + received.shape[0])
+            start += received.shape[0]
             summed[tile, here] = home[here, lanes] + received[:, lanes].astype(jnp.float32)
     for index, block in enumerate(blocks):
         tile_u, lines, _ = block.shape
@@ -417,21 +421,25 @@
     half_line = grid_u // 2
     by_half = teacher.reshape(lines, 2, half_line, teacher.shape[1])
     size = (lines * half_line, channels)
-    fourth = jax.ShapeDtypeStruct((size[0] // 2, channels), jnp.bfloat16)
+    third = lines // 3
+    pieces = [
+        jax.ShapeDtypeStruct((part * half_line, channels), jnp.bfloat16)
+        for part in (lines - 2 * third, third, third)
+    ]
     scratch = [
         pltpu.VMEM((lines, half_line, teacher.shape[1]), jnp.bfloat16),
         pltpu.SemaphoreType.DMA((COPIES,)),
     ]
-    upper, lower = call(
+    aways = call(
         functools.partial(project_kernel, True),
-        "project_away", [fourth] * 2, scratch, [scalar], [by_half, proj_weight], 1, 12, (0,),
+        "project_away", pieces, scratch, [scalar], [by_half, proj_weight], 1, 12, (0,),
     )
     (home,) = call(
         functools.partial(project_kernel, False),
         "project_home", [jax.ShapeDtypeStruct(size, jnp.float32)],
         scratch, [scalar], [by_half, proj_weight], 1, 12, (0,),
     )
-    received = [lax.ppermute(away, "col", SWAP) for away in (upper, lower)]
+    received = [lax.ppermute(away, "col", SWAP) for away in aways]
     turns = [lax.rem(turn + row, halves) * tile_u for turn in range(halves)]
     if lines % 16:
         received = jnp.concatenate(received).astype(jnp.float32)

time: 64 us -> 63.9 us (level)
  waiting for transfers between devices: 10.9 us -> 9.69 us
  Pallas kernels: 27.4 us -> 28.1 us
    ppermute x1, waiting for transfers between devices: 9.31 us -> 8.24 us  [on_device(): lax.ppermute(even_edge, ('row', 'col'), across(row_pairs(False)))]
    ppermute x1, waiting for transfers between devices: 1.36 us -> 0.51 us  [on_device(): second_side = lax.ppermute(second_block, 'row', row_pairs(False))]
    pallas_call x9, Pallas kernels: 27.4 us -> 28.1 us  [call(): pl.pallas_call(kernel, out_shape=tuple(outs), in_specs=[smem] * len(scala...]
  transfers between devices with their start and end apart: 15 -> 16, of which waited for: 3 -> 5; matrix products, arithmetic and copies ran while one was open for 3% -> 3% of each run, Pallas kernels for 30% -> 31%
where the time goes in v13:
time: 63.9 us; the launch traced here: 63.3 us
  Pallas kernels  28.1 us (44%)
  starting transfers between devices  22.1 us (35%)
  waiting for transfers between devices  9.69 us (15%)
  local copies, waits for them, and re-layouts  2.19 us (3%)
  other arithmetic  1.01 us (2%)
    pallas_call x9, Pallas kernels, call(): pl.pallas_call(kernel, out_shape=tuple(outs), in_specs=[smem] * len(scala...  28.1 us
    ppermute x1, waiting for transfers between devices, on_device(): lax.ppermute(even_edge, ('row', 'col'), across(row_pairs(False)))  8.24 us
    ppermute x4, starting transfers between devices, find_target(): pieces.append(lax.ppermute(blocks[turn], ('row', 'col'), pairs))  6.23 us
    ppermute x1, starting transfers between devices, on_device(): odd = lax.ppermute(odd, 'row', row_pairs(True))  3.55 us
    ppermute x1, starting transfers between devices, on_device(): first_side = lax.ppermute(first_block, 'row', row_pairs(True))  2.99 us
    ppermute x1, starting transfers between devices, on_device(): even = lax.ppermute(even, 'row', row_pairs(False))  2.5 us
    ppermute x1, starting transfers between devices, on_device(): odd_edge = lax.ppermute(odd_edge, ('row', 'col'), across(row_pairs(True)))  1.91 us
    ppermute x1, starting transfers between devices, on_device(): lax.ppermute(even_edge, ('row', 'col'), across(row_pairs(False)))  1.4 us
  transfers between devices with their start and end apart: 16, of which 5 were waited for; matrix products, arithmetic and copies ran while one was open for 3% of the time, Pallas kernels for 31%

profile of v13, /device:TPU:13, one launch (start us, length us, event | category | flops | bytes accessed | tf_op | source)
XLA Modules:
  0.0 63.3 jit_solution(3048721020491751409)
XLA Ops:
  0.0 1.3 %copy.19 = bf16[128,4,512]{2,0,1:T(8,128)(2,1)S(1)} copy(bf16[128,4,512]{2,1,0:T(4,128)(2,1)} %param.14) | data formatting | bytes 1048576 | tf_op args[2]
  1.3 0.7 %collective-permute-start = (bf16[4,8,512]{2,1,0:T(8,128)(2,1)S(1)}, bf16[4,8,512]{2,1,0:T(8,128)(2,1)S(1)}, u32[]{:S(2)}, u32[]{:S(2)}) collective-permute-start(bf16[4,8,512]{2,1,0:T(8,128)(2,1)S(1)} %dynamic-slice_bitcast_fusion.2), channel_id=1, source_target_pairs={{0,1},{1,0},{2,3},{3,2},{4,5},{5,4},{6,7},{7,6},{8,9},{9,8},{10,11... | collective-permute-start | bytes 98312 | tf_op jit(solution)/shard_map/ppermute | solution.py:504
  2.1 0.8 %dynamic-slice_bitcast_fusion = (bf16[3,128,512]{2,1,0:T(8,128)(2,1)}, bf16[3,128,512]{2,1,0:T(8,128)(2,1)S(1)}) fusion(bf16[128,4,512]{2,0,1:T(8,128)(2,1)S(1)} %copy.19, s32[]{:T(128)S(6)} %select_n.33, s32[]{:T(128)S(6)} %select_n.31), kind=kLoop, calls=%fused_computation.1 | loop fusion | bytes 1572872 | tf_op jit(solution)/shard_map/dynamic_slice | solution.py:399
  2.9 3.0 %collective-permute-start.2 = (bf16[3,128,512]{2,1,0:T(8,128)(2,1)}, bf16[3,128,512]{2,1,0:T(8,128)(2,1)S(1)}, u32[]{:S(2)}, u32[]{:S(2)}) collective-permute-start(bf16[3,128,512]{2,1,0:T(8,128)(2,1)} %get-tuple-element.47), channel_id=1, source_target_pairs={{2,4},{4,2},{6,8},{8,6},{10,12},{12,10},{3,5},{5,3},{7,9},{9,7},{1... | collective-permute-start | bytes 1179656 | tf_op jit(solution)/shard_map/ppermute | solution.py:503
  5.9 0.8 %pad_maximum_fusion = bf16[3,136,512]{2,1,0:T(8,128)(2,1)} fusion(bf16[3,8,512]{2,1,0:T(8,128)(2,1)S(1)} %constant_dynamic-slice_fusion.1, bf16[3,128,512]{2,1,0:T(8,128)(2,1)S(1)} %get-tuple-element.48), kind=kLoop, calls=%fused_computation | loop fusion | flops 835584 | bytes 835584 | tf_op jit(solution)/shard_map/concatenate | solution.py:505
  6.7 1.4 %collective-permute-start.1 = (bf16[3,136,512]{2,1,0:T(8,128)(2,1)}, bf16[3,136,512]{2,1,0:T(8,128)(2,1)}, u32[]{:S(2)}, u32[]{:S(2)}) collective-permute-start(bf16[3,136,512]{2,1,0:T(8,128)(2,1)} %pad_maximum_fusion), channel_id=1, source_target_pairs={{0,2},{2,0},{4,6},{6,4},{8,10},{10,8},{12,14},{14,12},{1,3},{3,1},... | collective-permute-start | bytes 1253384 | tf_op jit(solution)/shard_map/ppermute | solution.py:508
  8.1 3.5 %project_away.1 = (bf16[192,512]{1,0:T(8,128)(2,1)}, bf16[160,512]{1,0:T(8,128)(2,1)}, bf16[160,512]{1,0:T(8,128)(2,1)}) custom-call(s32[1]{0:T(128)} %bitcast.core_ref, bf16[32,2,16,2048]{3,2,1,0:T(8,128)(2,1)} %bitcast.34, bf16[2048,512]{1,0:T(8,128)(2,1)S(1)} %copy-done), custom_call_target="tpu_custom_call" | custom-call | flops 1 | bytes 1 | tf_op jit(solution)/shard_map/project_away/pallas_call | solution.py:379
  11.5 0.7 %collective-permute-start.4 = (bf16[160,512]{1,0:T(8,128)(2,1)}, bf16[160,512]{1,0:T(8,128)(2,1)S(1)}, u32[]{:S(2)}, u32[]{:S(2)}) collective-permute-start(bf16[160,512]{1,0:T(8,128)(2,1)} %get-tuple-element.28), channel_id=1, source_target_pairs={{0,1},{1,0},{2,3},{3,2},{4,5},{5,4},{6,7},{7,6},{8,9},{9,8},{10,11... | collective-permute-start | bytes 491528 | tf_op jit(solution)/shard_map/ppermute | solution.py:442
  12.2 0.1 collective-permute-start.5
  12.3 0.4 collective-permute-start.3
  12.9 2.7 %project_home.1.home = f32[512,512]{1,0:T(8,128)S(1)} custom-call(s32[1]{0:T(128)} %bitcast.core_ref, bf16[32,2,16,2048]{3,2,1,0:T(8,128)(2,1)} %bitcast.35, bf16[2048,512]{1,0:T(8,128)(2,1)S(1)} %copy-done), custom_call_target="tpu_custom_call" | custom-call | flops 1 | bytes 1 | tf_op jit(solution)/shard_map/project_home/pallas_call | solution.py:379
  15.6 1.1 %combine.1 = (bf16[4,32,512]{2,1,0:T(8,128)(2,1)S(1)}, bf16[4,32,512]{2,1,0:T(8,128)(2,1)S(1)}, bf16[4,32,512]{2,1,0:T(8,128)(2,1)S(1)}, bf16[4,32,512]{2,1,0:T(8,128)(2,1)S(1)}) custom-call(s32[4]{0:T(128)S(1)} %pad_add_fusion.2.turns_ref, f32[512,512]{1,0:T(8,128)S(1)} %project_home.1.home, bf16[192,512]{1,0:T(8,128)(2,1)S(1)} %collective-permute-done.3.first, ...), custom_call_target="tpu_custom_call" | custom-call | flops 1 | bytes 1 | tf_op jit(solution)/shard_map/combine/pallas_call | solution.py:379
  16.8 2.5 %inner_up.1.inner = f32[4,128,512]{2,1,0:T(8,128)S(1)} custom-call(s32[1]{0:T(128)} %bitcast.core_ref, bf16[4,128,512]{2,1,0:T(8,128)(2,1)S(1)} %bitcast.25, bf16[4,8,512]{2,1,0:T(8,128)(2,1)S(1)} %copy-done.3, f32[7,7,512]{2,1,0:T(8,128)S(1)} %copy-done.1, f32[1,512]{1,0:T(1,128)S(1)} %bitcast.27), custom_call_target="tpu_custom_call" | custom-call | flops 1 | bytes 1 | tf_op jit(solution)/shard_map/inner_up/pallas_call | solution.py:379
  19.3 0.1 collective-permute-start.6
  19.5 2.9 %collective-permute-start.7 = (bf16[4,32,512]{2,1,0:T(8,128)(2,1)S(1)}, bf16[4,32,512]{2,1,0:T(8,128)(2,1)S(1)}, u32[]{:S(2)}, u32[]{:S(2)}) collective-permute-start(bf16[4,32,512]{2,1,0:T(8,128)(2,1)S(1)} %get-tuple-element.30), channel_id=1, source_target_pairs={{0,0},{1,8},{2,2},{3,10},{4,4},{5,12},{6,6},{7,14},{8,1},{9,9},{10... | collective-permute-start | bytes 393224 | tf_op jit(solution)/shard_map/ppermute | solution.py:467
  22.4 1.5 %collective-permute-start.8 = (bf16[4,32,512]{2,1,0:T(8,128)(2,1)S(1)}, bf16[4,32,512]{2,1,0:T(8,128)(2,1)S(1)}, u32[]{:S(2)}, u32[]{:S(2)}) collective-permute-start(bf16[4,32,512]{2,1,0:T(8,128)(2,1)S(1)} %get-tuple-element.37), channel_id=1, source_target_pairs={{0,2},{1,10},{2,4},{3,12},{4,6},{5,14},{6,0},{7,8},{8,3},{9,11},{1... | collective-permute-start | bytes 393224 | tf_op jit(solution)/shard_map/ppermute | solution.py:467
  23.9 1.6 %collective-permute-start.9 = (bf16[4,32,512]{2,1,0:T(8,128)(2,1)S(1)}, bf16[4,32,512]{2,1,0:T(8,128)(2,1)S(1)}, u32[]{:S(2)}, u32[]{:S(2)}) collective-permute-start(bf16[4,32,512]{2,1,0:T(8,128)(2,1)S(1)} %get-tuple-element.38), channel_id=1, source_target_pairs={{0,4},{1,12},{2,6},{3,14},{4,0},{5,8},{6,2},{7,10},{8,5},{9,13},{1... | collective-permute-start | bytes 393224 | tf_op jit(solution)/shard_map/ppermute | solution.py:467
  25.5 0.2 collective-permute-start.10
  25.8 1.8 %side_up.1.inner = f32[4,128,512]{2,1,0:T(8,128)S(1)} custom-call(s32[2]{0:T(128)S(1)} %pad_add_fusion.place_ref, bf16[3,128,512]{2,1,0:T(8,128)(2,1)S(1)} %collective-permute-done.2.side, bf16[3,8,512]{2,1,0:T(8,128)(2,1)S(1)} %collective-permute-done.6.edge, f32[7,7,512]{2,1,0:T(8,128)S(1)} %copy-done.1, f32[4,128,512]{2,1,0:T(8,128)S(1)} %inner_up.1.inner), custom_call_target="tpu_custom_call" | custom-call | flops 1 | bytes 1 | tf_op jit(solution)/shard_map/side_up/pallas_call | solution.py:379
  27.5 0.5 collective-permute-done.1.side
  28.1 5.5 %up.1 = (f32[512,512]{1,0:T(8,128)S(1)}, f32[512,128]{1,0:T(8,128)S(1)}, bf16[512,2048]{1,0:T(8,128)(2,1)S(1)}, bf16[512,2048]{1,0:T(8,128)(2,1)S(1)}) custom-call(s32[2]{0:T(128)S(1)} %pad_add_fusion.place_ref, bf16[3,136,512]{2,1,0:T(8,128)(2,1)} %collective-permute-done.1.side, f32[7,7,512]{2,1,0:T(8,128)S(1)} %copy-done.1, ...), custom_call_target="tpu_custom_call" | custom-call | flops 4294967296 | bytes 9181184 | tf_op jit(solution)/shard_map/up/pallas_call | solution.py:379
  33.6 0.5 collective-permute-done.9.rest_2_
  34.1 0.2 collective-permute-done.10.rest_3_
  34.3 4.8 %back.1 = (f32[4,128,512]{2,1,0:T(8,128)S(1)}, bf16[4,128,512]{2,1,0:T(8,128)(2,1)S(1)}, bf16[3,128,512]{2,1,0:T(8,128)(2,1)S(1)}, bf16[3,128,512]{2,1,0:T(8,128...) custom-call(s32[2]{0:T(128)S(1)} %pad_add_fusion.place_ref, ...), custom_call_target="tpu_custom_call" | custom-call | flops 4294967296 | bytes 13195264 | tf_op jit(solution)/shard_map/back/pallas_call | solution.py:379
  39.1 2.5 %collective-permute-start.11 = (bf16[3,128,512]{2,1,0:T(8,128)(2,1)S(1)}, bf16[3,128,512]{2,1,0:T(8,128)(2,1)S(1)}, u32[]{:S(2)}, u32[]{:S(2)}) collective-permute-start(bf16[3,128,512]{2,1,0:T(8,128)(2,1)S(1)} %get-tuple-element.40), channel_id=1, source_target_pairs={{0,2},{2,0},{4,6},{6,4},{8,10},{10,8},{12,14},{14,12},{1,3},{3,1},... | collective-permute-start | bytes 1179656 | tf_op jit(solution)/shard_map/ppermute | solution.py:570
  41.6 3.5 %collective-permute-start.12 = (bf16[3,128,512]{2,1,0:T(8,128)(2,1)S(1)}, bf16[3,128,512]{2,1,0:T(8,128)(2,1)S(1)}, u32[]{:S(2)}, u32[]{:S(2)}) collective-permute-start(bf16[3,128,512]{2,1,0:T(8,128)(2,1)S(1)} %get-tuple-element.41), channel_id=1, source_target_pairs={{2,4},{4,2},{6,8},{8,6},{10,12},{12,10},{3,5},{5,3},{7,9},{9,7},{1... | collective-permute-start | bytes 1179656 | tf_op jit(solution)/shard_map/ppermute | solution.py:571
  45.2 1.4 %collective-permute-start.13 = (bf16[3,8,512]{2,1,0:T(8,128)(2,1)S(1)}, bf16[3,8,512]{2,1,0:T(8,128)(2,1)S(1)}, u32[]{:S(2)}, u32[]{:S(2)}) collective-permute-start(bf16[3,8,512]{2,1,0:T(8,128)(2,1)S(1)} %get-tuple-element.42), channel_id=1, source_target_pairs={{0,3},{1,2},{2,1},{3,0},{4,7},{5,6},{6,5},{7,4},{8,11},{9,10},{10,... | collective-permute-start | bytes 73736 | tf_op jit(solution)/shard_map/ppermute | solution.py:573
  46.6 1.9 %collective-permute-start.14 = (bf16[3,8,512]{2,1,0:T(8,128)(2,1)S(1)}, bf16[3,8,512]{2,1,0:T(8,128)(2,1)S(1)}, u32[]{:S(2)}, u32[]{:S(2)}) collective-permute-start(bf16[3,8,512]{2,1,0:T(8,128)(2,1)S(1)} %get-tuple-element.43), channel_id=1, source_target_pairs={{2,5},{3,4},{4,3},{5,2},{6,9},{7,8},{8,7},{9,6},{10,13},{11,12},{1... | collective-permute-start | bytes 73736 | tf_op jit(solution)/shard_map/ppermute | solution.py:574
  48.5 2.5 %inner_last.1.inner = f32[4,128,512]{2,1,0:T(8,128)S(1)} custom-call(s32[1]{0:T(128)} %bitcast.core_ref, bf16[4,128,512]{2,1,0:T(8,128)(2,1)S(1)} %get-tuple-element.44.middle, bf16[4,8,512]{2,1,0:T(8,128)(2,1)S(1)} %collective-permute-done.15.edge, f32[7,7,512]{2,1,0:T(8,128)S(1)} %copy-done.1, f32[4,128,512]{2,1,0:T(8,128)S(1)} %get-tuple-element.46.base_value), custom_call_target="tpu_custom_call" | custom-call | flops 1073741824 | bytes 2754560 | tf_op jit(solution)/shard_map/inner_last/pallas_call | solution.py:379
  51.1 8.2 %collective-permute-done.13.even_edge = bf16[3,8,512]{2,1,0:T(8,128)(2,1)S(1)} collective-permute-done((bf16[3,8,512]{2,1,0:T(8,128)(2,1)S(1)}, bf16[3,8,512]{2,1,0:T(8,128)(2,1)S(1)}, u32[]{:S(2)}, u32[]{:S(2)}) %collective-permute-start.13) | collective-permute-done | bytes 24608 | tf_op jit(solution)/shard_map/ppermute | solution.py:573
  59.3 0.3 collective-permute-done.11.even
  59.6 3.8 %last.1 = f32[128,4,512]{2,1,0:T(4,128)} custom-call(s32[2]{0:T(128)S(1)} %pad_add_fusion.place_ref, bf16[3,128,512]{2,1,0:T(8,128)(2,1)S(1)} %collective-permute-done.11.even, bf16[3,128,512]{2,1,0:T(8,128)(2,1)S(1)} %collective-permute-done.12.odd, bf16[3,8,512]{2,1,0:T(8,128)(2,1)S(1)} %collective-permute-done.13.even_edge, ...), custom_call_target="tpu_custom_call" | custom-call | flops 1 | bytes 1 | tf_op jit(solution)/shard_map/last/pallas_call | solution.py:379
  (42 shorter events, 0.4 us)
Async XLA Ops:
  0.0 8.1 %copy-start = (bf16[2048,512]{1,0:T(8,128)(2,1)S(1)}, bf16[2048,512]{1,0:T(8,128)(2,1)}, u32[]{:S(2)}) copy-start(bf16[2048,512]{1,0:T(8,128)(2,1)} %weight.1) | copy-start | bytes 6291460
  1.3 4.6 %collective-permute-start = (bf16[4,8,512]{2,1,0:T(8,128)(2,1)S(1)}, bf16[4,8,512]{2,1,0:T(8,128)(2,1)S(1)}, u32[]{:S(2)}, u32[]{:S(2)}) collective-permute-start(bf16[4,8,512]{2,1,0:T(8,128)(2,1)S(1)} %dynamic-slice_bitcast_fusion.2), channel_id=1, source_target_pairs={{0,1},{1,0},{2,3},{3,2},{4,5},{5,4},{6,7},{7,6},{8,9},{9,8},{10,11... | collective-permute-start | bytes 98312 | tf_op jit(solution)/shard_map/ppermute | solution.py:504
  2.9 16.4 %collective-permute-start.2 = (bf16[3,128,512]{2,1,0:T(8,128)(2,1)}, bf16[3,128,512]{2,1,0:T(8,128)(2,1)S(1)}, u32[]{:S(2)}, u32[]{:S(2)}) collective-permute-start(bf16[3,128,512]{2,1,0:T(8,128)(2,1)} %get-tuple-element.47), channel_id=1, source_target_pairs={{2,4},{4,2},{6,8},{8,6},{10,12},{12,10},{3,5},{5,3},{7,9},{9,7},{1... | collective-permute-start | bytes 1179656 | tf_op jit(solution)/shard_map/ppermute | solution.py:503
  5.9 5.7 %copy-start.2 = (bf16[4,8,512]{2,1,0:T(8,128)(2,1)}, bf16[4,8,512]{2,1,0:T(8,128)(2,1)S(1)}, u32[]{:S(2)}) copy-start(bf16[4,8,512]{2,1,0:T(8,128)(2,1)S(1)} %collective-permute-done.edge) | copy-start | bytes 98308
  6.7 21.3 %collective-permute-start.1 = (bf16[3,136,512]{2,1,0:T(8,128)(2,1)}, bf16[3,136,512]{2,1,0:T(8,128)(2,1)}, u32[]{:S(2)}, u32[]{:S(2)}) collective-permute-start(bf16[3,136,512]{2,1,0:T(8,128)(2,1)} %pad_maximum_fusion), channel_id=1, source_target_pairs={{0,2},{2,0},{4,6},{6,4},{8,10},{10,8},{12,14},{14,12},{1,3},{3,1},... | collective-permute-start | bytes 1253384 | tf_op jit(solution)/shard_map/ppermute | solution.py:508
  11.5 4.1 %collective-permute-start.4 = (bf16[160,512]{1,0:T(8,128)(2,1)}, bf16[160,512]{1,0:T(8,128)(2,1)S(1)}, u32[]{:S(2)}, u32[]{:S(2)}) collective-permute-start(bf16[160,512]{1,0:T(8,128)(2,1)} %get-tuple-element.28), channel_id=1, source_target_pairs={{0,1},{1,0},{2,3},{3,2},{4,5},{5,4},{6,7},{7,6},{8,9},{9,8},{10,11... | collective-permute-start | bytes 491528 | tf_op jit(solution)/shard_map/ppermute | solution.py:442
  12.2 3.4 %collective-permute-start.5 = (bf16[160,512]{1,0:T(8,128)(2,1)}, bf16[160,512]{1,0:T(8,128)(2,1)S(1)}, u32[]{:S(2)}, u32[]{:S(2)}) collective-permute-start(bf16[160,512]{1,0:T(8,128)(2,1)} %get-tuple-element.29), channel_id=1, source_target_pairs={{0,1},{1,0},{2,3},{3,2},{4,5},{5,4},{6,7},{7,6},{8,9},{9,8},{10,11... | collective-permute-start | bytes 491528 | tf_op jit(solution)/shard_map/ppermute | solution.py:442
  12.3 3.3 %collective-permute-start.3 = (bf16[192,512]{1,0:T(8,128)(2,1)}, bf16[192,512]{1,0:T(8,128)(2,1)S(1)}, u32[]{:S(2)}, u32[]{:S(2)}) collective-permute-start(bf16[192,512]{1,0:T(8,128)(2,1)} %get-tuple-element.27), channel_id=1, source_target_pairs={{0,1},{1,0},{2,3},{3,2},{4,5},{5,4},{6,7},{7,6},{8,9},{9,8},{10,11... | collective-permute-start | bytes 589832 | tf_op jit(solution)/shard_map/ppermute | solution.py:442
  12.9 3.9 %copy-start.1 = (f32[7,7,512]{2,1,0:T(8,128)S(1)}, f32[7,7,512]{2,1,0:T(8,128)}, u32[]{:S(2)}) copy-start(f32[7,7,512]{2,1,0:T(8,128)} %kernel.9) | copy-start | bytes 301060
  12.9 3.9 %copy-start.3 = (bf16[4,8,512]{2,1,0:T(8,128)(2,1)S(1)}, bf16[4,8,512]{2,1,0:T(8,128)(2,1)}, u32[]{:S(2)}) copy-start(bf16[4,8,512]{2,1,0:T(8,128)(2,1)} %copy-done.2) | copy-start | bytes 98308
  12.9 3.9 %copy-start.4 = (f32[512]{0:T(512)S(1)}, f32[512]{0:T(512)}, u32[]{:S(2)}) copy-start(f32[512]{0:T(512)} %param.16) | copy-start | bytes 6148
  16.8 11.3 %copy-start.7 = (f32[2048]{0:T(1024)S(1)}, f32[2048]{0:T(1024)}, u32[]{:S(2)}) copy-start(f32[2048]{0:T(1024)} %param.20) | copy-start | bytes 24580
  16.8 11.3 %copy-start.8 = (f32[512]{0:T(512)S(1)}, f32[512]{0:T(512)}, u32[]{:S(2)}) copy-start(f32[512]{0:T(512)} %param.18) | copy-start | bytes 6148
  16.8 11.2 %copy-start.9 = (f32[512]{0:T(512)S(1)}, f32[512]{0:T(512)}, u32[]{:S(2)}) copy-start(f32[512]{0:T(512)} %param.17) | copy-start | bytes 6148
  19.3 6.2 %collective-permute-start.6 = (bf16[3,8,512]{2,1,0:T(8,128)(2,1)S(1)}, bf16[3,8,512]{2,1,0:T(8,128)(2,1)S(1)}, u32[]{:S(2)}, u32[]{:S(2)}) collective-permute-start(bf16[3,8,512]{2,1,0:T(8,128)(2,1)S(1)} %constant_dynamic-slice_fusion), channel_id=1, source_target_pairs={{0,1},{1,0},{2,3},{3,2},{4,5},{5,4},{6,7},{7,6},{8,9},{9,8},{10,11... | collective-permute-start | bytes 73736 | tf_op jit(solution)/shard_map/ppermute | solution.py:527
  19.5 14.7 %collective-permute-start.7 = (bf16[4,32,512]{2,1,0:T(8,128)(2,1)S(1)}, bf16[4,32,512]{2,1,0:T(8,128)(2,1)S(1)}, u32[]{:S(2)}, u32[]{:S(2)}) collective-permute-start(bf16[4,32,512]{2,1,0:T(8,128)(2,1)S(1)} %get-tuple-element.30), channel_id=1, source_target_pairs={{0,0},{1,8},{2,2},{3,10},{4,4},{5,12},{6,6},{7,14},{8,1},{9,9},{10... | collective-permute-start | bytes 393224 | tf_op jit(solution)/shard_map/ppermute | solution.py:467
  22.4 11.2 %collective-permute-start.8 = (bf16[4,32,512]{2,1,0:T(8,128)(2,1)S(1)}, bf16[4,32,512]{2,1,0:T(8,128)(2,1)S(1)}, u32[]{:S(2)}, u32[]{:S(2)}) collective-permute-start(bf16[4,32,512]{2,1,0:T(8,128)(2,1)S(1)} %get-tuple-element.37), channel_id=1, source_target_pairs={{0,2},{1,10},{2,4},{3,12},{4,6},{5,14},{6,0},{7,8},{8,3},{9,11},{1... | collective-permute-start | bytes 393224 | tf_op jit(solution)/shard_map/ppermute | solution.py:467
  23.9 10.2 %collective-permute-start.9 = (bf16[4,32,512]{2,1,0:T(8,128)(2,1)S(1)}, bf16[4,32,512]{2,1,0:T(8,128)(2,1)S(1)}, u32[]{:S(2)}, u32[]{:S(2)}) collective-permute-start(bf16[4,32,512]{2,1,0:T(8,128)(2,1)S(1)} %get-tuple-element.38), channel_id=1, source_target_pairs={{0,4},{1,12},{2,6},{3,14},{4,0},{5,8},{6,2},{7,10},{8,5},{9,13},{1... | collective-permute-start | bytes 393224 | tf_op jit(solution)/shard_map/ppermute | solution.py:467
  25.5 8.7 %collective-permute-start.10 = (bf16[4,32,512]{2,1,0:T(8,128)(2,1)S(1)}, bf16[4,32,512]{2,1,0:T(8,128)(2,1)S(1)}, u32[]{:S(2)}, u32[]{:S(2)}) collective-permute-start(bf16[4,32,512]{2,1,0:T(8,128)(2,1)S(1)} %get-tuple-element.39), channel_id=1, source_target_pairs={{0,6},{1,14},{2,0},{3,8},{4,2},{5,10},{6,4},{7,12},{8,7},{9,15},{1... | collective-permute-start | bytes 393224 | tf_op jit(solution)/shard_map/ppermute | solution.py:467
  28.0 6.2 %copy-start.5 = (bf16[512,2048]{1,0:T(8,128)(2,1)S(1)}, bf16[512,2048]{1,0:T(8,128)(2,1)}, u32[]{:S(2)}) copy-start(bf16[512,2048]{1,0:T(8,128)(2,1)} %w_in.1) | copy-start | bytes 6291460
  28.0 6.2 %copy-start.6 = (bf16[2048,512]{1,0:T(8,128)(2,1)S(1)}, bf16[2048,512]{1,0:T(8,128)(2,1)}, u32[]{:S(2)}) copy-start(bf16[2048,512]{1,0:T(8,128)(2,1)} %w_out.1) | copy-start | bytes 6291460
  28.1 6.2 %copy-start.10 = (f32[512]{0:T(512)S(1)}, f32[512]{0:T(512)}, u32[]{:S(2)}) copy-start(f32[512]{0:T(512)} %param.22) | copy-start | bytes 6148
  28.1 6.2 %copy-start.11 = (f32[512]{0:T(512)S(1)}, f32[512]{0:T(512)}, u32[]{:S(2)}) copy-start(f32[512]{0:T(512)} %param.23) | copy-start | bytes 6148
  39.1 20.5 %collective-permute-start.11 = (bf16[3,128,512]{2,1,0:T(8,128)(2,1)S(1)}, bf16[3,128,512]{2,1,0:T(8,128)(2,1)S(1)}, u32[]{:S(2)}, u32[]{:S(2)}) collective-permute-start(bf16[3,128,512]{2,1,0:T(8,128)(2,1)S(1)} %get-tuple-element.40), channel_id=1, source_target_pairs={{0,2},{2,0},{4,6},{6,4},{8,10},{10,8},{12,14},{14,12},{1,3},{3,1},... | collective-permute-start | bytes 1179656 | tf_op jit(solution)/shard_map/ppermute | solution.py:570
  41.6 18.0 %collective-permute-start.12 = (bf16[3,128,512]{2,1,0:T(8,128)(2,1)S(1)}, bf16[3,128,512]{2,1,0:T(8,128)(2,1)S(1)}, u32[]{:S(2)}, u32[]{:S(2)}) collective-permute-start(bf16[3,128,512]{2,1,0:T(8,128)(2,1)S(1)} %get-tuple-element.41), channel_id=1, source_target_pairs={{2,4},{4,2},{6,8},{8,6},{10,12},{12,10},{3,5},{5,3},{7,9},{9,7},{1... | collective-permute-start | bytes 1179656 | tf_op jit(solution)/shard_map/ppermute | solution.py:571
  45.1 3.4 %collective-permute-start.15 = (bf16[4,8,512]{2,1,0:T(8,128)(2,1)S(1)}, bf16[4,8,512]{2,1,0:T(8,128)(2,1)S(1)}, u32[]{:S(2)}, u32[]{:S(2)}) collective-permute-start(bf16[4,8,512]{2,1,0:T(8,128)(2,1)S(1)} %get-tuple-element.45), channel_id=1, source_target_pairs={{0,1},{1,0},{2,3},{3,2},{4,5},{5,4},{6,7},{7,6},{8,9},{9,8},{10,11... | collective-permute-start | bytes 98312 | tf_op jit(solution)/shard_map/ppermute | solution.py:572
  45.2 14.1 %collective-permute-start.13 = (bf16[3,8,512]{2,1,0:T(8,128)(2,1)S(1)}, bf16[3,8,512]{2,1,0:T(8,128)(2,1)S(1)}, u32[]{:S(2)}, u32[]{:S(2)}) collective-permute-start(bf16[3,8,512]{2,1,0:T(8,128)(2,1)S(1)} %get-tuple-element.42), channel_id=1, source_target_pairs={{0,3},{1,2},{2,1},{3,0},{4,7},{5,6},{6,5},{7,4},{8,11},{9,10},{10,... | collective-permute-start | bytes 73736 | tf_op jit(solution)/shard_map/ppermute | solution.py:573
  46.6 12.7 %collective-permute-start.14 = (bf16[3,8,512]{2,1,0:T(8,128)(2,1)S(1)}, bf16[3,8,512]{2,1,0:T(8,128)(2,1)S(1)}, u32[]{:S(2)}, u32[]{:S(2)}) collective-permute-start(bf16[3,8,512]{2,1,0:T(8,128)(2,1)S(1)} %get-tuple-element.43), channel_id=1, source_target_pairs={{2,5},{3,4},{4,3},{5,2},{6,9},{7,8},{8,7},{9,6},{10,13},{11,12},{1... | collective-permute-start | bytes 73736 | tf_op jit(solution)/shard_map/ppermute | solution.py:574
